TPU v7x, 32 devices: a whole 2x2x4 slice. The times are simulated.
32 devices in a mesh: dp: 8 (over y, x, core), tensor: 4 (over z).
Axes of the slice: x: 2, y: 2, z: 4, core: 2. Of those that a mesh axis runs over, the one named last changes fastest.
Arguments:
- tokens: bfloat16 [8192, 2048], P(('dp', 'tensor')), may hold values from -6 to 6
- seq_start: int32 [8192], P('dp'), may hold values from 0 to 8191, as said below
- proj_weight: bfloat16 [2048, 3, 2048], P('dp', None, 'tensor'), may hold values from -0.125 to 0.125
- proj_bias: bfloat16 [3, 8, 256], P(None, 'tensor', 'dp'), may hold values from -3 to 3
- out_weight: bfloat16 [2048, 2048], P('tensor', 'dp'), may hold values from -1.5 to 1.5
- up_weight: bfloat16 [2048, 8192], P('dp', 'tensor'), may hold values from -0.125 to 0.125
- up_bias: bfloat16 [4, 2048], P('tensor', 'dp'), may hold values from -3 to 3
- down_weight: bfloat16 [8192, 2048], P('tensor', 'dp'), may hold values from -0.0625 to 0.0625
- norm_gains: bfloat16 [2, 2048], P(None, ('dp', 'tensor')), may hold values from 0.099609375 to 1.8984375
- biases: bfloat16 [4, 2048], P(None, ('dp', 'tensor')), may hold values from -3 to 3
- cotangent: bfloat16 [8192, 2048], P(('dp', 'tensor')), may hold values from -6 to 6
Outputs:
- output: bfloat16 [8192, 2048], P(('dp', 'tensor'))
- input_grad: float32 [8192, 2048], P(('dp', 'tensor'))
- proj_grad: float32 [2048, 3, 2048], P('dp', None, 'tensor')
- proj_bias_grad: float32 [3, 8, 256], P(None, 'tensor', 'dp')
- out_grad: float32 [2048, 2048], P('tensor', 'dp')
- up_grad: float32 [2048, 8192], P('dp', 'tensor')
- up_bias_grad: float32 [4, 2048], P('tensor', 'dp')
- down_grad: float32 [8192, 2048], P('tensor', 'dp')
- gains_grad: float32 [2, 2048], P(None, ('dp', 'tensor'))
- biases_grad: float32 [4, 2048], P(None, ('dp', 'tensor'))
Inputs may be any that keep to these rules, and one draw needn't show every extreme that they name: seq_start never falls along the tokens, is at most the token's own index, and every sequence lies inside one aligned block of 1024 tokens (the tokens of one index of dp); some block other than the last holds a single sequence of 1024 tokens, the others hold sequences of uneven lengths, and the last token begins a sequence of its own.
All inputs are finite; a program needn't handle non-finite values.
Results may differ from a plain program's by a relative error of at most 0.012.
Values may be sent and summed in bfloat16 or wider, within the bound.
No kernel may reach another device: no remote copies, remote signals or barrier semaphores. Data moves between devices by JAX's collectives and lax.ppermute only.
A program may use at most 192 MiB of HBM per device.

v0:
```python
import jax
import jax.numpy as jnp
from jax import lax
from jax.sharding import PartitionSpec as P

ROT = 64


EPSILON = 1e-05
ROTARY_BASE = 10000.0


def layer_norm(values, gain_row, shift_row):
    centered = values - jnp.mean(values, axis=-1, keepdims=True)
    spread = jnp.mean(centered * centered, axis=-1, keepdims=True)
    return centered * lax.rsqrt(spread + EPSILON) * gain_row + shift_row


def both_norms(values, gain_rows, shift_rows):
    return (
        layer_norm(values, gain_rows[0], shift_rows[0]),
        layer_norm(values, gain_rows[1], shift_rows[1]),
    )


def gelu_exact(inputs):
    return jax.nn.gelu(inputs, approximate=False)


def rotate(values, positions, turn_sign):
    half_rot = ROT // 2
    frequency = ROTARY_BASE ** (-(jnp.arange(half_rot, dtype=jnp.float32) * 2.0) / ROT)
    angles = positions.astype(jnp.float32)[:, None] * frequency[None, :]
    cosine = jnp.cos(angles)[:, None, :]
    sine_term = turn_sign * jnp.sin(angles)[:, None, :]
    first_half = values[..., :half_rot]
    second_half = values[..., half_rot:ROT]
    return jnp.concatenate(
        [
            first_half * cosine - second_half * sine_term,
            second_half * cosine + first_half * sine_term,
            values[..., ROT:],
        ],
        axis=-1,
    )


def masked_scores(query_block, key_rows, starts, block_start, block_rows):
    row_count = key_rows.shape[0]
    score_scale = key_rows.shape[-1] ** (-0.5)
    key_index = jnp.arange(row_count, dtype=jnp.int32)
    query_begin = lax.dynamic_slice_in_dim(starts, block_start, block_rows, 0)
    query_index = block_start + jnp.arange(block_rows, dtype=jnp.int32)
    scores = (
        jnp.einsum("qhe,khe->hqk", query_block, key_rows, preferred_element_type=jnp.float32)
        * score_scale
    )
    allowed = (query_begin[:, None] == starts[None, :]) & (
        key_index[None, :] <= query_index[:, None]
    )
    return jnp.where(allowed[None], scores, -1e30)


def attention_forward(queries, key_rows, value_rows, starts, block_rows):
    row_count = queries.shape[0]

    def one_block(block_start):
        query_block = lax.dynamic_slice_in_dim(queries, block_start, block_rows, 0)
        scores = masked_scores(query_block, key_rows, starts, block_start, block_rows)
        row_max = jnp.max(scores, axis=-1, keepdims=True)
        powers = jnp.exp(scores - row_max)
        row_total = jnp.sum(powers, axis=-1, keepdims=True)
        weights = (powers / row_total).astype(jnp.bfloat16)
        attended = jnp.einsum(
            "hqk,khe->qhe", weights, value_rows, preferred_element_type=jnp.float32
        )
        return (attended, (row_max + jnp.log(row_total))[..., 0])

    block_starts = jnp.arange(row_count // block_rows, dtype=jnp.int32) * block_rows
    attended, log_total = lax.map(one_block, block_starts)
    return (attended.reshape(queries.shape), log_total)


def attention_backward(queries, key_rows, value_rows, starts, log_total, grad_attended, block_rows):
    row_count = queries.shape[0]
    score_scale = queries.shape[-1] ** (-0.5)

    def one_block(accumulated, pieces):
        block_start, block_total = pieces
        grad_keys, grad_values = accumulated
        query_block = lax.dynamic_slice_in_dim(queries, block_start, block_rows, 0)
        grad_block = lax.dynamic_slice_in_dim(grad_attended, block_start, block_rows, 0)
        scores = masked_scores(query_block, key_rows, starts, block_start, block_rows)
        probs = jnp.exp(scores - block_total[..., None])
        grad_values = grad_values + jnp.einsum(
            "hqk,qhe->khe",
            probs.astype(jnp.bfloat16),
            grad_block,
            preferred_element_type=jnp.float32,
        )
        grad_probs = jnp.einsum(
            "qhe,khe->hqk", grad_block, value_rows, preferred_element_type=jnp.float32
        )
        inner_sum = jnp.sum(probs * grad_probs, axis=-1, keepdims=True)
        grad_scores = (probs * (grad_probs - inner_sum)).astype(jnp.bfloat16)
        grad_query = (
            jnp.einsum("hqk,khe->qhe", grad_scores, key_rows, preferred_element_type=jnp.float32)
            * score_scale
        )
        grad_keys = (
            grad_keys
            + jnp.einsum(
                "hqk,qhe->khe", grad_scores, query_block, preferred_element_type=jnp.float32
            )
            * score_scale
        )
        return ((grad_keys, grad_values), grad_query)

    block_starts = jnp.arange(row_count // block_rows, dtype=jnp.int32) * block_rows
    zeros_like_keys = jnp.zeros(queries.shape, jnp.float32)
    (grad_keys, grad_values), grad_queries = lax.scan(
        one_block, (zeros_like_keys, zeros_like_keys), (block_starts, log_total)
    )
    return (grad_queries.reshape(queries.shape), grad_keys, grad_values)


def shards(
    tokens,
    seq_start,
    proj_weight,
    proj_bias,
    out_weight,
    up_weight,
    up_bias,
    down_weight,
    norm_gains,
    biases,
    cotangent,
):
    local_rows = tokens.shape[0]
    row_count = local_rows * lax.axis_size("tensor")
    block_rows = min(512, row_count)
    dp_index = lax.axis_index("dp")
    gathered = (
        lax.all_gather(proj_weight, "dp", axis=0, tiled=True),
        lax.all_gather(proj_bias, "dp", axis=2, tiled=True),
        lax.all_gather(out_weight, "dp", axis=1, tiled=True),
        lax.all_gather(up_weight, "dp", axis=0, tiled=True),
        lax.all_gather(up_bias, "dp", axis=1, tiled=True),
        lax.all_gather(down_weight, "dp", axis=1, tiled=True),
    )
    joined_weight, joined_bias, mix_weight, hidden_weight, hidden_bias, back_weight = gathered
    gain_rows, shift_rows = (
        lax.all_gather(norm_gains, ("dp", "tensor"), axis=1, tiled=True),
        lax.all_gather(biases, ("dp", "tensor"), axis=1, tiled=True),
    )
    gain_rows = gain_rows.astype(jnp.float32)
    shift_rows = shift_rows.astype(jnp.float32)
    local_f = tokens.astype(jnp.float32)
    first_local, second_local = both_norms(local_f, gain_rows, shift_rows)
    first_rows, second_rows = (
        lax.all_gather(first_local.astype(jnp.bfloat16), "tensor", axis=0, tiled=True),
        lax.all_gather(second_local.astype(jnp.bfloat16), "tensor", axis=0, tiled=True),
    )
    heads_here = joined_bias.shape[1]
    head_size = joined_bias.shape[2]
    local_width = heads_here * head_size
    projected = jnp.einsum(
        "nd,dch->nch", first_rows, joined_weight, preferred_element_type=jnp.float32
    ) + joined_bias.astype(jnp.float32).reshape(3, local_width)
    positions = dp_index * row_count + jnp.arange(row_count, dtype=jnp.int32) - seq_start
    queries = rotate(
        projected[:, 0].reshape(row_count, heads_here, head_size), positions, 1.0
    ).astype(jnp.bfloat16)
    key_rows = rotate(
        projected[:, 1].reshape(row_count, heads_here, head_size), positions, 1.0
    ).astype(jnp.bfloat16)
    value_rows = projected[:, 2].reshape(row_count, heads_here, head_size).astype(jnp.bfloat16)
    attended, log_total = attention_forward(queries, key_rows, value_rows, seq_start, block_rows)
    attended = attended.reshape(row_count, local_width).astype(jnp.bfloat16)
    hidden = jnp.dot(
        second_rows, hidden_weight, preferred_element_type=jnp.float32
    ) + hidden_bias.astype(jnp.float32)
    activated = gelu_exact(hidden).astype(jnp.bfloat16)
    attn_part = jnp.dot(attended, mix_weight, preferred_element_type=jnp.float32)
    branches = lax.psum_scatter(
        attn_part + jnp.dot(activated, back_weight, preferred_element_type=jnp.float32),
        "tensor",
        scatter_dimension=0,
        tiled=True,
    )
    output = (local_f + branches + shift_rows[2] + shift_rows[3]).astype(jnp.bfloat16)
    grad_rows = lax.all_gather(cotangent, "tensor", axis=0, tiled=True)
    regathered = (
        lax.all_gather(proj_weight, "dp", axis=0, tiled=True),
        lax.all_gather(proj_bias, "dp", axis=2, tiled=True),
        lax.all_gather(out_weight, "dp", axis=1, tiled=True),
        lax.all_gather(up_weight, "dp", axis=0, tiled=True),
        lax.all_gather(up_bias, "dp", axis=1, tiled=True),
        lax.all_gather(down_weight, "dp", axis=1, tiled=True),
    )
    joined_again, _, mix_again, hidden_again, _, back_again = regathered
    grad_active = jnp.einsum("nd,fd->nf", grad_rows, back_again, preferred_element_type=jnp.float32)
    down_term = jnp.einsum("nf,nd->fd", activated, grad_rows, preferred_element_type=jnp.float32)
    _, gelu_back = jax.vjp(gelu_exact, hidden)
    grad_hidden = gelu_back(grad_active)[0].astype(jnp.bfloat16)
    up_term = jnp.einsum("nd,nf->df", second_rows, grad_hidden, preferred_element_type=jnp.float32)
    up_bias_term = jnp.sum(grad_hidden, axis=0, keepdims=True, dtype=jnp.float32)
    grad_second = jnp.einsum(
        "nf,df->nd", grad_hidden, hidden_again, preferred_element_type=jnp.float32
    )
    grad_attended = jnp.einsum(
        "nd,ed->ne", grad_rows, mix_again, preferred_element_type=jnp.float32
    ).astype(jnp.bfloat16)
    mix_term = jnp.einsum("ne,nd->ed", attended, grad_rows, preferred_element_type=jnp.float32)
    query_back, key_back, value_back = attention_backward(
        queries,
        key_rows,
        value_rows,
        seq_start,
        log_total,
        grad_attended.reshape(row_count, heads_here, head_size),
        block_rows,
    )
    query_back = rotate(query_back, positions, -1.0).reshape(row_count, local_width)
    key_back = rotate(key_back, positions, -1.0).reshape(row_count, local_width)
    grad_projected = jnp.stack(
        [query_back, key_back, value_back.reshape(row_count, local_width)], axis=1
    ).astype(jnp.bfloat16)
    joined_term = jnp.einsum(
        "nd,nch->dch", first_rows, grad_projected, preferred_element_type=jnp.float32
    )
    joined_bias_term = jnp.sum(grad_projected, axis=0, dtype=jnp.float32).reshape(
        3, heads_here, head_size
    )
    grad_first = jnp.einsum(
        "nch,dch->nd", grad_projected, joined_again, preferred_element_type=jnp.float32
    )
    grad_local = cotangent.astype(jnp.float32)
    first_sum, second_sum = (
        lax.psum_scatter(
            grad_first.astype(jnp.bfloat16), "tensor", scatter_dimension=0, tiled=True
        ).astype(jnp.float32),
        lax.psum_scatter(
            grad_second.astype(jnp.bfloat16), "tensor", scatter_dimension=0, tiled=True
        ).astype(jnp.float32),
    )
    _, norm_back = jax.vjp(both_norms, local_f, gain_rows, shift_rows)
    grad_norm_in, gain_term, shift_term = norm_back((first_sum, second_sum))
    input_grad = grad_local + grad_norm_in
    column_sums = jnp.sum(grad_local, axis=0)
    shift_term = jnp.concatenate([shift_term[:2], jnp.stack([column_sums, column_sums])], axis=0)
    gains_grad, biases_grad = (
        lax.psum_scatter(gain_term, ("dp", "tensor"), scatter_dimension=1, tiled=True),
        lax.psum_scatter(shift_term, ("dp", "tensor"), scatter_dimension=1, tiled=True),
    )
    summed = (
        lax.psum_scatter(joined_term, "dp", scatter_dimension=0, tiled=True),
        lax.psum_scatter(joined_bias_term, "dp", scatter_dimension=2, tiled=True),
        lax.psum_scatter(mix_term, "dp", scatter_dimension=1, tiled=True),
        lax.psum_scatter(up_term, "dp", scatter_dimension=0, tiled=True),
        lax.psum_scatter(up_bias_term, "dp", scatter_dimension=1, tiled=True),
        lax.psum_scatter(down_term, "dp", scatter_dimension=1, tiled=True),
    )
    return (
        output,
        input_grad,
        summed[0],
        summed[1],
        summed[2],
        summed[3],
        summed[4],
        summed[5],
        gains_grad,
        biases_grad,
    )


def solution(mesh):
    in_specs = (
        P(("dp", "tensor"), None),
        P("dp"),
        P("dp", None, "tensor"),
        P(None, "tensor", "dp"),
        P("tensor", "dp"),
        P("dp", "tensor"),
        P("tensor", "dp"),
        P("tensor", "dp"),
        P(None, ("dp", "tensor")),
        P(None, ("dp", "tensor")),
        P(("dp", "tensor"), None),
    )
    out_specs = (
        P(("dp", "tensor"), None),
        P(("dp", "tensor"), None),
        P("dp", None, "tensor"),
        P(None, "tensor", "dp"),
        P("tensor", "dp"),
        P("dp", "tensor"),
        P("tensor", "dp"),
        P("tensor", "dp"),
        P(None, ("dp", "tensor")),
        P(None, ("dp", "tensor")),
    )
    return jax.shard_map(shards, mesh=mesh, in_specs=in_specs, out_specs=out_specs, check_vma=False)
```

profile of v0, /device:TPU:0, one launch (start us, length us, event | category | flops | bytes accessed | tf_op | source)
XLA Modules:
  0.0 1526.5 jit_solution(3073304048536600505)
XLA Ops:
  8.7 71.2 %all-gather = bf16[32,64,2]{1,2,0:T(2,128)(2,1)S(1)} all-gather(bf16[1,64,2]{1,2,0:T(2,128)(2,1)} %bitcast.182), channel_id=1, replica_groups=mesh['dp'=8,'tensor'=4] {'dp','tensor'}, dimensions={0}, use_global_device_ids=true | all-gather | bytes 8448 | tf_op jit(solution)/shard_map/all_gather | solution.py:154
  80.0 66.0 %all-gather.1 = bf16[32,64,4]{1,2,0:T(4,128)(2,1)S(1)} all-gather(bf16[1,64,4]{1,2,0:T(4,128)(2,1)} %bitcast.181), channel_id=1, replica_groups=mesh['dp'=8,'tensor'=4] {'dp','tensor'}, dimensions={0}, use_global_device_ids=true | all-gather | bytes 16896 | tf_op jit(solution)/shard_map/all_gather | solution.py:155
  183.4 47.9 %all-gather.10.cloned.1.call-done = bf16[1024,2048]{1,0:T(8,128)(2,1)} async-done(((bf16[256,2048]{1,0:T(8,128)(2,1)}), bf16[1024,2048]{1,0:T(8,128)(2,1)}) %all-gather.10.cloned.1.call-update) | async-done | bytes 4194320 | tf_op jit(solution)/shard_map/all_gather | solution.py:162
  231.3 47.4 %all-gather.12.cloned.1.call-done = bf16[2048,3,512]{0,2,1:T(8,128)(2,1)} async-done(((bf16[256,3,512]{0,2,1:T(8,128)(2,1)}), bf16[2048,3,512]{0,2,1:T(8,128)(2,1)}) %all-gather.12.cloned.1.call-update) | async-done | bytes 6291472 | tf_op jit(solution)/shard_map/all_gather | solution.py:145
  324.7 20.5 %while.27 = (s32[]{:T(128)}, bf16[2,512,2,256]{3,1,2,0:T(8,128)(2,1)}, f32[2,2,512]{2,1,0:T(2,128)S(1)}, s32[2]{0:T(128)S(1)}, s32[1024]{0:T(1024)S(1)}, /*index...) while((s32[]{:T(128)}, ...), condition=%wide.region_5.6_spmd, body=%wide.region_2.5_spmd.sunk | while | flops 1087897088 | bytes 26786032 | solution.py:80
  345.3 30.6 %while.28 = (s32[]{:T(128)}, f32[1024,2,256]{0,2,1:T(8,128)S(1)}, f32[1024,2,256]{0,2,1:T(8,128)}, f32[2,512,2,256]{3,1,0,2:T(8,128)}, s32[2]{0:T(128)S(1)}, /*i...) while((s32[]{:T(128)}, f32[1024,2,256]{0,2,1:T(8,128)S(1)}, ...), condition=%wide.region_12.13_spmd.clone, body=%wide.region_10.12_spmd.clone.sunk | while | flops 2704539136 | bytes 94415280 | solution.py:121
  394.6 11.4 bitcast_convert_fusion
  416.0 14.7 fusion.78
  430.7 43.0 %all-gather.20.cloned.1.call-done = bf16[2048,2048]{1,0:T(8,128)(2,1)} async-done(((bf16[2048,256]{1,0:T(8,128)(2,1)}), bf16[2048,2048]{1,0:T(8,128)(2,1)}) %all-gather.20.cloned.1.call-update) | async-done | bytes 8388624 | tf_op jit(solution)/shard_map/all_gather | solution.py:150
  473.8 33.0 %convert_reduce_fusion = (f32[2048]{0:T(1024)S(1)}, bf16[1024,2048]{1,0:T(8,128)(2,1)S(1)}, f32[1024,2048]{1,0:T(8,128)}) fusion(f32[1024,2048]{1,0:T(8,128)} %fusion.78, f32[2048]{0:T(1024)S(1)} %bitcast.166, bf16[1024,2048]{1,0:T(8,128)(2,1)} %all-gather.22.cloned.1.call-done, bf16[2048,2048]{1,0:T(8,128)(2,1)} %all-gather.20.cloned.1.call-done), kind=kOutput, calls=%fused_computation.50 | convolution fusion | flops 8747218944 | bytes 33570816 | tf_op jit(solution)/shard_map/nd,fd->nf/dot_general | solution.py:203
  508.7 10.7 convolution_convert_fusion
  532.0 13.0 fusion.79
  556.7 75.8 %reduce-scatter.22.cloned.1.call-done = bf16[256,2048]{1,0:T(8,128)(2,1)} async-done(((bf16[1024,2048]{1,0:T(8,128)(2,1)}), bf16[256,2048]{1,0:T(8,128)(2,1)}) %reduce-scatter.22.cloned.1.call-update) | async-done | bytes 1048592 | tf_op jit(solution)/shard_map/reduce_scatter | solution.py:244
  640.1 139.7 %reduce-scatter.20.cloned.1.call-done = f32[256,2048]{1,0:T(8,128)} async-done(((f32[1024,2048]{1,0:T(8,128)}), f32[256,2048]{1,0:T(8,128)}) %reduce-scatter.20.cloned.1.call-update) | async-done | bytes 2097168 | tf_op jit(solution)/shard_map/reduce_scatter | solution.py:186
  794.9 11.7 fusion.41
  806.7 15.3 %fusion.82 = f32[2048,2048]{1,0:T(8,128)} fusion(bf16[1024,2048]{1,0:T(8,128)(2,1)} %multiply_convert_fusion.1, bf16[1024,2048]{1,0:T(8,128)(2,1)} %all-gather.22.cloned.1.call-done), kind=kOutput, calls=%fused_computation.157 | convolution fusion | flops 8589934592 | bytes 25165824 | tf_op jit(solution)/shard_map/nf,nd->fd/dot_general | solution.py:204
  822.3 15.3 %fusion.81 = f32[2048,2048]{1,0:T(8,128)} fusion(bf16[1024,2048]{1,0:T(8,128)(2,1)} %all-gather.16.cloned.1.call-done, bf16[1024,2048]{1,0:T(8,128)(2,1)} %copy-done.45), kind=kOutput, calls=%fused_computation.156 | convolution fusion | flops 8589934592 | bytes 25165824 | tf_op jit(solution)/shard_map/nd,nf->df/dot_general | solution.py:207
  839.2 16.9 %reduce-scatter.36.cloned.1.call-done = f32[256,1]{1,0:T(8,128)} async-done(((f32[2048,1]{1,0:T(8,128)}), f32[256,1]{1,0:T(8,128)}) %reduce-scatter.36.cloned.1.call-update) | async-done | bytes 1040
  857.6 138.1 %reduce-scatter.38.cloned.1.call-done = f32[64,2]{1,0:T(8,128)} async-done(((f32[2048,2]{1,0:T(8,128)}), f32[64,2]{1,0:T(8,128)}) %reduce-scatter.38.cloned.1.call-update) | async-done | bytes 528
  997.1 134.5 %reduce-scatter.40.cloned.1.call-done = f32[64,4]{1,0:T(8,128)} async-done(((f32[2048,4]{1,0:T(8,128)}), f32[64,4]{1,0:T(8,128)}) %reduce-scatter.40.cloned.1.call-update) | async-done | bytes 1040
  1133.1 50.1 %reduce-scatter.28.cloned.1.call-done = f32[512,256]{1,0:T(8,128)} async-done(((f32[512,2048]{1,0:T(8,128)}), f32[512,256]{1,0:T(8,128)}) %reduce-scatter.28.cloned.1.call-update) | async-done | bytes 524304 | tf_op jit(solution)/shard_map/reduce_scatter | solution.py:260
  1183.2 96.0 %reduce-scatter.26.cloned.1.call-done = f32[256,3,512]{2,0,1:T(8,128)} async-done(((f32[2048,3,512]{2,0,1:T(8,128)}), f32[256,3,512]{2,0,1:T(8,128)}) %reduce-scatter.26.cloned.1.call-update) | async-done | bytes 1572880 | tf_op jit(solution)/shard_map/reduce_scatter | solution.py:258
  1279.2 120.0 %reduce-scatter.32.cloned.1.call-done = f32[2048,256]{1,0:T(8,128)} async-done(((f32[2048,2048]{1,0:T(8,128)}), f32[2048,256]{1,0:T(8,128)}) %reduce-scatter.32.cloned.1.call-update) | async-done | bytes 2097168 | tf_op jit(solution)/shard_map/reduce_scatter | solution.py:263
  1399.2 120.2 %reduce-scatter.30.cloned.1.call-done = f32[256,2048]{1,0:T(8,128)} async-done(((f32[2048,2048]{1,0:T(8,128)}), f32[256,2048]{1,0:T(8,128)}) %reduce-scatter.30.cloned.1.call-update) | async-done | bytes 2097168 | tf_op jit(solution)/shard_map/reduce_scatter | solution.py:261
  (275 shorter events, 211.1 us)
Async XLA Ops:
  7.2 143.3 %copy-start.1 = (bf16[256,2048]{1,0:T(8,128)(2,1)S(1)}, bf16[256,2048]{1,0:T(8,128)(2,1)}, u32[]{:S(2)}) copy-start(bf16[256,2048]{1,0:T(8,128)(2,1)} %param.15) | copy-start | bytes 3145732
  7.2 145.4 %copy-start.28 = (bf16[256,3,512]{2,0,1:T(8,128)(2,1)S(1)}, bf16[256,3,512]{2,0,1:T(8,128)(2,1)}, u32[]{:S(2)}) copy-start(bf16[256,3,512]{2,0,1:T(8,128)(2,1)} %param.17) | copy-start | bytes 2359300
  7.2 170.0 %all-gather.14.cloned.1.call-start = ((), (), s32[]{:S(2)}) async-start(), calls=%async_computation.13 | async-start | bytes 2359296 | tf_op jit(solution)/shard_map/all_gather | solution.py:147
  7.9 169.3 %all-gather.22.cloned.1.call-start = ((), (), s32[]{:S(2)}) async-start(), calls=%async_computation.18 | async-start | bytes 5242880 | tf_op jit(solution)/shard_map/all_gather | solution.py:193
  8.7 222.6 %all-gather.10.cloned.1.call-start = ((), (), s32[]{:S(2)}) async-start(), calls=%async_computation.11 | async-start | bytes 5242880 | tf_op jit(solution)/shard_map/all_gather | solution.py:162
  152.5 126.2 %all-gather.12.cloned.1.call-start = ((), (), s32[]{:S(2)}) async-start(), calls=%async_computation.12 | async-start | bytes 7077888 | tf_op jit(solution)/shard_map/all_gather | solution.py:145
  153.8 252.3 %all-gather.16.cloned.1.call-start = ((), (), s32[]{:S(2)}) async-start(), calls=%async_computation.14 | async-start | bytes 5242880 | tf_op jit(solution)/shard_map/all_gather | solution.py:163
  154.4 261.6 %all-gather.18.cloned.1.call-start = ((), (), s32[]{:S(2)}) async-start(), calls=%async_computation.15 | async-start | bytes 9437184 | tf_op jit(solution)/shard_map/all_gather | solution.py:148
  155.0 318.8 %all-gather.20.cloned.1.call-start = ((), (), s32[]{:S(2)}) async-start(), calls=%async_computation.16 | async-start | bytes 9437184 | tf_op jit(solution)/shard_map/all_gather | solution.py:150
  155.7 400.9 %reduce-scatter.24.cloned.1.call-start = ((), (), s32[]{:S(2)}) async-start(), calls=%async_computation.20 | async-start | bytes 5242880 | tf_op jit(solution)/shard_map/reduce_scatter | solution.py:241
  406.0 226.5 %reduce-scatter.22.cloned.1.call-start = ((), (), s32[]{:S(2)}) async-start(), calls=%async_computation.19 | async-start | bytes 5242880 | tf_op jit(solution)/shard_map/reduce_scatter | solution.py:244
  519.4 260.4 %reduce-scatter.20.cloned.1.call-start = ((), (), s32[]{:S(2)}) async-start(), calls=%async_computation.17 | async-start | bytes 10485760 | tf_op jit(solution)/shard_map/reduce_scatter | solution.py:186
  550.7 84.5 %copy-start.39 = (f32[256]{0:T(256)S(1)}, f32[256]{0:T(256)}, u32[]{:S(2)}) copy-start(f32[256]{0:T(256)} %copy-done.38) | copy-start | bytes 3076
  550.8 286.9 %reduce-scatter.34.cloned.1.call-start = ((), (), s32[]{:S(2)}) async-start(), calls=%async_computation.25 | async-start | bytes 147456
  555.1 301.0 %reduce-scatter.36.cloned.1.call-start = ((), (), s32[]{:S(2)}) async-start(), calls=%async_computation.26 | async-start | bytes 1179648
  556.6 223.3 %copy-start.36 = (f32[1,2048]{1,0:T(1,128)S(1)}, f32[1,2048]{1,0:T(1,128)}, u32[]{:S(2)}) copy-start(f32[1,2048]{1,0:T(1,128)} %get-tuple-element.328) | copy-start | bytes 24580
  556.6 223.3 %copy-start.37 = (f32[1,2048]{1,0:T(1,128)S(1)}, f32[1,2048]{1,0:T(1,128)}, u32[]{:S(2)}) copy-start(f32[1,2048]{1,0:T(1,128)} %get-tuple-element.329) | copy-start | bytes 24580
  556.6 439.2 %reduce-scatter.38.cloned.1.call-start = ((), (), s32[]{:S(2)}) async-start(), calls=%async_computation.27 | async-start | bytes 1081344
  556.7 223.2 %copy-start.4 = (bf16[256,2048]{1,0:T(8,128)(2,1)S(1)}, bf16[256,2048]{1,0:T(8,128)(2,1)}, u32[]{:S(2)}) copy-start(bf16[256,2048]{1,0:T(8,128)(2,1)} %reduce-scatter.24.cloned.1.call-done) | copy-start | bytes 3145732
  640.1 491.6 %reduce-scatter.40.cloned.1.call-start = ((), (), s32[]{:S(2)}) async-start(), calls=%async_computation.28 | async-start | bytes 1081344
  786.3 396.9 %reduce-scatter.28.cloned.1.call-start = ((), (), s32[]{:S(2)}) async-start(), calls=%async_computation.22 | async-start | bytes 4718592 | tf_op jit(solution)/shard_map/reduce_scatter | solution.py:260
  793.1 486.1 %reduce-scatter.26.cloned.1.call-start = ((), (), s32[]{:S(2)}) async-start(), calls=%async_computation.21 | async-start | bytes 14155776 | tf_op jit(solution)/shard_map/reduce_scatter | solution.py:258
  806.6 592.6 %reduce-scatter.32.cloned.1.call-start = ((), (), s32[]{:S(2)}) async-start(), calls=%async_computation.24 | async-start | bytes 18874368 | tf_op jit(solution)/shard_map/reduce_scatter | solution.py:263
  822.0 697.4 %reduce-scatter.30.cloned.1.call-start = ((), (), s32[]{:S(2)}) async-start(), calls=%async_computation.23 | async-start | bytes 18874368 | tf_op jit(solution)/shard_map/reduce_scatter | solution.py:261
  (49 other events, 688.8 us)
Sparse Core Ops, SparseCore 0:
  9.9 30.8 all-gather.13
  42.3 81.0 all-gather.21
  152.7 78.5 all-gather.9
  233.6 45.0 all-gather.11
  280.7 80.7 all-gather.15
  363.2 52.7 all-gather.17
  417.9 55.8 all-gather.19
  476.0 76.7 reduce-scatter.23
  555.2 77.2 reduce-scatter.21
  634.7 145.1 reduce-scatter.19
  782.9 34.1 reduce-scatter.33
  820.1 35.9 reduce-scatter.35
  858.3 137.3 reduce-scatter.37
  997.9 133.7 reduce-scatter.39
  1135.5 47.6 reduce-scatter.27
  1187.1 92.0 reduce-scatter.25
  1283.2 115.9 reduce-scatter.31
  1403.2 116.1 reduce-scatter.29
where the time goes:
time: 1530 us
  waiting for transfers between devices  1040 us (68%)
  matrix products  177 us (12%)
  blocking collectives  155 us (10%)
  local copies, waits for them, and re-layouts  69.2 us (5%)
  other arithmetic  57.9 us (4%)
    unnamed x22, waiting for transfers between devices  293 us
    reduce_scatter x1, waiting for transfers between devices, shards(): lax.psum_scatter(attn_part + jnp.dot(activated, back_weight, preferred_el...  140 us
    reduce_scatter x1, waiting for transfers between devices, shards(): lax.psum_scatter(up_term, 'dp', scatter_dimension=0, tiled=True)  120 us
    reduce_scatter x1, waiting for transfers between devices, shards(): lax.psum_scatter(down_term, 'dp', scatter_dimension=1, tiled=True)  120 us
    reduce_scatter x1, waiting for transfers between devices, shards(): lax.psum_scatter(joined_term, 'dp', scatter_dimension=0, tiled=True)  96 us
    reduce_scatter x1, waiting for transfers between devices, shards(): lax.psum_scatter(grad_second.astype(jnp.bfloat16), 'tensor', scatter_dime...  75.8 us
    all_gather x1, blocking collectives, shards(): lax.all_gather(norm_gains, ('dp', 'tensor'), axis=1, tiled=True)  71.2 us
    all_gather x1, blocking collectives, shards(): lax.all_gather(biases, ('dp', 'tensor'), axis=1, tiled=True)  66 us
  transfers between devices with their start and end apart: 18, of which 13 were waited for; matrix products, arithmetic and copies ran while one was open for 19% of the time, Pallas kernels for 0%

commit v1 on v0

v1 whole, which is shorter than its diff:
```python
import jax
import jax.numpy as jnp
from jax import lax
from jax.sharding import PartitionSpec as P

ROT = 64
EPSILON = 1e-05
ROTARY_BASE = 10000.0
F32 = jnp.float32
BF16 = jnp.bfloat16


def xor_shift(values, axis, bit):
    size = lax.axis_size(axis)
    return lax.ppermute(values, axis, [(i, i ^ bit) for i in range(size)])


def is_power(n):
    return n & (n - 1) == 0


def butterfly(values, axis):
    size = lax.axis_size(axis)
    if not is_power(size):
        return lax.psum(values, axis)
    bit = 1
    while bit < size:
        values = values + xor_shift(values, axis, bit)
        bit *= 2
    return values


def dp_gather(shard):
    size = lax.axis_size("dp")
    if size != 8:
        return lax.all_gather(shard, "dp", axis=0, tiled=True)
    me = lax.axis_index("dp")
    rows = shard.shape[0]
    half = rows // 2
    from_x = xor_shift(shard, "dp", 2)
    from_y = xor_shift(shard, "dp", 4)
    far_a = xor_shift(from_x[:half], "dp", 4)
    far_b = xor_shift(from_y[half:], "dp", 2)
    mine = [(0, 0, shard), (2, 0, from_x), (4, 0, from_y), (6, 0, far_a), (6, half, far_b)]
    pieces = mine + [(p ^ 1, off, xor_shift(v, "dp", 1)) for p, off, v in mine]
    whole = jnp.zeros((size * rows,) + shard.shape[1:], shard.dtype)
    for p, off, v in pieces:
        start = (me ^ p) * rows + off
        whole = lax.dynamic_update_slice_in_dim(whole, v, start, 0)
    return whole


def dp_scatter(terms):
    size = lax.axis_size("dp")
    if size != 8:
        return lax.psum_scatter(terms, "dp", scatter_dimension=0, tiled=True).astype(F32)
    me = lax.axis_index("dp")
    core = me % 2
    chip = me // 2
    rows = terms.shape[0] // size
    half = rows // 2
    blocks = terms.reshape((4, 2, rows) + terms.shape[1:])
    away = lax.dynamic_index_in_dim(blocks, 1 - core, 1, keepdims=False)
    came = xor_shift(away, "dp", 1)

    def block(p):
        at = chip ^ p
        kept = lax.dynamic_index_in_dim(blocks, at, 0, keepdims=False)
        kept = lax.dynamic_index_in_dim(kept, core, 0, keepdims=False)
        return kept.astype(F32) + lax.dynamic_index_in_dim(came, at, 0, keepdims=False).astype(F32)

    far = block(3).astype(BF16)
    to_x = block(1)
    to_y = block(2)
    far_a = xor_shift(far[:half], "dp", 4)
    far_b = xor_shift(far[half:], "dp", 2)
    x_b = xor_shift(to_x[half:].astype(BF16), "dp", 2)
    y_a = xor_shift(to_y[:half].astype(BF16), "dp", 4)
    x_a = xor_shift((to_x[:half] + far_a.astype(F32)).astype(BF16), "dp", 2)
    y_b = xor_shift((to_y[half:] + far_b.astype(F32)).astype(BF16), "dp", 4)
    total = block(0)
    top = total[:half] + x_a.astype(F32) + y_a.astype(F32)
    low = total[half:] + x_b.astype(F32) + y_b.astype(F32)
    return jnp.concatenate([top, low], axis=0)


def standardize(values):
    values = values.astype(F32)
    centered = values - jnp.mean(values, axis=-1, keepdims=True)
    spread = jnp.mean(centered * centered, axis=-1, keepdims=True)
    scale = lax.rsqrt(spread + EPSILON)
    return centered * scale, scale


def rotate(values, positions, turn_sign):
    half_rot = ROT // 2
    frequency = ROTARY_BASE ** (-(jnp.arange(half_rot, dtype=F32) * 2.0) / ROT)
    angles = positions.astype(F32)[:, None] * frequency[None, :]
    cosine = jnp.cos(angles)[:, None, :]
    sine_term = turn_sign * jnp.sin(angles)[:, None, :]
    first_half = values[..., :half_rot]
    second_half = values[..., half_rot:ROT]
    return jnp.concatenate(
        [
            first_half * cosine - second_half * sine_term,
            second_half * cosine + first_half * sine_term,
            values[..., ROT:],
        ],
        axis=-1,
    )


def masked_scores(query_block, key_rows, starts, block_start, block_rows):
    row_count = key_rows.shape[0]
    score_scale = key_rows.shape[-1] ** (-0.5)
    key_index = jnp.arange(row_count, dtype=jnp.int32)
    query_begin = lax.dynamic_slice_in_dim(starts, block_start, block_rows, 0)
    query_index = block_start + jnp.arange(block_rows, dtype=jnp.int32)
    scores = (
        jnp.einsum("qhe,khe->hqk", query_block, key_rows, preferred_element_type=F32)
        * score_scale
    )
    allowed = (query_begin[:, None] == starts[None, :]) & (
        key_index[None, :] <= query_index[:, None]
    )
    return jnp.where(allowed[None], scores, -1e30)


def attention_forward(queries, key_rows, value_rows, starts, block_rows):
    row_count = queries.shape[0]

    def one_block(block_start):
        query_block = lax.dynamic_slice_in_dim(queries, block_start, block_rows, 0)
        scores = masked_scores(query_block, key_rows, starts, block_start, block_rows)
        row_max = jnp.max(scores, axis=-1, keepdims=True)
        powers = jnp.exp(scores - row_max)
        row_total = jnp.sum(powers, axis=-1, keepdims=True)
        weights = (powers / row_total).astype(BF16)
        attended = jnp.einsum("hqk,khe->qhe", weights, value_rows, preferred_element_type=F32)
        return (attended, (row_max + jnp.log(row_total))[..., 0])

    block_starts = jnp.arange(row_count // block_rows, dtype=jnp.int32) * block_rows
    attended, log_total = lax.map(one_block, block_starts)
    return (attended.reshape(queries.shape), log_total)


def attention_backward(queries, key_rows, value_rows, starts, log_total, grad_attended, block_rows):
    row_count = queries.shape[0]
    score_scale = queries.shape[-1] ** (-0.5)

    def one_block(accumulated, pieces):
        block_start, block_total = pieces
        grad_keys, grad_values = accumulated
        query_block = lax.dynamic_slice_in_dim(queries, block_start, block_rows, 0)
        grad_block = lax.dynamic_slice_in_dim(grad_attended, block_start, block_rows, 0)
        scores = masked_scores(query_block, key_rows, starts, block_start, block_rows)
        probs = jnp.exp(scores - block_total[..., None])
        grad_values = grad_values + jnp.einsum(
            "hqk,qhe->khe", probs.astype(BF16), grad_block, preferred_element_type=F32
        )
        grad_probs = jnp.einsum("qhe,khe->hqk", grad_block, value_rows, preferred_element_type=F32)
        inner_sum = jnp.sum(probs * grad_probs, axis=-1, keepdims=True)
        grad_scores = (probs * (grad_probs - inner_sum)).astype(BF16)
        grad_query = (
            jnp.einsum("hqk,khe->qhe", grad_scores, key_rows, preferred_element_type=F32)
            * score_scale
        )
        grad_keys = (
            grad_keys
            + jnp.einsum("hqk,qhe->khe", grad_scores, query_block, preferred_element_type=F32)
            * score_scale
        )
        return ((grad_keys, grad_values), grad_query)

    block_starts = jnp.arange(row_count // block_rows, dtype=jnp.int32) * block_rows
    zeros_like_keys = jnp.zeros(queries.shape, F32)
    (grad_keys, grad_values), grad_queries = lax.scan(
        one_block, (zeros_like_keys, zeros_like_keys), (block_starts, log_total)
    )
    return (grad_queries.reshape(queries.shape), grad_keys, grad_values)


def shards(
    tokens,
    seq_start,
    proj_weight,
    proj_bias,
    out_weight,
    up_weight,
    up_bias,
    down_weight,
    norm_gains,
    biases,
    cotangent,
):
    local_rows, width = tokens.shape
    n_dp, n_tensor = lax.axis_size("dp"), lax.axis_size("tensor")
    dp_index, tensor_index = lax.axis_index("dp"), lax.axis_index("tensor")
    row_count = local_rows * n_tensor
    block_rows = min(512, row_count)
    hidden_width = up_weight.shape[1]
    heads_here = proj_bias.shape[1]
    head_size = proj_bias.shape[2] * n_dp
    local_width = heads_here * head_size

    up_rows = dp_gather(up_weight)
    down_rows = dp_gather(down_weight.T)
    joined_rows = dp_gather(proj_weight.reshape(proj_weight.shape[0], 3 * local_width))
    mix_rows = dp_gather(out_weight.T)

    token_rows = lax.all_gather(tokens, "tensor", axis=0, tiled=True)
    grad_rows = lax.all_gather(cotangent, "tensor", axis=0, tiled=True)

    vectors = jnp.concatenate([norm_gains, biases], axis=0).reshape(1, -1)
    table = jnp.zeros((n_dp * n_tensor, vectors.shape[1]), BF16)
    table = lax.dynamic_update_slice(table, vectors, (dp_index * n_tensor + tensor_index, 0))
    shifts = jnp.concatenate([proj_bias.reshape(1, -1), up_bias.reshape(1, -1)], axis=1)
    shift_table = jnp.zeros((n_dp, shifts.shape[1]), BF16)
    shift_table = lax.dynamic_update_slice(shift_table, shifts, (dp_index, 0))
    table = butterfly(butterfly(table, "dp"), "tensor")
    shift_table = butterfly(shift_table, "dp")
    six_rows = (
        table.reshape(n_dp * n_tensor, 6, -1).transpose(1, 0, 2).reshape(6, width).astype(F32)
    )
    gain_rows, shift_rows = six_rows[:2], six_rows[2:]
    proj_part = proj_bias.size
    joined_bias = (
        shift_table[:, :proj_part]
        .reshape(n_dp, 3, heads_here, -1)
        .transpose(1, 2, 0, 3)
        .reshape(3 * local_width)
        .astype(F32)
    )
    hidden_bias = shift_table[:, proj_part:].reshape(hidden_width).astype(F32)

    xhat, _ = standardize(token_rows)
    first_rows = (xhat * gain_rows[0] + shift_rows[0]).astype(BF16)
    second_rows = (xhat * gain_rows[1] + shift_rows[1]).astype(BF16)

    hidden = jnp.dot(second_rows, up_rows, preferred_element_type=F32) + hidden_bias
    bell = lax.erf(hidden * (0.5**0.5))
    activated = (0.5 * hidden * (1.0 + bell)).astype(BF16)
    gelu_slope = 0.5 * (1.0 + bell) + hidden * jnp.exp(-0.5 * hidden * hidden) * 0.3989422804014327

    projected = jnp.dot(first_rows, joined_rows, preferred_element_type=F32) + joined_bias
    projected = projected.reshape(row_count, 3, local_width)
    positions = dp_index * row_count + jnp.arange(row_count, dtype=jnp.int32) - seq_start
    queries = rotate(
        projected[:, 0].reshape(row_count, heads_here, head_size), positions, 1.0
    ).astype(BF16)
    key_rows = rotate(
        projected[:, 1].reshape(row_count, heads_here, head_size), positions, 1.0
    ).astype(BF16)
    value_rows = projected[:, 2].reshape(row_count, heads_here, head_size).astype(BF16)
    attended, log_total = attention_forward(queries, key_rows, value_rows, seq_start, block_rows)
    attended = attended.reshape(row_count, local_width).astype(BF16)

    branch_terms = jnp.einsum(
        "ne,de->nd", attended, mix_rows, preferred_element_type=F32
    ) + jnp.einsum("nf,df->nd", activated, down_rows, preferred_element_type=F32)
    branches = lax.psum_scatter(
        branch_terms.astype(BF16), "tensor", scatter_dimension=0, tiled=True
    ).astype(F32)
    local_f = tokens.astype(F32)
    output = (local_f + branches + shift_rows[2] + shift_rows[3]).astype(BF16)

    grad_active = jnp.einsum("nd,df->nf", grad_rows, down_rows, preferred_element_type=F32)
    grad_hidden = (grad_active * gelu_slope).astype(BF16)
    down_term = jnp.einsum(
        "nd,nf->df", grad_rows, activated, preferred_element_type=F32
    ).astype(BF16)
    down_sum = dp_scatter(down_term)
    up_term = jnp.einsum(
        "nd,nf->df", second_rows, grad_hidden, preferred_element_type=F32
    ).astype(BF16)
    up_sum = dp_scatter(up_term)
    up_bias_term = jnp.sum(grad_hidden, axis=0, dtype=F32)
    grad_second = jnp.einsum("nf,df->nd", grad_hidden, up_rows, preferred_element_type=F32)
    grad_attended = jnp.einsum(
        "nd,de->ne", grad_rows, mix_rows, preferred_element_type=F32
    ).astype(BF16)
    mix_term = jnp.einsum(
        "nd,ne->de", grad_rows, attended, preferred_element_type=F32
    ).astype(BF16)
    mix_sum = dp_scatter(mix_term)
    query_back, key_back, value_back = attention_backward(
        queries,
        key_rows,
        value_rows,
        seq_start,
        log_total,
        grad_attended.reshape(row_count, heads_here, head_size),
        block_rows,
    )
    query_back = rotate(query_back, positions, -1.0).reshape(row_count, local_width)
    key_back = rotate(key_back, positions, -1.0).reshape(row_count, local_width)
    grad_projected = jnp.concatenate(
        [query_back, key_back, value_back.reshape(row_count, local_width)], axis=1
    ).astype(BF16)
    joined_term = jnp.einsum(
        "nd,nc->dc", first_rows, grad_projected, preferred_element_type=F32
    ).astype(BF16)
    joined_sum = dp_scatter(joined_term)
    joined_bias_term = jnp.sum(grad_projected, axis=0, dtype=F32)
    grad_first = jnp.einsum("nc,dc->nd", grad_projected, joined_rows, preferred_element_type=F32)

    back = grad_first * gain_rows[0] + grad_second * gain_rows[1]
    back = lax.psum_scatter(
        back.astype(BF16), "tensor", scatter_dimension=0, tiled=True
    ).astype(F32)
    xhat_local, scale_local = standardize(tokens)
    grad_norm_in = (
        back
        - jnp.mean(back, axis=-1, keepdims=True)
        - xhat_local * jnp.mean(back * xhat_local, axis=-1, keepdims=True)
    ) * scale_local
    grad_local = cotangent.astype(F32)
    input_grad = grad_local + grad_norm_in

    five = jnp.stack(
        [
            jnp.sum(grad_first * xhat, axis=0),
            jnp.sum(grad_second * xhat, axis=0),
            jnp.sum(grad_first, axis=0),
            jnp.sum(grad_second, axis=0),
            jnp.sum(grad_local, axis=0),
        ],
        axis=0,
    )
    shift_terms = jnp.concatenate([joined_bias_term, up_bias_term])[None]
    five, shift_terms = butterfly(butterfly(five, "dp"), "tensor"), butterfly(shift_terms, "dp")
    columns = norm_gains.shape[1]
    mine = lax.dynamic_slice_in_dim(five, (dp_index * n_tensor + tensor_index) * columns, columns, 1)
    gains_grad = mine[:2]
    biases_grad = jnp.concatenate([mine[2:], mine[4:]], axis=0)
    joined_bias_sum = lax.dynamic_slice_in_dim(
        shift_terms[0, : 3 * local_width].reshape(3, heads_here, head_size),
        dp_index * proj_bias.shape[2],
        proj_bias.shape[2],
        2,
    )
    up_bias_sum = lax.dynamic_slice_in_dim(
        shift_terms[:, 3 * local_width :], dp_index * up_bias.shape[1], up_bias.shape[1], 1
    )
    return (
        output,
        input_grad,
        joined_sum.reshape(proj_weight.shape),
        joined_bias_sum,
        mix_sum.T,
        up_sum,
        up_bias_sum,
        down_sum.T,
        gains_grad,
        biases_grad,
    )


def solution(mesh):
    in_specs = (
        P(("dp", "tensor"), None),
        P("dp"),
        P("dp", None, "tensor"),
        P(None, "tensor", "dp"),
        P("tensor", "dp"),
        P("dp", "tensor"),
        P("tensor", "dp"),
        P("tensor", "dp"),
        P(None, ("dp", "tensor")),
        P(None, ("dp", "tensor")),
        P(("dp", "tensor"), None),
    )
    out_specs = (
        P(("dp", "tensor"), None),
        P(("dp", "tensor"), None),
        P("dp", None, "tensor"),
        P(None, "tensor", "dp"),
        P("tensor", "dp"),
        P("dp", "tensor"),
        P("tensor", "dp"),
        P("tensor", "dp"),
        P(None, ("dp", "tensor")),
        P(None, ("dp", "tensor")),
    )
    return jax.shard_map(shards, mesh=mesh, in_specs=in_specs, out_specs=out_specs, check_vma=False)
```

time: 1530 us -> 689 us (0.45)
  waiting for transfers between devices: 1040 us -> 136 us
  blocking collectives: 155 us -> 0 us
  local copies, waits for them, and re-layouts: 69.2 us -> 222 us
  starting transfers between devices: 1.11 us -> 65.1 us
    reduce_scatter x7 -> x2, waiting for transfers between devices: 602 us -> 0.02 us  [the longest x1 0.02 us: shards(): lax.psum_scatter(branch_terms.astype(BF16), 'tensor', scatter_dimension=0...]
    unnamed x22 -> x4, waiting for transfers between devices: 293 us -> 0.73 us
    all_gather x4 -> x0, blocking collectives: 155 us -> none  [the longest x1 71.2 us: shards(): lax.all_gather(norm_gains, ('dp', 'tensor'), axis=1, tiled=True)]
    all_gather x6 -> x1, waiting for transfers between devices: 148 us -> 0.01 us  [shards(): token_rows = lax.all_gather(tokens, 'tensor', axis=0, tiled=True)]
    ppermute x0 -> x80, waiting for transfers between devices: none -> 136 us  [xor_shift(): return lax.ppermute(values, axis, [(i, i ^ bit) for i in range(size)])]
    ppermute x0 -> x80, starting transfers between devices: none -> 65 us  [xor_shift(): return lax.ppermute(values, axis, [(i, i ^ bit) for i in range(size)])]
    dynamic_update_slice x0 -> x42, local copies, waits for them, and re-layouts: none -> 57.8 us  [the longest x40 57.7 us: dp_gather(): whole = lax.dynamic_update_slice_in_dim(whole, v, start, 0)]
    dynamic_slice x0 -> x11, local copies, waits for them, and re-layouts: none -> 29 us  [the longest x6 19 us: dp_scatter(): away = lax.dynamic_index_in_dim(blocks, 1 - core, 1, keepdims=False)]
  transfers between devices with their start and end apart: 18 -> 84, of which waited for: 13 -> 26; matrix products, arithmetic and copies ran while one was open for 19% -> 55% of each run, Pallas kernels for 0% -> 0%
where the time goes in v1:
time: 689 us; the launch traced here: 681 us
  local copies, waits for them, and re-layouts  222 us (32%)
  matrix products  163 us (24%)
  waiting for transfers between devices  136 us (20%)
  other arithmetic  71.2 us (10%)
  starting transfers between devices  65.1 us (9%)
  between operations  15.3 us (2%)
  loops' own time  8.38 us (1%)
    ppermute x80, waiting for transfers between devices, xor_shift(): return lax.ppermute(values, axis, [(i, i ^ bit) for i in range(size)])  136 us
    ppermute x80, starting transfers between devices, xor_shift(): return lax.ppermute(values, axis, [(i, i ^ bit) for i in range(size)])  65 us
    dynamic_update_slice x40, local copies, waits for them, and re-layouts, dp_gather(): whole = lax.dynamic_update_slice_in_dim(whole, v, start, 0)  57.7 us
    unnamed x133, local copies, waits for them, and re-layouts  44.3 us
    dynamic_slice x6, local copies, waits for them, and re-layouts, dp_scatter(): away = lax.dynamic_index_in_dim(blocks, 1 - core, 1, keepdims=False)  19 us
    dot_general x1, matrix products, shards(): jnp.einsum('nf,df->nd', grad_hidden, up_rows, preferred_element_type=F32)  17.9 us
    dot_general x1, matrix products, shards(): jnp.einsum('nd,df->nf', grad_rows, down_rows, preferred_element_type=F32)  17 us
    dot_general x1, matrix products, shards(): jnp.dot(second_rows, up_rows, preferred_element_type=F32) + hidden_bias  16.9 us
  transfers between devices with their start and end apart: 84, of which 26 were waited for; matrix products, arithmetic and copies ran while one was open for 55% of the time, Pallas kernels for 0%

profile of v1, /device:TPU:0, one launch (start us, length us, event | category | flops | bytes accessed | tf_op | source)
XLA Modules:
  0.0 681.2 jit_solution(11050236762153446284)
XLA Ops:
  85.0 9.9 %collective-permute-done.6 = bf16[256,1536]{0,1:T(8,128)(2,1)} collective-permute-done((bf16[256,1536]{0,1:T(8,128)(2,1)}, bf16[256,1536]{0,1:T(8,128)(2,1)}, u32[]{:S(2)}, u32[]{:S(2)}) %collective-permute-start.6) | collective-permute-done | bytes 786464 | tf_op jit(solution)/shard_map/ppermute | solution.py:15
  101.2 17.4 %collective-permute-done.26 = bf16[256,2048]{1,0:T(8,128)(2,1)S(1)} collective-permute-done((bf16[256,2048]{1,0:T(8,128)(2,1)}, bf16[256,2048]{1,0:T(8,128)(2,1)S(1)}, u32[]{:S(2)}, u32[]{:S(2)}) %collective-permute-start.26) | collective-permute-done | bytes 1048608 | tf_op jit(solution)/shard_map/ppermute | solution.py:15
  127.5 11.7 %collective-permute-done.35 = bf16[256,2048]{0,1:T(8,128)(2,1)} collective-permute-done((bf16[256,2048]{0,1:T(8,128)(2,1)}, bf16[256,2048]{0,1:T(8,128)(2,1)}, u32[]{:S(2)}, u32[]{:S(2)}) %collective-permute-start.35) | collective-permute-done | bytes 1048608 | tf_op jit(solution)/shard_map/ppermute | solution.py:15
  162.7 6.6 collective-permute-done.28
  219.0 11.7 %convolution_add_fusion = f32[1024,1536]{1,0:T(8,128)} fusion(bf16[2048,1536]{0,1:T(8,128)(2,1)} %constant_dynamic-update-slice_fusion.30, f32[1536]{0:T(1024)S(1)} %copy-done.59, bf16[1024,2048]{1,0:T(8,128)(2,1)S(1)} %copy-done.4, f32[2048]{0:T(1024)S(1)} %copy-done.56, f32[2048]{0:T(1024)S(1)} %copy-done.54, f32[1024]{0:T(1024)S(1)} %add_rsqrt_fusion, ...), kind=kOutput, calls=%fused_computation.78 | convolution fusion | flops 6456606720 | bytes 16807936 | tf_op jit(solution)/shard_map/dot_general | solution.py:245
  230.7 6.5 copy.100
  273.1 20.1 %while.27 = (s32[]{:T(128)}, bf16[2,512,2,256]{3,1,2,0:T(8,128)(2,1)}, f32[2,2,512]{2,1,0:T(2,128)S(1)}, s32[2]{0:T(128)S(1)}, s32[1024]{0:T(1024)S(1)}, /*index...) while((s32[]{:T(128)}, ...), condition=%wide.region_5.6_spmd, body=%wide.region_2.5_spmd.sunk | while | flops 1087897088 | bytes 26786032 | solution.py:143
  293.2 6.2 convolution_convert_fusion.4
  299.4 30.9 %while.28 = (s32[]{:T(128)}, f32[1024,2,256]{0,2,1:T(8,128)S(1)}, f32[1024,2,256]{0,2,1:T(8,128)}, f32[2,512,2,256]{3,1,0,2:T(8,128)}, s32[2]{0:T(128)S(1)}, /*i...) while((s32[]{:T(128)}, f32[1024,2,256]{0,2,1:T(8,128)S(1)}, ...), condition=%wide.region_9.10_spmd.clone, body=%wide.region_7.9_spmd.clone.sunk | while | flops 2704539136 | bytes 94415280 | solution.py:177
  344.5 11.1 %fusion.88 = f32[1024,2048]{1,0:T(8,128)} fusion(bf16[2048,1536]{0,1:T(8,128)(2,1)} %constant_dynamic-update-slice_fusion.30, bf16[1024,512]{0,1:T(8,128)(2,1)S(1)} %bitcast.256, bf16[1024,512]{0,1:T(8,128)(2,1)S(1)} %bitcast.262, bf16[1024,512]{0,1:T(8,128)(2,1)S(1)} %bitcast.259), kind=kOutput, calls=%fused_computation.277 | convolution fusion | flops 6451888128 | bytes 17825792 | tf_op jit(solution)/shard_map/nc,dc->nd/dot_general | solution.py:305
  368.9 11.1 %convolution_convert_fusion.2 = bf16[2048,1536]{1,0:T(8,128)(2,1)S(1)} fusion(bf16[1024,512]{0,1:T(8,128)(2,1)S(1)} %bitcast.257, bf16[1024,512]{0,1:T(8,128)(2,1)S(1)} %bitcast.263, bf16[1024,512]{0,1:T(8,128)(2,1)S(1)} %bitcast.260, bf16[1024,2048]{1,0:T(8,128)(2,1)S(1)} %copy-done.5, f32[2048]{0:T(1024)S(1)} %copy-done.57, f32[2048]{0:T(1024)S(1)} %copy-done.55, ...), kind=kOutput, calls=%fused_computation.76 | convolution fusion | flops 6467616768 | bytes 13656064 | tf_op jit(solution)/shard_map/nd,nc->dc/dot_general | solution.py:300
  389.3 16.9 %multiply_convert_fusion.1 = (bf16[1024,2048]{1,0:T(8,128)(2,1)}, f32[1024,2048]{1,0:T(8,128)}) fusion(f32[2048]{0:T(1024)S(1)} %bitcast.276, bf16[2048,2048]{0,1:T(8,128)(2,1)} %constant_dynamic-update-slice_fusion.10, bf16[1024,2048]{1,0:T(8,128)(2,1)} %all-gather.3.cloned.1.call-done, f32[2048]{0:T(1024)S(1)} %copy-done.53, f32[2048]{0:T(1024)S(1)} %copy-done.52, ...), kind=kOutput, calls=%fused_computation.72 | convolution fusion | flops 8615100416 | bytes 25198592 | tf_op jit(solution)/shard_map/dot_general | solution.py:240
  406.2 17.0 %convert_reduce_fusion.1 = (f32[2048]{0:T(1024)S(1)}, bf16[1024,2048]{1,0:T(8,128)(2,1)}) fusion(f32[1024,2048]{1,0:T(8,128)} %get-tuple-element.356, f32[2048]{0:T(1024)S(1)} %bitcast.277, bf16[2048,2048]{0,1:T(8,128)(2,1)} %constant_dynamic-update-slice_fusion, bf16[1024,2048]{1,0:T(8,128)(2,1)S(1)} %copy-done.64), kind=kOutput, calls=%fused_computation.69 | convolution fusion | flops 8617195520 | bytes 25182208 | tf_op jit(solution)/shard_map/nd,df->nf/dot_general | solution.py:267
  423.2 17.9 %fusion.94 = (f32[2048]{0:T(1024)S(1)}, f32[2048]{0:T(1024)S(1)}, bf16[1024,2048]{1,0:T(8,128)(2,1)}, f32[2048]{0:T(1024)S(1)}, f32[2048]{0:T(1024)S(1)}) fusion(f32[1024]{0:T(1024)S(1)} %copy-done.61, f32[1024]{0:T(1024)S(1)} %copy-done.48, bf16[1024,2048]{1,0:T(8,128)(2,1)S(1)} %copy-done.6, f32[2048]{0:T(1024)S(1)} %copy-done.52, ...), kind=kOutput, calls=%fused_computation.279 | convolution fusion | flops 8617189376 | bytes 29417472 | tf_op jit(solution)/shard_map/nf,df->nd/dot_general | solution.py:278
  441.6 12.1 %convolution_convert_fusion = bf16[2048,2048]{0,1:T(8,128)(2,1)S(1)} fusion(bf16[1024,2048]{1,0:T(8,128)(2,1)} %get-tuple-element.355, bf16[1024,2048]{1,0:T(8,128)(2,1)} %all-gather.5.cloned.1.call-done), kind=kOutput, calls=%fused_computation.74 | convolution fusion | flops 8594128896 | bytes 16777216 | tf_op jit(solution)/shard_map/nd,nf->df/dot_general | solution.py:269
  460.2 11.4 %fusion.103 = f32[1024,2048]{1,0:T(8,128)S(1)} fusion(bf16[1024,2048]{1,0:T(8,128)(2,1)S(1)} %copy-done.65, bf16[2048,2048]{0,1:T(8,128)(2,1)} %constant_dynamic-update-slice_fusion), kind=kOutput, calls=%fused_computation.288 | convolution fusion | flops 8589934592 | bytes 20971520 | tf_op jit(solution)/shard_map/nf,df->nd/dot_general | solution.py:260
  471.6 14.2 %convolution_convert_fusion.1 = bf16[2048,2048]{1,0:T(8,128)(2,1)} fusion(bf16[1024,2048]{1,0:T(8,128)(2,1)} %get-tuple-element.358, bf16[1024,2048]{1,0:T(8,128)(2,1)S(1)} %copy-done.7, f32[2048]{0:T(1024)S(1)} %copy-done.53, f32[2048]{0:T(1024)S(1)} %copy-done.52, f32[1024]{0:T(1024)S(1)} %copy-done.61, f32[1024]{0:T(1024)S(1)} %copy-done.48), kind=kOutput, calls=%fused_computation.75 | convolution fusion | flops 8606711808 | bytes 16801792 | tf_op jit(solution)/shard_map/nd,nf->df/dot_general | solution.py:273
  514.4 6.3 copy.138
  539.2 7.9 %collective-permute-done.45 = bf16[128,1536]{0,1:T(8,128)(2,1)S(1)} collective-permute-done((bf16[128,1536]{0,1:T(8,128)(2,1)S(1)}, bf16[128,1536]{0,1:T(8,128)(2,1)S(1)}, u32[]{:S(2)}, u32[]{:S(2)}) %collective-permute-start.45) | collective-permute-done | bytes 393248 | tf_op jit(solution)/shard_map/ppermute | solution.py:15
  550.2 8.0 %collective-permute-done.49 = bf16[128,1536]{0,1:T(8,128)(2,1)S(1)} collective-permute-done((bf16[128,1536]{0,1:T(8,128)(2,1)S(1)}, bf16[128,1536]{0,1:T(8,128)(2,1)S(1)}, u32[]{:S(2)}, u32[]{:S(2)}) %collective-permute-start.49) | collective-permute-done | bytes 393248 | tf_op jit(solution)/shard_map/ppermute | solution.py:15
  561.6 6.1 collective-permute-done.47
  589.1 6.6 convert_add_fusion.8
  599.1 12.0 %collective-permute-done.69 = bf16[128,2048]{0,1:T(8,128)(2,1)S(1)} collective-permute-done((bf16[128,2048]{0,1:T(8,128)(2,1)S(1)}, bf16[128,2048]{0,1:T(8,128)(2,1)S(1)}, u32[]{:S(2)}, u32[]{:S(2)}) %collective-permute-start.69) | collective-permute-done | bytes 524320 | tf_op jit(solution)/shard_map/ppermute | solution.py:15
  637.1 21.0 %collective-permute-done.76 = f32[5,2048]{1,0:T(8,128)S(1)} collective-permute-done((f32[5,2048]{1,0:T(8,128)S(1)}, f32[5,2048]{1,0:T(8,128)S(1)}, u32[]{:S(2)}, u32[]{:S(2)}) %collective-permute-start.76) | collective-permute-done | bytes 40992 | tf_op jit(solution)/shard_map/ppermute | solution.py:15
  (568 shorter events, 407.9 us)
Async XLA Ops:
  7.2 207.0 %all-gather.3.cloned.1.call-start = ((), (), s32[]{:S(2)}) async-start(), calls=%async_computation.2 | async-start | bytes 5242880 | tf_op jit(solution)/shard_map/all_gather | solution.py:211
  7.9 285.3 %all-gather.5.cloned.1.call-start = ((), (), s32[]{:S(2)}) async-start(), calls=%async_computation.4 | async-start | bytes 5242880 | tf_op jit(solution)/shard_map/all_gather | solution.py:212
  8.0 60.5 %collective-permute-start.18 = (bf16[256,512]{0,1:T(8,128)(2,1)}, bf16[256,512]{0,1:T(8,128)(2,1)S(1)}, u32[]{:S(2)}, u32[]{:S(2)}) collective-permute-start(bf16[256,512]{0,1:T(8,128)(2,1)} %bitcast.271), channel_id=1, source_target_pairs={{0,16},{4,20},{8,24},{12,28},{16,0},{20,4},{24,8},{28,12},{1,17},{... | collective-permute-start | bytes 786440 | tf_op jit(solution)/shard_map/ppermute | solution.py:15
  11.0 59.0 %collective-permute-start.17 = (bf16[256,512]{0,1:T(8,128)(2,1)}, bf16[256,512]{0,1:T(8,128)(2,1)S(1)}, u32[]{:S(2)}, u32[]{:S(2)}) collective-permute-start(bf16[256,512]{0,1:T(8,128)(2,1)} %bitcast.272), channel_id=1, source_target_pairs={{0,8},{4,12},{8,0},{12,4},{16,24},{20,28},{24,16},{28,20},{1,9},{5... | collective-permute-start | bytes 786440 | tf_op jit(solution)/shard_map/ppermute | solution.py:15
  12.5 65.1 %collective-permute-start.21 = (bf16[256,512]{0,1:T(8,128)(2,1)}, bf16[256,512]{0,1:T(8,128)(2,1)S(1)}, u32[]{:S(2)}, u32[]{:S(2)}) collective-permute-start(bf16[256,512]{0,1:T(8,128)(2,1)} %bitcast.273), channel_id=1, source_target_pairs={{0,4},{4,0},{8,12},{12,8},{16,20},{20,16},{24,28},{28,24},{1,5},{5... | collective-permute-start | bytes 786440 | tf_op jit(solution)/shard_map/ppermute | solution.py:15
  14.1 29.1 %collective-permute-start.14 = (bf16[8,448]{1,0:T(8,128)(2,1)S(1)}, bf16[8,448]{1,0:T(8,128)(2,1)S(1)}, u32[]{:S(2)}, u32[]{:S(2)}) collective-permute-start(bf16[8,448]{1,0:T(8,128)(2,1)S(1)} %dynamic_update_slice.153), channel_id=1, source_target_pairs={{0,4},{4,0},{8,12},{12,8},{16,20},{20,16},{24,28},{28,24},{1,5},{5... | collective-permute-start | bytes 21512 | tf_op jit(solution)/shard_map/ppermute | solution.py:15
  15.6 605.3 %reduce-scatter.5.cloned.1.call-start = ((), (), s32[]{:S(2)}) async-start(), calls=%async_computation.5 | async-start | bytes 5242880 | tf_op jit(solution)/shard_map/reduce_scatter | solution.py:308
  77.7 40.9 %collective-permute-start.26 = (bf16[256,2048]{1,0:T(8,128)(2,1)}, bf16[256,2048]{1,0:T(8,128)(2,1)S(1)}, u32[]{:S(2)}, u32[]{:S(2)}) collective-permute-start(bf16[256,2048]{1,0:T(8,128)(2,1)} %param.20), channel_id=1, source_target_pairs={{0,8},{4,12},{8,0},{12,4},{16,24},{20,28},{24,16},{28,20},{1,9},{5... | collective-permute-start | bytes 3145736 | tf_op jit(solution)/shard_map/ppermute | solution.py:15
  78.9 42.3 %collective-permute-start.27 = (bf16[256,2048]{1,0:T(8,128)(2,1)}, bf16[256,2048]{1,0:T(8,128)(2,1)}, u32[]{:S(2)}, u32[]{:S(2)}) collective-permute-start(bf16[256,2048]{1,0:T(8,128)(2,1)} %param.20), channel_id=1, source_target_pairs={{0,16},{4,20},{8,24},{12,28},{16,0},{20,4},{24,8},{28,12},{1,17},{... | collective-permute-start | bytes 3145736 | tf_op jit(solution)/shard_map/ppermute | solution.py:15
  83.1 56.1 %collective-permute-start.35 = (bf16[256,2048]{0,1:T(8,128)(2,1)}, bf16[256,2048]{0,1:T(8,128)(2,1)}, u32[]{:S(2)}, u32[]{:S(2)}) collective-permute-start(bf16[256,2048]{0,1:T(8,128)(2,1)} %bitcast.12), channel_id=1, source_target_pairs={{0,8},{4,12},{8,0},{12,4},{16,24},{20,28},{24,16},{28,20},{1,9},{5... | collective-permute-start | bytes 3145736 | tf_op jit(solution)/shard_map/ppermute | solution.py:15
  94.9 52.2 %collective-permute-start.36 = (bf16[256,2048]{0,1:T(8,128)(2,1)}, bf16[256,2048]{0,1:T(8,128)(2,1)}, u32[]{:S(2)}, u32[]{:S(2)}) collective-permute-start(bf16[256,2048]{0,1:T(8,128)(2,1)} %bitcast.12), channel_id=1, source_target_pairs={{0,16},{4,20},{8,24},{12,28},{16,0},{20,4},{24,8},{28,12},{1,17},{... | collective-permute-start | bytes 3145736 | tf_op jit(solution)/shard_map/ppermute | solution.py:15
  96.2 54.1 %collective-permute-start.30 = (bf16[256,2048]{1,0:T(8,128)(2,1)}, bf16[256,2048]{1,0:T(8,128)(2,1)}, u32[]{:S(2)}, u32[]{:S(2)}) collective-permute-start(bf16[256,2048]{1,0:T(8,128)(2,1)} %param.20), channel_id=1, source_target_pairs={{0,4},{4,0},{8,12},{12,8},{16,20},{20,16},{24,28},{28,24},{1,5},{5... | collective-permute-start | bytes 3145736 | tf_op jit(solution)/shard_map/ppermute | solution.py:15
  119.5 40.2 %collective-permute-start.9 = (bf16[256,1536]{0,1:T(8,128)(2,1)}, bf16[256,1536]{0,1:T(8,128)(2,1)}, u32[]{:S(2)}, u32[]{:S(2)}) collective-permute-start(bf16[256,1536]{0,1:T(8,128)(2,1)} %bitcast.5), channel_id=1, source_target_pairs={{0,4},{4,0},{8,12},{12,8},{16,20},{20,16},{24,28},{28,24},{1,5},{5... | collective-permute-start | bytes 2359304 | tf_op jit(solution)/shard_map/ppermute | solution.py:15
  121.2 64.4 %collective-permute-start.39 = (bf16[256,2048]{0,1:T(8,128)(2,1)}, bf16[256,2048]{0,1:T(8,128)(2,1)}, u32[]{:S(2)}, u32[]{:S(2)}) collective-permute-start(bf16[256,2048]{0,1:T(8,128)(2,1)} %bitcast.12), channel_id=1, source_target_pairs={{0,4},{4,0},{8,12},{12,8},{16,20},{20,16},{24,28},{28,24},{1,5},{5... | collective-permute-start | bytes 3145736 | tf_op jit(solution)/shard_map/ppermute | solution.py:15
  150.3 40.4 %collective-permute-start.11 = (bf16[256,1536]{0,1:T(8,128)(2,1)}, bf16[256,1536]{0,1:T(8,128)(2,1)}, u32[]{:S(2)}, u32[]{:S(2)}) collective-permute-start(bf16[256,1536]{0,1:T(8,128)(2,1)} %collective-permute-done.6), channel_id=1, source_target_pairs={{0,4},{4,0},{8,12},{12,8},{16,20},{20,16},{24,28},{28,24},{1,5},{5... | collective-permute-start | bytes 2359304 | tf_op jit(solution)/shard_map/ppermute | solution.py:15
  368.5 157.8 %collective-permute-start.54 = (bf16[4,256,512]{1,2,0:T(8,128)(2,1)}, bf16[4,256,512]{1,2,0:T(8,128)(2,1)}, u32[]{:S(2)}, u32[]{:S(2)}) collective-permute-start(bf16[4,256,512]{1,2,0:T(8,128)(2,1)} %bitcast.207), channel_id=1, source_target_pairs={{0,4},{4,0},{8,12},{12,8},{16,20},{20,16},{24,28},{28,24},{1,5},{5... | collective-permute-start | bytes 3145736 | tf_op jit(solution)/shard_map/ppermute | solution.py:15
  389.1 141.5 %collective-permute-start.44 = (bf16[4,256,1536]{1,2,0:T(8,128)(2,1)}, bf16[4,256,1536]{1,2,0:T(8,128)(2,1)}, u32[]{:S(2)}, u32[]{:S(2)}) collective-permute-start(bf16[4,256,1536]{1,2,0:T(8,128)(2,1)} %bitcast.267), channel_id=1, source_target_pairs={{0,4},{4,0},{8,12},{12,8},{16,20},{20,16},{24,28},{28,24},{1,5},{5... | collective-permute-start | bytes 9437192 | tf_op jit(solution)/shard_map/ppermute | solution.py:15
  441.1 181.7 %reduce-scatter.3.cloned.1.call-start = ((), (), s32[]{:S(2)}) async-start(), calls=%async_computation.3 | async-start | bytes 5242880 | tf_op jit(solution)/shard_map/reduce_scatter | solution.py:261
  441.2 52.4 %collective-permute-start.51 = (f32[1,3584]{1,0:T(1,128)S(1)}, f32[1,3584]{1,0:T(1,128)S(1)}, u32[]{:S(2)}, u32[]{:S(2)}) collective-permute-start(f32[1,3584]{1,0:T(1,128)S(1)} %broadcast_in_dim.63), channel_id=1, source_target_pairs={{0,4},{4,0},{8,12},{12,8},{16,20},{20,16},{24,28},{28,24},{1,5},{5... | collective-permute-start | bytes 43016 | tf_op jit(solution)/shard_map/ppermute | solution.py:15
  525.0 53.8 %collective-permute-start.68 = (bf16[4,256,2048]{1,2,0:T(8,128)(2,1)}, bf16[4,256,2048]{1,2,0:T(8,128)(2,1)}, u32[]{:S(2)}, u32[]{:S(2)}) collective-permute-start(bf16[4,256,2048]{1,2,0:T(8,128)(2,1)} %bitcast.264), channel_id=1, source_target_pairs={{0,4},{4,0},{8,12},{12,8},{16,20},{20,16},{24,28},{28,24},{1,5},{5... | collective-permute-start | bytes 12582920 | tf_op jit(solution)/shard_map/ppermute | solution.py:15
  525.1 64.0 %collective-permute-start.61 = (bf16[4,256,2048]{2,1,0:T(8,128)(2,1)}, bf16[4,256,2048]{2,1,0:T(8,128)(2,1)}, u32[]{:S(2)}, u32[]{:S(2)}) collective-permute-start(bf16[4,256,2048]{2,1,0:T(8,128)(2,1)} %dynamic-slice_bitcast_fusion.1), channel_id=1, source_target_pairs={{0,4},{4,0},{8,12},{12,8},{16,20},{20,16},{24,28},{28,24},{1,5},{5... | collective-permute-start | bytes 12582920 | tf_op jit(solution)/shard_map/ppermute | solution.py:15
  584.9 46.3 %collective-permute-start.71 = (bf16[128,2048]{0,1:T(8,128)(2,1)}, bf16[128,2048]{0,1:T(8,128)(2,1)}, u32[]{:S(2)}, u32[]{:S(2)}) collective-permute-start(bf16[128,2048]{0,1:T(8,128)(2,1)} %slice.446), channel_id=1, source_target_pairs={{0,16},{4,20},{8,24},{12,28},{16,0},{20,4},{24,8},{28,12},{1,17},{... | collective-permute-start | bytes 1572872 | tf_op jit(solution)/shard_map/ppermute | solution.py:15
  585.6 46.9 %collective-permute-start.72 = (bf16[128,2048]{0,1:T(8,128)(2,1)}, bf16[128,2048]{0,1:T(8,128)(2,1)}, u32[]{:S(2)}, u32[]{:S(2)}) collective-permute-start(bf16[128,2048]{0,1:T(8,128)(2,1)} %slice.445), channel_id=1, source_target_pairs={{0,8},{4,12},{8,0},{12,4},{16,24},{20,28},{24,16},{28,20},{1,9},{5... | collective-permute-start | bytes 1572872 | tf_op jit(solution)/shard_map/ppermute | solution.py:15
  629.6 29.0 %collective-permute-start.64 = (bf16[128,2048]{1,0:T(8,128)(2,1)}, bf16[128,2048]{1,0:T(8,128)(2,1)S(1)}, u32[]{:S(2)}, u32[]{:S(2)}) collective-permute-start(bf16[128,2048]{1,0:T(8,128)(2,1)} %slice.448), channel_id=1, source_target_pairs={{0,16},{4,20},{8,24},{12,28},{16,0},{20,4},{24,8},{28,12},{1,17},{... | collective-permute-start | bytes 1572872 | tf_op jit(solution)/shard_map/ppermute | solution.py:15
  (136 other events, 1320.8 us)
Sparse Core Ops, SparseCore 0:
  9.6 84.4 all-gather.2
  95.6 79.2 all-gather.4
  441.2 78.6 reduce-scatter.4
  525.7 78.0 reduce-scatter.2

commit v2 on v1

v2 whole, which is shorter than its diff:
```python
import functools

import jax
import jax.numpy as jnp
from jax import lax
from jax.experimental import pallas as pl
from jax.experimental.pallas import tpu as pltpu
from jax.sharding import PartitionSpec as P

ROT = 64
EPSILON = 1e-05
ROTARY_BASE = 10000.0
F32 = jnp.float32
BF16 = jnp.bfloat16
HALVES = [(0, 0), (0, 1), (2, 1), (2, 0), (6, 0), (6, 1), (4, 1), (4, 0)]
ORDER = HALVES + [(p ^ 1, h) for p, h in HALVES]


def cut(*values):
    return lax.optimization_barrier(values)


def is_power(n):
    return n & (n - 1) == 0


def fast_dp():
    return lax.axis_size("dp") == 8


def xor_shift(values, axis, bit):
    size = lax.axis_size(axis)
    return lax.ppermute(values, axis, [(i, i ^ bit) for i in range(size)])


def butterfly(values, axis):
    size = lax.axis_size(axis)
    if not is_power(size):
        return lax.psum(values, axis)
    bit = 1
    while bit < size:
        values = values + xor_shift(values, axis, bit)
        bit *= 2
    return values


def columns_kernel(index_ref, x_ref, o_ref, *, count, step):
    for j in range(count):
        at = pl.multiple_of(index_ref[j] * step, step)
        o_ref[:, j * step : (j + 1) * step] = x_ref[:, pl.ds(at, step)]


def take_columns(values, index):
    rows, width = values.shape
    count = index.shape[0]
    return pl.pallas_call(
        functools.partial(columns_kernel, count=count, step=width // count),
        out_shape=jax.ShapeDtypeStruct(values.shape, values.dtype),
        grid_spec=pltpu.PrefetchScalarGridSpec(
            num_scalar_prefetch=1,
            grid=(1,),
            in_specs=[pl.BlockSpec((rows, width), lambda i, s: (0, 0))],
            out_specs=pl.BlockSpec((rows, width), lambda i, s: (0, 0)),
        ),
        name="columns",
    )(index, values)


def frame_index():
    me = lax.axis_index("dp")
    return jnp.stack([(me ^ p) * 2 + h for p, h in ORDER]).astype(jnp.int32)


def plain_index():
    me = lax.axis_index("dp")
    spot = jnp.array([ORDER.index((k // 2, k % 2)) for k in range(16)], jnp.int32)
    return jnp.stack([jnp.take(spot, (me ^ (k // 2)) * 2 + k % 2) for k in range(16)])


def to_frame(values):
    return take_columns(values, frame_index()) if fast_dp() else values


def from_frame(values):
    return take_columns(values, plain_index()) if fast_dp() else values


def dp_gather(shard):
    if not fast_dp():
        return [lax.all_gather(shard, "dp", axis=0, tiled=True)]
    half = shard.shape[0] // 2
    from_x = xor_shift(shard, "dp", 2)
    from_y = xor_shift(shard, "dp", 4)
    far_1 = xor_shift(from_y[:half], "dp", 2)
    far_2 = xor_shift(from_x[half:], "dp", 4)
    far = jnp.concatenate([far_1, far_2], axis=0)
    near = xor_shift(shard, "dp", 1)
    near_x = xor_shift(from_x, "dp", 1)
    near_y = xor_shift(from_y, "dp", 1)
    near_far = xor_shift(far, "dp", 1)
    out = []
    for own, x, f, y in ((shard, from_x, far, from_y), (near, near_x, near_far, near_y)):
        out += [own, x[half:], x[:half], f, y[half:], y[:half]]
    return out


def join(pieces, start, stop):
    return jnp.concatenate([p[:, start:stop] for p in pieces], axis=0)


def dp_scatter(make):
    away = make(1)
    came = xor_shift(away, "dp", 1)
    kept = make(0)
    rows = kept.shape[0] // 4
    half = rows // 2

    def summed(start, stop):
        return kept[start:stop].astype(F32) + came[start:stop].astype(F32)

    first_x = xor_shift(summed(rows + half, 2 * rows + half).astype(BF16), "dp", 2)
    first_y = xor_shift(summed(2 * rows + half, 3 * rows + half).astype(BF16), "dp", 4)
    last_x = summed(rows, rows + half) + first_y[:half].astype(F32)
    last_y = summed(3 * rows + half, 4 * rows) + first_x[half:].astype(F32)
    last_x = xor_shift(last_x.astype(BF16), "dp", 2)
    last_y = xor_shift(last_y.astype(BF16), "dp", 4)
    top = summed(0, half) + first_x[:half].astype(F32) + last_y.astype(F32)
    low = summed(half, rows) + first_y[half:].astype(F32) + last_x.astype(F32)
    return jnp.concatenate([top, low], axis=0)


def weight_grad(rows, columns):
    def make(part):
        width = rows.shape[1] // 2
        chosen = rows[:, part * width : (part + 1) * width]
        return jnp.einsum("nd,nf->df", chosen, columns, preferred_element_type=F32).astype(BF16)

    if fast_dp():
        return dp_scatter(make)
    whole = jnp.einsum("nd,nf->df", rows, columns, preferred_element_type=F32).astype(BF16)
    return lax.psum_scatter(whole, "dp", scatter_dimension=0, tiled=True).astype(F32)


def line_gather(block):
    size = lax.axis_size("tensor")
    me = lax.axis_index("tensor")
    up = down = block
    ups, downs = [block], [block]
    for s in range(size - 1):
        up = lax.ppermute(up, "tensor", [(i, i + 1) for i in range(s, size - 1)])
        down = lax.ppermute(down, "tensor", [(i + 1, i) for i in range(size - 1 - s)])
        ups.append(up)
        downs.append(down)
    blocks = [block]
    for r in range(1, size):
        blocks.append(jnp.where(me + r < size, downs[r], ups[size - r]))
    return jnp.concatenate(blocks, axis=0)


def line_scatter(terms):
    size = lax.axis_size("tensor")
    rows = terms.shape[0] // size

    def block(r):
        return terms[r * rows : (r + 1) * rows]

    up = down = None
    for s in range(1, size):
        to_up, to_down = block(size - s), block(s)
        if s > 1:
            to_up = (to_up.astype(F32) + up.astype(F32)).astype(BF16)
            to_down = (to_down.astype(F32) + down.astype(F32)).astype(BF16)
        up = lax.ppermute(to_up, "tensor", [(i, i + 1) for i in range(s)])
        down = lax.ppermute(to_down, "tensor", [(i, i - 1) for i in range(size - s, size)])
    return block(0).astype(F32) + up.astype(F32) + down.astype(F32)


def turn(values, cosine, low_sine, high_sine, sign):
    half = ROT // 2
    lanes = cosine.shape[-1]
    head = values[:, :lanes]
    turned = (
        head * cosine
        - sign * pltpu.roll(head, lanes - half, 1) * low_sine
        + sign * pltpu.roll(head, half, 1) * high_sine
    )
    return jnp.concatenate([turned, values[:, lanes:]], axis=1)


def contract(a, b, dims):
    return lax.dot_general(a, b, (dims, ((), ())), preferred_element_type=F32)


def masked(scores, column_starts, row_starts, query_block, block):
    keys = scores.shape[1]
    query = lax.broadcasted_iota(jnp.int32, scores.shape, 0) + query_block * block
    key = lax.broadcasted_iota(jnp.int32, scores.shape, 1)
    allowed = (column_starts == row_starts[:, :keys]) & (key <= query)
    return allowed, jnp.where(allowed, scores, -1e30)


def forward_kernel(
    me_ref, q_ref, k_ref, v_ref, cos_ref, low_ref, high_ref, col_ref, row_ref,
    q_out, k_out, v_out, att_ref, log_ref, *, size, block,
):
    def spot(b):
        return pl.ds(pl.multiple_of(lax.rem(b - me_ref[0] + size, size) * block, block), block)

    scale = q_ref.shape[-1] ** (-0.5)
    for b in range(size):
        here = slice(b * block, (b + 1) * block)
        at = spot(b)
        tables = cos_ref[here, :], low_ref[here, :], high_ref[here, :]
        q_out[at, :] = turn(q_ref[at, :], *tables, 1.0).astype(BF16)
        k_out[at, :] = turn(k_ref[at, :], *tables, 1.0).astype(BF16)
        v_out[at, :] = v_ref[at, :].astype(BF16)
    for b in range(size):
        here = slice(b * block, (b + 1) * block)
        query = q_out[spot(b), :]
        scores = jnp.concatenate(
            [contract(query, k_out[spot(c), :], ((1,), (1,))) for c in range(b + 1)], axis=1
        ) * scale
        _, scores = masked(scores, col_ref[here, :1], row_ref[:1, :], b, block)
        top = jnp.max(scores, axis=1, keepdims=True)
        powers = jnp.exp(scores - top)
        total = jnp.sum(powers, axis=1, keepdims=True)
        weights = (powers / total).astype(BF16)
        attended = contract(weights[:, :block], v_out[spot(0), :], ((1,), (0,)))
        for c in range(1, b + 1):
            attended = attended + contract(
                weights[:, c * block : (c + 1) * block], v_out[spot(c), :], ((1,), (0,))
            )
        att_ref[spot(b), :] = attended.astype(BF16)
        log_ref[0, here, :] = jnp.broadcast_to(top + jnp.log(total), (block, log_ref.shape[2]))


def backward_kernel(
    me_ref, q_ref, k_ref, v_ref, g_ref, log_ref, cos_ref, low_ref, high_ref, col_ref, row_ref,
    dq_ref, dk_ref, dv_ref, k_acc, v_acc, *, size, block,
):
    def spot(b):
        return pl.ds(pl.multiple_of(lax.rem(b - me_ref[0] + size, size) * block, block), block)

    scale = q_ref.shape[-1] ** (-0.5)
    for b in range(size):
        here = slice(b * block, (b + 1) * block)
        query, grad = q_ref[spot(b), :], g_ref[spot(b), :]
        scores = jnp.concatenate(
            [contract(query, k_ref[spot(c), :], ((1,), (1,))) for c in range(b + 1)], axis=1
        ) * scale
        allowed, scores = masked(scores, col_ref[here, :1], row_ref[:1, :], b, block)
        probs = jnp.where(allowed, jnp.exp(scores - log_ref[0, here, :1]), 0.0)
        grad_probs = jnp.concatenate(
            [contract(grad, v_ref[spot(c), :], ((1,), (1,))) for c in range(b + 1)], axis=1
        )
        inner = jnp.sum(probs * grad_probs, axis=1, keepdims=True)
        weights = probs.astype(BF16)
        grad_scores = (probs * (grad_probs - inner)).astype(BF16)
        back = None
        for c in range(b + 1):
            part = slice(c * block, (c + 1) * block)
            key_term = contract(grad_scores[:, part], query, ((0,), (0,)))
            value_term = contract(weights[:, part], grad, ((0,), (0,)))
            query_term = contract(grad_scores[:, part], k_ref[spot(c), :], ((1,), (0,)))
            back = query_term if c == 0 else back + query_term
            if c == b:
                k_acc[part, :] = key_term
                v_acc[part, :] = value_term
            else:
                k_acc[part, :] += key_term
                v_acc[part, :] += value_term
        tables = cos_ref[here, :], low_ref[here, :], high_ref[here, :]
        dq_ref[spot(b), :] = turn(back * scale, *tables, -1.0).astype(BF16)
    for b in range(size):
        here = slice(b * block, (b + 1) * block)
        tables = cos_ref[here, :], low_ref[here, :], high_ref[here, :]
        dk_ref[spot(b), :] = turn(k_acc[here, :] * scale, *tables, -1.0).astype(BF16)
        dv_ref[spot(b), :] = v_acc[here, :].astype(BF16)


def attention_tables(positions, starts):
    half = ROT // 2
    frequency = ROTARY_BASE ** (-(jnp.arange(half, dtype=F32) * 2.0) / ROT)
    angles = positions.astype(F32)[:, None] * frequency[None, :]
    cosine, sine = jnp.cos(angles), jnp.sin(angles)
    rows = positions.shape[0]
    cosines = jnp.concatenate([cosine, cosine, jnp.ones((rows, 128 - ROT), F32)], axis=1)
    low = jnp.concatenate([sine, jnp.zeros((rows, 128 - half), F32)], axis=1)
    high = jnp.concatenate([jnp.zeros((rows, half), F32), sine, jnp.zeros((rows, 128 - ROT), F32)], axis=1)
    columns = jnp.broadcast_to(starts[:, None], (rows, 128))
    across = jnp.broadcast_to(starts[None, :], (8, rows))
    return cosines, low, high, columns, across


def attention_forward(projected, tables, me, heads, size):
    rows = projected.shape[0]
    head = projected.shape[1] // (3 * heads)
    block = rows // size
    whole = lambda h, s: (0, 0)
    table_specs = [pl.BlockSpec((rows, 128), whole)] * 4 + [pl.BlockSpec((8, rows), whole)]
    by_head = pl.BlockSpec((rows, head), lambda h, s: (0, h))
    wide = jax.ShapeDtypeStruct((rows, heads * head), BF16)
    return pl.pallas_call(
        functools.partial(forward_kernel, size=size, block=block),
        out_shape=(wide, wide, wide, wide, jax.ShapeDtypeStruct((heads, rows, 128), F32)),
        grid_spec=pltpu.PrefetchScalarGridSpec(
            num_scalar_prefetch=1,
            grid=(heads,),
            in_specs=[
                pl.BlockSpec((rows, head), lambda h, s, k=k: (0, k * heads + h)) for k in range(3)
            ]
            + table_specs,
            out_specs=(by_head,) * 4 + (pl.BlockSpec((1, rows, 128), lambda h, s: (h, 0, 0)),),
        ),
        cost_estimate=pl.CostEstimate(
            flops=heads * rows * rows * head * 40, bytes_accessed=rows * head * heads * 24,
            transcendentals=heads * rows * rows // 2,
        ),
        name="attention_forward",
    )(me, projected, projected, projected, *tables)


def attention_backward(queries, keys, values, grads, log_total, tables, me, heads, size):
    rows = queries.shape[0]
    head = queries.shape[1] // heads
    block = rows // size
    whole = lambda h, s: (0, 0)
    table_specs = [pl.BlockSpec((rows, 128), whole)] * 4 + [pl.BlockSpec((8, rows), whole)]
    by_head = pl.BlockSpec((rows, head), lambda h, s: (0, h))
    wide = jax.ShapeDtypeStruct((rows, heads * head), BF16)
    return pl.pallas_call(
        functools.partial(backward_kernel, size=size, block=block),
        out_shape=(wide, wide, wide),
        grid_spec=pltpu.PrefetchScalarGridSpec(
            num_scalar_prefetch=1,
            grid=(heads,),
            in_specs=[by_head] * 4
            + [pl.BlockSpec((1, rows, 128), lambda h, s: (h, 0, 0))]
            + table_specs,
            out_specs=(by_head,) * 3,
            scratch_shapes=[pltpu.VMEM((rows, head), F32)] * 2,
        ),
        cost_estimate=pl.CostEstimate(
            flops=heads * rows * rows * head * 60, bytes_accessed=rows * head * heads * 24,
            transcendentals=heads * rows * rows // 2,
        ),
        name="attention_backward",
    )(me, queries, keys, values, grads, log_total, *tables)


def standardize(values):
    values = values.astype(F32)
    centered = values - jnp.mean(values, axis=-1, keepdims=True)
    spread = jnp.mean(centered * centered, axis=-1, keepdims=True)
    scale = lax.rsqrt(spread + EPSILON)
    return centered * scale, scale


def norm_rows(token_rows, gain_rows, shift_rows):
    xhat, _ = standardize(token_rows)
    first_rows = (xhat * gain_rows[0] + shift_rows[0]).astype(BF16)
    second_rows = (xhat * gain_rows[1] + shift_rows[1]).astype(BF16)
    return first_rows, second_rows


def hidden_units(second_rows, up_rows, hidden_bias):
    hidden = jnp.dot(second_rows, up_rows, preferred_element_type=F32) + hidden_bias
    bell = lax.erf(hidden * (0.5**0.5))
    activated = (0.5 * hidden * (1.0 + bell)).astype(BF16)
    slope = 0.5 * (1.0 + bell) + hidden * jnp.exp(-0.5 * hidden * hidden) * 0.3989422804014327
    return activated, slope.astype(BF16)


def branch_rows(attended, mix_rows, activated, down_rows):
    return (
        jnp.einsum("ne,de->nd", attended, mix_rows, preferred_element_type=F32)
        + jnp.einsum("nf,df->nd", activated, down_rows, preferred_element_type=F32)
    ).astype(BF16)


def hidden_grads(grad_rows, down_rows, slope):
    grad_active = jnp.einsum("nd,df->nf", grad_rows, down_rows, preferred_element_type=F32)
    return (grad_active * slope.astype(F32)).astype(BF16)


def attended_grads(grad_rows, mix_rows):
    return jnp.einsum("nd,de->ne", grad_rows, mix_rows, preferred_element_type=F32).astype(BF16)


def back_rows(grads, weight_rows):
    return jnp.einsum("nf,df->nd", grads, weight_rows, preferred_element_type=F32)


def grad_half(rows, columns, part):
    width = rows.shape[1] // 2
    chosen = rows[:, part * width : (part + 1) * width]
    return jnp.einsum("nd,nf->df", chosen, columns, preferred_element_type=F32).astype(BF16)


def plus(*terms):
    return functools.reduce(lambda a, b: a + b, [t.astype(F32) for t in terms])


def width_sums(grad_first, grad_second, xhat, grad_local):
    return jnp.stack(
        [
            jnp.sum(grad_first * xhat, axis=0),
            jnp.sum(grad_second * xhat, axis=0),
            jnp.sum(grad_first, axis=0),
            jnp.sum(grad_second, axis=0),
            jnp.sum(grad_local.astype(F32), axis=0),
        ],
        axis=0,
    )


def shards(
    tokens,
    seq_start,
    proj_weight,
    proj_bias,
    out_weight,
    up_weight,
    up_bias,
    down_weight,
    norm_gains,
    biases,
    cotangent,
):
    local_rows, width = tokens.shape
    n_dp, n_tensor = lax.axis_size("dp"), lax.axis_size("tensor")
    dp_index, tensor_index = lax.axis_index("dp"), lax.axis_index("tensor")
    row_count = local_rows * n_tensor
    hidden_width = up_weight.shape[1]
    heads_here = proj_bias.shape[1]
    head_size = proj_bias.shape[2] * n_dp
    local_width = heads_here * head_size
    joined_width = 3 * local_width
    columns = norm_gains.shape[1]

    vectors = jnp.concatenate(
        [norm_gains.reshape(1, -1), biases.reshape(1, -1), proj_bias.reshape(1, -1), up_bias.reshape(1, -1)],
        axis=1,
    )
    table = jnp.zeros((n_dp * n_tensor, vectors.shape[1]), BF16)
    table = lax.dynamic_update_slice(table, vectors, (dp_index * n_tensor + tensor_index, 0))
    table = butterfly(butterfly(table, "dp"), "tensor")
    local_tokens, local_grads = to_frame(tokens), to_frame(cotangent)
    positions = dp_index * row_count + jnp.arange(row_count, dtype=jnp.int32) - seq_start
    tables = attention_tables(positions, seq_start)
    me = tensor_index.astype(jnp.int32).reshape(1)
    flat_proj = proj_weight.reshape(-1, joined_width)

    def small_parameters(table):
        six_rows = table[:, : 6 * columns].reshape(n_dp * n_tensor, 6, columns).transpose(1, 0, 2)
        six_rows = to_frame(six_rows.reshape(6, width).astype(F32))
        of_tensor = lax.dynamic_index_in_dim(
            table[:, 6 * columns :].reshape(n_dp, n_tensor, -1), tensor_index, 1, keepdims=False
        ).astype(F32)
        joined_bias = (
            of_tensor[:, : proj_bias.size]
            .reshape(n_dp, 3, heads_here, -1)
            .transpose(1, 2, 0, 3)
            .reshape(joined_width)
        )
        hidden_bias = of_tensor[:, proj_bias.size :].reshape(hidden_width)
        return six_rows[:2], six_rows[2:], joined_bias, hidden_bias

    def attend(first_rows, joined_rows, joined_bias):
        projected = jnp.dot(first_rows, joined_rows, preferred_element_type=F32) + joined_bias
        return attention_forward(projected, tables, me, heads_here, n_tensor)

    def attend_back(kept, grad_attended):
        queries, keys, values, log_total = kept
        backs = attention_backward(
            queries, keys, values, grad_attended, log_total, tables, me, heads_here, n_tensor
        )
        return jnp.concatenate(backs, axis=1)

    def finish_output(branches, shift_rows):
        output = local_tokens.astype(F32) + branches + shift_rows[2] + shift_rows[3]
        return from_frame(output.astype(BF16))

    def finish_input_grad(back):
        xhat_local, scale_local = standardize(local_tokens)
        grad_norm_in = (
            back
            - jnp.mean(back, axis=-1, keepdims=True)
            - xhat_local * jnp.mean(back * xhat_local, axis=-1, keepdims=True)
        ) * scale_local
        return from_frame(local_grads.astype(F32) + grad_norm_in)

    def small_grads(five, joined_bias_term, up_bias_term):
        five = from_frame(five).reshape(1, -1)
        terms = jnp.concatenate([five, joined_bias_term[None], up_bias_term[None]], axis=1)
        terms = butterfly(terms, "dp")
        five = butterfly(terms[:, : 5 * width], "tensor").reshape(5, width)
        mine = lax.dynamic_slice_in_dim(
            five, (dp_index * n_tensor + tensor_index) * columns, columns, 1
        )
        biases_grad = jnp.concatenate([mine[2:], mine[4:]], axis=0)
        joined_bias_sum = lax.dynamic_slice_in_dim(
            terms[0, 5 * width : 5 * width + joined_width].reshape(3, heads_here, head_size),
            dp_index * proj_bias.shape[2],
            proj_bias.shape[2],
            2,
        )
        up_bias_sum = lax.dynamic_slice_in_dim(
            terms[:, 5 * width + joined_width :], dp_index * up_bias.shape[1], up_bias.shape[1], 1
        )
        return mine[:2], biases_grad, joined_bias_sum, up_bias_sum

    def plain():
        token_rows, grad_rows = line_gather(local_tokens), line_gather(local_grads)
        up_rows, down_rows = dp_gather(up_weight), dp_gather(down_weight.T)
        joined_rows, mix_rows = dp_gather(flat_proj), dp_gather(out_weight.T)
        up_rows, down_rows, joined_rows, mix_rows = (
            join(w, 0, None) for w in (up_rows, down_rows, joined_rows, mix_rows)
        )
        gain_rows, shift_rows, joined_bias, hidden_bias = small_parameters(table)
        first_rows, second_rows = norm_rows(token_rows, gain_rows, shift_rows)
        activated, slope = cut(*hidden_units(second_rows, up_rows, hidden_bias))
        *kept, attended, log_total = attend(first_rows, joined_rows, joined_bias)
        branches = line_scatter(branch_rows(attended, mix_rows, activated, down_rows))
        output = finish_output(branches, shift_rows)
        grad_hidden = hidden_grads(grad_rows, down_rows, slope)
        down_sum = weight_grad(grad_rows, activated)
        up_sum = weight_grad(second_rows, grad_hidden)
        grad_second = back_rows(grad_hidden, up_rows)
        grad_attended = attended_grads(grad_rows, mix_rows)
        mix_sum = weight_grad(grad_rows, attended)
        grad_projected = attend_back((*kept, log_total), grad_attended)
        joined_sum = weight_grad(first_rows, grad_projected)
        grad_first = back_rows(grad_projected, joined_rows)
        back = grad_first * gain_rows[0] + grad_second * gain_rows[1]
        input_grad = finish_input_grad(line_scatter(back.astype(BF16)))
        five = width_sums(grad_first, grad_second, standardize(token_rows)[0], local_grads)
        small = small_grads(
            five, jnp.sum(grad_projected, axis=0, dtype=F32), jnp.sum(grad_hidden, axis=0, dtype=F32)
        )
        return output, input_grad, joined_sum, mix_sum, up_sum, down_sum, small

    def staged():
        half = local_rows // 2
        first, second = slice(0, half), slice(half, 2 * half)

        def x(values):
            return xor_shift(values, "dp", 2)

        def y(values):
            return xor_shift(values, "dp", 4)

        def core(values):
            return xor_shift(values, "dp", 1)

        def gather_step(up, down, s):
            up = lax.ppermute(up, "tensor", [(i, i + 1) for i in range(s, 3)])
            down = lax.ppermute(down, "tensor", [(i + 1, i) for i in range(3 - s)])
            return up, down

        def scatter_step(terms, up, down, s):
            to_up = terms[(4 - s) * local_rows : (5 - s) * local_rows]
            to_down = terms[s * local_rows : (s + 1) * local_rows]
            if s > 1:
                to_up, to_down = plus(to_up, up).astype(BF16), plus(to_down, down).astype(BF16)
            up = lax.ppermute(to_up, "tensor", [(i, i + 1) for i in range(s)])
            down = lax.ppermute(to_down, "tensor", [(i, i - 1) for i in range(4 - s, 4)])
            return up, down

        def in_turn(block, ups, downs):
            blocks = [block] + [
                jnp.where(tensor_index + r < 4, downs[r - 1], ups[3 - r]) for r in range(1, 4)
            ]
            return jnp.concatenate(blocks, axis=0)

        def pair(top, low):
            return jnp.concatenate([top, low], axis=0)

        wa = up_weight
        wb = jnp.concatenate([flat_proj, out_weight.T], axis=1)
        wc = down_weight.T

        tu1, td1 = gather_step(local_tokens, local_tokens, 0)
        ax, ay, na = x(wa), y(wa), core(wa)
        tu1, td1, ax, ay, na, table1, wb, wc = cut(tu1, td1, ax, ay, na, table, wb, wc)
        tu2, td2 = gather_step(tu1, td1, 1)
        p2x, p2y = x(pair(ay[first], wb[second])), y(pair(ax[second], wb[first]))
        nax, nay = core(ax), core(ay)
        gain_rows, shift_rows, joined_bias, hidden_bias = small_parameters(table1)
        tu2, td2, p2x, p2y, nax, nay = cut(tu2, td2, p2x, p2y, nax, nay)
        tu3, td3 = gather_step(tu2, td2, 2)
        p3x, p3y = x(pair(p2y[second], wb[first])), y(pair(p2x[second], wb[second]))
        n2x, n2y, nb = core(p2x), core(p2y), core(wb)
        tu3, td3, p3x, p3y, n2x, n2y, nb, local_grads1 = cut(
            tu3, td3, p3x, p3y, n2x, n2y, nb, local_grads
        )
        cu1, cd1 = gather_step(local_grads1, local_grads1, 0)
        cx, cy = x(wc), y(wc)
        n3x, n3y, nc = core(p3x), core(p3y), core(wc)
        token_rows = in_turn(local_tokens, (tu1, tu2, tu3), (td1, td2, td3))
        first_rows, second_rows = norm_rows(token_rows, gain_rows, shift_rows)
        up_rows = jnp.concatenate(
            [wa, ax[second], ax[first], p2x[first], p2y[first], ay[second], ay[first]]
            + [na, nax[second], nax[first], n2x[first], n2y[first], nay[second], nay[first]],
            axis=0,
        )
        activated, slope = hidden_units(second_rows, up_rows, hidden_bias)
        cu1, cd1, cx, cy, n3x, n3y, nc, first_rows, activated, slope = cut(
            cu1, cd1, cx, cy, n3x, n3y, nc, first_rows, activated, slope
        )
        cu2, cd2 = gather_step(cu1, cd1, 1)
        fcx, fcy = x(cy[first]), y(cx[second])
        ncx, ncy = core(cx), core(cy)
        second_pieces = [wb, p2x[second], p3x[second], p3x[first], p3y[first], p3y[second], p2y[second]] + [
            nb, n2x[second], n3x[second], n3x[first], n3y[first], n3y[second], n2y[second]
        ]
        joined_rows = join(second_pieces, 0, joined_width)
        mix_rows = join(second_pieces, joined_width, None)
        *kept, attended, log_total = attend(first_rows, joined_rows, joined_bias)
        kept = (*kept, log_total)
        cu2, cd2, fcx, fcy, ncx, ncy, attended = cut(cu2, cd2, fcx, fcy, ncx, ncy, attended)
        cu3, cd3 = gather_step(cu2, cd2, 2)
        nfx, nfy = core(fcx), core(fcy)
        down_rows = jnp.concatenate(
            [wc, cx[second], cx[first], fcx, fcy, cy[second], cy[first]]
            + [nc, ncx[second], ncx[first], nfx, nfy, ncy[second], ncy[first]],
            axis=0,
        )
        branch_terms = branch_rows(attended, mix_rows, activated, down_rows)
        cu3, cd3, branch_terms, activated = cut(cu3, cd3, branch_terms, activated)
        bu, bd = scatter_step(branch_terms, None, None, 1)
        grad_rows = in_turn(local_grads1, (cu1, cu2, cu3), (cd1, cd2, cd3))
        away = grad_half(grad_rows, activated, 1)
        came = core(away)
        keep_d = grad_half(grad_rows, activated, 0)
        grad_hidden = hidden_grads(grad_rows, down_rows, slope)
        bu, bd, came_d, keep_d, grad_hidden, grad_rows = cut(
            bu, bd, came, keep_d, grad_hidden, grad_rows
        )

        def at(keep, came, start, stop):
            return plus(keep[start * half : stop * half], came[start * half : stop * half])

        bu, bd = scatter_step(branch_terms, bu, bd, 2)
        d1x = x(at(keep_d, came_d, 3, 5).astype(BF16))
        d1y = y(at(keep_d, came_d, 5, 7).astype(BF16))
        came_u = core(grad_half(second_rows, grad_hidden, 1))
        keep_u = grad_half(second_rows, grad_hidden, 0)
        grad_projected = attend_back(kept, attended_grads(grad_rows, mix_rows))
        bu, bd, d1x, d1y, came_u, keep_u, grad_projected, grad_hidden = cut(
            bu, bd, d1x, d1y, came_u, keep_u, grad_projected, grad_hidden
        )
        bu, bd = scatter_step(branch_terms, bu, bd, 3)
        d2x = plus(at(keep_d, came_d, 2, 3), d1y[first]).astype(BF16)
        d2y = plus(at(keep_d, came_d, 7, 8), d1x[second]).astype(BF16)
        s9x = x(pair(d2x, at(keep_u, came_u, 4, 5).astype(BF16)))
        s9y = y(pair(d2y, at(keep_u, came_u, 5, 6).astype(BF16)))
        grad_second = back_rows(grad_hidden, up_rows)
        grad_first = back_rows(grad_projected, joined_rows)
        back = (grad_first * gain_rows[0] + grad_second * gain_rows[1]).astype(BF16)
        bu, bd, s9x, s9y, back, grad_projected, attended = cut(
            bu, bd, s9x, s9y, back, grad_projected, attended
        )
        eu, ed = scatter_step(back, None, None, 1)
        s10x = x(pair(plus(at(keep_u, came_u, 2, 3), s9y[second]), at(keep_u, came_u, 3, 4)).astype(BF16))
        s10y = y(pair(at(keep_u, came_u, 6, 7), plus(at(keep_u, came_u, 7, 8), s9x[second])).astype(BF16))

        def joined_half(part):
            return jnp.concatenate(
                [grad_half(first_rows, grad_projected, part), grad_half(grad_rows, attended, part)], axis=1
            )

        came_j = core(joined_half(1))
        keep_j = joined_half(0)
        output = finish_output(plus(branch_terms[:local_rows], bu, bd), shift_rows)
        down_sum = pair(
            plus(at(keep_d, came_d, 0, 1), d1x[first], s9y[first]),
            plus(at(keep_d, came_d, 1, 2), d1y[second], s9x[first]),
        )
        eu, ed, s10x, s10y, came_j, keep_j = cut(eu, ed, s10x, s10y, came_j, keep_j)
        eu, ed = scatter_step(back, eu, ed, 2)
        j1x = x(at(keep_j, came_j, 3, 5).astype(BF16))
        j1y = y(at(keep_j, came_j, 5, 7).astype(BF16))
        up_sum = pair(
            plus(at(keep_u, came_u, 0, 1), s10x[second], s10y[second]),
            plus(at(keep_u, came_u, 1, 2), s10x[first], s10y[first]),
        )
        five = width_sums(grad_first, grad_second, standardize(token_rows)[0], local_grads)
        small = small_grads(
            five, jnp.sum(grad_projected, axis=0, dtype=F32), jnp.sum(grad_hidden, axis=0, dtype=F32)
        )
        eu, ed, j1x, j1y = cut(eu, ed, j1x, j1y)
        eu, ed = scatter_step(back, eu, ed, 3)
        j2x = x(plus(at(keep_j, came_j, 2, 3), j1y[first]).astype(BF16))
        j2y = y(plus(at(keep_j, came_j, 7, 8), j1x[second]).astype(BF16))
        joined_mix = pair(
            plus(at(keep_j, came_j, 0, 1), j1x[first], j2y),
            plus(at(keep_j, came_j, 1, 2), j1y[second], j2x),
        )
        input_grad = finish_input_grad(plus(back[:local_rows], eu, ed))
        return (
            output, input_grad, joined_mix[:, :joined_width], joined_mix[:, joined_width:], up_sum, down_sum, small
        )

    parts = staged() if fast_dp() and n_tensor == 4 else plain()
    output, input_grad, joined_sum, mix_sum, up_sum, down_sum, small = parts
    gains_grad, biases_grad, joined_bias_sum, up_bias_sum = small
    return (
        output,
        input_grad,
        joined_sum.reshape(proj_weight.shape),
        joined_bias_sum,
        mix_sum.T,
        up_sum,
        up_bias_sum,
        down_sum.T,
        gains_grad,
        biases_grad,
    )


def solution(mesh):
    in_specs = (
        P(("dp", "tensor"), None),
        P("dp"),
        P("dp", None, "tensor"),
        P(None, "tensor", "dp"),
        P("tensor", "dp"),
        P("dp", "tensor"),
        P("tensor", "dp"),
        P("tensor", "dp"),
        P(None, ("dp", "tensor")),
        P(None, ("dp", "tensor")),
        P(("dp", "tensor"), None),
    )
    out_specs = (
        P(("dp", "tensor"), None),
        P(("dp", "tensor"), None),
        P("dp", None, "tensor"),
        P(None, "tensor", "dp"),
        P("tensor", "dp"),
        P("dp", "tensor"),
        P("tensor", "dp"),
        P("tensor", "dp"),
        P(None, ("dp", "tensor")),
        P(None, ("dp", "tensor")),
    )
    return jax.shard_map(shards, mesh=mesh, in_specs=in_specs, out_specs=out_specs, check_vma=False)
```

time: 689 us -> 681 us (0.988)
  local copies, waits for them, and re-layouts: 222 us -> 135 us
  matrix products: 163 us -> 123 us
  Pallas kernels: 0 us -> 38 us
  waiting for transfers between devices: 136 us -> 170 us
  starting transfers between devices: 65.1 us -> 96.8 us
  other arithmetic: 71.2 us -> 93.9 us
  loops' own time: 8.38 us -> 0 us
    ppermute x0 -> x24, waiting for transfers between devices: none -> 83.3 us  [the longest x6 35 us: gather_step(): down = lax.ppermute(down, 'tensor', [(i + 1, i) for i in range(3 - s)])]
    ppermute x0 -> x24, starting transfers between devices: none -> 64 us  [the longest x6 30.4 us: scatter_step(): up = lax.ppermute(to_up, 'tensor', [(i, i + 1) for i in range(s)])]
    dynamic_update_slice x41 -> x0, local copies, waits for them, and re-layouts: 57.8 us -> none  [the longest x40 57.7 us: dp_gather(): whole = lax.dynamic_update_slice_in_dim(whole, v, start, 0)]
    ppermute x80 -> x46, waiting for transfers between devices: 136 us -> 87.1 us  [xor_shift(): return lax.ppermute(values, axis, [(i, i ^ bit) for i in range(size)])]
    dot_general x26 -> x16, matrix products: 163 us -> 123 us  [the longest x8 42.5 us: grad_half(): jnp.einsum('nd,nf->df', chosen, columns, preferred_element_type=F32)]
    pallas_call x0 -> x8, Pallas kernels: none -> 38 us  [the longest x6 17.6 us: take_columns(): pl.pallas_call(functools.partial(columns_kernel, count=count, step=width...]
    unnamed x133 -> x186, local copies, waits for them, and re-layouts: 44.3 us -> 77.4 us
    ppermute x80 -> x46, starting transfers between devices: 65 us -> 32.8 us  [xor_shift(): return lax.ppermute(values, axis, [(i, i ^ bit) for i in range(size)])]
  transfers between devices with their start and end apart: 84 -> 70, of which waited for: 26 -> 22; matrix products, arithmetic and copies ran while one was open for 55% -> 45% of each run, Pallas kernels for 0% -> 6%
where the time goes in v2:
time: 681 us; the launch traced here: 671 us
  waiting for transfers between devices  170 us (25%)
  local copies, waits for them, and re-layouts  135 us (20%)
  matrix products  123 us (18%)
  starting transfers between devices  96.8 us (14%)
  other arithmetic  93.9 us (14%)
  Pallas kernels  38 us (6%)
  between operations  13.1 us (2%)
    ppermute x46, waiting for transfers between devices, xor_shift(): return lax.ppermute(values, axis, [(i, i ^ bit) for i in range(size)])  87.1 us
    unnamed x186, local copies, waits for them, and re-layouts  77.4 us
    dot_general x8, matrix products, grad_half(): jnp.einsum('nd,nf->df', chosen, columns, preferred_element_type=F32)  42.5 us
    ppermute x6, waiting for transfers between devices, gather_step(): down = lax.ppermute(down, 'tensor', [(i + 1, i) for i in range(3 - s)])  35 us
    ppermute x46, starting transfers between devices, xor_shift(): return lax.ppermute(values, axis, [(i, i ^ bit) for i in range(size)])  32.8 us
    ppermute x6, starting transfers between devices, scatter_step(): up = lax.ppermute(to_up, 'tensor', [(i, i + 1) for i in range(s)])  30.4 us
    dot_general x2, matrix products, back_rows(): jnp.einsum('nf,df->nd', grads, weight_rows, preferred_element_type=F32)  26.1 us
    ppermute x6, waiting for transfers between devices, scatter_step(): up = lax.ppermute(to_up, 'tensor', [(i, i + 1) for i in range(s)])  25.6 us
  transfers between devices with their start and end apart: 70, of which 22 were waited for; matrix products, arithmetic and copies ran while one was open for 45% of the time, Pallas kernels for 6%

profile of v2, /device:TPU:0, one launch (start us, length us, event | category | flops | bytes accessed | tf_op | source)
XLA Modules:
  0.0 670.5 jit_solution(14897505041234736178)
XLA Ops:
  36.2 17.4 %collective-permute-done.9 = bf16[32,832]{1,0:T(8,128)(2,1)S(1)} collective-permute-done((bf16[32,832]{1,0:T(8,128)(2,1)S(1)}, bf16[32,832]{1,0:T(8,128)(2,1)S(1)}, u32[]{:S(2)}, u32[]{:S(2)}) %collective-permute-start.9) | collective-permute-done | bytes 53280 | tf_op jit(solution)/shard_map/ppermute | solution.py:33
  79.4 13.5 %collective-permute-done.12 = bf16[256,2048]{0,1:T(8,128)(2,1)} collective-permute-done((bf16[256,2048]{0,1:T(8,128)(2,1)}, bf16[256,2048]{0,1:T(8,128)(2,1)}, u32[]{:S(2)}, u32[]{:S(2)}) %collective-permute-start.12) | collective-permute-done | bytes 1048608 | tf_op jit(solution)/shard_map/ppermute | solution.py:33
  101.7 18.8 %collective-permute-done.11 = bf16[256,2048]{1,0:T(8,128)(2,1)} collective-permute-done((bf16[256,2048]{1,0:T(8,128)(2,1)}, bf16[256,2048]{1,0:T(8,128)(2,1)}, u32[]{:S(2)}, u32[]{:S(2)}) %collective-permute-start.11) | collective-permute-done | bytes 1048608 | tf_op jit(solution)/shard_map/ppermute | solution.py:558
  151.2 14.1 %collective-permute-done.19 = bf16[256,2048]{0,1:T(8,128)(2,1)} collective-permute-done((bf16[256,2048]{0,1:T(8,128)(2,1)S(1)}, bf16[256,2048]{0,1:T(8,128)(2,1)}, u32[]{:S(2)}, u32[]{:S(2)}) %collective-permute-start.19) | collective-permute-done | bytes 1048608 | tf_op jit(solution)/shard_map/ppermute | solution.py:33
  175.5 16.2 %collective-permute-done.17 = bf16[256,2048]{1,0:T(8,128)(2,1)} collective-permute-done((bf16[256,2048]{1,0:T(8,128)(2,1)}, bf16[256,2048]{1,0:T(8,128)(2,1)}, u32[]{:S(2)}, u32[]{:S(2)}) %collective-permute-start.17) | collective-permute-done | bytes 1048608 | tf_op jit(solution)/shard_map/ppermute | solution.py:558
  222.3 9.7 %fusion.9 = (bf16[1024,2048]{1,0:T(8,128)(2,1)S(1)}, bf16[1024,2048]{1,0:T(8,128)(2,1)S(1)}) fusion(f32[2048]{0:T(1024)S(1)} %bitcast.116, f32[2048]{0:T(1024)S(1)} %bitcast.112, f32[1024]{0:T(1024)S(1)} %add_rsqrt_fusion, f32[1024]{0:T(1024)S(1)} %broadcast_multiply_fusion, bf16[256,2048]{1,0:T(8,128)(2,1)S(1)} %get-tuple-element.614, ...), kind=kLoop, calls=%fused_computation.12 | loop fusion | flops 33554432 | bytes 12623872 | tf_op jit(solution)/shard_map/convert_element_type | solution.py:362
  232.2 13.8 %fusion.17 = (bf16[1024,2048]{1,0:T(8,128)(2,1)}, bf16[1024,2048]{1,0:T(8,128)(2,1)}) fusion(f32[2048]{0:T(1024)S(1)} %bitcast.118, bf16[1024,2048]{1,0:T(8,128)(2,1)S(1)} %get-tuple-element.553, bf16[2048,2048]{1,0:T(8,128)(2,1)S(1)} %copy-done.45), kind=kOutput, calls=%fused_computation.20 | convolution fusion | flops 8617197568 | bytes 20979712 | tf_op jit(solution)/shard_map/dot_general | solution.py:367
  258.7 18.5 %collective-permute-done.23 = bf16[256,2048]{1,0:T(8,128)(2,1)S(1)} collective-permute-done((bf16[256,2048]{1,0:T(8,128)(2,1)S(1)}, bf16[256,2048]{1,0:T(8,128)(2,1)S(1)}, u32[]{:S(2)}, u32[]{:S(2)}) %collective-permute-start.23) | collective-permute-done | bytes 1048608 | tf_op jit(solution)/shard_map/ppermute | solution.py:557
  288.0 8.6 %convolution_add_fusion.q_ref.k_ref.v_ref = f32[1024,1536]{1,0:T(8,128)} fusion(bf16[1024,2048]{1,0:T(8,128)(2,1)S(1)} %get-tuple-element.117, bf16[2048,1536]{0,1:T(8,128)(2,1)S(1)} %slice_dynamic-update-slice_fusion.10, f32[1536]{0:T(1024)S(1)} %add.528), kind=kOutput, calls=%fused_computation.28 | convolution fusion | flops 6444023808 | bytes 16783360 | tf_op jit(solution)/shard_map/dot_general | solution.py:470
  298.2 9.7 %attention_forward.1 = (bf16[1024,512]{1,0:T(8,128)(2,1)}, bf16[1024,512]{1,0:T(8,128)(2,1)}, bf16[1024,512]{1,0:T(8,128)(2,1)}, bf16[1024,512]{1,0:T(8,128)(2,1)}, f32[2,1024,128]{2,1,0:T(8,128)}) custom-call(s32[1]{0:T(128)} %bitcast.41.me_ref, f32[1024,1536]{1,0:T(8,128)} %convolution_add_fusion.q_ref.k_ref.v_ref, ...), custom_call_target="tpu_custom_call" | custom-call | flops 21474836480 | bytes 12582912 | tf_op jit(solution)/shard_map/attention_forward/pallas_call | solution.py:303
  315.1 8.7 %collective-permute-done.32 = bf16[128,2048]{0,1:T(8,128)(2,1)S(1)} collective-permute-done((bf16[128,2048]{0,1:T(8,128)(2,1)S(1)}, bf16[128,2048]{0,1:T(8,128)(2,1)S(1)}, u32[]{:S(2)}, u32[]{:S(2)}) %collective-permute-start.32) | collective-permute-done | bytes 524320 | tf_op jit(solution)/shard_map/ppermute | solution.py:33
  346.6 11.3 %fusion.66 = f32[1024,2048]{1,0:T(8,128)S(1)} fusion(bf16[1024,2048]{1,0:T(8,128)(2,1)S(1)} %copy-done.60, bf16[2048,2048]{0,1:T(8,128)(2,1)} %slice_dynamic-update-slice_fusion.4), kind=kOutput, calls=%fused_computation.217 | convolution fusion | flops 8589934592 | bytes 20971520 | tf_op jit(solution)/shard_map/nf,df->nd/dot_general | solution.py:377
  364.8 6.3 convolution_convert_fusion.5
  374.4 7.8 %collective-permute-start.40 = (bf16[256,2048]{1,0:T(8,128)(2,1)}, bf16[256,2048]{1,0:T(8,128)(2,1)}, u32[]{:S(2)}, u32[]{:S(2)}) collective-permute-start(bf16[256,2048]{1,0:T(8,128)(2,1)} %get-tuple-element.566), channel_id=1, source_target_pairs={{0,1},{4,5},{8,9},{12,13},{16,17},{20,21},{24,25},{28,29}} | collective-permute-start | bytes 3145736 | tf_op jit(solution)/shard_map/ppermute | solution.py:566
  382.2 12.0 %multiply_convert_fusion = bf16[1024,2048]{1,0:T(8,128)(2,1)S(1)} fusion(bf16[1024,2048]{1,0:T(8,128)(2,1)} %get-tuple-element.135, bf16[2048,2048]{0,1:T(8,128)(2,1)} %slice_dynamic-update-slice_fusion.4, bf16[256,2048]{1,0:T(8,128)(2,1)S(1)} %broadcast_select_fusion, bf16[256,2048]{1,0:T(8,128)(2,1)S(1)} %broadcast_select_fusion.2, ...), kind=kOutput, calls=%fused_computation.23 | convolution fusion | flops 8613003264 | bytes 20971520 | tf_op jit(solution)/shard_map/nd,df->nf/dot_general | solution.py:382
  394.2 8.9 %convolution_convert_fusion.4 = bf16[1024,2048]{1,0:T(8,128)(2,1)S(1)} fusion(bf16[1024,2048]{1,0:T(8,128)(2,1)} %get-tuple-element.134, bf16[1024,2048]{1,0:T(8,128)(2,1)} %copy-done.21), kind=kOutput, calls=%fused_computation.37 | convolution fusion | flops 4297064448 | bytes 10485760 | tf_op jit(solution)/shard_map/nd,nf->df/dot_general | solution.py:397
  431.8 10.7 %attention_backward.1 = (bf16[1024,512]{1,0:T(8,128)(2,1)}, bf16[1024,512]{1,0:T(8,128)(2,1)}, bf16[1024,512]{1,0:T(8,128)(2,1)}) custom-call(s32[1]{0:T(128)} %bitcast.41.me_ref, bf16[1024,512]{1,0:T(8,128)(2,1)} %get-tuple-element.141.q_ref, bf16[1024,512]{1,0:T(8,128)(2,1)} %get-tuple-element.142.k_ref, bf16[1024,512]{1,0:T(8,128)(2,1)} %get-tuple-element.143.v_ref, ...), custom_call_target="tpu_custom_call" | custom-call | flops 32212254720 | bytes 12582912 | tf_op jit(solution)/shard_map/attention_backward/pallas_call | solution.py:331
  445.6 7.9 %convolution_convert_fusion.2 = bf16[1024,2048]{1,0:T(8,128)(2,1)S(1)} fusion(bf16[1024,2048]{1,0:T(8,128)(2,1)S(1)} %copy-done.19, bf16[1024,2048]{1,0:T(8,128)(2,1)} %copy-done.30), kind=kOutput, calls=%fused_computation.35 | convolution fusion | flops 4297064448 | bytes 10485760 | tf_op jit(solution)/shard_map/nd,nf->df/dot_general | solution.py:397
  473.5 8.8 %fusion.67 = f32[1024,2048]{1,0:T(8,128)} fusion(bf16[1024,1536]{1,0:T(8,128)(2,1)S(1)} %pad_maximum_fusion.4, bf16[2048,1536]{0,1:T(8,128)(2,1)S(1)} %bitcast.105), kind=kOutput, calls=%fused_computation.218 | convolution fusion | flops 6442450944 | bytes 17825792 | tf_op jit(solution)/shard_map/nf,df->nd/dot_general | solution.py:391
  482.3 17.3 %fusion.53 = (f32[2048]{0:T(1024)S(1)}, f32[2048]{0:T(1024)S(1)}, bf16[1024,2048]{1,0:T(8,128)(2,1)}, f32[2048]{0:T(1024)S(1)}, f32[2048]{0:T(1024)S(1)}) fusion(f32[1024]{0:T(1024)S(1)} %copy-done.57, f32[1024]{0:T(1024)S(1)} %copy-done.49, bf16[256,2048]{1,0:T(8,128)(2,1)S(1)} %copy-done.6, bf16[256,2048]{1,0:T(8,128)(2,1)S(1)} %copy-done.4, ...), kind=kOutput, calls=%fused_computation.204 | convolution fusion | flops 8631869440 | bytes 29417472 | tf_op jit(solution)/shard_map/nf,df->nd/dot_general | solution.py:391
  545.9 8.6 %collective-permute-done.54 = bf16[256,2048]{1,0:T(8,128)(2,1)} collective-permute-done((bf16[256,2048]{1,0:T(8,128)(2,1)}, bf16[256,2048]{1,0:T(8,128)(2,1)}, u32[]{:S(2)}, u32[]{:S(2)}) %collective-permute-start.54) | collective-permute-done | bytes 1048608 | tf_op jit(solution)/shard_map/ppermute | solution.py:33
  580.3 10.6 %collective-permute-done.57 = bf16[256,2048]{1,0:T(8,128)(2,1)} collective-permute-done((bf16[256,2048]{1,0:T(8,128)(2,1)}, bf16[256,2048]{1,0:T(8,128)(2,1)}, u32[]{:S(2)}, u32[]{:S(2)}) %collective-permute-start.57) | collective-permute-done | bytes 1048608 | tf_op jit(solution)/shard_map/ppermute | solution.py:566
  590.9 6.9 %collective-permute-done.60 = bf16[256,2048]{1,0:T(8,128)(2,1)} collective-permute-done((bf16[256,2048]{1,0:T(8,128)(2,1)}, bf16[256,2048]{1,0:T(8,128)(2,1)}, u32[]{:S(2)}, u32[]{:S(2)}) %collective-permute-start.60) | collective-permute-done | bytes 1048608 | tf_op jit(solution)/shard_map/ppermute | solution.py:33
  617.6 9.7 %collective-permute-done.61 = bf16[256,2048]{1,0:T(8,128)(2,1)S(1)} collective-permute-done((bf16[256,2048]{1,0:T(8,128)(2,1)S(1)}, bf16[256,2048]{1,0:T(8,128)(2,1)S(1)}, u32[]{:S(2)}, u32[]{:S(2)}) %collective-permute-start.61) | collective-permute-done | bytes 1048608 | tf_op jit(solution)/shard_map/ppermute | solution.py:566
  (466 shorter events, 381.6 us)
Async XLA Ops:
  19.9 41.8 %collective-permute-start.3 = (bf16[256,2048]{0,1:T(8,128)(2,1)}, bf16[256,2048]{0,1:T(8,128)(2,1)}, u32[]{:S(2)}, u32[]{:S(2)}) collective-permute-start(bf16[256,2048]{0,1:T(8,128)(2,1)} %copy.54), channel_id=1, source_target_pairs={{0,16},{4,20},{8,24},{12,28},{16,0},{20,4},{24,8},{28,12},{1,17},{... | collective-permute-start | bytes 3145736 | tf_op jit(solution)/shard_map/ppermute | solution.py:33
  21.4 40.3 %collective-permute-start.2 = (bf16[256,2048]{0,1:T(8,128)(2,1)}, bf16[256,2048]{0,1:T(8,128)(2,1)}, u32[]{:S(2)}, u32[]{:S(2)}) collective-permute-start(bf16[256,2048]{0,1:T(8,128)(2,1)} %copy.54), channel_id=1, source_target_pairs={{0,8},{4,12},{8,0},{12,4},{16,24},{20,28},{24,16},{28,20},{1,9},{5... | collective-permute-start | bytes 3145736 | tf_op jit(solution)/shard_map/ppermute | solution.py:33
  26.7 35.0 %collective-permute-start.1 = (bf16[256,2048]{1,0:T(8,128)(2,1)}, bf16[256,2048]{1,0:T(8,128)(2,1)}, u32[]{:S(2)}, u32[]{:S(2)}) collective-permute-start(bf16[256,2048]{1,0:T(8,128)(2,1)} %columns.6), channel_id=1, source_target_pairs={{1,0},{2,1},{3,2},{5,4},{6,5},{7,6},{9,8},{10,9},{11,10},{13,12},{... | collective-permute-start | bytes 3145736 | tf_op jit(solution)/shard_map/ppermute | solution.py:558
  69.7 50.8 %collective-permute-start.15 = (bf16[256,2048]{0,1:T(8,128)(2,1)}, bf16[256,2048]{0,1:T(8,128)(2,1)}, u32[]{:S(2)}, u32[]{:S(2)}) collective-permute-start(bf16[256,2048]{0,1:T(8,128)(2,1)} %collective-permute-done.3), channel_id=1, source_target_pairs={{0,4},{4,0},{8,12},{12,8},{16,20},{20,16},{24,28},{28,24},{1,5},{5... | collective-permute-start | bytes 3145736 | tf_op jit(solution)/shard_map/ppermute | solution.py:33
  69.9 50.6 %collective-permute-start.14 = (bf16[256,2048]{0,1:T(8,128)(2,1)}, bf16[256,2048]{0,1:T(8,128)(2,1)}, u32[]{:S(2)}, u32[]{:S(2)}) collective-permute-start(bf16[256,2048]{0,1:T(8,128)(2,1)} %collective-permute-done.2), channel_id=1, source_target_pairs={{0,4},{4,0},{8,12},{12,8},{16,20},{20,16},{24,28},{28,24},{1,5},{5... | collective-permute-start | bytes 3145736 | tf_op jit(solution)/shard_map/ppermute | solution.py:33
  101.7 47.9 %collective-permute-start.22 = (bf16[256,2048]{0,1:T(8,128)(2,1)S(1)}, bf16[256,2048]{0,1:T(8,128)(2,1)}, u32[]{:S(2)}, u32[]{:S(2)}) collective-permute-start(bf16[256,2048]{0,1:T(8,128)(2,1)S(1)} %pad_maximum_fusion.10), channel_id=1, source_target_pairs={{0,4},{4,0},{8,12},{12,8},{16,20},{20,16},{24,28},{28,24},{1,5},{5... | collective-permute-start | bytes 3145736 | tf_op jit(solution)/shard_map/ppermute | solution.py:33
  122.7 69.5 %collective-permute-start.21 = (bf16[256,2048]{0,1:T(8,128)(2,1)}, bf16[256,2048]{0,1:T(8,128)(2,1)}, u32[]{:S(2)}, u32[]{:S(2)}) collective-permute-start(bf16[256,2048]{0,1:T(8,128)(2,1)} %collective-permute-done.13), channel_id=1, source_target_pairs={{0,4},{4,0},{8,12},{12,8},{16,20},{20,16},{24,28},{28,24},{1,5},{5... | collective-permute-start | bytes 3145736 | tf_op jit(solution)/shard_map/ppermute | solution.py:33
  125.0 67.2 %collective-permute-start.20 = (bf16[256,2048]{0,1:T(8,128)(2,1)}, bf16[256,2048]{0,1:T(8,128)(2,1)}, u32[]{:S(2)}, u32[]{:S(2)}) collective-permute-start(bf16[256,2048]{0,1:T(8,128)(2,1)} %collective-permute-done.12), channel_id=1, source_target_pairs={{0,4},{4,0},{8,12},{12,8},{16,20},{20,16},{24,28},{28,24},{1,5},{5... | collective-permute-start | bytes 3145736 | tf_op jit(solution)/shard_map/ppermute | solution.py:33
  174.8 75.2 %collective-permute-start.29 = (bf16[256,2048]{0,1:T(8,128)(2,1)}, bf16[256,2048]{0,1:T(8,128)(2,1)}, u32[]{:S(2)}, u32[]{:S(2)}) collective-permute-start(bf16[256,2048]{0,1:T(8,128)(2,1)} %bitcast.94), channel_id=1, source_target_pairs={{0,4},{4,0},{8,12},{12,8},{16,20},{20,16},{24,28},{28,24},{1,5},{5... | collective-permute-start | bytes 3145736 | tf_op jit(solution)/shard_map/ppermute | solution.py:33
  174.9 79.8 %collective-permute-start.26 = (bf16[256,2048]{0,1:T(8,128)(2,1)}, bf16[256,2048]{0,1:T(8,128)(2,1)}, u32[]{:S(2)}, u32[]{:S(2)}) collective-permute-start(bf16[256,2048]{0,1:T(8,128)(2,1)} %bitcast.95), channel_id=1, source_target_pairs={{0,16},{4,20},{8,24},{12,28},{16,0},{20,4},{24,8},{28,12},{1,17},{... | collective-permute-start | bytes 3145736 | tf_op jit(solution)/shard_map/ppermute | solution.py:33
  191.7 67.0 %collective-permute-start.25 = (bf16[256,2048]{0,1:T(8,128)(2,1)}, bf16[256,2048]{0,1:T(8,128)(2,1)}, u32[]{:S(2)}, u32[]{:S(2)}) collective-permute-start(bf16[256,2048]{0,1:T(8,128)(2,1)} %bitcast.96), channel_id=1, source_target_pairs={{0,8},{4,12},{8,0},{12,4},{16,24},{20,28},{24,16},{28,20},{1,9},{5... | collective-permute-start | bytes 3145736 | tf_op jit(solution)/shard_map/ppermute | solution.py:33
  206.2 52.5 %collective-permute-start.28 = (bf16[256,2048]{0,1:T(8,128)(2,1)}, bf16[256,2048]{0,1:T(8,128)(2,1)S(1)}, u32[]{:S(2)}, u32[]{:S(2)}) collective-permute-start(bf16[256,2048]{0,1:T(8,128)(2,1)} %collective-permute-done.19), channel_id=1, source_target_pairs={{0,4},{4,0},{8,12},{12,8},{16,20},{20,16},{24,28},{28,24},{1,5},{5... | collective-permute-start | bytes 3145736 | tf_op jit(solution)/shard_map/ppermute | solution.py:33
  206.3 52.4 %collective-permute-start.24 = (bf16[256,2048]{1,0:T(8,128)(2,1)}, bf16[256,2048]{1,0:T(8,128)(2,1)}, u32[]{:S(2)}, u32[]{:S(2)}) collective-permute-start(bf16[256,2048]{1,0:T(8,128)(2,1)} %columns.7), channel_id=1, source_target_pairs={{1,0},{2,1},{3,2},{5,4},{6,5},{7,6},{9,8},{10,9},{11,10},{13,12},{... | collective-permute-start | bytes 3145736 | tf_op jit(solution)/shard_map/ppermute | solution.py:558
  277.2 46.6 %collective-permute-start.34 = (bf16[256,2048]{0,1:T(8,128)(2,1)}, bf16[256,2048]{0,1:T(8,128)(2,1)}, u32[]{:S(2)}, u32[]{:S(2)}) collective-permute-start(bf16[256,2048]{0,1:T(8,128)(2,1)} %collective-permute-done.25), channel_id=1, source_target_pairs={{0,4},{4,0},{8,12},{12,8},{16,20},{20,16},{24,28},{28,24},{1,5},{5... | collective-permute-start | bytes 3145736 | tf_op jit(solution)/shard_map/ppermute | solution.py:33
  284.3 39.5 %collective-permute-start.30 = (bf16[256,2048]{1,0:T(8,128)(2,1)S(1)}, bf16[256,2048]{1,0:T(8,128)(2,1)}, u32[]{:S(2)}, u32[]{:S(2)}) collective-permute-start(bf16[256,2048]{1,0:T(8,128)(2,1)S(1)} %collective-permute-done.23), channel_id=1, source_target_pairs={{1,2},{2,3},{5,6},{6,7},{9,10},{10,11},{13,14},{14,15},{17,18},{18... | collective-permute-start | bytes 3145736 | tf_op jit(solution)/shard_map/ppermute | solution.py:557
  285.9 37.9 %collective-permute-start.31 = (bf16[256,2048]{1,0:T(8,128)(2,1)}, bf16[256,2048]{1,0:T(8,128)(2,1)}, u32[]{:S(2)}, u32[]{:S(2)}) collective-permute-start(bf16[256,2048]{1,0:T(8,128)(2,1)} %collective-permute-done.24), channel_id=1, source_target_pairs={{1,0},{2,1},{5,4},{6,5},{9,8},{10,9},{13,12},{14,13},{17,16},{18,1... | collective-permute-start | bytes 3145736 | tf_op jit(solution)/shard_map/ppermute | solution.py:558
  287.7 36.1 %collective-permute-start.35 = (bf16[256,2048]{0,1:T(8,128)(2,1)}, bf16[256,2048]{0,1:T(8,128)(2,1)}, u32[]{:S(2)}, u32[]{:S(2)}) collective-permute-start(bf16[256,2048]{0,1:T(8,128)(2,1)} %collective-permute-done.26), channel_id=1, source_target_pairs={{0,4},{4,0},{8,12},{12,8},{16,20},{20,16},{24,28},{28,24},{1,5},{5... | collective-permute-start | bytes 3145736 | tf_op jit(solution)/shard_map/ppermute | solution.py:33
  323.8 38.0 %collective-permute-start.36 = (bf16[256,2048]{1,0:T(8,128)(2,1)}, bf16[256,2048]{1,0:T(8,128)(2,1)S(1)}, u32[]{:S(2)}, u32[]{:S(2)}) collective-permute-start(bf16[256,2048]{1,0:T(8,128)(2,1)} %collective-permute-done.30), channel_id=1, source_target_pairs={{2,3},{6,7},{10,11},{14,15},{18,19},{22,23},{26,27},{30,31}} | collective-permute-start | bytes 3145736 | tf_op jit(solution)/shard_map/ppermute | solution.py:557
  325.9 36.0 %collective-permute-start.37 = (bf16[256,2048]{1,0:T(8,128)(2,1)}, bf16[256,2048]{1,0:T(8,128)(2,1)S(1)}, u32[]{:S(2)}, u32[]{:S(2)}) collective-permute-start(bf16[256,2048]{1,0:T(8,128)(2,1)} %collective-permute-done.31), channel_id=1, source_target_pairs={{1,0},{5,4},{9,8},{13,12},{17,16},{21,20},{25,24},{29,28}} | collective-permute-start | bytes 3145736 | tf_op jit(solution)/shard_map/ppermute | solution.py:558
  411.7 41.8 %collective-permute-start.44 = (bf16[256,2048]{1,0:T(8,128)(2,1)S(1)}, bf16[256,2048]{1,0:T(8,128)(2,1)}, u32[]{:S(2)}, u32[]{:S(2)}) collective-permute-start(bf16[256,2048]{1,0:T(8,128)(2,1)S(1)} %get-tuple-element.563), channel_id=1, source_target_pairs={{2,1},{3,2},{6,5},{7,6},{10,9},{11,10},{14,13},{15,14},{18,17},{19... | collective-permute-start | bytes 3145736 | tf_op jit(solution)/shard_map/ppermute | solution.py:567
  413.5 40.0 %collective-permute-start.43 = (bf16[256,2048]{1,0:T(8,128)(2,1)S(1)}, bf16[256,2048]{1,0:T(8,128)(2,1)}, u32[]{:S(2)}, u32[]{:S(2)}) collective-permute-start(bf16[256,2048]{1,0:T(8,128)(2,1)S(1)} %get-tuple-element.564), channel_id=1, source_target_pairs={{0,1},{1,2},{4,5},{5,6},{8,9},{9,10},{12,13},{13,14},{16,17},{17,1... | collective-permute-start | bytes 3145736 | tf_op jit(solution)/shard_map/ppermute | solution.py:566
  460.4 39.3 %collective-permute-start.50 = (bf16[256,2048]{1,0:T(8,128)(2,1)}, bf16[256,2048]{1,0:T(8,128)(2,1)}, u32[]{:S(2)}, u32[]{:S(2)}) collective-permute-start(bf16[256,2048]{1,0:T(8,128)(2,1)} %pad_maximum_fusion.11), channel_id=1, source_target_pairs={{0,8},{4,12},{8,0},{12,4},{16,24},{20,28},{24,16},{28,20},{1,9},{5... | collective-permute-start | bytes 3145736 | tf_op jit(solution)/shard_map/ppermute | solution.py:33
  462.0 37.7 %collective-permute-start.51 = (bf16[256,2048]{1,0:T(8,128)(2,1)}, bf16[256,2048]{1,0:T(8,128)(2,1)}, u32[]{:S(2)}, u32[]{:S(2)}) collective-permute-start(bf16[256,2048]{1,0:T(8,128)(2,1)} %pad_maximum_fusion.12), channel_id=1, source_target_pairs={{0,16},{4,20},{8,24},{12,28},{16,0},{20,4},{24,8},{28,12},{1,17},{... | collective-permute-start | bytes 3145736 | tf_op jit(solution)/shard_map/ppermute | solution.py:33
  510.5 50.4 %collective-permute-start.56 = (bf16[1024,2048]{1,0:T(8,128)(2,1)}, bf16[1024,2048]{1,0:T(8,128)(2,1)}, u32[]{:S(2)}, u32[]{:S(2)}) collective-permute-start(bf16[1024,2048]{1,0:T(8,128)(2,1)} %pad_maximum_fusion.2), channel_id=1, source_target_pairs={{0,4},{4,0},{8,12},{12,8},{16,20},{20,16},{24,28},{28,24},{1,5},{5... | collective-permute-start | bytes 12582920 | tf_op jit(solution)/shard_map/ppermute | solution.py:33
  (111 other events, 2399.9 us)

commit v3 on v2

--- a/solution.py
+++ b/solution.py
@@ -199,14 +199,42 @@
     return allowed, jnp.where(allowed, scores, -1e30)
 
 
+SMALL = pl.CostEstimate(flops=1000, bytes_accessed=1000, transcendentals=0)
+
+
+def spots(me_ref, size, block):
+    def spot(b):
+        return pl.ds(pl.multiple_of(lax.rem(b - me_ref[0] + size, size) * block, block), block)
+
+    return spot
+
+
+def forward_block(q_out, k_out, v_out, att_ref, log_ref, col_ref, row_ref, spot, b, block):
+    scale = q_out.shape[-1] ** (-0.5)
+    here = slice(b * block, (b + 1) * block)
+    query = q_out[spot(b), :]
+    scores = jnp.concatenate(
+        [contract(query, k_out[spot(c), :], ((1,), (1,))) for c in range(b + 1)], axis=1
+    ) * scale
+    _, scores = masked(scores, col_ref[here, :1], row_ref[:1, :], b, block)
+    top = jnp.max(scores, axis=1, keepdims=True)
+    powers = jnp.exp(scores - top)
+    total = jnp.sum(powers, axis=1, keepdims=True)
+    weights = (powers / total).astype(BF16)
+    attended = contract(weights[:, :block], v_out[spot(0), :], ((1,), (0,)))
+    for c in range(1, b + 1):
+        attended = attended + contract(
+            weights[:, c * block : (c + 1) * block], v_out[spot(c), :], ((1,), (0,))
+        )
+    att_ref[spot(b), :] = attended.astype(BF16)
+    log_ref[0, here, :] = jnp.broadcast_to(top + jnp.log(total), (block, log_ref.shape[2]))
+
+
 def forward_kernel(
     me_ref, q_ref, k_ref, v_ref, cos_ref, low_ref, high_ref, col_ref, row_ref,
     q_out, k_out, v_out, att_ref, log_ref, *, size, block,
 ):
-    def spot(b):
-        return pl.ds(pl.multiple_of(lax.rem(b - me_ref[0] + size, size) * block, block), block)
-
-    scale = q_ref.shape[-1] ** (-0.5)
+    spot = spots(me_ref, size, block)
     for b in range(size):
         here = slice(b * block, (b + 1) * block)
         at = spot(b)
@@ -215,32 +243,35 @@
         k_out[at, :] = turn(k_ref[at, :], *tables, 1.0).astype(BF16)
         v_out[at, :] = v_ref[at, :].astype(BF16)
     for b in range(size):
+        forward_block(q_out, k_out, v_out, att_ref, log_ref, col_ref, row_ref, spot, b, block)
+
+
+def joined_forward_kernel(
+    me_ref, rows_ref, qa_ref, ka_ref, va_ref, qb_ref, kb_ref, vb_ref, q_bias, k_bias, v_bias,
+    cos_ref, low_ref, high_ref, col_ref, row_ref,
+    q_out, k_out, v_out, att_ref, log_ref, *, size, block,
+):
+    spot = spots(me_ref, size, block)
+    middle = qa_ref.shape[0]
+    for b in range(size):
         here = slice(b * block, (b + 1) * block)
-        query = q_out[spot(b), :]
-        scores = jnp.concatenate(
-            [contract(query, k_out[spot(c), :], ((1,), (1,))) for c in range(b + 1)], axis=1
-        ) * scale
-        _, scores = masked(scores, col_ref[here, :1], row_ref[:1, :], b, block)
-        top = jnp.max(scores, axis=1, keepdims=True)
-        powers = jnp.exp(scores - top)
-        total = jnp.sum(powers, axis=1, keepdims=True)
-        weights = (powers / total).astype(BF16)
-        attended = contract(weights[:, :block], v_out[spot(0), :], ((1,), (0,)))
-        for c in range(1, b + 1):
-            attended = attended + contract(
-                weights[:, c * block : (c + 1) * block], v_out[spot(c), :], ((1,), (0,))
-            )
-        att_ref[spot(b), :] = attended.astype(BF16)
-        log_ref[0, here, :] = jnp.broadcast_to(top + jnp.log(total), (block, log_ref.shape[2]))
-
-
-def backward_kernel(
-    me_ref, q_ref, k_ref, v_ref, g_ref, log_ref, cos_ref, low_ref, high_ref, col_ref, row_ref,
-    dq_ref, dk_ref, dv_ref, k_acc, v_acc, *, size, block,
+        at = spot(b)
+        tables = cos_ref[here, :], low_ref[here, :], high_ref[here, :]
+        top, low = rows_ref[at, :middle], rows_ref[at, middle:]
+
+        def project(one, two, bias):
+            return contract(top, one[:, :], ((1,), (0,))) + contract(low, two[:, :], ((1,), (0,))) + bias[:, :]
+
+        q_out[at, :] = turn(project(qa_ref, qb_ref, q_bias), *tables, 1.0).astype(BF16)
+        k_out[at, :] = turn(project(ka_ref, kb_ref, k_bias), *tables, 1.0).astype(BF16)
+        v_out[at, :] = project(va_ref, vb_ref, v_bias).astype(BF16)
+        forward_block(q_out, k_out, v_out, att_ref, log_ref, col_ref, row_ref, spot, b, block)
+
+
+def backward_pass(
+    q_ref, k_ref, v_ref, g_ref, log_ref, cos_ref, low_ref, high_ref, col_ref, row_ref,
+    put, k_acc, v_acc, spot, size, block,
 ):
-    def spot(b):
-        return pl.ds(pl.multiple_of(lax.rem(b - me_ref[0] + size, size) * block, block), block)
-
     scale = q_ref.shape[-1] ** (-0.5)
     for b in range(size):
         here = slice(b * block, (b + 1) * block)
@@ -270,12 +301,232 @@
                 k_acc[part, :] += key_term
                 v_acc[part, :] += value_term
         tables = cos_ref[here, :], low_ref[here, :], high_ref[here, :]
-        dq_ref[spot(b), :] = turn(back * scale, *tables, -1.0).astype(BF16)
+        put(0, spot(b), turn(back * scale, *tables, -1.0).astype(BF16))
     for b in range(size):
         here = slice(b * block, (b + 1) * block)
         tables = cos_ref[here, :], low_ref[here, :], high_ref[here, :]
-        dk_ref[spot(b), :] = turn(k_acc[here, :] * scale, *tables, -1.0).astype(BF16)
-        dv_ref[spot(b), :] = v_acc[here, :].astype(BF16)
+        put(1, spot(b), turn(k_acc[here, :] * scale, *tables, -1.0).astype(BF16))
+        put(2, spot(b), v_acc[here, :].astype(BF16))
+
+
+def backward_kernel(
+    me_ref, q_ref, k_ref, v_ref, g_ref, log_ref, cos_ref, low_ref, high_ref, col_ref, row_ref,
+    dq_ref, dk_ref, dv_ref, k_acc, v_acc, *, size, block,
+):
+    outs = (dq_ref, dk_ref, dv_ref)
+
+    def put(k, at, value):
+        outs[k][at, :] = value
+
+    backward_pass(
+        q_ref, k_ref, v_ref, g_ref, log_ref, cos_ref, low_ref, high_ref, col_ref, row_ref,
+        put, k_acc, v_acc, spots(me_ref, size, block), size, block,
+    )
+
+
+def mixed_backward_kernel(
+    me_ref, q_ref, k_ref, v_ref, g_ref, a_ref, b_ref, log_ref, cos_ref, low_ref, high_ref, col_ref, row_ref,
+    d_ref, k_acc, v_acc, g_acc, *, size, block, heads,
+):
+    middle = a_ref.shape[0]
+    head = q_ref.shape[1]
+    for b in range(size):
+        here = slice(b * block, (b + 1) * block)
+        g_acc[here, :] = (
+            contract(g_ref[here, :middle], a_ref[:, :], ((1,), (0,)))
+            + contract(g_ref[here, middle:], b_ref[:, :], ((1,), (0,)))
+        ).astype(BF16)
+    h = pl.program_id(0)
+
+    def put(k, at, value):
+        d_ref[at, pl.ds(pl.multiple_of((k * heads + h) * head, head), head)] = value
+
+    backward_pass(
+        q_ref, k_ref, v_ref, g_acc, log_ref, cos_ref, low_ref, high_ref, col_ref, row_ref,
+        put, k_acc, v_acc, spots(me_ref, size, block), size, block,
+    )
+
+
+def hidden_kernel(rows_ref, a_ref, b_ref, bias_ref, act_ref, slope_ref, *, step):
+    middle = a_ref.shape[0]
+    for i in range(rows_ref.shape[0] // step):
+        here = slice(i * step, (i + 1) * step)
+        hidden = contract(rows_ref[here, :middle], a_ref[:, :], ((1,), (0,)))
+        hidden = hidden + contract(rows_ref[here, middle:], b_ref[:, :], ((1,), (0,))) + bias_ref[:, :]
+        bell = lax.erf(hidden * (0.5**0.5))
+        act_ref[here, :] = (0.5 * hidden * (1.0 + bell)).astype(BF16)
+        slope = 0.5 * (1.0 + bell) + hidden * jnp.exp(-0.5 * hidden * hidden) * 0.3989422804014327
+        slope_ref[here, :] = slope.astype(BF16)
+
+
+def hidden_half(rows, top, low, bias):
+    count, width = rows.shape
+    out = top.shape[1]
+    tile = 512
+    half = pl.BlockSpec((top.shape[0], tile), lambda j: (0, j))
+    made = pl.BlockSpec((count, tile), lambda j: (0, j))
+    return pl.pallas_call(
+        functools.partial(hidden_kernel, step=256),
+        out_shape=(jax.ShapeDtypeStruct((count, out), BF16),) * 2,
+        grid=(out // tile,),
+        in_specs=[
+            pl.BlockSpec((count, width), lambda j: (0, 0)), half, half, pl.BlockSpec((1, tile), lambda j: (0, j))
+        ],
+        out_specs=(made, made),
+        cost_estimate=SMALL,
+        name="hidden",
+    )(rows, top, low, bias.reshape(1, -1))
+
+
+def slope_kernel(rows_ref, a_ref, b_ref, slope_ref, out_ref, *, step):
+    middle = a_ref.shape[0]
+    for i in range(rows_ref.shape[0] // step):
+        here = slice(i * step, (i + 1) * step)
+        active = contract(rows_ref[here, :middle], a_ref[:, :], ((1,), (0,)))
+        active = active + contract(rows_ref[here, middle:], b_ref[:, :], ((1,), (0,)))
+        out_ref[here, :] = (active * slope_ref[here, :].astype(F32)).astype(BF16)
+
+
+def hidden_back(rows, top, low, slope):
+    count, width = rows.shape
+    out = top.shape[1]
+    tile = 512
+    half = pl.BlockSpec((top.shape[0], tile), lambda j: (0, j))
+    made = pl.BlockSpec((count, tile), lambda j: (0, j))
+    return pl.pallas_call(
+        functools.partial(slope_kernel, step=256),
+        out_shape=jax.ShapeDtypeStruct((count, out), BF16),
+        grid=(out // tile,),
+        in_specs=[pl.BlockSpec((count, width), lambda j: (0, 0)), half, half, made],
+        out_specs=made,
+        cost_estimate=SMALL,
+        name="hidden_back",
+    )(rows, top, low, slope)
+
+
+def branch_kernel(att_ref, mix_ref, act_ref, down_ref, out_ref, *, step):
+    for i in range(att_ref.shape[0] // step):
+        here = slice(i * step, (i + 1) * step)
+        total = contract(att_ref[here, :], mix_ref[:, :], ((1,), (1,)))
+        total = total + contract(act_ref[here, :], down_ref[:, :], ((1,), (1,)))
+        out_ref[here, :] = total.astype(BF16)
+
+
+def branch_half(attended, mixed, activated, down):
+    count, inner = attended.shape
+    units = activated.shape[1]
+    width = down.shape[0]
+    tile = 256
+    spot = mixed.shape[1] // inner - 1
+    return pl.pallas_call(
+        functools.partial(branch_kernel, step=256),
+        out_shape=jax.ShapeDtypeStruct((count, width), BF16),
+        grid=(width // tile,),
+        in_specs=[
+            pl.BlockSpec((count, inner), lambda j: (0, 0)),
+            pl.BlockSpec((tile, inner), lambda j: (j, spot)),
+            pl.BlockSpec((count, units), lambda j: (0, 0)),
+            pl.BlockSpec((tile, units), lambda j: (j, 0)),
+        ],
+        out_specs=pl.BlockSpec((count, tile), lambda j: (0, j)),
+        cost_estimate=SMALL,
+        name="branches",
+    )(attended, mixed, activated, down)
+
+
+def back_kernel(
+    hid_ref, proj_ref, up_ref, join_ref, tok_ref, mean_ref, scale_ref, gain_ref, back_ref, sum_ref, *, step
+):
+    sums = [0.0] * 4
+    for i in range(hid_ref.shape[0] // step):
+        here = slice(i * step, (i + 1) * step)
+        two = contract(hid_ref[here, :], up_ref[:, :], ((1,), (1,)))
+        one = contract(proj_ref[here, :], join_ref[:, :], ((1,), (1,)))
+        back_ref[here, :] = (one * gain_ref[:1, :] + two * gain_ref[1:2, :]).astype(BF16)
+        xhat = (tok_ref[here, :].astype(F32) - mean_ref[here, :1]) * scale_ref[here, :1]
+        for k, term in enumerate((one * xhat, two * xhat, one, two)):
+            sums[k] = sums[k] + jnp.sum(term, axis=0, keepdims=True)
+    for k in range(4):
+        sum_ref[k : k + 1, :] = sums[k]
+
+
+def back_half(grad_hidden, grad_projected, up, mixed, token_rows, mean, scale, gains, part):
+    count, units = grad_hidden.shape
+    joined = grad_projected.shape[1]
+    width = up.shape[0]
+    tile = 256
+    tiles = width // tile
+    whole = lambda j: (0, 0)
+    return pl.pallas_call(
+        functools.partial(back_kernel, step=256),
+        out_shape=(jax.ShapeDtypeStruct((count, width), BF16), jax.ShapeDtypeStruct((8, width), F32)),
+        grid=(tiles,),
+        in_specs=[
+            pl.BlockSpec((count, units), whole),
+            pl.BlockSpec((count, joined), whole),
+            pl.BlockSpec((tile, units), lambda j: (j, 0)),
+            pl.BlockSpec((tile, joined), lambda j: (j, 0)),
+            pl.BlockSpec((count, tile), lambda j: (0, j + part * tiles)),
+            pl.BlockSpec((count, 128), whole),
+            pl.BlockSpec((count, 128), whole),
+            pl.BlockSpec((2, tile), lambda j: (0, j + part * tiles)),
+        ],
+        out_specs=(pl.BlockSpec((count, tile), lambda j: (0, j)), pl.BlockSpec((8, tile), lambda j: (0, j))),
+        cost_estimate=SMALL,
+        name="back",
+    )(grad_hidden, grad_projected, up, mixed, token_rows, mean, scale, gains)
+
+
+def joined_forward(rows, top, low, bias, tables, me, heads, head, size):
+    count, width = rows.shape
+    block = count // size
+    whole = lambda h, s: (0, 0)
+    table_specs = [pl.BlockSpec((count, 128), whole)] * 4 + [pl.BlockSpec((8, count), whole)]
+    by_head = pl.BlockSpec((count, head), lambda h, s: (0, h))
+    wide = jax.ShapeDtypeStruct((count, heads * head), BF16)
+
+    def thirds(n):
+        return [pl.BlockSpec((n, head), lambda h, s, k=k: (0, k * heads + h)) for k in range(3)]
+
+    return pl.pallas_call(
+        functools.partial(joined_forward_kernel, size=size, block=block),
+        out_shape=(wide, wide, wide, wide, jax.ShapeDtypeStruct((heads, count, 128), F32)),
+        grid_spec=pltpu.PrefetchScalarGridSpec(
+            num_scalar_prefetch=1,
+            grid=(heads,),
+            in_specs=[pl.BlockSpec((count, width), whole)]
+            + thirds(top.shape[0]) + thirds(low.shape[0]) + thirds(1) + table_specs,
+            out_specs=(by_head,) * 4 + (pl.BlockSpec((1, count, 128), lambda h, s: (h, 0, 0)),),
+        ),
+        cost_estimate=SMALL,
+        name="joined_forward",
+    )(me, rows, top, top, top, low, low, low, bias, bias, bias, *tables)
+
+
+def mixed_backward(queries, keys, values, grads, top, low, log_total, tables, me, heads, size):
+    count = queries.shape[0]
+    head = queries.shape[1] // heads
+    block = count // size
+    whole = lambda h, s: (0, 0)
+    table_specs = [pl.BlockSpec((count, 128), whole)] * 4 + [pl.BlockSpec((8, count), whole)]
+    by_head = pl.BlockSpec((count, head), lambda h, s: (0, h))
+    mix = pl.BlockSpec((top.shape[0], head), lambda h, s: (0, 3 * heads + h))
+    return pl.pallas_call(
+        functools.partial(mixed_backward_kernel, size=size, block=block, heads=heads),
+        out_shape=jax.ShapeDtypeStruct((count, 3 * heads * head), BF16),
+        grid_spec=pltpu.PrefetchScalarGridSpec(
+            num_scalar_prefetch=1,
+            grid=(heads,),
+            in_specs=[by_head] * 3
+            + [pl.BlockSpec((count, grads.shape[1]), whole), mix, mix]
+            + [pl.BlockSpec((1, count, 128), lambda h, s: (h, 0, 0))]
+            + table_specs,
+            out_specs=pl.BlockSpec((count, 3 * heads * head), whole),
+            scratch_shapes=[pltpu.VMEM((count, head), F32)] * 2 + [pltpu.VMEM((count, head), BF16)],
+        ),
+        cost_estimate=SMALL,
+        name="mixed_backward",
+    )(me, queries, keys, values, grads, top, low, log_total, *tables)
 
 
 def attention_tables(positions, starts):
@@ -444,7 +695,6 @@
     )
     table = jnp.zeros((n_dp * n_tensor, vectors.shape[1]), BF16)
     table = lax.dynamic_update_slice(table, vectors, (dp_index * n_tensor + tensor_index, 0))
-    table = butterfly(butterfly(table, "dp"), "tensor")
     local_tokens, local_grads = to_frame(tokens), to_frame(cotangent)
     positions = dp_index * row_count + jnp.arange(row_count, dtype=jnp.int32) - seq_start
     tables = attention_tables(positions, seq_start)
@@ -490,25 +740,31 @@
         ) * scale_local
         return from_frame(local_grads.astype(F32) + grad_norm_in)
 
+    def small_shares(five, joined_bias_sums, up_bias_sums):
+        five = five.reshape(5, width)
+        mine = lax.dynamic_slice_in_dim(
+            five, (dp_index * n_tensor + tensor_index) * columns, columns, 1
+        )
+        biases_grad = jnp.concatenate([mine[2:], mine[4:]], axis=0)
+        joined_bias_sum = lax.dynamic_slice_in_dim(
+            joined_bias_sums.reshape(3, heads_here, head_size),
+            dp_index * proj_bias.shape[2],
+            proj_bias.shape[2],
+            2,
+        )
+        up_bias_sum = lax.dynamic_slice_in_dim(
+            up_bias_sums.reshape(1, -1), dp_index * up_bias.shape[1], up_bias.shape[1], 1
+        )
+        return mine[:2], biases_grad, joined_bias_sum, up_bias_sum
+
     def small_grads(five, joined_bias_term, up_bias_term):
         five = from_frame(five).reshape(1, -1)
         terms = jnp.concatenate([five, joined_bias_term[None], up_bias_term[None]], axis=1)
         terms = butterfly(terms, "dp")
-        five = butterfly(terms[:, : 5 * width], "tensor").reshape(5, width)
-        mine = lax.dynamic_slice_in_dim(
-            five, (dp_index * n_tensor + tensor_index) * columns, columns, 1
-        )
-        biases_grad = jnp.concatenate([mine[2:], mine[4:]], axis=0)
-        joined_bias_sum = lax.dynamic_slice_in_dim(
-            terms[0, 5 * width : 5 * width + joined_width].reshape(3, heads_here, head_size),
-            dp_index * proj_bias.shape[2],
-            proj_bias.shape[2],
-            2,
-        )
-        up_bias_sum = lax.dynamic_slice_in_dim(
-            terms[:, 5 * width + joined_width :], dp_index * up_bias.shape[1], up_bias.shape[1], 1
-        )
-        return mine[:2], biases_grad, joined_bias_sum, up_bias_sum
+        five = butterfly(terms[:, : 5 * width], "tensor")
+        return small_shares(
+            five, terms[0, 5 * width : 5 * width + joined_width], terms[:, 5 * width + joined_width :]
+        )
 
     def plain():
         token_rows, grad_rows = line_gather(local_tokens), line_gather(local_grads)
@@ -517,7 +773,9 @@
         up_rows, down_rows, joined_rows, mix_rows = (
             join(w, 0, None) for w in (up_rows, down_rows, joined_rows, mix_rows)
         )
-        gain_rows, shift_rows, joined_bias, hidden_bias = small_parameters(table)
+        gain_rows, shift_rows, joined_bias, hidden_bias = small_parameters(
+            butterfly(butterfly(table, "dp"), "tensor")
+        )
         first_rows, second_rows = norm_rows(token_rows, gain_rows, shift_rows)
         activated, slope = cut(*hidden_units(second_rows, up_rows, hidden_bias))
         *kept, attended, log_total = attend(first_rows, joined_rows, joined_bias)
@@ -558,9 +816,11 @@
             down = lax.ppermute(down, "tensor", [(i + 1, i) for i in range(3 - s)])
             return up, down
 
-        def scatter_step(terms, up, down, s):
-            to_up = terms[(4 - s) * local_rows : (5 - s) * local_rows]
-            to_down = terms[s * local_rows : (s + 1) * local_rows]
+        def scatter_step(halves, up, down, s):
+            def block(r):
+                return jnp.concatenate([h[r * local_rows : (r + 1) * local_rows] for h in halves], axis=1)
+
+            to_up, to_down = block(4 - s), block(s)
             if s > 1:
                 to_up, to_down = plus(to_up, up).astype(BF16), plus(to_down, down).astype(BF16)
             up = lax.ppermute(to_up, "tensor", [(i, i + 1) for i in range(s)])
@@ -576,94 +836,88 @@
         def pair(top, low):
             return jnp.concatenate([top, low], axis=0)
 
+        def lay(own, from_x, far_x, far_y, from_y):
+            return jnp.concatenate(
+                [own, from_x[second], from_x[first], far_x, far_y, from_y[second], from_y[first]], axis=0
+            )
+
         wa = up_weight
         wb = jnp.concatenate([flat_proj, out_weight.T], axis=1)
         wc = down_weight.T
 
         tu1, td1 = gather_step(local_tokens, local_tokens, 0)
-        ax, ay, na = x(wa), y(wa), core(wa)
-        tu1, td1, ax, ay, na, table1, wb, wc = cut(tu1, td1, ax, ay, na, table, wb, wc)
+        table1 = table + core(table)
+        table1 = table1 + x(table1) + y(table1) + xor_shift(table1, "dp", 6)
+        wa1, table1 = cut(wa, table1)
+        ax, ay = x(wa1), y(wa1)
+        table1 = table1 + xor_shift(table1, "tensor", 1)
+        tu1, td1, ax, ay, table1, wb, wc, tables1 = cut(tu1, td1, ax, ay, table1, wb, wc, tables)
         tu2, td2 = gather_step(tu1, td1, 1)
         p2x, p2y = x(pair(ay[first], wb[second])), y(pair(ax[second], wb[first]))
-        nax, nay = core(ax), core(ay)
-        gain_rows, shift_rows, joined_bias, hidden_bias = small_parameters(table1)
-        tu2, td2, p2x, p2y, nax, nay = cut(tu2, td2, p2x, p2y, nax, nay)
+        table2 = table1 + xor_shift(table1, "tensor", 2)
+        tu2, td2, p2x, p2y, table2 = cut(tu2, td2, p2x, p2y, table2)
         tu3, td3 = gather_step(tu2, td2, 2)
         p3x, p3y = x(pair(p2y[second], wb[first])), y(pair(p2x[second], wb[second]))
-        n2x, n2y, nb = core(p2x), core(p2y), core(wb)
-        tu3, td3, p3x, p3y, n2x, n2y, nb, local_grads1 = cut(
-            tu3, td3, p3x, p3y, n2x, n2y, nb, local_grads
+        up_1 = lay(wa, ax, p2x[first], p2y[first], ay)
+        up_2 = core(up_1)
+        gain_rows, shift_rows, joined_bias, hidden_bias = small_parameters(table2)
+        tu3, td3, p3x, p3y, up_1, up_2, local_grads1, gain_rows, shift_rows = cut(
+            tu3, td3, p3x, p3y, up_1, up_2, local_grads, gain_rows, shift_rows
         )
         cu1, cd1 = gather_step(local_grads1, local_grads1, 0)
         cx, cy = x(wc), y(wc)
-        n3x, n3y, nc = core(p3x), core(p3y), core(wc)
+        mix_1 = pair(
+            jnp.concatenate([wb, p2x[second], p3x[second], p3x[first]], axis=0),
+            jnp.concatenate([p3y[first], p3y[second], p2y[second]], axis=0),
+        )
+        mix_2 = core(mix_1)
         token_rows = in_turn(local_tokens, (tu1, tu2, tu3), (td1, td2, td3))
         first_rows, second_rows = norm_rows(token_rows, gain_rows, shift_rows)
-        up_rows = jnp.concatenate(
-            [wa, ax[second], ax[first], p2x[first], p2y[first], ay[second], ay[first]]
-            + [na, nax[second], nax[first], n2x[first], n2y[first], nay[second], nay[first]],
-            axis=0,
-        )
-        activated, slope = hidden_units(second_rows, up_rows, hidden_bias)
-        cu1, cd1, cx, cy, n3x, n3y, nc, first_rows, activated, slope = cut(
-            cu1, cd1, cx, cy, n3x, n3y, nc, first_rows, activated, slope
+        activated, slope = hidden_half(second_rows, up_1, up_2, hidden_bias)
+        cu1, cd1, cx, cy, mix_1, mix_2, first_rows, activated, slope = cut(
+            cu1, cd1, cx, cy, mix_1, mix_2, first_rows, activated, slope
         )
         cu2, cd2 = gather_step(cu1, cd1, 1)
         fcx, fcy = x(cy[first]), y(cx[second])
-        ncx, ncy = core(cx), core(cy)
-        second_pieces = [wb, p2x[second], p3x[second], p3x[first], p3y[first], p3y[second], p2y[second]] + [
-            nb, n2x[second], n3x[second], n3x[first], n3y[first], n3y[second], n2y[second]
-        ]
-        joined_rows = join(second_pieces, 0, joined_width)
-        mix_rows = join(second_pieces, joined_width, None)
-        *kept, attended, log_total = attend(first_rows, joined_rows, joined_bias)
-        kept = (*kept, log_total)
-        cu2, cd2, fcx, fcy, ncx, ncy, attended = cut(cu2, cd2, fcx, fcy, ncx, ncy, attended)
+        *kept, attended, log_total = joined_forward(
+            first_rows, mix_1, mix_2, joined_bias.reshape(1, -1), tables1, me, heads_here, head_size, n_tensor
+        )
+        cu2, cd2, fcx, fcy, attended = cut(cu2, cd2, fcx, fcy, attended)
         cu3, cd3 = gather_step(cu2, cd2, 2)
-        nfx, nfy = core(fcx), core(fcy)
-        down_rows = jnp.concatenate(
-            [wc, cx[second], cx[first], fcx, fcy, cy[second], cy[first]]
-            + [nc, ncx[second], ncx[first], nfx, nfy, ncy[second], ncy[first]],
-            axis=0,
-        )
-        branch_terms = branch_rows(attended, mix_rows, activated, down_rows)
-        cu3, cd3, branch_terms, activated = cut(cu3, cd3, branch_terms, activated)
-        bu, bd = scatter_step(branch_terms, None, None, 1)
+        down_1 = lay(wc, cx, fcx, fcy, cy)
+        down_2 = core(down_1)
+        branch_1 = branch_half(attended, mix_1, activated, down_1)
+        branch_2 = branch_half(attended, mix_2, activated, down_2)
+        cu3, cd3, branch_1, branch_2, activated = cut(cu3, cd3, branch_1, branch_2, activated)
+        branches = (branch_1, branch_2)
+        bu, bd = scatter_step(branches, None, None, 1)
         grad_rows = in_turn(local_grads1, (cu1, cu2, cu3), (cd1, cd2, cd3))
-        away = grad_half(grad_rows, activated, 1)
-        came = core(away)
+        came_d = core(grad_half(grad_rows, activated, 1))
         keep_d = grad_half(grad_rows, activated, 0)
-        grad_hidden = hidden_grads(grad_rows, down_rows, slope)
+        grad_hidden = hidden_back(grad_rows, down_1, down_2, slope)
         bu, bd, came_d, keep_d, grad_hidden, grad_rows = cut(
-            bu, bd, came, keep_d, grad_hidden, grad_rows
+            bu, bd, came_d, keep_d, grad_hidden, grad_rows
         )
 
         def at(keep, came, start, stop):
             return plus(keep[start * half : stop * half], came[start * half : stop * half])
 
-        bu, bd = scatter_step(branch_terms, bu, bd, 2)
+        bu, bd = scatter_step(branches, bu, bd, 2)
         d1x = x(at(keep_d, came_d, 3, 5).astype(BF16))
         d1y = y(at(keep_d, came_d, 5, 7).astype(BF16))
         came_u = core(grad_half(second_rows, grad_hidden, 1))
         keep_u = grad_half(second_rows, grad_hidden, 0)
-        grad_projected = attend_back(kept, attended_grads(grad_rows, mix_rows))
+        grad_projected = mixed_backward(
+            *kept, grad_rows, mix_1, mix_2, log_total, tables1, me, heads_here, n_tensor
+        )
         bu, bd, d1x, d1y, came_u, keep_u, grad_projected, grad_hidden = cut(
             bu, bd, d1x, d1y, came_u, keep_u, grad_projected, grad_hidden
         )
-        bu, bd = scatter_step(branch_terms, bu, bd, 3)
+        bu, bd = scatter_step(branches, bu, bd, 3)
         d2x = plus(at(keep_d, came_d, 2, 3), d1y[first]).astype(BF16)
         d2y = plus(at(keep_d, came_d, 7, 8), d1x[second]).astype(BF16)
         s9x = x(pair(d2x, at(keep_u, came_u, 4, 5).astype(BF16)))
         s9y = y(pair(d2y, at(keep_u, came_u, 5, 6).astype(BF16)))
-        grad_second = back_rows(grad_hidden, up_rows)
-        grad_first = back_rows(grad_projected, joined_rows)
-        back = (grad_first * gain_rows[0] + grad_second * gain_rows[1]).astype(BF16)
-        bu, bd, s9x, s9y, back, grad_projected, attended = cut(
-            bu, bd, s9x, s9y, back, grad_projected, attended
-        )
-        eu, ed = scatter_step(back, None, None, 1)
-        s10x = x(pair(plus(at(keep_u, came_u, 2, 3), s9y[second]), at(keep_u, came_u, 3, 4)).astype(BF16))
-        s10y = y(pair(at(keep_u, came_u, 6, 7), plus(at(keep_u, came_u, 7, 8), s9x[second])).astype(BF16))
 
         def joined_half(part):
             return jnp.concatenate(
@@ -671,33 +925,67 @@
             )
 
         came_j = core(joined_half(1))
+        values = token_rows.astype(F32)
+        mean = jnp.mean(values, axis=-1, keepdims=True)
+        _, scale = standardize(token_rows)
+        mean, scale = (jnp.broadcast_to(v, (row_count, 128)) for v in (mean, scale))
+        back_1, sums_1 = back_half(grad_hidden, grad_projected, up_1, mix_1, token_rows, mean, scale, gain_rows, 0)
+        back_2, sums_2 = back_half(grad_hidden, grad_projected, up_2, mix_2, token_rows, mean, scale, gain_rows, 1)
+        bu, bd, s9x, s9y, came_j, back_1, back_2, sums_1, sums_2, grad_projected, attended = cut(
+            bu, bd, s9x, s9y, came_j, back_1, back_2, sums_1, sums_2, grad_projected, attended
+        )
+        backs = (back_1, back_2)
+        eu, ed = scatter_step(backs, None, None, 1)
+        s10x = x(pair(plus(at(keep_u, came_u, 2, 3), s9y[second]), at(keep_u, came_u, 3, 4)).astype(BF16))
+        s10y = y(pair(at(keep_u, came_u, 6, 7), plus(at(keep_u, came_u, 7, 8), s9x[second])).astype(BF16))
+        five = jnp.concatenate(
+            [
+                jnp.concatenate([sums_1[:4], sums_2[:4]], axis=1),
+                jnp.sum(local_grads.astype(F32), axis=0, keepdims=True),
+            ],
+            axis=0,
+        )
+        five = from_frame(five).reshape(1, -1)
+        five = five + xor_shift(five, "tensor", 1)
         keep_j = joined_half(0)
-        output = finish_output(plus(branch_terms[:local_rows], bu, bd), shift_rows)
+        own = jnp.concatenate([h[:local_rows] for h in branches], axis=1)
+        output = finish_output(plus(own, bu, bd), shift_rows)
         down_sum = pair(
             plus(at(keep_d, came_d, 0, 1), d1x[first], s9y[first]),
             plus(at(keep_d, came_d, 1, 2), d1y[second], s9x[first]),
         )
-        eu, ed, s10x, s10y, came_j, keep_j = cut(eu, ed, s10x, s10y, came_j, keep_j)
-        eu, ed = scatter_step(back, eu, ed, 2)
+        eu, ed, s10x, s10y, keep_j, five = cut(eu, ed, s10x, s10y, keep_j, five)
+        eu, ed = scatter_step(backs, eu, ed, 2)
         j1x = x(at(keep_j, came_j, 3, 5).astype(BF16))
         j1y = y(at(keep_j, came_j, 5, 7).astype(BF16))
+        five = five + xor_shift(five, "tensor", 2)
         up_sum = pair(
             plus(at(keep_u, came_u, 0, 1), s10x[second], s10y[second]),
             plus(at(keep_u, came_u, 1, 2), s10x[first], s10y[first]),
         )
-        five = width_sums(grad_first, grad_second, standardize(token_rows)[0], local_grads)
-        small = small_grads(
-            five, jnp.sum(grad_projected, axis=0, dtype=F32), jnp.sum(grad_hidden, axis=0, dtype=F32)
-        )
-        eu, ed, j1x, j1y = cut(eu, ed, j1x, j1y)
-        eu, ed = scatter_step(back, eu, ed, 3)
+        terms = jnp.concatenate(
+            [
+                five,
+                jnp.sum(grad_projected, axis=0, dtype=F32, keepdims=True),
+                jnp.sum(grad_hidden, axis=0, dtype=F32, keepdims=True),
+            ],
+            axis=1,
+        )
+        eu, ed, j1x, j1y, terms = cut(eu, ed, j1x, j1y, terms)
+        eu, ed = scatter_step(backs, eu, ed, 3)
         j2x = x(plus(at(keep_j, came_j, 2, 3), j1y[first]).astype(BF16))
         j2y = y(plus(at(keep_j, came_j, 7, 8), j1x[second]).astype(BF16))
+        terms = butterfly(terms, "dp")
+        small = small_shares(
+            terms[:, : 5 * width], terms[0, 5 * width : 5 * width + joined_width],
+            terms[:, 5 * width + joined_width :],
+        )
         joined_mix = pair(
             plus(at(keep_j, came_j, 0, 1), j1x[first], j2y),
             plus(at(keep_j, came_j, 1, 2), j1y[second], j2x),
         )
-        input_grad = finish_input_grad(plus(back[:local_rows], eu, ed))
+        own = jnp.concatenate([h[:local_rows] for h in backs], axis=1)
+        input_grad = finish_input_grad(plus(own, eu, ed))
         return (
             output, input_grad, joined_mix[:, :joined_width], joined_mix[:, joined_width:], up_sum, down_sum, small
         )

time: 681 us -> 563 us (0.83)
  Pallas kernels: 38 us -> 130 us
  matrix products: 123 us -> 42.6 us
  waiting for transfers between devices: 170 us -> 99.7 us
  local copies, waits for them, and re-layouts: 135 us -> 68.1 us
  starting transfers between devices: 96.8 us -> 113 us
    pallas_call x2 -> x8, Pallas kernels: 20.4 us -> 113 us  [the longest x2 27.8 us: back_half(): pl.pallas_call(functools.partial(back_kernel, step=256), out_shape=(jax.S...]
    dot_general x8 -> x0, matrix products: 80.9 us -> none  [the longest x2 26.1 us: back_rows(): jnp.einsum('nf,df->nd', grads, weight_rows, preferred_element_type=F32)]
    unnamed x186 -> x139, local copies, waits for them, and re-layouts: 77.4 us -> 37.7 us
    slice x25 -> x15, local copies, waits for them, and re-layouts: 36.9 us -> 7.3 us  [the longest x2 2.44 us: staged(): own = jnp.concatenate([h[:local_rows] for h in branches], axis=1)]
    ppermute x6, waiting for transfers between devices: 35 us -> 7.08 us  [gather_step(): down = lax.ppermute(down, 'tensor', [(i + 1, i) for i in range(3 - s)])]
    ppermute x6, waiting for transfers between devices: 18.5 us -> 0.02 us  [gather_step(): up = lax.ppermute(up, 'tensor', [(i, i + 1) for i in range(s, 3)])]
    ppermute x6, waiting for transfers between devices: 25.6 us -> 13.9 us  [scatter_step(): up = lax.ppermute(to_up, 'tensor', [(i, i + 1) for i in range(s)])]
    ppermute x6, starting transfers between devices: 8.83 us -> 19.1 us  [gather_step(): down = lax.ppermute(down, 'tensor', [(i + 1, i) for i in range(3 - s)])]
  transfers between devices with their start and end apart: 70 -> 61, of which waited for: 22 -> 20; matrix products, arithmetic and copies ran while one was open for 45% -> 27% of each run, Pallas kernels for 6% -> 22%
where the time goes in v3:
time: 563 us; the launch traced here: 558 us
  Pallas kernels  130 us (23%)
  starting transfers between devices  113 us (20%)
  waiting for transfers between devices  99.7 us (18%)
  other arithmetic  92.6 us (16%)
  local copies, waits for them, and re-layouts  68.1 us (12%)
  matrix products  42.6 us (8%)
  between operations  12.2 us (2%)
    ppermute x37, waiting for transfers between devices, xor_shift(): return lax.ppermute(values, axis, [(i, i ^ bit) for i in range(size)])  77.2 us
    dot_general x8, matrix products, grad_half(): jnp.einsum('nd,nf->df', chosen, columns, preferred_element_type=F32)  42.6 us
    unnamed x139, local copies, waits for them, and re-layouts  37.7 us
    ppermute x37, starting transfers between devices, xor_shift(): return lax.ppermute(values, axis, [(i, i ^ bit) for i in range(size)])  36.3 us
    ppermute x6, starting transfers between devices, scatter_step(): up = lax.ppermute(to_up, 'tensor', [(i, i + 1) for i in range(s)])  34.5 us
    pallas_call x2, Pallas kernels, back_half(): pl.pallas_call(functools.partial(back_kernel, step=256), out_shape=(jax.S...  27.8 us
    pallas_call x2, Pallas kernels, branch_half(): pl.pallas_call(functools.partial(branch_kernel, step=256), out_shape=jax....  20.1 us
    ppermute x6, starting transfers between devices, gather_step(): down = lax.ppermute(down, 'tensor', [(i + 1, i) for i in range(3 - s)])  19.1 us
  transfers between devices with their start and end apart: 61, of which 20 were waited for; matrix products, arithmetic and copies ran while one was open for 27% of the time, Pallas kernels for 22%

profile of v3, /device:TPU:0, one launch (start us, length us, event | category | flops | bytes accessed | tf_op | source)
XLA Modules:
  0.0 558.1 jit_solution(4813509659077667836)
XLA Ops:
  34.8 7.5 %collective-permute-done.8 = bf16[32,832]{1,0:T(8,128)(2,1)S(1)} collective-permute-done((bf16[32,832]{1,0:T(8,128)(2,1)S(1)}, bf16[32,832]{1,0:T(8,128)(2,1)S(1)}, u32[]{:S(2)}, u32[]{:S(2)}) %collective-permute-start.8) | collective-permute-done | bytes 53280 | tf_op jit(solution)/shard_map/ppermute | solution.py:33
  42.4 5.6 collective-permute-done.6
  60.3 5.7 %collective-permute-start.13 = (bf16[32,832]{1,0:T(8,128)(2,1)S(1)}, bf16[32,832]{1,0:T(8,128)(2,1)S(1)}, u32[]{:S(2)}, u32[]{:S(2)}) collective-permute-start(bf16[32,832]{1,0:T(8,128)(2,1)S(1)} %add.481), channel_id=1, source_target_pairs={{0,2},{1,3},{2,0},{3,1},{4,6},{5,7},{6,4},{7,5},{8,10},{9,11},{10,... | collective-permute-start | bytes 159752 | tf_op jit(solution)/shard_map/ppermute | solution.py:33
  67.0 18.2 %collective-permute-done.13 = bf16[32,832]{1,0:T(8,128)(2,1)S(1)} collective-permute-done((bf16[32,832]{1,0:T(8,128)(2,1)S(1)}, bf16[32,832]{1,0:T(8,128)(2,1)S(1)}, u32[]{:S(2)}, u32[]{:S(2)}) %collective-permute-start.13) | collective-permute-done | bytes 53280 | tf_op jit(solution)/shard_map/ppermute | solution.py:33
  108.3 14.2 %collective-permute-done.17 = bf16[256,2048]{1,0:T(8,128)(2,1)} collective-permute-done((bf16[256,2048]{1,0:T(8,128)(2,1)}, bf16[256,2048]{1,0:T(8,128)(2,1)}, u32[]{:S(2)}, u32[]{:S(2)}) %collective-permute-start.17) | collective-permute-done | bytes 1048608 | tf_op jit(solution)/shard_map/ppermute | solution.py:33
  151.2 17.6 %hidden.1 = (bf16[1024,2048]{1,0:T(8,128)(2,1)}, bf16[1024,2048]{1,0:T(8,128)(2,1)}) custom-call(bf16[1024,2048]{1,0:T(8,128)(2,1)} %get-tuple-element.560.rows_ref, bf16[1024,2048]{1,0:T(8,128)(2,1)} %constant_dynamic-update-slice_fusion.a_ref.up_ref, bf16[1024,2048]{1,0:T(8,128)(2,1)} %collective-permute-done.18.b_ref.up_ref, f32[1,2048]{1,0:T(1,128)} %bitcast.86), custom_call_target="tpu_custom_call" | custom-call | flops 1000 | bytes 1000 | tf_op jit(solution)/shard_map/hidden/pallas_call | solution.py:368
  181.0 17.7 %joined_forward.1 = (bf16[1024,512]{1,0:T(8,128)(2,1)}, bf16[1024,512]{1,0:T(8,128)(2,1)}, bf16[1024,512]{1,0:T(8,128)(2,1)}, bf16[1024,512]{1,0:T(8,128)(2,1)}, f32[2,1024,128]{2,1,0:T(8,128)}) custom-call(s32[1]{0:T(128)} %bitcast.41.me_ref, bf16[1024,2048]{1,0:T(8,128)(2,1)} %get-tuple-element.133.rows_ref, ...), custom_call_target="tpu_custom_call" | custom-call | flops 1000 | bytes 1000 | tf_op jit(solution)/shard_map/joined_forward/pallas_call | solution.py:491
  209.8 12.4 %collective-permute-start.29 = (bf16[256,2048]{1,0:T(8,128)(2,1)}, bf16[256,2048]{1,0:T(8,128)(2,1)}, u32[]{:S(2)}, u32[]{:S(2)}) collective-permute-start(bf16[256,2048]{1,0:T(8,128)(2,1)} %collective-permute-done.25), channel_id=1, source_target_pairs={{1,0},{5,4},{9,8},{13,12},{17,16},{21,20},{25,24},{29,28}} | collective-permute-start | bytes 3145736 | tf_op jit(solution)/shard_map/ppermute | solution.py:816
  222.2 10.1 %branches.2 = bf16[1024,1024]{1,0:T(8,128)(2,1)} custom-call(bf16[1024,512]{1,0:T(8,128)(2,1)} %get-tuple-element.183.att_ref, bf16[1024,2048]{1,0:T(8,128)(2,1)} %constant_dynamic-update-slice_fusion.3.qa_ref.ka_ref.va_ref.mix_ref.a_ref.join_ref, bf16[1024,2048]{1,0:T(8,128)(2,1)} %get-tuple-element.152.act_ref, ...), custom_call_target="tpu_custom_call" | custom-call | flops 1000 | bytes 1000 | tf_op jit(solution)/shard_map/branches/pallas_call | solution.py:421
  233.6 10.1 %branches.3 = bf16[1024,1024]{1,0:T(8,128)(2,1)} custom-call(bf16[1024,512]{1,0:T(8,128)(2,1)} %get-tuple-element.183.att_ref, bf16[1024,2048]{1,0:T(8,128)(2,1)} %collective-permute-done.23.qb_ref.kb_ref.vb_ref.mix_ref.b_ref.join_ref, bf16[1024,2048]{1,0:T(8,128)(2,1)} %get-tuple-element.152.act_ref, bf16[1024,2048]{1,0:T(8,128)(2,1)} %collective-permute-done.30.down_ref.b_ref), custom_call_target="tpu_custom_call" | custom-call | flops 1000 | bytes 1000 | tf_op jit(solution)/shard_map/branches/pallas_call | solution.py:421
  248.6 6.3 %convolution_convert_fusion.5 = bf16[1024,2048]{1,0:T(8,128)(2,1)} fusion(bf16[1024,2048]{1,0:T(8,128)(2,1)S(1)} %copy-done.11, bf16[1024,2048]{1,0:T(8,128)(2,1)S(1)} %pad_maximum_fusion.1.rows_ref.g_ref), kind=kOutput, calls=%fused_computation.22 | convolution fusion | flops 4297064448 | bytes 10485760 | tf_op jit(solution)/shard_map/nd,nf->df/dot_general | solution.py:648
  261.7 6.4 %collective-permute-start.31 = (bf16[256,2048]{1,0:T(8,128)(2,1)}, bf16[256,2048]{1,0:T(8,128)(2,1)}, u32[]{:S(2)}, u32[]{:S(2)}) collective-permute-start(bf16[256,2048]{1,0:T(8,128)(2,1)} %pad_maximum_fusion.12), channel_id=1, source_target_pairs={{0,1},{4,5},{8,9},{12,13},{16,17},{20,21},{24,25},{28,29}} | collective-permute-start | bytes 3145736 | tf_op jit(solution)/shard_map/ppermute | solution.py:826
  268.1 14.3 %hidden_back.1.hid_ref = bf16[1024,2048]{1,0:T(8,128)(2,1)} custom-call(bf16[1024,2048]{1,0:T(8,128)(2,1)} %copy-done.4, bf16[1024,2048]{1,0:T(8,128)(2,1)} %constant_dynamic-update-slice_fusion.7.down_ref.a_ref, bf16[1024,2048]{1,0:T(8,128)(2,1)} %collective-permute-done.30.down_ref.b_ref, bf16[1024,2048]{1,0:T(8,128)(2,1)} %get-tuple-element.153.slope_ref), custom_call_target="tpu_custom_call" | custom-call | flops 1000 | bytes 1000 | tf_op jit(solution)/shard_map/hidden_back/pallas_call | solution.py:396
  282.4 7.5 %convolution_convert_fusion.4 = bf16[1024,2048]{1,0:T(8,128)(2,1)S(1)} fusion(bf16[1024,2048]{1,0:T(8,128)(2,1)} %get-tuple-element.152.act_ref, bf16[1024,2048]{1,0:T(8,128)(2,1)} %copy-done.4), kind=kOutput, calls=%fused_computation.21 | convolution fusion | flops 4297064448 | bytes 10485760 | tf_op jit(solution)/shard_map/nd,nf->df/dot_general | solution.py:648
  290.8 6.3 %convolution_convert_fusion.3 = bf16[1024,2048]{1,0:T(8,128)(2,1)} fusion(bf16[1024,2048]{1,0:T(8,128)(2,1)S(1)} %copy-done.1, bf16[1024,2048]{1,0:T(8,128)(2,1)S(1)} %copy-done.10), kind=kOutput, calls=%fused_computation.20 | convolution fusion | flops 4297064448 | bytes 10485760 | tf_op jit(solution)/shard_map/nd,nf->df/dot_general | solution.py:648
  316.4 15.2 %mixed_backward.1.proj_ref = bf16[1024,1536]{1,0:T(8,128)(2,1)} custom-call(s32[1]{0:T(128)} %bitcast.41.me_ref, bf16[1024,512]{1,0:T(8,128)(2,1)} %get-tuple-element.159.q_ref, bf16[1024,512]{1,0:T(8,128)(2,1)} %get-tuple-element.160.k_ref, bf16[1024,512]{1,0:T(8,128)(2,1)} %get-tuple-element.161.v_ref, bf16[1024,2048]{1,0:T(8,128)(2,1)} %copy-done.4, ...), custom_call_target="tpu_custom_call" | custom-call | flops 1000 | bytes 1000 | tf_op jit(solution)/shard_map/mixed_backward/pallas_call | solution.py:514
  331.7 9.5 %convolution_convert_fusion.2 = bf16[1024,2048]{1,0:T(8,128)(2,1)} fusion(bf16[1024,2048]{1,0:T(8,128)(2,1)} %hidden_back.1.hid_ref, bf16[1024,2048]{1,0:T(8,128)(2,1)} %get-tuple-element.560.rows_ref), kind=kOutput, calls=%fused_computation.19 | convolution fusion | flops 4297064448 | bytes 10485760 | tf_op jit(solution)/shard_map/nd,nf->df/dot_general | solution.py:648
  382.2 13.9 %back.3 = (bf16[1024,1024]{1,0:T(8,128)(2,1)}, f32[8,1024]{1,0:T(8,128)}) custom-call(bf16[1024,2048]{1,0:T(8,128)(2,1)} %hidden_back.1.hid_ref, bf16[1024,1536]{1,0:T(8,128)(2,1)} %mixed_backward.1.proj_ref, bf16[1024,2048]{1,0:T(8,128)(2,1)} %collective-permute-done.18.b_ref.up_ref, ...), custom_call_target="tpu_custom_call" | custom-call | flops 1000 | bytes 1000 | tf_op jit(solution)/shard_map/back/pallas_call | solution.py:460
  396.1 13.9 %back.2 = (bf16[1024,1024]{1,0:T(8,128)(2,1)}, f32[8,1024]{1,0:T(8,128)}) custom-call(bf16[1024,2048]{1,0:T(8,128)(2,1)} %hidden_back.1.hid_ref, bf16[1024,1536]{1,0:T(8,128)(2,1)} %mixed_backward.1.proj_ref, bf16[1024,2048]{1,0:T(8,128)(2,1)} %constant_dynamic-update-slice_fusion.a_ref.up_ref, ...), custom_call_target="tpu_custom_call" | custom-call | flops 1000 | bytes 1000 | tf_op jit(solution)/shard_map/back/pallas_call | solution.py:460
  416.8 5.5 convolution_convert_fusion
  454.4 8.7 %collective-permute-done.44 = bf16[256,2048]{1,0:T(8,128)(2,1)} collective-permute-done((bf16[256,2048]{1,0:T(8,128)(2,1)}, bf16[256,2048]{1,0:T(8,128)(2,1)}, u32[]{:S(2)}, u32[]{:S(2)}) %collective-permute-start.44) | collective-permute-done | bytes 1048608 | tf_op jit(solution)/shard_map/ppermute | solution.py:826
  479.7 8.8 %collective-permute-done.51 = bf16[256,2048]{1,0:T(8,128)(2,1)S(1)} collective-permute-done((bf16[256,2048]{1,0:T(8,128)(2,1)S(1)}, bf16[256,2048]{1,0:T(8,128)(2,1)S(1)}, u32[]{:S(2)}, u32[]{:S(2)}) %collective-permute-start.51) | collective-permute-done | bytes 1048608 | tf_op jit(solution)/shard_map/ppermute | solution.py:33
  498.8 7.8 %collective-permute-start.54 = (bf16[256,2048]{1,0:T(8,128)(2,1)}, bf16[256,2048]{1,0:T(8,128)(2,1)}, u32[]{:S(2)}, u32[]{:S(2)}) collective-permute-start(bf16[256,2048]{1,0:T(8,128)(2,1)} %add_convert_fusion.1), channel_id=1, source_target_pairs={{0,1},{1,2},{2,3},{4,5},{5,6},{6,7},{8,9},{9,10},{10,11},{12,13},{... | collective-permute-start | bytes 3145736 | tf_op jit(solution)/shard_map/ppermute | solution.py:826
  522.2 9.5 %collective-permute-done.56 = bf16[128,2048]{1,0:T(8,128)(2,1)} collective-permute-done((bf16[128,2048]{1,0:T(8,128)(2,1)}, bf16[128,2048]{1,0:T(8,128)(2,1)}, u32[]{:S(2)}, u32[]{:S(2)}) %collective-permute-start.56) | collective-permute-done | bytes 524320 | tf_op jit(solution)/shard_map/ppermute | solution.py:33
  (394 shorter events, 293.4 us)
Async XLA Ops:
  8.3 34.1 %collective-permute-start = (bf16[256,2048]{1,0:T(8,128)(2,1)}, bf16[256,2048]{1,0:T(8,128)(2,1)}, u32[]{:S(2)}, u32[]{:S(2)}) collective-permute-start(bf16[256,2048]{1,0:T(8,128)(2,1)} %columns.6), channel_id=1, source_target_pairs={{0,1},{1,2},{2,3},{4,5},{5,6},{6,7},{8,9},{9,10},{10,11},{12,13},{... | collective-permute-start | bytes 3145736 | tf_op jit(solution)/shard_map/ppermute | solution.py:815
  54.0 31.3 %collective-permute-start.12 = (bf16[256,2048]{1,0:T(8,128)(2,1)S(1)}, bf16[256,2048]{1,0:T(8,128)(2,1)S(1)}, u32[]{:S(2)}, u32[]{:S(2)}) collective-permute-start(bf16[256,2048]{1,0:T(8,128)(2,1)S(1)} %pad_maximum_fusion.8), channel_id=1, source_target_pairs={{0,16},{4,20},{8,24},{12,28},{16,0},{20,4},{24,8},{28,12},{1,17},{... | collective-permute-start | bytes 3145736 | tf_op jit(solution)/shard_map/ppermute | solution.py:33
  91.3 37.0 %collective-permute-start.18 = (bf16[1024,2048]{1,0:T(8,128)(2,1)}, bf16[1024,2048]{1,0:T(8,128)(2,1)}, u32[]{:S(2)}, u32[]{:S(2)}) collective-permute-start(bf16[1024,2048]{1,0:T(8,128)(2,1)} %constant_dynamic-update-slice_fusion.a_ref.up_ref), channel_id=1, source_target_pairs={{0,4},{4,0},{8,12},{12,8},{16,20},{20,16},{24,28},{28,24},{1,5},{5... | collective-permute-start | bytes 12582920 | tf_op jit(solution)/shard_map/ppermute | solution.py:33
  122.5 46.3 %collective-permute-start.21 = (bf16[256,2048]{1,0:T(8,128)(2,1)S(1)}, bf16[256,2048]{1,0:T(8,128)(2,1)}, u32[]{:S(2)}, u32[]{:S(2)}) collective-permute-start(bf16[256,2048]{1,0:T(8,128)(2,1)S(1)} %bitcast.75), channel_id=1, source_target_pairs={{0,8},{4,12},{8,0},{12,4},{16,24},{20,28},{24,16},{28,20},{1,9},{5... | collective-permute-start | bytes 3145736 | tf_op jit(solution)/shard_map/ppermute | solution.py:33
  124.7 44.1 %collective-permute-start.22 = (bf16[256,2048]{1,0:T(8,128)(2,1)S(1)}, bf16[256,2048]{1,0:T(8,128)(2,1)}, u32[]{:S(2)}, u32[]{:S(2)}) collective-permute-start(bf16[256,2048]{1,0:T(8,128)(2,1)S(1)} %bitcast.76), channel_id=1, source_target_pairs={{0,16},{4,20},{8,24},{12,28},{16,0},{20,4},{24,8},{28,12},{1,17},{... | collective-permute-start | bytes 3145736 | tf_op jit(solution)/shard_map/ppermute | solution.py:33
  135.3 33.5 %collective-permute-start.23 = (bf16[1024,2048]{1,0:T(8,128)(2,1)}, bf16[1024,2048]{1,0:T(8,128)(2,1)}, u32[]{:S(2)}, u32[]{:S(2)}) collective-permute-start(bf16[1024,2048]{1,0:T(8,128)(2,1)} %constant_dynamic-update-slice_fusion.3.qa_ref.ka_ref.va_ref.mix_ref.a_ref.join_ref), channel_id=1, source_target_pairs={{0,4},{4,0},{8,12},{12,8},{16,20},{20,16},{24,28},{28,24},{1,5},{5... | collective-permute-start | bytes 12582920 | tf_op jit(solution)/shard_map/ppermute | solution.py:33
  136.0 32.8 %collective-permute-start.19 = (bf16[256,2048]{1,0:T(8,128)(2,1)S(1)}, bf16[256,2048]{1,0:T(8,128)(2,1)}, u32[]{:S(2)}, u32[]{:S(2)}) collective-permute-start(bf16[256,2048]{1,0:T(8,128)(2,1)S(1)} %copy-done.12), channel_id=1, source_target_pairs={{0,1},{1,2},{2,3},{4,5},{5,6},{6,7},{8,9},{9,10},{10,11},{12,13},{... | collective-permute-start | bytes 3145736 | tf_op jit(solution)/shard_map/ppermute | solution.py:815
  170.5 32.2 %collective-permute-start.25 = (bf16[256,2048]{1,0:T(8,128)(2,1)}, bf16[256,2048]{1,0:T(8,128)(2,1)}, u32[]{:S(2)}, u32[]{:S(2)}) collective-permute-start(bf16[256,2048]{1,0:T(8,128)(2,1)} %collective-permute-done.20), channel_id=1, source_target_pairs={{1,0},{2,1},{5,4},{6,5},{9,8},{10,9},{13,12},{14,13},{17,16},{18,1... | collective-permute-start | bytes 3145736 | tf_op jit(solution)/shard_map/ppermute | solution.py:816
  208.2 35.5 %collective-permute-start.28 = (bf16[256,2048]{1,0:T(8,128)(2,1)}, bf16[256,2048]{1,0:T(8,128)(2,1)}, u32[]{:S(2)}, u32[]{:S(2)}) collective-permute-start(bf16[256,2048]{1,0:T(8,128)(2,1)} %collective-permute-done.24), channel_id=1, source_target_pairs={{2,3},{6,7},{10,11},{14,15},{18,19},{22,23},{26,27},{30,31}} | collective-permute-start | bytes 3145736 | tf_op jit(solution)/shard_map/ppermute | solution.py:815
  209.8 33.9 %collective-permute-start.29 = (bf16[256,2048]{1,0:T(8,128)(2,1)}, bf16[256,2048]{1,0:T(8,128)(2,1)}, u32[]{:S(2)}, u32[]{:S(2)}) collective-permute-start(bf16[256,2048]{1,0:T(8,128)(2,1)} %collective-permute-done.25), channel_id=1, source_target_pairs={{1,0},{5,4},{9,8},{13,12},{17,16},{21,20},{25,24},{29,28}} | collective-permute-start | bytes 3145736 | tf_op jit(solution)/shard_map/ppermute | solution.py:816
  254.9 35.9 %collective-permute-start.33 = (bf16[1024,2048]{1,0:T(8,128)(2,1)}, bf16[1024,2048]{1,0:T(8,128)(2,1)}, u32[]{:S(2)}, u32[]{:S(2)}) collective-permute-start(bf16[1024,2048]{1,0:T(8,128)(2,1)} %convolution_convert_fusion.5), channel_id=1, source_target_pairs={{0,4},{4,0},{8,12},{12,8},{16,20},{20,16},{24,28},{28,24},{1,5},{5... | collective-permute-start | bytes 12582920 | tf_op jit(solution)/shard_map/ppermute | solution.py:33
  259.0 30.9 %collective-permute-start.32 = (bf16[256,2048]{1,0:T(8,128)(2,1)}, bf16[256,2048]{1,0:T(8,128)(2,1)}, u32[]{:S(2)}, u32[]{:S(2)}) collective-permute-start(bf16[256,2048]{1,0:T(8,128)(2,1)} %pad_maximum_fusion.10), channel_id=1, source_target_pairs={{3,2},{7,6},{11,10},{15,14},{19,18},{23,22},{27,26},{31,30}} | collective-permute-start | bytes 3145736 | tf_op jit(solution)/shard_map/ppermute | solution.py:827
  297.0 44.2 %collective-permute-start.38 = (bf16[1024,2048]{1,0:T(8,128)(2,1)}, bf16[1024,2048]{1,0:T(8,128)(2,1)}, u32[]{:S(2)}, u32[]{:S(2)}) collective-permute-start(bf16[1024,2048]{1,0:T(8,128)(2,1)} %convolution_convert_fusion.3), channel_id=1, source_target_pairs={{0,4},{4,0},{8,12},{12,8},{16,20},{20,16},{24,28},{28,24},{1,5},{5... | collective-permute-start | bytes 12582920 | tf_op jit(solution)/shard_map/ppermute | solution.py:33
  300.8 40.4 %collective-permute-start.36 = (bf16[256,2048]{1,0:T(8,128)(2,1)}, bf16[256,2048]{1,0:T(8,128)(2,1)}, u32[]{:S(2)}, u32[]{:S(2)}) collective-permute-start(bf16[256,2048]{1,0:T(8,128)(2,1)} %get-tuple-element.559), channel_id=1, source_target_pairs={{0,8},{4,12},{8,0},{12,4},{16,24},{20,28},{24,16},{28,20},{1,9},{5... | collective-permute-start | bytes 3145736 | tf_op jit(solution)/shard_map/ppermute | solution.py:33
  301.9 39.3 %collective-permute-start.37 = (bf16[256,2048]{1,0:T(8,128)(2,1)}, bf16[256,2048]{1,0:T(8,128)(2,1)}, u32[]{:S(2)}, u32[]{:S(2)}) collective-permute-start(bf16[256,2048]{1,0:T(8,128)(2,1)} %get-tuple-element.558), channel_id=1, source_target_pairs={{0,16},{4,20},{8,24},{12,28},{16,0},{20,4},{24,8},{28,12},{1,17},{... | collective-permute-start | bytes 3145736 | tf_op jit(solution)/shard_map/ppermute | solution.py:33
  306.7 34.4 %collective-permute-start.34 = (bf16[256,2048]{1,0:T(8,128)(2,1)}, bf16[256,2048]{1,0:T(8,128)(2,1)}, u32[]{:S(2)}, u32[]{:S(2)}) collective-permute-start(bf16[256,2048]{1,0:T(8,128)(2,1)} %get-tuple-element.585), channel_id=1, source_target_pairs={{0,1},{1,2},{4,5},{5,6},{8,9},{9,10},{12,13},{13,14},{16,17},{17,1... | collective-permute-start | bytes 3145736 | tf_op jit(solution)/shard_map/ppermute | solution.py:826
  347.7 65.3 %collective-permute-start.43 = (bf16[1024,2048]{1,0:T(8,128)(2,1)}, bf16[1024,2048]{1,0:T(8,128)(2,1)}, u32[]{:S(2)}, u32[]{:S(2)}) collective-permute-start(bf16[1024,2048]{1,0:T(8,128)(2,1)} %pad_maximum_fusion.2), channel_id=1, source_target_pairs={{0,4},{4,0},{8,12},{12,8},{16,20},{20,16},{24,28},{28,24},{1,5},{5... | collective-permute-start | bytes 12582920 | tf_op jit(solution)/shard_map/ppermute | solution.py:33
  364.8 48.2 %collective-permute-start.42 = (bf16[256,2048]{1,0:T(8,128)(2,1)}, bf16[256,2048]{1,0:T(8,128)(2,1)}, u32[]{:S(2)}, u32[]{:S(2)}) collective-permute-start(bf16[256,2048]{1,0:T(8,128)(2,1)} %pad_maximum_fusion.14), channel_id=1, source_target_pairs={{0,16},{4,20},{8,24},{12,28},{16,0},{20,4},{24,8},{28,12},{1,17},{... | collective-permute-start | bytes 3145736 | tf_op jit(solution)/shard_map/ppermute | solution.py:33
  366.6 46.4 %collective-permute-start.41 = (bf16[256,2048]{1,0:T(8,128)(2,1)}, bf16[256,2048]{1,0:T(8,128)(2,1)}, u32[]{:S(2)}, u32[]{:S(2)}) collective-permute-start(bf16[256,2048]{1,0:T(8,128)(2,1)} %pad_maximum_fusion.13), channel_id=1, source_target_pairs={{0,8},{4,12},{8,0},{12,4},{16,24},{20,28},{24,16},{28,20},{1,9},{5... | collective-permute-start | bytes 3145736 | tf_op jit(solution)/shard_map/ppermute | solution.py:33
  370.1 42.9 %collective-permute-start.40 = (bf16[256,2048]{1,0:T(8,128)(2,1)}, bf16[256,2048]{1,0:T(8,128)(2,1)}, u32[]{:S(2)}, u32[]{:S(2)}) collective-permute-start(bf16[256,2048]{1,0:T(8,128)(2,1)} %add_convert_fusion.4), channel_id=1, source_target_pairs={{1,0},{2,1},{3,2},{5,4},{6,5},{7,6},{9,8},{10,9},{11,10},{13,12},{... | collective-permute-start | bytes 3145736 | tf_op jit(solution)/shard_map/ppermute | solution.py:827
  374.0 39.0 %collective-permute-start.39 = (bf16[256,2048]{1,0:T(8,128)(2,1)}, bf16[256,2048]{1,0:T(8,128)(2,1)}, u32[]{:S(2)}, u32[]{:S(2)}) collective-permute-start(bf16[256,2048]{1,0:T(8,128)(2,1)} %add_convert_fusion.5), channel_id=1, source_target_pairs={{0,1},{1,2},{2,3},{4,5},{5,6},{6,7},{8,9},{9,10},{10,11},{12,13},{... | collective-permute-start | bytes 3145736 | tf_op jit(solution)/shard_map/ppermute | solution.py:826
  416.7 34.5 %collective-permute-start.48 = (f32[1,10240]{1,0:T(1,128)S(1)}, f32[1,10240]{1,0:T(1,128)S(1)}, u32[]{:S(2)}, u32[]{:S(2)}) collective-permute-start(f32[1,10240]{1,0:T(1,128)S(1)} %bitcast.81), channel_id=1, source_target_pairs={{0,1},{1,0},{2,3},{3,2},{4,5},{5,4},{6,7},{7,6},{8,9},{9,8},{10,11... | collective-permute-start | bytes 122888 | tf_op jit(solution)/shard_map/ppermute | solution.py:33
  498.8 43.3 %collective-permute-start.54 = (bf16[256,2048]{1,0:T(8,128)(2,1)}, bf16[256,2048]{1,0:T(8,128)(2,1)}, u32[]{:S(2)}, u32[]{:S(2)}) collective-permute-start(bf16[256,2048]{1,0:T(8,128)(2,1)} %add_convert_fusion.1), channel_id=1, source_target_pairs={{0,1},{1,2},{2,3},{4,5},{5,6},{6,7},{8,9},{9,10},{10,11},{12,13},{... | collective-permute-start | bytes 3145736 | tf_op jit(solution)/shard_map/ppermute | solution.py:826
  513.7 29.8 %collective-permute-start.55 = (bf16[256,2048]{1,0:T(8,128)(2,1)}, bf16[256,2048]{1,0:T(8,128)(2,1)}, u32[]{:S(2)}, u32[]{:S(2)}) collective-permute-start(bf16[256,2048]{1,0:T(8,128)(2,1)} %add_convert_fusion), channel_id=1, source_target_pairs={{1,0},{2,1},{3,2},{5,4},{6,5},{7,6},{9,8},{10,9},{11,10},{13,12},{... | collective-permute-start | bytes 3145736 | tf_op jit(solution)/shard_map/ppermute | solution.py:827
  (94 other events, 1353.3 us)

commit v4 on v3

--- a/solution.py
+++ b/solution.py
@@ -53,28 +53,30 @@
 def take_columns(values, index):
     rows, width = values.shape
     count = index.shape[0]
+    tile = rows // 2 if rows % 64 == 0 else rows
     return pl.pallas_call(
         functools.partial(columns_kernel, count=count, step=width // count),
         out_shape=jax.ShapeDtypeStruct(values.shape, values.dtype),
         grid_spec=pltpu.PrefetchScalarGridSpec(
             num_scalar_prefetch=1,
-            grid=(1,),
-            in_specs=[pl.BlockSpec((rows, width), lambda i, s: (0, 0))],
-            out_specs=pl.BlockSpec((rows, width), lambda i, s: (0, 0)),
+            grid=(rows // tile,),
+            in_specs=[pl.BlockSpec((tile, width), lambda i, s: (i, 0))],
+            out_specs=pl.BlockSpec((tile, width), lambda i, s: (i, 0)),
         ),
         name="columns",
     )(index, values)
 
 
+FRAME = [[(me ^ p) * 2 + h for p, h in ORDER] for me in range(8)]
+PLAIN = [[row.index(k) for k in range(16)] for row in FRAME]
+
+
 def frame_index():
-    me = lax.axis_index("dp")
-    return jnp.stack([(me ^ p) * 2 + h for p, h in ORDER]).astype(jnp.int32)
+    return lax.dynamic_index_in_dim(jnp.array(FRAME, jnp.int32), lax.axis_index("dp"), 0, keepdims=False)
 
 
 def plain_index():
-    me = lax.axis_index("dp")
-    spot = jnp.array([ORDER.index((k // 2, k % 2)) for k in range(16)], jnp.int32)
-    return jnp.stack([jnp.take(spot, (me ^ (k // 2)) * 2 + k % 2) for k in range(16)])
+    return lax.dynamic_index_in_dim(jnp.array(PLAIN, jnp.int32), lax.axis_index("dp"), 0, keepdims=False)
 
 
 def to_frame(values):
@@ -363,7 +365,7 @@
     count, width = rows.shape
     out = top.shape[1]
     tile = 512
-    half = pl.BlockSpec((top.shape[0], tile), lambda j: (0, j))
+    half = pl.BlockSpec((width // 2, tile), lambda j: (0, j))
     made = pl.BlockSpec((count, tile), lambda j: (0, j))
     return pl.pallas_call(
         functools.partial(hidden_kernel, step=256),
@@ -424,7 +426,7 @@
         grid=(width // tile,),
         in_specs=[
             pl.BlockSpec((count, inner), lambda j: (0, 0)),
-            pl.BlockSpec((tile, inner), lambda j: (j, spot)),
+            pl.BlockSpec((tile, inner), lambda j: (j + width // tile, spot)),
             pl.BlockSpec((count, units), lambda j: (0, 0)),
             pl.BlockSpec((tile, units), lambda j: (j, 0)),
         ],
@@ -450,10 +452,10 @@
         sum_ref[k : k + 1, :] = sums[k]
 
 
-def back_half(grad_hidden, grad_projected, up, mixed, token_rows, mean, scale, gains, part):
+def back_half(grad_hidden, grad_projected, both, token_rows, mean, scale, gains, part):
     count, units = grad_hidden.shape
     joined = grad_projected.shape[1]
-    width = up.shape[0]
+    width = both.shape[0] // 2
     tile = 256
     tiles = width // tile
     whole = lambda j: (0, 0)
@@ -465,7 +467,7 @@
             pl.BlockSpec((count, units), whole),
             pl.BlockSpec((count, joined), whole),
             pl.BlockSpec((tile, units), lambda j: (j, 0)),
-            pl.BlockSpec((tile, joined), lambda j: (j, 0)),
+            pl.BlockSpec((tile, joined), lambda j: (j + tiles, 0)),
             pl.BlockSpec((count, tile), lambda j: (0, j + part * tiles)),
             pl.BlockSpec((count, 128), whole),
             pl.BlockSpec((count, 128), whole),
@@ -474,7 +476,69 @@
         out_specs=(pl.BlockSpec((count, tile), lambda j: (0, j)), pl.BlockSpec((8, tile), lambda j: (0, j))),
         cost_estimate=SMALL,
         name="back",
-    )(grad_hidden, grad_projected, up, mixed, token_rows, mean, scale, gains)
+    )(grad_hidden, grad_projected, both, both, token_rows, mean, scale, gains)
+
+
+def terms_kernel(*refs):
+    *ins, to_up, to_down = refs
+    up = jnp.concatenate([ins[0][:, :], ins[1][:, :]], axis=1)
+    down = jnp.concatenate([ins[2][:, :], ins[3][:, :]], axis=1)
+    if len(ins) > 4:
+        up = (up.astype(F32) + ins[4][:, :].astype(F32)).astype(BF16)
+        down = (down.astype(F32) + ins[5][:, :].astype(F32)).astype(BF16)
+    to_up[:, :] = up
+    to_down[:, :] = down
+
+
+def step_terms(halves, up_block, down_block, rows, *came):
+    width = halves[0].shape[1]
+    tiles = 2
+    tile = rows // tiles
+
+    def of(block):
+        return [pl.BlockSpec((tile, width), lambda i: (block * tiles + i, 0))] * 2
+
+    full = pl.BlockSpec((tile, 2 * width), lambda i: (i, 0))
+    return pl.pallas_call(
+        terms_kernel,
+        out_shape=(jax.ShapeDtypeStruct((rows, 2 * width), BF16),) * 2,
+        grid=(tiles,),
+        in_specs=of(up_block) + of(down_block) + [full] * len(came),
+        out_specs=(full, full),
+        cost_estimate=SMALL,
+        name="terms",
+    )(*halves, *halves, *came)
+
+
+def input_grad_kernel(index_ref, one_ref, two_ref, up_ref, down_ref, tok_ref, grad_ref, out_ref):
+    back = jnp.concatenate([one_ref[:, :], two_ref[:, :]], axis=1).astype(F32)
+    back = back + up_ref[:, :].astype(F32) + down_ref[:, :].astype(F32)
+    xhat, scale = standardize(tok_ref[:, :])
+    back = back - jnp.mean(back, axis=-1, keepdims=True) - xhat * jnp.mean(back * xhat, axis=-1, keepdims=True)
+    total = grad_ref[:, :].astype(F32) + back * scale
+    count = index_ref.shape[0]
+    step = total.shape[1] // count
+    for j in range(count):
+        out_ref[:, pl.ds(pl.multiple_of(index_ref[j] * step, step), step)] = total[:, j * step : (j + 1) * step]
+
+
+def input_grad_rows(one, two, up, down, tokens, grads):
+    rows, width = tokens.shape
+    tile = rows // 4
+    half = pl.BlockSpec((tile, width // 2), lambda i, s: (i, 0))
+    full = pl.BlockSpec((tile, width), lambda i, s: (i, 0))
+    return pl.pallas_call(
+        input_grad_kernel,
+        out_shape=jax.ShapeDtypeStruct((rows, width), F32),
+        grid_spec=pltpu.PrefetchScalarGridSpec(
+            num_scalar_prefetch=1,
+            grid=(rows // tile,),
+            in_specs=[half, half, full, full, full, full],
+            out_specs=full,
+        ),
+        cost_estimate=SMALL,
+        name="input_grad",
+    )(frame_index(), one, two, up, down, tokens, grads)
 
 
 def joined_forward(rows, top, low, bias, tables, me, heads, head, size):
@@ -485,8 +549,8 @@
     by_head = pl.BlockSpec((count, head), lambda h, s: (0, h))
     wide = jax.ShapeDtypeStruct((count, heads * head), BF16)
 
-    def thirds(n):
-        return [pl.BlockSpec((n, head), lambda h, s, k=k: (0, k * heads + h)) for k in range(3)]
+    def thirds(n, spot):
+        return [pl.BlockSpec((n, head), lambda h, s, k=k: (spot, k * heads + h)) for k in range(3)]
 
     return pl.pallas_call(
         functools.partial(joined_forward_kernel, size=size, block=block),
@@ -495,7 +559,7 @@
             num_scalar_prefetch=1,
             grid=(heads,),
             in_specs=[pl.BlockSpec((count, width), whole)]
-            + thirds(top.shape[0]) + thirds(low.shape[0]) + thirds(1) + table_specs,
+            + thirds(width // 2, 1) + thirds(width // 2, 1) + thirds(1, 0) + table_specs,
             out_specs=(by_head,) * 4 + (pl.BlockSpec((1, count, 128), lambda h, s: (h, 0, 0)),),
         ),
         cost_estimate=SMALL,
@@ -510,7 +574,7 @@
     whole = lambda h, s: (0, 0)
     table_specs = [pl.BlockSpec((count, 128), whole)] * 4 + [pl.BlockSpec((8, count), whole)]
     by_head = pl.BlockSpec((count, head), lambda h, s: (0, h))
-    mix = pl.BlockSpec((top.shape[0], head), lambda h, s: (0, 3 * heads + h))
+    mix = pl.BlockSpec((grads.shape[1] // 2, head), lambda h, s: (1, 3 * heads + h))
     return pl.pallas_call(
         functools.partial(mixed_backward_kernel, size=size, block=block, heads=heads),
         out_shape=jax.ShapeDtypeStruct((count, 3 * heads * head), BF16),
@@ -796,7 +860,7 @@
         small = small_grads(
             five, jnp.sum(grad_projected, axis=0, dtype=F32), jnp.sum(grad_hidden, axis=0, dtype=F32)
         )
-        return output, input_grad, joined_sum, mix_sum, up_sum, down_sum, small
+        return output, input_grad, joined_sum, mix_sum.T, up_sum, down_sum.T, small
 
     def staged():
         half = local_rows // 2
@@ -816,13 +880,11 @@
             down = lax.ppermute(down, "tensor", [(i + 1, i) for i in range(3 - s)])
             return up, down
 
-        def scatter_step(halves, up, down, s):
-            def block(r):
-                return jnp.concatenate([h[r * local_rows : (r + 1) * local_rows] for h in halves], axis=1)
-
-            to_up, to_down = block(4 - s), block(s)
-            if s > 1:
-                to_up, to_down = plus(to_up, up).astype(BF16), plus(to_down, down).astype(BF16)
+        def scatter_terms(halves, up, down, s):
+            came = () if s == 1 else (up, down)
+            return step_terms(halves, 4 - s, s, local_rows, *came)
+
+        def scatter_step(to_up, to_down, s):
             up = lax.ppermute(to_up, "tensor", [(i, i + 1) for i in range(s)])
             down = lax.ppermute(to_down, "tensor", [(i, i - 1) for i in range(4 - s, 4)])
             return up, down
@@ -836,61 +898,70 @@
         def pair(top, low):
             return jnp.concatenate([top, low], axis=0)
 
-        def lay(own, from_x, far_x, far_y, from_y):
+        def laid(own, from_x, from_y):
+            return [own, from_x[second], from_x[first], jnp.zeros_like(own), from_y[second], from_y[first]]
+
+        def place(base, piece, part):
+            return lax.dynamic_update_slice(base, piece, ((4 * part + 2) * local_rows, 0))
+
+        def at(keep, came, start, stop):
+            return plus(keep[start * half : stop * half], came[start * half : stop * half])
+
+        def joined_half(first_rows, grad_projected, grad_rows, attended, part):
             return jnp.concatenate(
-                [own, from_x[second], from_x[first], far_x, far_y, from_y[second], from_y[first]], axis=0
+                [grad_half(first_rows, grad_projected, part), grad_half(grad_rows, attended, part)], axis=1
             )
 
         wa = up_weight
         wb = jnp.concatenate([flat_proj, out_weight.T], axis=1)
         wc = down_weight.T
 
+        ax, ay = x(wa), y(wa)
         tu1, td1 = gather_step(local_tokens, local_tokens, 0)
         table1 = table + core(table)
+        table1, ax, ay = cut(table1, ax, ay)
         table1 = table1 + x(table1) + y(table1) + xor_shift(table1, "dp", 6)
-        wa1, table1 = cut(wa, table1)
-        ax, ay = x(wa1), y(wa1)
-        table1 = table1 + xor_shift(table1, "tensor", 1)
         tu1, td1, ax, ay, table1, wb, wc, tables1 = cut(tu1, td1, ax, ay, table1, wb, wc, tables)
         tu2, td2 = gather_step(tu1, td1, 1)
-        p2x, p2y = x(pair(ay[first], wb[second])), y(pair(ax[second], wb[first]))
-        table2 = table1 + xor_shift(table1, "tensor", 2)
-        tu2, td2, p2x, p2y, table2 = cut(tu2, td2, p2x, p2y, table2)
+        bx, by = x(wb), y(wb)
+        table2 = table1 + xor_shift(table1, "tensor", 1)
+        tu2, td2, bx, by, table2, local_grads1 = cut(tu2, td2, bx, by, table2, local_grads)
         tu3, td3 = gather_step(tu2, td2, 2)
-        p3x, p3y = x(pair(p2y[second], wb[first])), y(pair(p2x[second], wb[second]))
-        up_1 = lay(wa, ax, p2x[first], p2y[first], ay)
-        up_2 = core(up_1)
-        gain_rows, shift_rows, joined_bias, hidden_bias = small_parameters(table2)
-        tu3, td3, p3x, p3y, up_1, up_2, local_grads1, gain_rows, shift_rows = cut(
-            tu3, td3, p3x, p3y, up_1, up_2, local_grads, gain_rows, shift_rows
-        )
+        fa, fb = x(ay), y(bx)
+        table3 = table2 + xor_shift(table2, "tensor", 2)
+        both = jnp.concatenate(laid(wa, ax, ay) + laid(wb, bx, by), axis=0)
+        tu3, td3, fa, fb, table3, both = cut(tu3, td3, fa, fb, table3, both)
+        both_1 = place(place(both, fa, 0), fb, 1)
+        both_1, wc, local_grads1 = cut(both_1, wc, local_grads1)
         cu1, cd1 = gather_step(local_grads1, local_grads1, 0)
         cx, cy = x(wc), y(wc)
-        mix_1 = pair(
-            jnp.concatenate([wb, p2x[second], p3x[second], p3x[first]], axis=0),
-            jnp.concatenate([p3y[first], p3y[second], p2y[second]], axis=0),
-        )
-        mix_2 = core(mix_1)
+        both_2 = core(both_1)
+        gain_rows, shift_rows, joined_bias, hidden_bias = small_parameters(table3)
         token_rows = in_turn(local_tokens, (tu1, tu2, tu3), (td1, td2, td3))
         first_rows, second_rows = norm_rows(token_rows, gain_rows, shift_rows)
-        activated, slope = hidden_half(second_rows, up_1, up_2, hidden_bias)
-        cu1, cd1, cx, cy, mix_1, mix_2, first_rows, activated, slope = cut(
-            cu1, cd1, cx, cy, mix_1, mix_2, first_rows, activated, slope
+        mean = jnp.mean(token_rows.astype(F32), axis=-1, keepdims=True)
+        _, scale = standardize(token_rows)
+        mean, scale = (jnp.broadcast_to(v, (row_count, 128)) for v in (mean, scale))
+        activated, slope = hidden_half(second_rows, both_1, both_2, hidden_bias)
+        cu1, cd1, cx, cy, both_1, both_2, first_rows, activated, slope = cut(
+            cu1, cd1, cx, cy, both_1, both_2, first_rows, activated, slope
         )
         cu2, cd2 = gather_step(cu1, cd1, 1)
-        fcx, fcy = x(cy[first]), y(cx[second])
+        fc = x(cy)
+        down_0 = jnp.concatenate(laid(wc, cx, cy), axis=0)
         *kept, attended, log_total = joined_forward(
-            first_rows, mix_1, mix_2, joined_bias.reshape(1, -1), tables1, me, heads_here, head_size, n_tensor
-        )
-        cu2, cd2, fcx, fcy, attended = cut(cu2, cd2, fcx, fcy, attended)
+            first_rows, both_1, both_2, joined_bias.reshape(1, -1), tables1, me, heads_here, head_size, n_tensor
+        )
+        cu2, cd2, fc, attended, down_0, mean, scale = cut(cu2, cd2, fc, attended, down_0, mean, scale)
         cu3, cd3 = gather_step(cu2, cd2, 2)
-        down_1 = lay(wc, cx, fcx, fcy, cy)
+        down_1 = place(down_0, fc, 0)
         down_2 = core(down_1)
-        branch_1 = branch_half(attended, mix_1, activated, down_1)
-        branch_2 = branch_half(attended, mix_2, activated, down_2)
+        branch_1 = branch_half(attended, both_1, activated, down_1)
+        branch_2 = branch_half(attended, both_2, activated, down_2)
         cu3, cd3, branch_1, branch_2, activated = cut(cu3, cd3, branch_1, branch_2, activated)
         branches = (branch_1, branch_2)
-        bu, bd = scatter_step(branches, None, None, 1)
+        zu, zd, activated, cu3, cd3 = cut(*scatter_terms(branches, None, None, 1), activated, cu3, cd3)
+        bu, bd = scatter_step(zu, zd, 1)
         grad_rows = in_turn(local_grads1, (cu1, cu2, cu3), (cd1, cd2, cd3))
         came_d = core(grad_half(grad_rows, activated, 1))
         keep_d = grad_half(grad_rows, activated, 0)
@@ -898,46 +969,49 @@
         bu, bd, came_d, keep_d, grad_hidden, grad_rows = cut(
             bu, bd, came_d, keep_d, grad_hidden, grad_rows
         )
-
-        def at(keep, came, start, stop):
-            return plus(keep[start * half : stop * half], came[start * half : stop * half])
-
-        bu, bd = scatter_step(branches, bu, bd, 2)
-        d1x = x(at(keep_d, came_d, 3, 5).astype(BF16))
-        d1y = y(at(keep_d, came_d, 5, 7).astype(BF16))
+        zu, zd, sx, sy, second_rows, grad_hidden, grad_rows = cut(
+            *scatter_terms(branches, bu, bd, 2),
+            at(keep_d, came_d, 3, 5).astype(BF16),
+            at(keep_d, came_d, 5, 7).astype(BF16),
+            second_rows, grad_hidden, grad_rows,
+        )
+        bu, bd = scatter_step(zu, zd, 2)
+        d1x, d1y = x(sx), y(sy)
         came_u = core(grad_half(second_rows, grad_hidden, 1))
         keep_u = grad_half(second_rows, grad_hidden, 0)
         grad_projected = mixed_backward(
-            *kept, grad_rows, mix_1, mix_2, log_total, tables1, me, heads_here, n_tensor
+            *kept, grad_rows, both_1, both_2, log_total, tables1, me, heads_here, n_tensor
         )
         bu, bd, d1x, d1y, came_u, keep_u, grad_projected, grad_hidden = cut(
             bu, bd, d1x, d1y, came_u, keep_u, grad_projected, grad_hidden
         )
-        bu, bd = scatter_step(branches, bu, bd, 3)
         d2x = plus(at(keep_d, came_d, 2, 3), d1y[first]).astype(BF16)
         d2y = plus(at(keep_d, came_d, 7, 8), d1x[second]).astype(BF16)
-        s9x = x(pair(d2x, at(keep_u, came_u, 4, 5).astype(BF16)))
-        s9y = y(pair(d2y, at(keep_u, came_u, 5, 6).astype(BF16)))
-
-        def joined_half(part):
-            return jnp.concatenate(
-                [grad_half(first_rows, grad_projected, part), grad_half(grad_rows, attended, part)], axis=1
-            )
-
-        came_j = core(joined_half(1))
-        values = token_rows.astype(F32)
-        mean = jnp.mean(values, axis=-1, keepdims=True)
-        _, scale = standardize(token_rows)
-        mean, scale = (jnp.broadcast_to(v, (row_count, 128)) for v in (mean, scale))
-        back_1, sums_1 = back_half(grad_hidden, grad_projected, up_1, mix_1, token_rows, mean, scale, gain_rows, 0)
-        back_2, sums_2 = back_half(grad_hidden, grad_projected, up_2, mix_2, token_rows, mean, scale, gain_rows, 1)
-        bu, bd, s9x, s9y, came_j, back_1, back_2, sums_1, sums_2, grad_projected, attended = cut(
-            bu, bd, s9x, s9y, came_j, back_1, back_2, sums_1, sums_2, grad_projected, attended
+        zu, zd, sx, sy, grad_hidden, grad_projected = cut(
+            *scatter_terms(branches, bu, bd, 3),
+            pair(d2x, at(keep_u, came_u, 4, 5).astype(BF16)),
+            pair(d2y, at(keep_u, came_u, 5, 6).astype(BF16)),
+            grad_hidden, grad_projected,
+        )
+        bu, bd = scatter_step(zu, zd, 3)
+        s9x, s9y = x(sx), y(sy)
+        back_1, sums_1 = back_half(grad_hidden, grad_projected, both_1, token_rows, mean, scale, gain_rows, 0)
+        back_2, sums_2 = back_half(grad_hidden, grad_projected, both_2, token_rows, mean, scale, gain_rows, 1)
+        bu, bd, s9x, s9y, back_1, back_2, sums_1, sums_2, first_rows, grad_rows, grad_projected, attended = cut(
+            bu, bd, s9x, s9y, back_1, back_2, sums_1, sums_2, first_rows, grad_rows, grad_projected, attended
         )
         backs = (back_1, back_2)
-        eu, ed = scatter_step(backs, None, None, 1)
-        s10x = x(pair(plus(at(keep_u, came_u, 2, 3), s9y[second]), at(keep_u, came_u, 3, 4)).astype(BF16))
-        s10y = y(pair(at(keep_u, came_u, 6, 7), plus(at(keep_u, came_u, 7, 8), s9x[second])).astype(BF16))
+        none = jnp.zeros((half, s9x.shape[1]), BF16)
+        zu, zd, sx, sy, first_rows, grad_rows, bu, bd, sums_1, sums_2 = cut(
+            *scatter_terms(backs, None, None, 1),
+            plus(at(keep_u, came_u, 2, 4), pair(s9y[second], none)).astype(BF16),
+            plus(at(keep_u, came_u, 6, 8), pair(none, s9x[second])).astype(BF16),
+            first_rows, grad_rows, bu, bd, sums_1, sums_2,
+        )
+        eu, ed = scatter_step(zu, zd, 1)
+        s10x, s10y = x(sx), y(sy)
+        came_j = core(joined_half(first_rows, grad_projected, grad_rows, attended, 1))
+        keep_j = joined_half(first_rows, grad_projected, grad_rows, attended, 0)
         five = jnp.concatenate(
             [
                 jnp.concatenate([sums_1[:4], sums_2[:4]], axis=1),
@@ -945,24 +1019,28 @@
             ],
             axis=0,
         )
-        five = from_frame(five).reshape(1, -1)
+        eu, ed, s10x, s10y, keep_j, five, bu, bd = cut(eu, ed, s10x, s10y, keep_j, five, bu, bd)
+        zu, zd, sx, sy, s10x, s10y, five = cut(
+            *scatter_terms(backs, eu, ed, 2),
+            at(keep_j, came_j, 3, 5).astype(BF16),
+            at(keep_j, came_j, 5, 7).astype(BF16),
+            s10x, s10y, five,
+        )
+        eu, ed = scatter_step(zu, zd, 2)
+        j1x, j1y = x(sx), y(sy)
+        five = five.reshape(1, -1)
         five = five + xor_shift(five, "tensor", 1)
-        keep_j = joined_half(0)
         own = jnp.concatenate([h[:local_rows] for h in branches], axis=1)
         output = finish_output(plus(own, bu, bd), shift_rows)
         down_sum = pair(
             plus(at(keep_d, came_d, 0, 1), d1x[first], s9y[first]),
             plus(at(keep_d, came_d, 1, 2), d1y[second], s9x[first]),
-        )
-        eu, ed, s10x, s10y, keep_j, five = cut(eu, ed, s10x, s10y, keep_j, five)
-        eu, ed = scatter_step(backs, eu, ed, 2)
-        j1x = x(at(keep_j, came_j, 3, 5).astype(BF16))
-        j1y = y(at(keep_j, came_j, 5, 7).astype(BF16))
-        five = five + xor_shift(five, "tensor", 2)
+        ).T
         up_sum = pair(
             plus(at(keep_u, came_u, 0, 1), s10x[second], s10y[second]),
             plus(at(keep_u, came_u, 1, 2), s10x[first], s10y[first]),
         )
+        five = from_frame(five.reshape(5, width)).reshape(1, -1)
         terms = jnp.concatenate(
             [
                 five,
@@ -971,24 +1049,32 @@
             ],
             axis=1,
         )
-        eu, ed, j1x, j1y, terms = cut(eu, ed, j1x, j1y, terms)
-        eu, ed = scatter_step(backs, eu, ed, 3)
-        j2x = x(plus(at(keep_j, came_j, 2, 3), j1y[first]).astype(BF16))
-        j2y = y(plus(at(keep_j, came_j, 7, 8), j1x[second]).astype(BF16))
+        eu, ed, j1x, j1y, terms, down_sum, up_sum, output = cut(
+            eu, ed, j1x, j1y, terms, down_sum, up_sum, output
+        )
+        zu, zd, sx, sy, terms = cut(
+            *scatter_terms(backs, eu, ed, 3),
+            plus(at(keep_j, came_j, 2, 3), j1y[first]).astype(BF16),
+            plus(at(keep_j, came_j, 7, 8), j1x[second]).astype(BF16),
+            terms,
+        )
+        eu, ed = scatter_step(zu, zd, 3)
+        j2x, j2y = x(sx), y(sy)
+        terms, j2x, j2y = cut(terms, j2x, j2y)
         terms = butterfly(terms, "dp")
+        five = terms[:, : 5 * width]
+        five = five + xor_shift(five, "tensor", 2)
         small = small_shares(
-            terms[:, : 5 * width], terms[0, 5 * width : 5 * width + joined_width],
-            terms[:, 5 * width + joined_width :],
+            five, terms[0, 5 * width : 5 * width + joined_width], terms[:, 5 * width + joined_width :]
         )
         joined_mix = pair(
             plus(at(keep_j, came_j, 0, 1), j1x[first], j2y),
             plus(at(keep_j, came_j, 1, 2), j1y[second], j2x),
         )
-        own = jnp.concatenate([h[:local_rows] for h in backs], axis=1)
-        input_grad = finish_input_grad(plus(own, eu, ed))
-        return (
-            output, input_grad, joined_mix[:, :joined_width], joined_mix[:, joined_width:], up_sum, down_sum, small
-        )
+        joined_sum, mix_sum = joined_mix[:, :joined_width], joined_mix[:, joined_width:].T
+        eu, ed, joined_sum, mix_sum = cut(eu, ed, joined_sum, mix_sum)
+        input_grad = input_grad_rows(*backs, eu, ed, local_tokens, local_grads)
+        return output, input_grad, joined_sum, mix_sum, up_sum, down_sum, small
 
     parts = staged() if fast_dp() and n_tensor == 4 else plain()
     output, input_grad, joined_sum, mix_sum, up_sum, down_sum, small = parts
@@ -998,10 +1084,10 @@
         input_grad,
         joined_sum.reshape(proj_weight.shape),
         joined_bias_sum,
-        mix_sum.T,
+        mix_sum,
         up_sum,
         up_bias_sum,
-        down_sum.T,
+        down_sum,
         gains_grad,
         biases_grad,
     )

time: 563 us -> 506 us (0.90)
  starting transfers between devices: 113 us -> 81.6 us
  other arithmetic: 92.6 us -> 66.8 us
  Pallas kernels: 130 us -> 151 us
  between operations: 12.2 us -> 2.31 us
  waiting for transfers between devices: 99.7 us -> 91.5 us
    ppermute x37 -> x35, waiting for transfers between devices: 77.2 us -> 37.1 us  [xor_shift(): return lax.ppermute(values, axis, [(i, i ^ bit) for i in range(size)])]
    ppermute x6, waiting for transfers between devices: 7.08 us -> 35.2 us  [gather_step(): down = lax.ppermute(down, 'tensor', [(i + 1, i) for i in range(3 - s)])]
    pallas_call x0 -> x7, Pallas kernels: none -> 25.2 us  [the longest x6 19.1 us: step_terms(): pl.pallas_call(terms_kernel, out_shape=(jax.ShapeDtypeStruct((rows, 2 * w...]
    ppermute x6, starting transfers between devices: 34.5 us -> 22.4 us  [scatter_step(): up = lax.ppermute(to_up, 'tensor', [(i, i + 1) for i in range(s)])]
    ppermute x6, starting transfers between devices: 19.1 us -> 8.1 us  [gather_step(): down = lax.ppermute(down, 'tensor', [(i + 1, i) for i in range(3 - s)])]
    slice x8 -> x3, local copies, waits for them, and re-layouts: 8.78 us -> 1.5 us  [the longest x1 1.46 us: staged(): s9y[second]]
    pallas_call x6 -> x5, Pallas kernels: 17.6 us -> 12.9 us  [take_columns(): pl.pallas_call(functools.partial(columns_kernel, count=count, step=width...]
    convert_element_type x10 -> x6, other arithmetic: 23.8 us -> 20.6 us  [the longest x1 4.62 us: staged(): plus(at(keep_u, came_u, 6, 8), pair(none, s9x[second])).astype(BF16)]
  transfers between devices with their start and end apart: 61 -> 59, of which waited for: 20 -> 23; matrix products, arithmetic and copies ran while one was open for 27% -> 20% of each run, Pallas kernels for 22% -> 26%
where the time goes in v4:
time: 506 us; the launch traced here: 498 us
  Pallas kernels  151 us (30%)
  waiting for transfers between devices  91.5 us (18%)
  starting transfers between devices  81.6 us (16%)
  other arithmetic  66.8 us (13%)
  local copies, waits for them, and re-layouts  63 us (12%)
  matrix products  42.2 us (8%)
    dot_general x8, matrix products, grad_half(): jnp.einsum('nd,nf->df', chosen, columns, preferred_element_type=F32)  42.2 us
    unnamed x130, local copies, waits for them, and re-layouts  40.3 us
    ppermute x35, waiting for transfers between devices, xor_shift(): return lax.ppermute(values, axis, [(i, i ^ bit) for i in range(size)])  37.1 us
    ppermute x6, waiting for transfers between devices, gather_step(): down = lax.ppermute(down, 'tensor', [(i + 1, i) for i in range(3 - s)])  35.2 us
    ppermute x35, starting transfers between devices, xor_shift(): return lax.ppermute(values, axis, [(i, i ^ bit) for i in range(size)])  33.5 us
    pallas_call x2, Pallas kernels, back_half(): pl.pallas_call(functools.partial(back_kernel, step=256), out_shape=(jax.S...  27.9 us
    ppermute x6, starting transfers between devices, scatter_step(): up = lax.ppermute(to_up, 'tensor', [(i, i + 1) for i in range(s)])  22.4 us
    pallas_call x2, Pallas kernels, branch_half(): pl.pallas_call(functools.partial(branch_kernel, step=256), out_shape=jax....  20.1 us
  transfers between devices with their start and end apart: 59, of which 23 were waited for; matrix products, arithmetic and copies ran while one was open for 20% of the time, Pallas kernels for 26%

profile of v4, /device:TPU:0, one launch (start us, length us, event | category | flops | bytes accessed | tf_op | source)
XLA Modules:
  0.0 498.3 jit_solution(7943632502038149481)
XLA Ops:
  56.7 11.1 %collective-permute-done.10 = bf16[256,2048]{1,0:T(8,128)(2,1)S(1)} collective-permute-done((bf16[256,2048]{1,0:T(8,128)(2,1)S(1)}, bf16[256,2048]{1,0:T(8,128)(2,1)S(1)}, u32[]{:S(2)}, u32[]{:S(2)}) %collective-permute-start.10) | collective-permute-done | bytes 1048608 | tf_op jit(solution)/shard_map/ppermute | solution.py:33
  67.8 7.2 %collective-permute-done.9 = bf16[256,2048]{1,0:T(8,128)(2,1)S(1)} collective-permute-done((bf16[256,2048]{1,0:T(8,128)(2,1)}, bf16[256,2048]{1,0:T(8,128)(2,1)S(1)}, u32[]{:S(2)}, u32[]{:S(2)}) %collective-permute-start.9) | collective-permute-done | bytes 1048608 | tf_op jit(solution)/shard_map/ppermute | solution.py:880
  87.4 15.7 %collective-permute-done.14 = bf16[256,2048]{1,0:T(8,128)(2,1)S(1)} collective-permute-done((bf16[256,2048]{1,0:T(8,128)(2,1)S(1)}, bf16[256,2048]{1,0:T(8,128)(2,1)S(1)}, u32[]{:S(2)}, u32[]{:S(2)}) %collective-permute-start.14) | collective-permute-done | bytes 1048608 | tf_op jit(solution)/shard_map/ppermute | solution.py:880
  125.8 6.3 %fusion.7 = (bf16[1024,2048]{1,0:T(8,128)(2,1)}, bf16[1024,2048]{1,0:T(8,128)(2,1)}) fusion(bf16[1024,2048]{1,0:T(8,128)(2,1)} %copy-done, f32[2048]{0:T(1024)S(1)} %bitcast.66, f32[2048]{0:T(1024)S(1)} %bitcast.67, f32[1024]{0:T(1024)S(1)} %add_rsqrt_fusion, f32[1024]{0:T(1024)S(1)} %broadcast_multiply_fusion, f32[2048]{0:T(1024)S(1)} %bitcast.68, ...), kind=kLoop, calls=%fused_computation.9 | loop fusion | flops 18874368 | bytes 12623872 | tf_op jit(solution)/shard_map/convert_element_type | solution.py:677
  132.1 17.5 %hidden.1 = (bf16[1024,2048]{1,0:T(8,128)(2,1)}, bf16[1024,2048]{1,0:T(8,128)(2,1)}) custom-call(bf16[1024,2048]{1,0:T(8,128)(2,1)} %get-tuple-element.244.rows_ref, bf16[2048,2048]{1,0:T(8,128)(2,1)} %constant_dynamic-update-slice_fusion.4.a_ref.qa_ref.ka_ref.va_ref.mix_ref.up_ref.join_ref, ...), custom_call_target="tpu_custom_call" | custom-call | flops 1000 | bytes 1000 | tf_op jit(solution)/shard_map/hidden/pallas_call | solution.py:370
  157.5 17.7 %joined_forward.1 = (bf16[1024,512]{1,0:T(8,128)(2,1)}, bf16[1024,512]{1,0:T(8,128)(2,1)}, bf16[1024,512]{1,0:T(8,128)(2,1)}, bf16[1024,512]{1,0:T(8,128)(2,1)}, f32[2,1024,128]{2,1,0:T(8,128)}) custom-call(s32[1]{0:T(128)} %bitcast.10.me_ref, bf16[1024,2048]{1,0:T(8,128)(2,1)} %get-tuple-element.289.rows_ref, ...), custom_call_target="tpu_custom_call" | custom-call | flops 1000 | bytes 1000 | tf_op jit(solution)/shard_map/joined_forward/pallas_call | solution.py:555
  178.9 4.6 collective-permute-done.24
  189.6 10.1 %branches.2.refs_0_.refs_2_ = bf16[1024,1024]{1,0:T(8,128)(2,1)} custom-call(bf16[1024,512]{1,0:T(8,128)(2,1)} %get-tuple-element.292.att_ref, bf16[2048,2048]{1,0:T(8,128)(2,1)} %constant_dynamic-update-slice_fusion.4.a_ref.qa_ref.ka_ref.va_ref.mix_ref.up_ref.join_ref, bf16[1024,2048]{1,0:T(8,128)(2,1)} %get-tuple-element.230.act_ref, ...), custom_call_target="tpu_custom_call" | custom-call | flops 1000 | bytes 1000 | tf_op jit(solution)/shard_map/branches/pallas_call | solution.py:423
  201.0 10.1 %branches.3.refs_1_.refs_3_ = bf16[1024,1024]{1,0:T(8,128)(2,1)} custom-call(bf16[1024,512]{1,0:T(8,128)(2,1)} %get-tuple-element.292.att_ref, bf16[2048,2048]{1,0:T(8,128)(2,1)} %collective-permute-done.22.b_ref.qb_ref.kb_ref.vb_ref.mix_ref.up_ref.join_ref, bf16[1024,2048]{1,0:T(8,128)(2,1)} %get-tuple-element.230.act_ref, ...), custom_call_target="tpu_custom_call" | custom-call | flops 1000 | bytes 1000 | tf_op jit(solution)/shard_map/branches/pallas_call | solution.py:423
  211.1 5.0 %collective-permute-done.27 = bf16[256,2048]{1,0:T(8,128)(2,1)} collective-permute-done((bf16[256,2048]{1,0:T(8,128)(2,1)}, bf16[256,2048]{1,0:T(8,128)(2,1)}, u32[]{:S(2)}, u32[]{:S(2)}) %collective-permute-start.27) | collective-permute-done | bytes 1048608 | tf_op jit(solution)/shard_map/ppermute | solution.py:880
  223.5 6.3 %convolution_convert_fusion.5 = bf16[1024,2048]{1,0:T(8,128)(2,1)} fusion(bf16[1024,2048]{1,0:T(8,128)(2,1)S(1)} %copy-done.5, bf16[1024,2048]{1,0:T(8,128)(2,1)S(1)} %pad_maximum_fusion.1.rows_ref.g_ref), kind=kOutput, calls=%fused_computation.22 | convolution fusion | flops 4297064448 | bytes 10485760 | tf_op jit(solution)/shard_map/nd,nf->df/dot_general | solution.py:712
  232.5 14.3 %hidden_back.1.hid_ref = bf16[1024,2048]{1,0:T(8,128)(2,1)} custom-call(bf16[1024,2048]{1,0:T(8,128)(2,1)} %copy-done.3, bf16[1024,2048]{1,0:T(8,128)(2,1)} %constant_dynamic-update-slice_fusion.3.down_ref.a_ref, bf16[1024,2048]{1,0:T(8,128)(2,1)} %collective-permute-done.28.down_ref.b_ref, bf16[1024,2048]{1,0:T(8,128)(2,1)} %get-tuple-element.231.slope_ref), custom_call_target="tpu_custom_call" | custom-call | flops 1000 | bytes 1000 | tf_op jit(solution)/shard_map/hidden_back/pallas_call | solution.py:398
  246.8 7.4 %convolution_convert_fusion.4 = bf16[1024,2048]{1,0:T(8,128)(2,1)S(1)} fusion(bf16[1024,2048]{1,0:T(8,128)(2,1)} %get-tuple-element.230.act_ref, bf16[1024,2048]{1,0:T(8,128)(2,1)} %copy-done.3), kind=kOutput, calls=%fused_computation.21 | convolution fusion | flops 4297064448 | bytes 10485760 | tf_op jit(solution)/shard_map/nd,nf->df/dot_general | solution.py:712
  263.5 9.3 %convolution_convert_fusion.3 = bf16[1024,2048]{1,0:T(8,128)(2,1)} fusion(bf16[1024,2048]{1,0:T(8,128)(2,1)} %hidden_back.1.hid_ref, bf16[1024,2048]{1,0:T(8,128)(2,1)} %get-tuple-element.244.rows_ref), kind=kOutput, calls=%fused_computation.20 | convolution fusion | flops 4297064448 | bytes 10485760 | tf_op jit(solution)/shard_map/nd,nf->df/dot_general | solution.py:712
  278.8 15.3 %mixed_backward.1.proj_ref = bf16[1024,1536]{1,0:T(8,128)(2,1)} custom-call(s32[1]{0:T(128)} %bitcast.10.me_ref, bf16[1024,512]{1,0:T(8,128)(2,1)} %get-tuple-element.246.q_ref, bf16[1024,512]{1,0:T(8,128)(2,1)} %get-tuple-element.247.k_ref, bf16[1024,512]{1,0:T(8,128)(2,1)} %get-tuple-element.248.v_ref, bf16[1024,2048]{1,0:T(8,128)(2,1)} %copy-done.3, ...), custom_call_target="tpu_custom_call" | custom-call | flops 1000 | bytes 1000 | tf_op jit(solution)/shard_map/mixed_backward/pallas_call | solution.py:578
  294.1 7.4 %convolution_convert_fusion.2 = bf16[1024,2048]{1,0:T(8,128)(2,1)S(1)} fusion(bf16[1024,2048]{1,0:T(8,128)(2,1)} %hidden_back.1.hid_ref, bf16[1024,2048]{1,0:T(8,128)(2,1)} %get-tuple-element.244.rows_ref), kind=kOutput, calls=%fused_computation.19 | convolution fusion | flops 4297064448 | bytes 10485760 | tf_op jit(solution)/shard_map/nd,nf->df/dot_general | solution.py:712
  321.4 13.9 %back.3 = (bf16[1024,1024]{1,0:T(8,128)(2,1)}, f32[8,1024]{1,0:T(8,128)}) custom-call(bf16[1024,2048]{1,0:T(8,128)(2,1)} %hidden_back.1.hid_ref, bf16[1024,1536]{1,0:T(8,128)(2,1)} %mixed_backward.1.proj_ref, bf16[2048,2048]{1,0:T(8,128)(2,1)} %collective-permute-done.22.b_ref.qb_ref.kb_ref.vb_ref.mix_ref.up_ref.join_ref, ...), custom_call_target="tpu_custom_call" | custom-call | flops 1000 | bytes 1000 | tf_op jit(solution)/shard_map/back/pallas_call | solution.py:462
  335.3 14.0 %back.2 = (bf16[1024,1024]{1,0:T(8,128)(2,1)}, f32[8,1024]{1,0:T(8,128)}) custom-call(bf16[1024,2048]{1,0:T(8,128)(2,1)} %hidden_back.1.hid_ref, bf16[1024,1536]{1,0:T(8,128)(2,1)} %mixed_backward.1.proj_ref, bf16[2048,2048]{1,0:T(8,128)(2,1)} %constant_dynamic-update-slice_fusion.4.a_ref.qa_ref.ka_ref.va_ref.mix_ref.up_ref.join_ref, ...), custom_call_target="tpu_custom_call" | custom-call | flops 1000 | bytes 1000 | tf_op jit(solution)/shard_map/back/pallas_call | solution.py:462
  358.5 5.5 %convolution_convert_fusion = bf16[1024,1536]{1,0:T(8,128)(2,1)S(1)} fusion(bf16[1024,1536]{1,0:T(8,128)(2,1)S(1)} %copy-done.2, bf16[1024,2048]{1,0:T(8,128)(2,1)} %get-tuple-element.289.rows_ref), kind=kOutput, calls=%fused_computation.17 | convolution fusion | flops 3222798336 | bytes 8388608 | tf_op jit(solution)/shard_map/nd,nf->df/dot_general | solution.py:712
  370.6 5.2 %collective-permute-start.41 = (bf16[256,2048]{1,0:T(8,128)(2,1)S(1)}, bf16[256,2048]{1,0:T(8,128)(2,1)S(1)}, u32[]{:S(2)}, u32[]{:S(2)}) collective-permute-start(bf16[256,2048]{1,0:T(8,128)(2,1)S(1)} %copy-done.50), channel_id=1, source_target_pairs={{0,1},{4,5},{8,9},{12,13},{16,17},{20,21},{24,25},{28,29}} | collective-permute-start | bytes 3145736 | tf_op jit(solution)/shard_map/ppermute | solution.py:888
  391.3 7.2 %collective-permute-done.41.refs_4_ = bf16[256,2048]{1,0:T(8,128)(2,1)S(1)} collective-permute-done((bf16[256,2048]{1,0:T(8,128)(2,1)S(1)}, bf16[256,2048]{1,0:T(8,128)(2,1)S(1)}, u32[]{:S(2)}, u32[]{:S(2)}) %collective-permute-start.41) | collective-permute-done | bytes 1048608 | tf_op jit(solution)/shard_map/ppermute | solution.py:888
  431.1 11.4 %collective-permute-done.46.refs_4_ = bf16[256,2048]{1,0:T(8,128)(2,1)S(1)} collective-permute-done((bf16[256,2048]{1,0:T(8,128)(2,1)}, bf16[256,2048]{1,0:T(8,128)(2,1)S(1)}, u32[]{:S(2)}, u32[]{:S(2)}) %collective-permute-start.46) | collective-permute-done | bytes 1048608 | tf_op jit(solution)/shard_map/ppermute | solution.py:888
  454.8 5.5 %collective-permute-start.51 = (bf16[256,2048]{1,0:T(8,128)(2,1)}, bf16[256,2048]{1,0:T(8,128)(2,1)}, u32[]{:S(2)}, u32[]{:S(2)}) collective-permute-start(bf16[256,2048]{1,0:T(8,128)(2,1)} %get-tuple-element.322), channel_id=1, source_target_pairs={{0,1},{1,2},{2,3},{4,5},{5,6},{6,7},{8,9},{9,10},{10,11},{12,13},{... | collective-permute-start | bytes 3145736 | tf_op jit(solution)/shard_map/ppermute | solution.py:888
  491.7 6.1 %input_grad.1 = f32[256,2048]{1,0:T(8,128)} custom-call(s32[16]{0:T(128)} %fusion.28.index_ref, bf16[1024,1024]{1,0:T(8,128)(2,1)} %get-tuple-element.273.refs_0_.refs_2_.one_ref, bf16[1024,1024]{1,0:T(8,128)(2,1)} %get-tuple-element.274.refs_1_.refs_3_.two_ref, bf16[256,2048]{1,0:T(8,128)(2,1)} %collective-permute-done.51.up_ref, ...), custom_call_target="tpu_custom_call" | custom-call | flops 1000 | bytes 1000 | tf_op jit(solution)/shard_map/input_grad/pallas_call | solution.py:530
  (363 shorter events, 262.0 us)
Async XLA Ops:
  0.7 26.5 %collective-permute-start.3 = (bf16[256,2048]{1,0:T(8,128)(2,1)}, bf16[256,2048]{1,0:T(8,128)(2,1)}, u32[]{:S(2)}, u32[]{:S(2)}) collective-permute-start(bf16[256,2048]{1,0:T(8,128)(2,1)} %param.22), channel_id=1, source_target_pairs={{0,8},{4,12},{8,0},{12,4},{16,24},{20,28},{24,16},{28,20},{1,9},{5... | collective-permute-start | bytes 3145736 | tf_op jit(solution)/shard_map/ppermute | solution.py:33
  9.5 28.1 %collective-permute-start = (bf16[256,2048]{1,0:T(8,128)(2,1)}, bf16[256,2048]{1,0:T(8,128)(2,1)}, u32[]{:S(2)}, u32[]{:S(2)}) collective-permute-start(bf16[256,2048]{1,0:T(8,128)(2,1)} %columns.5.tok_ref), channel_id=1, source_target_pairs={{0,1},{1,2},{2,3},{4,5},{5,6},{6,7},{8,9},{9,10},{10,11},{12,13},{... | collective-permute-start | bytes 3145736 | tf_op jit(solution)/shard_map/ppermute | solution.py:879
  13.9 26.3 %collective-permute-start.1 = (bf16[256,2048]{1,0:T(8,128)(2,1)}, bf16[256,2048]{1,0:T(8,128)(2,1)}, u32[]{:S(2)}, u32[]{:S(2)}) collective-permute-start(bf16[256,2048]{1,0:T(8,128)(2,1)} %columns.5.tok_ref), channel_id=1, source_target_pairs={{1,0},{2,1},{3,2},{5,4},{6,5},{7,6},{9,8},{10,9},{11,10},{13,12},{... | collective-permute-start | bytes 3145736 | tf_op jit(solution)/shard_map/ppermute | solution.py:880
  41.8 26.0 %collective-permute-start.10 = (bf16[256,2048]{1,0:T(8,128)(2,1)S(1)}, bf16[256,2048]{1,0:T(8,128)(2,1)S(1)}, u32[]{:S(2)}, u32[]{:S(2)}) collective-permute-start(bf16[256,2048]{1,0:T(8,128)(2,1)S(1)} %pad_maximum_fusion.5), channel_id=1, source_target_pairs={{0,8},{4,12},{8,0},{12,4},{16,24},{20,28},{24,16},{28,20},{1,9},{5... | collective-permute-start | bytes 3145736 | tf_op jit(solution)/shard_map/ppermute | solution.py:33
  55.2 32.2 %collective-permute-start.15 = (bf16[256,2048]{1,0:T(8,128)(2,1)}, bf16[256,2048]{1,0:T(8,128)(2,1)S(1)}, u32[]{:S(2)}, u32[]{:S(2)}) collective-permute-start(bf16[256,2048]{1,0:T(8,128)(2,1)} %collective-permute-done.4), channel_id=1, source_target_pairs={{0,8},{4,12},{8,0},{12,4},{16,24},{20,28},{24,16},{28,20},{1,9},{5... | collective-permute-start | bytes 3145736 | tf_op jit(solution)/shard_map/ppermute | solution.py:33
  75.0 28.2 %collective-permute-start.16 = (bf16[256,2048]{1,0:T(8,128)(2,1)S(1)}, bf16[256,2048]{1,0:T(8,128)(2,1)S(1)}, u32[]{:S(2)}, u32[]{:S(2)}) collective-permute-start(bf16[256,2048]{1,0:T(8,128)(2,1)S(1)} %collective-permute-done.10), channel_id=1, source_target_pairs={{0,16},{4,20},{8,24},{12,28},{16,0},{20,4},{24,8},{28,12},{1,17},{... | collective-permute-start | bytes 3145736 | tf_op jit(solution)/shard_map/ppermute | solution.py:33
  105.4 26.7 %collective-permute-start.22 = (bf16[2048,2048]{1,0:T(8,128)(2,1)}, bf16[2048,2048]{1,0:T(8,128)(2,1)}, u32[]{:S(2)}, u32[]{:S(2)}) collective-permute-start(bf16[2048,2048]{1,0:T(8,128)(2,1)} %constant_dynamic-update-slice_fusion.4.a_ref.qa_ref.ka_ref.va_ref.mix_ref.up_ref.join_ref), channel_id=1, source_target_pairs={{0,4},{4,0},{8,12},{12,8},{16,20},{20,16},{24,28},{28,24},{1,5},{5... | collective-permute-start | bytes 25165832 | tf_op jit(solution)/shard_map/ppermute | solution.py:33
  107.8 41.8 %collective-permute-start.18 = (bf16[256,2048]{1,0:T(8,128)(2,1)S(1)}, bf16[256,2048]{1,0:T(8,128)(2,1)}, u32[]{:S(2)}, u32[]{:S(2)}) collective-permute-start(bf16[256,2048]{1,0:T(8,128)(2,1)S(1)} %copy-done.8), channel_id=1, source_target_pairs={{0,1},{1,2},{2,3},{4,5},{5,6},{6,7},{8,9},{9,10},{10,11},{12,13},{... | collective-permute-start | bytes 3145736 | tf_op jit(solution)/shard_map/ppermute | solution.py:879
  110.4 39.3 %collective-permute-start.19 = (bf16[256,2048]{1,0:T(8,128)(2,1)S(1)}, bf16[256,2048]{1,0:T(8,128)(2,1)}, u32[]{:S(2)}, u32[]{:S(2)}) collective-permute-start(bf16[256,2048]{1,0:T(8,128)(2,1)S(1)} %copy-done.8), channel_id=1, source_target_pairs={{1,0},{2,1},{3,2},{5,4},{6,5},{7,6},{9,8},{10,9},{11,10},{13,12},{... | collective-permute-start | bytes 3145736 | tf_op jit(solution)/shard_map/ppermute | solution.py:880
  111.8 37.8 %collective-permute-start.20 = (bf16[256,2048]{1,0:T(8,128)(2,1)S(1)}, bf16[256,2048]{1,0:T(8,128)(2,1)}, u32[]{:S(2)}, u32[]{:S(2)}) collective-permute-start(bf16[256,2048]{1,0:T(8,128)(2,1)S(1)} %bitcast.49), channel_id=1, source_target_pairs={{0,8},{4,12},{8,0},{12,4},{16,24},{20,28},{24,16},{28,20},{1,9},{5... | collective-permute-start | bytes 3145736 | tf_op jit(solution)/shard_map/ppermute | solution.py:33
  113.4 36.3 %collective-permute-start.21 = (bf16[256,2048]{1,0:T(8,128)(2,1)S(1)}, bf16[256,2048]{1,0:T(8,128)(2,1)}, u32[]{:S(2)}, u32[]{:S(2)}) collective-permute-start(bf16[256,2048]{1,0:T(8,128)(2,1)S(1)} %bitcast.50), channel_id=1, source_target_pairs={{0,16},{4,20},{8,24},{12,28},{16,0},{20,4},{24,8},{28,12},{1,17},{... | collective-permute-start | bytes 3145736 | tf_op jit(solution)/shard_map/ppermute | solution.py:33
  154.2 29.4 %collective-permute-start.24 = (bf16[256,2048]{1,0:T(8,128)(2,1)}, bf16[256,2048]{1,0:T(8,128)(2,1)}, u32[]{:S(2)}, u32[]{:S(2)}) collective-permute-start(bf16[256,2048]{1,0:T(8,128)(2,1)} %collective-permute-done.19), channel_id=1, source_target_pairs={{1,0},{2,1},{5,4},{6,5},{9,8},{10,9},{13,12},{14,13},{17,16},{18,1... | collective-permute-start | bytes 3145736 | tf_op jit(solution)/shard_map/ppermute | solution.py:880
  155.7 27.9 %collective-permute-start.25 = (bf16[256,2048]{1,0:T(8,128)(2,1)}, bf16[256,2048]{1,0:T(8,128)(2,1)S(1)}, u32[]{:S(2)}, u32[]{:S(2)}) collective-permute-start(bf16[256,2048]{1,0:T(8,128)(2,1)} %collective-permute-done.21), channel_id=1, source_target_pairs={{0,8},{4,12},{8,0},{12,4},{16,24},{20,28},{24,16},{28,20},{1,9},{5... | collective-permute-start | bytes 3145736 | tf_op jit(solution)/shard_map/ppermute | solution.py:33
  188.3 27.8 %collective-permute-start.27 = (bf16[256,2048]{1,0:T(8,128)(2,1)}, bf16[256,2048]{1,0:T(8,128)(2,1)}, u32[]{:S(2)}, u32[]{:S(2)}) collective-permute-start(bf16[256,2048]{1,0:T(8,128)(2,1)} %collective-permute-done.24), channel_id=1, source_target_pairs={{1,0},{5,4},{9,8},{13,12},{17,16},{21,20},{25,24},{29,28}} | collective-permute-start | bytes 3145736 | tf_op jit(solution)/shard_map/ppermute | solution.py:880
  272.8 30.5 %collective-permute-start.36 = (bf16[1024,2048]{1,0:T(8,128)(2,1)}, bf16[1024,2048]{1,0:T(8,128)(2,1)}, u32[]{:S(2)}, u32[]{:S(2)}) collective-permute-start(bf16[1024,2048]{1,0:T(8,128)(2,1)} %convolution_convert_fusion.3), channel_id=1, source_target_pairs={{0,4},{4,0},{8,12},{12,8},{16,20},{20,16},{24,28},{28,24},{1,5},{5... | collective-permute-start | bytes 12582920 | tf_op jit(solution)/shard_map/ppermute | solution.py:33
  273.2 28.3 %collective-permute-start.32 = (bf16[256,2048]{1,0:T(8,128)(2,1)}, bf16[256,2048]{1,0:T(8,128)(2,1)S(1)}, u32[]{:S(2)}, u32[]{:S(2)}) collective-permute-start(bf16[256,2048]{1,0:T(8,128)(2,1)} %get-tuple-element.240), channel_id=1, source_target_pairs={{0,1},{1,2},{4,5},{5,6},{8,9},{9,10},{12,13},{13,14},{16,17},{17,1... | collective-permute-start | bytes 3145736 | tf_op jit(solution)/shard_map/ppermute | solution.py:888
  313.2 36.1 %collective-permute-start.37 = (bf16[256,2048]{1,0:T(8,128)(2,1)}, bf16[256,2048]{1,0:T(8,128)(2,1)S(1)}, u32[]{:S(2)}, u32[]{:S(2)}) collective-permute-start(bf16[256,2048]{1,0:T(8,128)(2,1)} %get-tuple-element.261), channel_id=1, source_target_pairs={{0,1},{1,2},{2,3},{4,5},{5,6},{6,7},{8,9},{9,10},{10,11},{12,13},{... | collective-permute-start | bytes 3145736 | tf_op jit(solution)/shard_map/ppermute | solution.py:888
  316.6 32.7 %collective-permute-start.38 = (bf16[256,2048]{1,0:T(8,128)(2,1)}, bf16[256,2048]{1,0:T(8,128)(2,1)S(1)}, u32[]{:S(2)}, u32[]{:S(2)}) collective-permute-start(bf16[256,2048]{1,0:T(8,128)(2,1)} %get-tuple-element.262), channel_id=1, source_target_pairs={{1,0},{2,1},{3,2},{5,4},{6,5},{7,6},{9,8},{10,9},{11,10},{13,12},{... | collective-permute-start | bytes 3145736 | tf_op jit(solution)/shard_map/ppermute | solution.py:889
  318.1 31.2 %collective-permute-start.39 = (bf16[256,2048]{1,0:T(8,128)(2,1)}, bf16[256,2048]{1,0:T(8,128)(2,1)S(1)}, u32[]{:S(2)}, u32[]{:S(2)}) collective-permute-start(bf16[256,2048]{1,0:T(8,128)(2,1)} %pad_maximum_fusion.6), channel_id=1, source_target_pairs={{0,8},{4,12},{8,0},{12,4},{16,24},{20,28},{24,16},{28,20},{1,9},{5... | collective-permute-start | bytes 3145736 | tf_op jit(solution)/shard_map/ppermute | solution.py:33
  319.6 29.8 %collective-permute-start.40 = (bf16[256,2048]{1,0:T(8,128)(2,1)}, bf16[256,2048]{1,0:T(8,128)(2,1)}, u32[]{:S(2)}, u32[]{:S(2)}) collective-permute-start(bf16[256,2048]{1,0:T(8,128)(2,1)} %pad_maximum_fusion.7), channel_id=1, source_target_pairs={{0,16},{4,20},{8,24},{12,28},{16,0},{20,4},{24,8},{28,12},{1,17},{... | collective-permute-start | bytes 3145736 | tf_op jit(solution)/shard_map/ppermute | solution.py:33
  368.1 44.1 %collective-permute-start.45 = (bf16[1024,2048]{1,0:T(8,128)(2,1)}, bf16[1024,2048]{1,0:T(8,128)(2,1)}, u32[]{:S(2)}, u32[]{:S(2)}) collective-permute-start(bf16[1024,2048]{1,0:T(8,128)(2,1)} %pad_maximum_fusion.3), channel_id=1, source_target_pairs={{0,4},{4,0},{8,12},{12,8},{16,20},{20,16},{24,28},{28,24},{1,5},{5... | collective-permute-start | bytes 12582920 | tf_op jit(solution)/shard_map/ppermute | solution.py:33
  370.6 27.8 %collective-permute-start.41 = (bf16[256,2048]{1,0:T(8,128)(2,1)S(1)}, bf16[256,2048]{1,0:T(8,128)(2,1)S(1)}, u32[]{:S(2)}, u32[]{:S(2)}) collective-permute-start(bf16[256,2048]{1,0:T(8,128)(2,1)S(1)} %copy-done.50), channel_id=1, source_target_pairs={{0,1},{4,5},{8,9},{12,13},{16,17},{20,21},{24,25},{28,29}} | collective-permute-start | bytes 3145736 | tf_op jit(solution)/shard_map/ppermute | solution.py:888
  454.8 32.8 %collective-permute-start.51 = (bf16[256,2048]{1,0:T(8,128)(2,1)}, bf16[256,2048]{1,0:T(8,128)(2,1)}, u32[]{:S(2)}, u32[]{:S(2)}) collective-permute-start(bf16[256,2048]{1,0:T(8,128)(2,1)} %get-tuple-element.322), channel_id=1, source_target_pairs={{0,1},{1,2},{2,3},{4,5},{5,6},{6,7},{8,9},{9,10},{10,11},{12,13},{... | collective-permute-start | bytes 3145736 | tf_op jit(solution)/shard_map/ppermute | solution.py:888
  460.3 27.3 %collective-permute-start.52 = (bf16[256,2048]{1,0:T(8,128)(2,1)}, bf16[256,2048]{1,0:T(8,128)(2,1)}, u32[]{:S(2)}, u32[]{:S(2)}) collective-permute-start(bf16[256,2048]{1,0:T(8,128)(2,1)} %get-tuple-element.323), channel_id=1, source_target_pairs={{1,0},{2,1},{3,2},{5,4},{6,5},{7,6},{9,8},{10,9},{11,10},{13,12},{... | collective-permute-start | bytes 3145736 | tf_op jit(solution)/shard_map/ppermute | solution.py:889
  (89 other events, 1070.5 us)

commit v5 on v4

--- a/solution.py
+++ b/solution.py
@@ -477,6 +477,35 @@
         cost_estimate=SMALL,
         name="back",
     )(grad_hidden, grad_projected, both, both, token_rows, mean, scale, gains)
+
+
+def lay_kernel(*refs):
+    *ins, out_ref = refs
+    rows = ins[0].shape[0]
+    half = rows // 2
+    for w in range(len(ins) // 3):
+        own, from_x, from_y = ins[3 * w : 3 * w + 3]
+        base = 4 * w * rows
+        out_ref[base : base + rows, :] = own[:, :]
+        out_ref[base + 2 * rows : base + 3 * rows, :] = jnp.zeros(own.shape, BF16)
+        for piece, at in ((from_x, base + rows), (from_y, base + 3 * rows)):
+            out_ref[at : at + half, :] = piece[half:, :]
+            out_ref[at + half : at + rows, :] = piece[:half, :]
+
+
+def lay(*pieces):
+    rows, width = pieces[0].shape
+    weights = len(pieces) // 3
+    tile = width // 4
+    return pl.pallas_call(
+        lay_kernel,
+        out_shape=jax.ShapeDtypeStruct((4 * rows * weights, width), BF16),
+        grid=(4,),
+        in_specs=[pl.BlockSpec((rows, tile), lambda j: (0, j))] * len(pieces),
+        out_specs=pl.BlockSpec((4 * rows * weights, tile), lambda j: (0, j)),
+        cost_estimate=SMALL,
+        name="lay",
+    )(*pieces)
 
 
 def terms_kernel(*refs):
@@ -898,9 +927,6 @@
         def pair(top, low):
             return jnp.concatenate([top, low], axis=0)
 
-        def laid(own, from_x, from_y):
-            return [own, from_x[second], from_x[first], jnp.zeros_like(own), from_y[second], from_y[first]]
-
         def place(base, piece, part):
             return lax.dynamic_update_slice(base, piece, ((4 * part + 2) * local_rows, 0))
 
@@ -929,7 +955,7 @@
         tu3, td3 = gather_step(tu2, td2, 2)
         fa, fb = x(ay), y(bx)
         table3 = table2 + xor_shift(table2, "tensor", 2)
-        both = jnp.concatenate(laid(wa, ax, ay) + laid(wb, bx, by), axis=0)
+        both = lay(wa, ax, ay, wb, bx, by)
         tu3, td3, fa, fb, table3, both = cut(tu3, td3, fa, fb, table3, both)
         both_1 = place(place(both, fa, 0), fb, 1)
         both_1, wc, local_grads1 = cut(both_1, wc, local_grads1)
@@ -948,7 +974,7 @@
         )
         cu2, cd2 = gather_step(cu1, cd1, 1)
         fc = x(cy)
-        down_0 = jnp.concatenate(laid(wc, cx, cy), axis=0)
+        down_0 = lay(wc, cx, cy)
         *kept, attended, log_total = joined_forward(
             first_rows, both_1, both_2, joined_bias.reshape(1, -1), tables1, me, heads_here, head_size, n_tensor
         )
@@ -995,10 +1021,11 @@
         )
         bu, bd = scatter_step(zu, zd, 3)
         s9x, s9y = x(sx), y(sy)
+        came_j = core(joined_half(first_rows, grad_projected, grad_rows, attended, 1))
         back_1, sums_1 = back_half(grad_hidden, grad_projected, both_1, token_rows, mean, scale, gain_rows, 0)
         back_2, sums_2 = back_half(grad_hidden, grad_projected, both_2, token_rows, mean, scale, gain_rows, 1)
-        bu, bd, s9x, s9y, back_1, back_2, sums_1, sums_2, first_rows, grad_rows, grad_projected, attended = cut(
-            bu, bd, s9x, s9y, back_1, back_2, sums_1, sums_2, first_rows, grad_rows, grad_projected, attended
+        bu, bd, s9x, s9y, came_j, back_1, back_2, sums_1, sums_2, grad_projected, attended = cut(
+            bu, bd, s9x, s9y, came_j, back_1, back_2, sums_1, sums_2, grad_projected, attended
         )
         backs = (back_1, back_2)
         none = jnp.zeros((half, s9x.shape[1]), BF16)
@@ -1010,7 +1037,6 @@
         )
         eu, ed = scatter_step(zu, zd, 1)
         s10x, s10y = x(sx), y(sy)
-        came_j = core(joined_half(first_rows, grad_projected, grad_rows, attended, 1))
         keep_j = joined_half(first_rows, grad_projected, grad_rows, attended, 0)
         five = jnp.concatenate(
             [
@@ -1019,19 +1045,17 @@
             ],
             axis=0,
         )
-        eu, ed, s10x, s10y, keep_j, five, bu, bd = cut(eu, ed, s10x, s10y, keep_j, five, bu, bd)
+        sx, sy = at(keep_j, came_j, 3, 5).astype(BF16), at(keep_j, came_j, 5, 7).astype(BF16)
+        eu, ed, s10x, s10y, keep_j, five, bu, bd, sx, sy = cut(
+            eu, ed, s10x, s10y, keep_j, five, bu, bd, sx, sy
+        )
         zu, zd, sx, sy, s10x, s10y, five = cut(
-            *scatter_terms(backs, eu, ed, 2),
-            at(keep_j, came_j, 3, 5).astype(BF16),
-            at(keep_j, came_j, 5, 7).astype(BF16),
-            s10x, s10y, five,
+            *scatter_terms(backs, eu, ed, 2), sx, sy, s10x, s10y, five
         )
         eu, ed = scatter_step(zu, zd, 2)
         j1x, j1y = x(sx), y(sy)
         five = five.reshape(1, -1)
         five = five + xor_shift(five, "tensor", 1)
-        own = jnp.concatenate([h[:local_rows] for h in branches], axis=1)
-        output = finish_output(plus(own, bu, bd), shift_rows)
         down_sum = pair(
             plus(at(keep_d, came_d, 0, 1), d1x[first], s9y[first]),
             plus(at(keep_d, came_d, 1, 2), d1y[second], s9x[first]),
@@ -1049,8 +1073,8 @@
             ],
             axis=1,
         )
-        eu, ed, j1x, j1y, terms, down_sum, up_sum, output = cut(
-            eu, ed, j1x, j1y, terms, down_sum, up_sum, output
+        eu, ed, j1x, j1y, terms, down_sum, up_sum, bu, bd = cut(
+            eu, ed, j1x, j1y, terms, down_sum, up_sum, bu, bd
         )
         zu, zd, sx, sy, terms = cut(
             *scatter_terms(backs, eu, ed, 3),
@@ -1060,7 +1084,9 @@
         )
         eu, ed = scatter_step(zu, zd, 3)
         j2x, j2y = x(sx), y(sy)
-        terms, j2x, j2y = cut(terms, j2x, j2y)
+        terms, j2x, j2y, bu, bd = cut(terms, j2x, j2y, bu, bd)
+        own = jnp.concatenate([h[:local_rows] for h in branches], axis=1)
+        output = finish_output(plus(own, bu, bd), shift_rows)
         terms = butterfly(terms, "dp")
         five = terms[:, : 5 * width]
         five = five + xor_shift(five, "tensor", 2)
@@ -1072,7 +1098,6 @@
             plus(at(keep_j, came_j, 1, 2), j1y[second], j2x),
         )
         joined_sum, mix_sum = joined_mix[:, :joined_width], joined_mix[:, joined_width:].T
-        eu, ed, joined_sum, mix_sum = cut(eu, ed, joined_sum, mix_sum)
         input_grad = input_grad_rows(*backs, eu, ed, local_tokens, local_grads)
         return output, input_grad, joined_sum, mix_sum, up_sum, down_sum, small
 

time: 506 us -> 494 us (0.976)
  local copies, waits for them, and re-layouts: 63 us -> 36.7 us
  Pallas kernels: 151 us -> 162 us
    unnamed x130 -> x114, local copies, waits for them, and re-layouts: 40.3 us -> 14.4 us
    ppermute x6, waiting for transfers between devices: 35.2 us -> 17.1 us  [gather_step(): down = lax.ppermute(down, 'tensor', [(i + 1, i) for i in range(3 - s)])]
    ppermute x35, waiting for transfers between devices: 37.1 us -> 48.7 us  [xor_shift(): return lax.ppermute(values, axis, [(i, i ^ bit) for i in range(size)])]
    pallas_call x0 -> x2, Pallas kernels: none -> 10.9 us  [lay(): pl.pallas_call(lay_kernel, out_shape=jax.ShapeDtypeStruct((4 * rows * wei...]
  transfers between devices with their start and end apart: 59 -> 59, of which waited for: 23 -> 20; matrix products, arithmetic and copies ran while one was open for 20% -> 16% of each run, Pallas kernels for 26% -> 28%
where the time goes in v5:
time: 494 us; the launch traced here: 487 us
  Pallas kernels  162 us (33%)
  waiting for transfers between devices  87.9 us (18%)
  starting transfers between devices  85.7 us (17%)
  other arithmetic  67.2 us (14%)
  matrix products  45.5 us (9%)
  local copies, waits for them, and re-layouts  36.7 us (7%)
    ppermute x35, waiting for transfers between devices, xor_shift(): return lax.ppermute(values, axis, [(i, i ^ bit) for i in range(size)])  48.7 us
    dot_general x8, matrix products, grad_half(): jnp.einsum('nd,nf->df', chosen, columns, preferred_element_type=F32)  45.5 us
    ppermute x35, starting transfers between devices, xor_shift(): return lax.ppermute(values, axis, [(i, i ^ bit) for i in range(size)])  34.1 us
    pallas_call x2, Pallas kernels, back_half(): pl.pallas_call(functools.partial(back_kernel, step=256), out_shape=(jax.S...  27.9 us
    ppermute x6, waiting for transfers between devices, scatter_step(): up = lax.ppermute(to_up, 'tensor', [(i, i + 1) for i in range(s)])  22.1 us
    ppermute x6, starting transfers between devices, scatter_step(): up = lax.ppermute(to_up, 'tensor', [(i, i + 1) for i in range(s)])  21.6 us
    pallas_call x2, Pallas kernels, branch_half(): pl.pallas_call(functools.partial(branch_kernel, step=256), out_shape=jax....  20.2 us
    pallas_call x6, Pallas kernels, step_terms(): pl.pallas_call(terms_kernel, out_shape=(jax.ShapeDtypeStruct((rows, 2 * w...  19.2 us
  transfers between devices with their start and end apart: 59, of which 20 were waited for; matrix products, arithmetic and copies ran while one was open for 16% of the time, Pallas kernels for 28%

profile of v5, /device:TPU:0, one launch (start us, length us, event | category | flops | bytes accessed | tf_op | source)
XLA Modules:
  0.0 487.0 jit_solution(12451962472748098832)
XLA Ops:
  52.5 19.1 %collective-permute-done.12 = bf16[32,832]{1,0:T(8,128)(2,1)S(1)} collective-permute-done((bf16[32,832]{1,0:T(8,128)(2,1)S(1)}, bf16[32,832]{1,0:T(8,128)(2,1)S(1)}, u32[]{:S(2)}, u32[]{:S(2)}) %collective-permute-start.12) | collective-permute-done | bytes 53280 | tf_op jit(solution)/shard_map/ppermute | solution.py:33
  78.2 6.5 %lay.2 = bf16[2048,2048]{1,0:T(8,128)(2,1)} custom-call(bf16[256,2048]{1,0:T(8,128)(2,1)} %refs_0_.1, bf16[256,2048]{1,0:T(8,128)(2,1)} %copy-done.21, bf16[256,2048]{1,0:T(8,128)(2,1)} %collective-permute-done.4.refs_2_, bf16[256,2048]{1,0:T(8,128)(2,1)} %copy-done.11, bf16[256,2048]{1,0:T(8,128)(2,1)} %collective-permute-done.10.refs_4_, ...), custom_call_target="tpu_custom_call" | custom-call | flops 1000 | bytes 1000 | tf_op jit(solution)/shard_map/lay/pallas_call | solution.py:500
  84.7 9.2 %collective-permute-done.15 = bf16[256,2048]{1,0:T(8,128)(2,1)} collective-permute-done((bf16[256,2048]{1,0:T(8,128)(2,1)}, bf16[256,2048]{1,0:T(8,128)(2,1)}, u32[]{:S(2)}, u32[]{:S(2)}) %collective-permute-start.15) | collective-permute-done | bytes 1048608 | tf_op jit(solution)/shard_map/ppermute | solution.py:33
  93.9 6.1 %collective-permute-done.14 = bf16[256,2048]{1,0:T(8,128)(2,1)} collective-permute-done((bf16[256,2048]{1,0:T(8,128)(2,1)}, bf16[256,2048]{1,0:T(8,128)(2,1)}, u32[]{:S(2)}, u32[]{:S(2)}) %collective-permute-start.14) | collective-permute-done | bytes 1048608 | tf_op jit(solution)/shard_map/ppermute | solution.py:909
  123.6 5.0 %fusion.7 = (bf16[1024,2048]{1,0:T(8,128)(2,1)}, bf16[1024,2048]{1,0:T(8,128)(2,1)}) fusion(bf16[1024,2048]{1,0:T(8,128)(2,1)S(1)} %get-tuple-element.357.tok_ref, f32[2048]{0:T(1024)S(1)} %bitcast.66, f32[2048]{0:T(1024)S(1)} %bitcast.67, f32[1024]{0:T(1024)S(1)} %add_rsqrt_fusion, f32[1024]{0:T(1024)S(1)} %broadcast_multiply_fusion, f32[2048]{0:T(1024)S(1)} %bitcast.68, ...), kind=kLoop, calls=%fused_computation.9 | loop fusion | flops 18874368 | bytes 12623872 | tf_op jit(solution)/shard_map/convert_element_type | solution.py:706
  128.5 17.5 %hidden.1 = (bf16[1024,2048]{1,0:T(8,128)(2,1)}, bf16[1024,2048]{1,0:T(8,128)(2,1)}) custom-call(bf16[1024,2048]{1,0:T(8,128)(2,1)} %get-tuple-element.244.rows_ref, bf16[2048,2048]{1,0:T(8,128)(2,1)} %constant_dynamic-update-slice_fusion.1.a_ref.qa_ref.ka_ref.va_ref.mix_ref.up_ref.join_ref, ...), custom_call_target="tpu_custom_call" | custom-call | flops 1000 | bytes 1000 | tf_op jit(solution)/shard_map/hidden/pallas_call | solution.py:370
  155.5 17.6 %joined_forward.1 = (bf16[1024,512]{1,0:T(8,128)(2,1)}, bf16[1024,512]{1,0:T(8,128)(2,1)}, bf16[1024,512]{1,0:T(8,128)(2,1)}, bf16[1024,512]{1,0:T(8,128)(2,1)}, f32[2,1024,128]{2,1,0:T(8,128)}) custom-call(s32[1]{0:T(128)} %bitcast.11.me_ref, bf16[1024,2048]{1,0:T(8,128)(2,1)} %get-tuple-element.287.rows_ref, ...), custom_call_target="tpu_custom_call" | custom-call | flops 1000 | bytes 1000 | tf_op jit(solution)/shard_map/joined_forward/pallas_call | solution.py:584
  181.0 10.1 %branches.2.refs_0_.refs_2_ = bf16[1024,1024]{1,0:T(8,128)(2,1)} custom-call(bf16[1024,512]{1,0:T(8,128)(2,1)} %get-tuple-element.290.att_ref, bf16[2048,2048]{1,0:T(8,128)(2,1)} %constant_dynamic-update-slice_fusion.1.a_ref.qa_ref.ka_ref.va_ref.mix_ref.up_ref.join_ref, bf16[1024,2048]{1,0:T(8,128)(2,1)} %get-tuple-element.230.act_ref, ...), custom_call_target="tpu_custom_call" | custom-call | flops 1000 | bytes 1000 | tf_op jit(solution)/shard_map/branches/pallas_call | solution.py:423
  192.4 10.1 %branches.3.refs_1_.refs_3_ = bf16[1024,1024]{1,0:T(8,128)(2,1)} custom-call(bf16[1024,512]{1,0:T(8,128)(2,1)} %get-tuple-element.290.att_ref, bf16[2048,2048]{1,0:T(8,128)(2,1)} %collective-permute-done.22.b_ref.qb_ref.kb_ref.vb_ref.mix_ref.up_ref.join_ref, bf16[1024,2048]{1,0:T(8,128)(2,1)} %get-tuple-element.230.act_ref, ...), custom_call_target="tpu_custom_call" | custom-call | flops 1000 | bytes 1000 | tf_op jit(solution)/shard_map/branches/pallas_call | solution.py:423
  202.5 4.9 %collective-permute-done.27 = bf16[256,2048]{1,0:T(8,128)(2,1)} collective-permute-done((bf16[256,2048]{1,0:T(8,128)(2,1)}, bf16[256,2048]{1,0:T(8,128)(2,1)}, u32[]{:S(2)}, u32[]{:S(2)}) %collective-permute-start.27) | collective-permute-done | bytes 1048608 | tf_op jit(solution)/shard_map/ppermute | solution.py:909
  215.0 6.3 %convolution_convert_fusion.5 = bf16[1024,2048]{1,0:T(8,128)(2,1)} fusion(bf16[1024,2048]{1,0:T(8,128)(2,1)S(1)} %copy-done.6, bf16[1024,2048]{1,0:T(8,128)(2,1)S(1)} %pad_maximum_fusion.2.rows_ref.g_ref), kind=kOutput, calls=%fused_computation.26 | convolution fusion | flops 4297064448 | bytes 10485760 | tf_op jit(solution)/shard_map/nd,nf->df/dot_general | solution.py:741
  223.7 14.2 %hidden_back.1.hid_ref = bf16[1024,2048]{1,0:T(8,128)(2,1)} custom-call(bf16[1024,2048]{1,0:T(8,128)(2,1)} %copy-done.3, bf16[1024,2048]{1,0:T(8,128)(2,1)} %constant_dynamic-update-slice_fusion.down_ref.a_ref, bf16[1024,2048]{1,0:T(8,128)(2,1)} %collective-permute-done.28.down_ref.b_ref, bf16[1024,2048]{1,0:T(8,128)(2,1)} %get-tuple-element.231.slope_ref), custom_call_target="tpu_custom_call" | custom-call | flops 1000 | bytes 1000 | tf_op jit(solution)/shard_map/hidden_back/pallas_call | solution.py:398
  238.0 7.4 %convolution_convert_fusion.4 = bf16[1024,2048]{1,0:T(8,128)(2,1)S(1)} fusion(bf16[1024,2048]{1,0:T(8,128)(2,1)} %get-tuple-element.230.act_ref, bf16[1024,2048]{1,0:T(8,128)(2,1)} %copy-done.3), kind=kOutput, calls=%fused_computation.25 | convolution fusion | flops 4297064448 | bytes 10485760 | tf_op jit(solution)/shard_map/nd,nf->df/dot_general | solution.py:741
  254.6 9.5 %convolution_convert_fusion.3 = bf16[1024,2048]{1,0:T(8,128)(2,1)} fusion(bf16[1024,2048]{1,0:T(8,128)(2,1)} %hidden_back.1.hid_ref, bf16[1024,2048]{1,0:T(8,128)(2,1)} %get-tuple-element.244.rows_ref), kind=kOutput, calls=%fused_computation.24 | convolution fusion | flops 4297064448 | bytes 10485760 | tf_op jit(solution)/shard_map/nd,nf->df/dot_general | solution.py:741
  273.4 15.3 %mixed_backward.1.proj_ref = bf16[1024,1536]{1,0:T(8,128)(2,1)} custom-call(s32[1]{0:T(128)} %bitcast.11.me_ref, bf16[1024,512]{1,0:T(8,128)(2,1)} %get-tuple-element.246.q_ref, bf16[1024,512]{1,0:T(8,128)(2,1)} %get-tuple-element.247.k_ref, bf16[1024,512]{1,0:T(8,128)(2,1)} %get-tuple-element.248.v_ref, bf16[1024,2048]{1,0:T(8,128)(2,1)} %copy-done.3, ...), custom_call_target="tpu_custom_call" | custom-call | flops 1000 | bytes 1000 | tf_op jit(solution)/shard_map/mixed_backward/pallas_call | solution.py:607
  288.7 7.4 %convolution_convert_fusion.2 = bf16[1024,2048]{1,0:T(8,128)(2,1)S(1)} fusion(bf16[1024,2048]{1,0:T(8,128)(2,1)} %hidden_back.1.hid_ref, bf16[1024,2048]{1,0:T(8,128)(2,1)} %get-tuple-element.244.rows_ref), kind=kOutput, calls=%fused_computation.23 | convolution fusion | flops 4297064448 | bytes 10485760 | tf_op jit(solution)/shard_map/nd,nf->df/dot_general | solution.py:741
  307.9 5.8 %convolution_convert_fusion.1 = bf16[1024,1536]{1,0:T(8,128)(2,1)S(1)} fusion(bf16[1024,1536]{1,0:T(8,128)(2,1)S(1)} %copy-done.1, bf16[1024,2048]{1,0:T(8,128)(2,1)} %get-tuple-element.287.rows_ref), kind=kOutput, calls=%fused_computation.22 | convolution fusion | flops 3222798336 | bytes 8388608 | tf_op jit(solution)/shard_map/nd,nf->df/dot_general | solution.py:741
  325.1 14.0 %back.3 = (bf16[1024,1024]{1,0:T(8,128)(2,1)}, f32[8,1024]{1,0:T(8,128)}) custom-call(bf16[1024,2048]{1,0:T(8,128)(2,1)} %hidden_back.1.hid_ref, bf16[1024,1536]{1,0:T(8,128)(2,1)} %mixed_backward.1.proj_ref, bf16[2048,2048]{1,0:T(8,128)(2,1)} %collective-permute-done.22.b_ref.qb_ref.kb_ref.vb_ref.mix_ref.up_ref.join_ref, ...), custom_call_target="tpu_custom_call" | custom-call | flops 1000 | bytes 1000 | tf_op jit(solution)/shard_map/back/pallas_call | solution.py:462
  339.1 13.9 %back.2 = (bf16[1024,1024]{1,0:T(8,128)(2,1)}, f32[8,1024]{1,0:T(8,128)}) custom-call(bf16[1024,2048]{1,0:T(8,128)(2,1)} %hidden_back.1.hid_ref, bf16[1024,1536]{1,0:T(8,128)(2,1)} %mixed_backward.1.proj_ref, bf16[2048,2048]{1,0:T(8,128)(2,1)} %constant_dynamic-update-slice_fusion.1.a_ref.qa_ref.ka_ref.va_ref.mix_ref.up_ref.join_ref, ...), custom_call_target="tpu_custom_call" | custom-call | flops 1000 | bytes 1000 | tf_op jit(solution)/shard_map/back/pallas_call | solution.py:462
  369.4 5.5 %convolution_convert_fusion = bf16[1024,1536]{1,0:T(8,128)(2,1)S(1)} fusion(bf16[1024,1536]{1,0:T(8,128)(2,1)S(1)} %copy-done.2, bf16[1024,2048]{1,0:T(8,128)(2,1)} %get-tuple-element.287.rows_ref), kind=kOutput, calls=%fused_computation.21 | convolution fusion | flops 3222798336 | bytes 8388608 | tf_op jit(solution)/shard_map/nd,nf->df/dot_general | solution.py:741
  375.0 5.1 %collective-permute-start.42 = (bf16[256,2048]{1,0:T(8,128)(2,1)S(1)}, bf16[256,2048]{1,0:T(8,128)(2,1)S(1)}, u32[]{:S(2)}, u32[]{:S(2)}) collective-permute-start(bf16[256,2048]{1,0:T(8,128)(2,1)S(1)} %copy-done.50), channel_id=1, source_target_pairs={{0,1},{4,5},{8,9},{12,13},{16,17},{20,21},{24,25},{28,29}} | collective-permute-start | bytes 3145736 | tf_op jit(solution)/shard_map/ppermute | solution.py:917
  391.1 11.3 %collective-permute-done.42.refs_4_ = bf16[256,2048]{1,0:T(8,128)(2,1)S(1)} collective-permute-done((bf16[256,2048]{1,0:T(8,128)(2,1)S(1)}, bf16[256,2048]{1,0:T(8,128)(2,1)S(1)}, u32[]{:S(2)}, u32[]{:S(2)}) %collective-permute-start.42) | collective-permute-done | bytes 1048608 | tf_op jit(solution)/shard_map/ppermute | solution.py:917
  426.4 9.9 %collective-permute-done.46.refs_4_ = bf16[256,2048]{1,0:T(8,128)(2,1)S(1)} collective-permute-done((bf16[256,2048]{1,0:T(8,128)(2,1)}, bf16[256,2048]{1,0:T(8,128)(2,1)S(1)}, u32[]{:S(2)}, u32[]{:S(2)}) %collective-permute-start.46) | collective-permute-done | bytes 1048608 | tf_op jit(solution)/shard_map/ppermute | solution.py:917
  480.7 6.1 %input_grad.1 = f32[256,2048]{1,0:T(8,128)} custom-call(s32[16]{0:T(128)} %fusion.31.index_ref, bf16[1024,1024]{1,0:T(8,128)(2,1)} %get-tuple-element.273.refs_0_.refs_2_.one_ref, bf16[1024,1024]{1,0:T(8,128)(2,1)} %get-tuple-element.274.refs_1_.refs_3_.two_ref, bf16[256,2048]{1,0:T(8,128)(2,1)} %collective-permute-done.53.up_ref, ...), custom_call_target="tpu_custom_call" | custom-call | flops 1000 | bytes 1000 | tf_op jit(solution)/shard_map/input_grad/pallas_call | solution.py:559
  (347 shorter events, 246.9 us)
Async XLA Ops:
  9.3 26.5 %collective-permute-start = (bf16[256,2048]{1,0:T(8,128)(2,1)}, bf16[256,2048]{1,0:T(8,128)(2,1)}, u32[]{:S(2)}, u32[]{:S(2)}) collective-permute-start(bf16[256,2048]{1,0:T(8,128)(2,1)} %columns.5.tok_ref), channel_id=1, source_target_pairs={{0,1},{1,2},{2,3},{4,5},{5,6},{6,7},{8,9},{9,10},{10,11},{12,13},{... | collective-permute-start | bytes 3145736 | tf_op jit(solution)/shard_map/ppermute | solution.py:908
  41.6 31.6 %collective-permute-start.10 = (bf16[256,2048]{1,0:T(8,128)(2,1)S(1)}, bf16[256,2048]{1,0:T(8,128)(2,1)}, u32[]{:S(2)}, u32[]{:S(2)}) collective-permute-start(bf16[256,2048]{1,0:T(8,128)(2,1)S(1)} %pad_maximum_fusion.5.refs_3_), channel_id=1, source_target_pairs={{0,8},{4,12},{8,0},{12,4},{16,24},{20,28},{24,16},{28,20},{1,9},{5... | collective-permute-start | bytes 3145736 | tf_op jit(solution)/shard_map/ppermute | solution.py:33
  42.1 31.1 %collective-permute-start.11 = (bf16[256,2048]{1,0:T(8,128)(2,1)S(1)}, bf16[256,2048]{1,0:T(8,128)(2,1)S(1)}, u32[]{:S(2)}, u32[]{:S(2)}) collective-permute-start(bf16[256,2048]{1,0:T(8,128)(2,1)S(1)} %pad_maximum_fusion.5.refs_3_), channel_id=1, source_target_pairs={{0,16},{4,20},{8,24},{12,28},{16,0},{20,4},{24,8},{28,12},{1,17},{... | collective-permute-start | bytes 3145736 | tf_op jit(solution)/shard_map/ppermute | solution.py:33
  42.6 30.6 %collective-permute-start.8 = (bf16[256,2048]{1,0:T(8,128)(2,1)}, bf16[256,2048]{1,0:T(8,128)(2,1)}, u32[]{:S(2)}, u32[]{:S(2)}) collective-permute-start(bf16[256,2048]{1,0:T(8,128)(2,1)} %collective-permute-done), channel_id=1, source_target_pairs={{1,2},{2,3},{5,6},{6,7},{9,10},{10,11},{13,14},{14,15},{17,18},{18... | collective-permute-start | bytes 3145736 | tf_op jit(solution)/shard_map/ppermute | solution.py:908
  44.3 29.0 %collective-permute-start.9 = (bf16[256,2048]{1,0:T(8,128)(2,1)}, bf16[256,2048]{1,0:T(8,128)(2,1)}, u32[]{:S(2)}, u32[]{:S(2)}) collective-permute-start(bf16[256,2048]{1,0:T(8,128)(2,1)} %collective-permute-done.1), channel_id=1, source_target_pairs={{1,0},{2,1},{5,4},{6,5},{9,8},{10,9},{13,12},{14,13},{17,16},{18,1... | collective-permute-start | bytes 3145736 | tf_op jit(solution)/shard_map/ppermute | solution.py:909
  106.9 39.1 %collective-permute-start.18 = (bf16[256,2048]{1,0:T(8,128)(2,1)S(1)}, bf16[256,2048]{1,0:T(8,128)(2,1)}, u32[]{:S(2)}, u32[]{:S(2)}) collective-permute-start(bf16[256,2048]{1,0:T(8,128)(2,1)S(1)} %copy-done.9), channel_id=1, source_target_pairs={{0,1},{1,2},{2,3},{4,5},{5,6},{6,7},{8,9},{9,10},{10,11},{12,13},{... | collective-permute-start | bytes 3145736 | tf_op jit(solution)/shard_map/ppermute | solution.py:908
  111.5 34.6 %collective-permute-start.19 = (bf16[256,2048]{1,0:T(8,128)(2,1)S(1)}, bf16[256,2048]{1,0:T(8,128)(2,1)}, u32[]{:S(2)}, u32[]{:S(2)}) collective-permute-start(bf16[256,2048]{1,0:T(8,128)(2,1)S(1)} %copy-done.9), channel_id=1, source_target_pairs={{1,0},{2,1},{3,2},{5,4},{6,5},{7,6},{9,8},{10,9},{11,10},{13,12},{... | collective-permute-start | bytes 3145736 | tf_op jit(solution)/shard_map/ppermute | solution.py:909
  113.1 33.0 %collective-permute-start.20 = (bf16[256,2048]{1,0:T(8,128)(2,1)S(1)}, bf16[256,2048]{1,0:T(8,128)(2,1)}, u32[]{:S(2)}, u32[]{:S(2)}) collective-permute-start(bf16[256,2048]{1,0:T(8,128)(2,1)S(1)} %bitcast.49), channel_id=1, source_target_pairs={{0,8},{4,12},{8,0},{12,4},{16,24},{20,28},{24,16},{28,20},{1,9},{5... | collective-permute-start | bytes 3145736 | tf_op jit(solution)/shard_map/ppermute | solution.py:33
  113.7 32.4 %collective-permute-start.21 = (bf16[256,2048]{1,0:T(8,128)(2,1)S(1)}, bf16[256,2048]{1,0:T(8,128)(2,1)}, u32[]{:S(2)}, u32[]{:S(2)}) collective-permute-start(bf16[256,2048]{1,0:T(8,128)(2,1)S(1)} %bitcast.50), channel_id=1, source_target_pairs={{0,16},{4,20},{8,24},{12,28},{16,0},{20,4},{24,8},{28,12},{1,17},{... | collective-permute-start | bytes 3145736 | tf_op jit(solution)/shard_map/ppermute | solution.py:33
  146.1 27.0 %collective-permute-start.23 = (bf16[256,2048]{1,0:T(8,128)(2,1)}, bf16[256,2048]{1,0:T(8,128)(2,1)S(1)}, u32[]{:S(2)}, u32[]{:S(2)}) collective-permute-start(bf16[256,2048]{1,0:T(8,128)(2,1)} %collective-permute-done.18), channel_id=1, source_target_pairs={{1,2},{2,3},{5,6},{6,7},{9,10},{10,11},{13,14},{14,15},{17,18},{18... | collective-permute-start | bytes 3145736 | tf_op jit(solution)/shard_map/ppermute | solution.py:908
  146.8 28.2 %collective-permute-start.24 = (bf16[256,2048]{1,0:T(8,128)(2,1)}, bf16[256,2048]{1,0:T(8,128)(2,1)}, u32[]{:S(2)}, u32[]{:S(2)}) collective-permute-start(bf16[256,2048]{1,0:T(8,128)(2,1)} %collective-permute-done.19), channel_id=1, source_target_pairs={{1,0},{2,1},{5,4},{6,5},{9,8},{10,9},{13,12},{14,13},{17,16},{18,1... | collective-permute-start | bytes 3145736 | tf_op jit(solution)/shard_map/ppermute | solution.py:909
  179.7 27.8 %collective-permute-start.27 = (bf16[256,2048]{1,0:T(8,128)(2,1)}, bf16[256,2048]{1,0:T(8,128)(2,1)}, u32[]{:S(2)}, u32[]{:S(2)}) collective-permute-start(bf16[256,2048]{1,0:T(8,128)(2,1)} %collective-permute-done.24), channel_id=1, source_target_pairs={{1,0},{5,4},{9,8},{13,12},{17,16},{21,20},{25,24},{29,28}} | collective-permute-start | bytes 3145736 | tf_op jit(solution)/shard_map/ppermute | solution.py:909
  264.1 32.1 %collective-permute-start.36 = (bf16[1024,2048]{1,0:T(8,128)(2,1)}, bf16[1024,2048]{1,0:T(8,128)(2,1)}, u32[]{:S(2)}, u32[]{:S(2)}) collective-permute-start(bf16[1024,2048]{1,0:T(8,128)(2,1)} %convolution_convert_fusion.3), channel_id=1, source_target_pairs={{0,4},{4,0},{8,12},{12,8},{16,20},{20,16},{24,28},{28,24},{1,5},{5... | collective-permute-start | bytes 12582920 | tf_op jit(solution)/shard_map/ppermute | solution.py:33
  264.4 31.6 %collective-permute-start.32 = (bf16[256,2048]{1,0:T(8,128)(2,1)}, bf16[256,2048]{1,0:T(8,128)(2,1)S(1)}, u32[]{:S(2)}, u32[]{:S(2)}) collective-permute-start(bf16[256,2048]{1,0:T(8,128)(2,1)} %get-tuple-element.240), channel_id=1, source_target_pairs={{0,1},{1,2},{4,5},{5,6},{8,9},{9,10},{12,13},{13,14},{16,17},{17,1... | collective-permute-start | bytes 3145736 | tf_op jit(solution)/shard_map/ppermute | solution.py:917
  268.0 28.0 %collective-permute-start.33 = (bf16[256,2048]{1,0:T(8,128)(2,1)}, bf16[256,2048]{1,0:T(8,128)(2,1)S(1)}, u32[]{:S(2)}, u32[]{:S(2)}) collective-permute-start(bf16[256,2048]{1,0:T(8,128)(2,1)} %get-tuple-element.241), channel_id=1, source_target_pairs={{2,1},{3,2},{6,5},{7,6},{10,9},{11,10},{14,13},{15,14},{18,17},{19... | collective-permute-start | bytes 3145736 | tf_op jit(solution)/shard_map/ppermute | solution.py:918
  269.0 27.1 %collective-permute-start.34 = (bf16[256,2048]{1,0:T(8,128)(2,1)}, bf16[256,2048]{1,0:T(8,128)(2,1)S(1)}, u32[]{:S(2)}, u32[]{:S(2)}) collective-permute-start(bf16[256,2048]{1,0:T(8,128)(2,1)} %get-tuple-element.242), channel_id=1, source_target_pairs={{0,8},{4,12},{8,0},{12,4},{16,24},{20,28},{24,16},{28,20},{1,9},{5... | collective-permute-start | bytes 3145736 | tf_op jit(solution)/shard_map/ppermute | solution.py:33
  316.3 39.7 %collective-permute-start.41 = (bf16[1024,2048]{1,0:T(8,128)(2,1)}, bf16[1024,2048]{1,0:T(8,128)(2,1)}, u32[]{:S(2)}, u32[]{:S(2)}) collective-permute-start(bf16[1024,2048]{1,0:T(8,128)(2,1)} %pad_maximum_fusion.3), channel_id=1, source_target_pairs={{0,4},{4,0},{8,12},{12,8},{16,20},{20,16},{24,28},{28,24},{1,5},{5... | collective-permute-start | bytes 12582920 | tf_op jit(solution)/shard_map/ppermute | solution.py:33
  316.3 39.7 %collective-permute-start.37 = (bf16[256,2048]{1,0:T(8,128)(2,1)}, bf16[256,2048]{1,0:T(8,128)(2,1)S(1)}, u32[]{:S(2)}, u32[]{:S(2)}) collective-permute-start(bf16[256,2048]{1,0:T(8,128)(2,1)} %get-tuple-element.261), channel_id=1, source_target_pairs={{0,1},{1,2},{2,3},{4,5},{5,6},{6,7},{8,9},{9,10},{10,11},{12,13},{... | collective-permute-start | bytes 3145736 | tf_op jit(solution)/shard_map/ppermute | solution.py:917
  319.7 36.3 %collective-permute-start.38 = (bf16[256,2048]{1,0:T(8,128)(2,1)}, bf16[256,2048]{1,0:T(8,128)(2,1)S(1)}, u32[]{:S(2)}, u32[]{:S(2)}) collective-permute-start(bf16[256,2048]{1,0:T(8,128)(2,1)} %get-tuple-element.262), channel_id=1, source_target_pairs={{1,0},{2,1},{3,2},{5,4},{6,5},{7,6},{9,8},{10,9},{11,10},{13,12},{... | collective-permute-start | bytes 3145736 | tf_op jit(solution)/shard_map/ppermute | solution.py:918
  321.0 35.0 %collective-permute-start.39 = (bf16[256,2048]{1,0:T(8,128)(2,1)}, bf16[256,2048]{1,0:T(8,128)(2,1)S(1)}, u32[]{:S(2)}, u32[]{:S(2)}) collective-permute-start(bf16[256,2048]{1,0:T(8,128)(2,1)} %pad_maximum_fusion.6), channel_id=1, source_target_pairs={{0,8},{4,12},{8,0},{12,4},{16,24},{20,28},{24,16},{28,20},{1,9},{5... | collective-permute-start | bytes 3145736 | tf_op jit(solution)/shard_map/ppermute | solution.py:33
  321.6 34.4 %collective-permute-start.40 = (bf16[256,2048]{1,0:T(8,128)(2,1)}, bf16[256,2048]{1,0:T(8,128)(2,1)}, u32[]{:S(2)}, u32[]{:S(2)}) collective-permute-start(bf16[256,2048]{1,0:T(8,128)(2,1)} %pad_maximum_fusion.7), channel_id=1, source_target_pairs={{0,16},{4,20},{8,24},{12,28},{16,0},{20,4},{24,8},{28,12},{1,17},{... | collective-permute-start | bytes 3145736 | tf_op jit(solution)/shard_map/ppermute | solution.py:33
  375.0 27.3 %collective-permute-start.42 = (bf16[256,2048]{1,0:T(8,128)(2,1)S(1)}, bf16[256,2048]{1,0:T(8,128)(2,1)S(1)}, u32[]{:S(2)}, u32[]{:S(2)}) collective-permute-start(bf16[256,2048]{1,0:T(8,128)(2,1)S(1)} %copy-done.50), channel_id=1, source_target_pairs={{0,1},{4,5},{8,9},{12,13},{16,17},{20,21},{24,25},{28,29}} | collective-permute-start | bytes 3145736 | tf_op jit(solution)/shard_map/ppermute | solution.py:917
  449.1 31.5 %collective-permute-start.53 = (bf16[256,2048]{1,0:T(8,128)(2,1)}, bf16[256,2048]{1,0:T(8,128)(2,1)}, u32[]{:S(2)}, u32[]{:S(2)}) collective-permute-start(bf16[256,2048]{1,0:T(8,128)(2,1)} %get-tuple-element.329), channel_id=1, source_target_pairs={{0,1},{1,2},{2,3},{4,5},{5,6},{6,7},{8,9},{9,10},{10,11},{12,13},{... | collective-permute-start | bytes 3145736 | tf_op jit(solution)/shard_map/ppermute | solution.py:917
  453.2 27.5 %collective-permute-start.54 = (bf16[256,2048]{1,0:T(8,128)(2,1)}, bf16[256,2048]{1,0:T(8,128)(2,1)}, u32[]{:S(2)}, u32[]{:S(2)}) collective-permute-start(bf16[256,2048]{1,0:T(8,128)(2,1)} %get-tuple-element.330), channel_id=1, source_target_pairs={{1,0},{2,1},{3,2},{5,4},{6,5},{7,6},{9,8},{10,9},{11,10},{13,12},{... | collective-permute-start | bytes 3145736 | tf_op jit(solution)/shard_map/ppermute | solution.py:918
  (89 other events, 1134.9 us)

commit v6 on v5

--- a/solution.py
+++ b/solution.py
@@ -14,6 +14,9 @@
 BF16 = jnp.bfloat16
 HALVES = [(0, 0), (0, 1), (2, 1), (2, 0), (6, 0), (6, 1), (4, 1), (4, 0)]
 ORDER = HALVES + [(p ^ 1, h) for p, h in HALVES]
+
+
+SMALL = pl.CostEstimate(flops=1000, bytes_accessed=1000, transcendentals=0)
 
 
 def cut(*values):
@@ -63,6 +66,7 @@
             in_specs=[pl.BlockSpec((tile, width), lambda i, s: (i, 0))],
             out_specs=pl.BlockSpec((tile, width), lambda i, s: (i, 0)),
         ),
+        cost_estimate=SMALL,
         name="columns",
     )(index, values)
 
@@ -199,9 +203,6 @@
     key = lax.broadcasted_iota(jnp.int32, scores.shape, 1)
     allowed = (column_starts == row_starts[:, :keys]) & (key <= query)
     return allowed, jnp.where(allowed, scores, -1e30)
-
-
-SMALL = pl.CostEstimate(flops=1000, bytes_accessed=1000, transcendentals=0)
 
 
 def spots(me_ref, size, block):
@@ -380,13 +381,17 @@
     )(rows, top, low, bias.reshape(1, -1))
 
 
-def slope_kernel(rows_ref, a_ref, b_ref, slope_ref, out_ref, *, step):
+def slope_kernel(rows_ref, a_ref, b_ref, slope_ref, out_ref, sum_ref, *, step):
     middle = a_ref.shape[0]
+    total = 0.0
     for i in range(rows_ref.shape[0] // step):
         here = slice(i * step, (i + 1) * step)
         active = contract(rows_ref[here, :middle], a_ref[:, :], ((1,), (0,)))
         active = active + contract(rows_ref[here, middle:], b_ref[:, :], ((1,), (0,)))
-        out_ref[here, :] = (active * slope_ref[here, :].astype(F32)).astype(BF16)
+        made = (active * slope_ref[here, :].astype(F32)).astype(BF16)
+        out_ref[here, :] = made
+        total = total + jnp.sum(made.astype(F32), axis=0, keepdims=True)
+    sum_ref[:, :] = total
 
 
 def hidden_back(rows, top, low, slope):
@@ -397,10 +402,10 @@
     made = pl.BlockSpec((count, tile), lambda j: (0, j))
     return pl.pallas_call(
         functools.partial(slope_kernel, step=256),
-        out_shape=jax.ShapeDtypeStruct((count, out), BF16),
+        out_shape=(jax.ShapeDtypeStruct((count, out), BF16), jax.ShapeDtypeStruct((1, out), F32)),
         grid=(out // tile,),
         in_specs=[pl.BlockSpec((count, width), lambda j: (0, 0)), half, half, made],
-        out_specs=made,
+        out_specs=(made, pl.BlockSpec((1, tile), lambda j: (0, j))),
         cost_estimate=SMALL,
         name="hidden_back",
     )(rows, top, low, slope)
@@ -506,6 +511,50 @@
         cost_estimate=SMALL,
         name="lay",
     )(*pieces)
+
+
+def pair_sums_kernel(kept_x, came_x, kept_y, came_y, to_x, to_y):
+    to_x[:, :] = (kept_x[:, :].astype(F32) + came_x[:, :].astype(F32)).astype(BF16)
+    to_y[:, :] = (kept_y[:, :].astype(F32) + came_y[:, :].astype(F32)).astype(BF16)
+
+
+def pair_sums(kept, came, half):
+    width = kept.shape[1]
+    of_x = pl.BlockSpec((half, width), lambda i: (3 + i, 0))
+    of_y = pl.BlockSpec((half, width), lambda i: (5 + i, 0))
+    out = pl.BlockSpec((half, width), lambda i: (i, 0))
+    return pl.pallas_call(
+        pair_sums_kernel,
+        out_shape=(jax.ShapeDtypeStruct((2 * half, width), BF16),) * 2,
+        grid=(2,),
+        in_specs=[of_x, of_x, of_y, of_y],
+        out_specs=(out, out),
+        cost_estimate=SMALL,
+        name="pair_sums",
+    )(kept, came, kept, came)
+
+
+def own_sums_kernel(kept, came, a, b, c, d, out):
+    half = a.shape[0]
+    top, low = slice(0, half), slice(half, 2 * half)
+    for part, one, two in ((top, a, b), (low, c, d)):
+        total = kept[part, :].astype(F32) + came[part, :].astype(F32)
+        out[part, :] = total + one[:, :].astype(F32) + two[:, :].astype(F32)
+
+
+def own_sums(kept, came, half, *came_in):
+    width = kept.shape[1]
+    tile = width // 4
+    rows = pl.BlockSpec((2 * half, tile), lambda j: (0, j))
+    return pl.pallas_call(
+        own_sums_kernel,
+        out_shape=jax.ShapeDtypeStruct((2 * half, width), F32),
+        grid=(4,),
+        in_specs=[rows, rows] + [pl.BlockSpec((half, tile), lambda j, k=k: (k, j)) for _, k in came_in],
+        out_specs=rows,
+        cost_estimate=SMALL,
+        name="own_sums",
+    )(kept, came, *(v for v, _ in came_in))
 
 
 def terms_kernel(*refs):
@@ -991,14 +1040,13 @@
         grad_rows = in_turn(local_grads1, (cu1, cu2, cu3), (cd1, cd2, cd3))
         came_d = core(grad_half(grad_rows, activated, 1))
         keep_d = grad_half(grad_rows, activated, 0)
-        grad_hidden = hidden_back(grad_rows, down_1, down_2, slope)
+        grad_hidden, up_bias_term = hidden_back(grad_rows, down_1, down_2, slope)
         bu, bd, came_d, keep_d, grad_hidden, grad_rows = cut(
             bu, bd, came_d, keep_d, grad_hidden, grad_rows
         )
         zu, zd, sx, sy, second_rows, grad_hidden, grad_rows = cut(
             *scatter_terms(branches, bu, bd, 2),
-            at(keep_d, came_d, 3, 5).astype(BF16),
-            at(keep_d, came_d, 5, 7).astype(BF16),
+            *pair_sums(keep_d, came_d, half),
             second_rows, grad_hidden, grad_rows,
         )
         bu, bd = scatter_step(zu, zd, 2)
@@ -1045,7 +1093,10 @@
             ],
             axis=0,
         )
-        sx, sy = at(keep_j, came_j, 3, 5).astype(BF16), at(keep_j, came_j, 5, 7).astype(BF16)
+        sx, sy = pair_sums(keep_j, came_j, half)
+        five = five.reshape(1, -1)
+        five = five + xor_shift(five, "tensor", 1)
+        five = from_frame(five.reshape(5, width)).reshape(1, -1)
         eu, ed, s10x, s10y, keep_j, five, bu, bd, sx, sy = cut(
             eu, ed, s10x, s10y, keep_j, five, bu, bd, sx, sy
         )
@@ -1054,50 +1105,37 @@
         )
         eu, ed = scatter_step(zu, zd, 2)
         j1x, j1y = x(sx), y(sy)
-        five = five.reshape(1, -1)
-        five = five + xor_shift(five, "tensor", 1)
-        down_sum = pair(
-            plus(at(keep_d, came_d, 0, 1), d1x[first], s9y[first]),
-            plus(at(keep_d, came_d, 1, 2), d1y[second], s9x[first]),
-        ).T
-        up_sum = pair(
-            plus(at(keep_u, came_u, 0, 1), s10x[second], s10y[second]),
-            plus(at(keep_u, came_u, 1, 2), s10x[first], s10y[first]),
-        )
-        five = from_frame(five.reshape(5, width)).reshape(1, -1)
+        five = five + xor_shift(five, "tensor", 2)
+        down_sum = own_sums(keep_d, came_d, half, (d1x, 0), (s9y, 0), (d1y, 1), (s9x, 0)).T
+        up_sum = own_sums(keep_u, came_u, half, (s10x, 1), (s10y, 1), (s10x, 0), (s10y, 0))
         terms = jnp.concatenate(
             [
-                five,
                 jnp.sum(grad_projected, axis=0, dtype=F32, keepdims=True),
-                jnp.sum(grad_hidden, axis=0, dtype=F32, keepdims=True),
+                up_bias_term,
             ],
             axis=1,
         )
-        eu, ed, j1x, j1y, terms, down_sum, up_sum, bu, bd = cut(
-            eu, ed, j1x, j1y, terms, down_sum, up_sum, bu, bd
-        )
-        zu, zd, sx, sy, terms = cut(
+        eu, ed, j1x, j1y, five, terms, down_sum, up_sum, bu, bd = cut(
+            eu, ed, j1x, j1y, five, terms, down_sum, up_sum, bu, bd
+        )
+        zu, zd, sx, sy, five, bu, bd = cut(
             *scatter_terms(backs, eu, ed, 3),
             plus(at(keep_j, came_j, 2, 3), j1y[first]).astype(BF16),
             plus(at(keep_j, came_j, 7, 8), j1x[second]).astype(BF16),
-            terms,
+            five, bu, bd,
         )
         eu, ed = scatter_step(zu, zd, 3)
         j2x, j2y = x(sx), y(sy)
-        terms, j2x, j2y, bu, bd = cut(terms, j2x, j2y, bu, bd)
         own = jnp.concatenate([h[:local_rows] for h in branches], axis=1)
         output = finish_output(plus(own, bu, bd), shift_rows)
-        terms = butterfly(terms, "dp")
-        five = terms[:, : 5 * width]
-        five = five + xor_shift(five, "tensor", 2)
+        terms = butterfly(jnp.concatenate([five, terms], axis=1), "dp")
         small = small_shares(
-            five, terms[0, 5 * width : 5 * width + joined_width], terms[:, 5 * width + joined_width :]
-        )
-        joined_mix = pair(
-            plus(at(keep_j, came_j, 0, 1), j1x[first], j2y),
-            plus(at(keep_j, came_j, 1, 2), j1y[second], j2x),
-        )
-        joined_sum, mix_sum = joined_mix[:, :joined_width], joined_mix[:, joined_width:].T
+            terms[:, : 5 * width], terms[0, 5 * width : 5 * width + joined_width],
+            terms[:, 5 * width + joined_width :],
+        )
+        joined_mix = own_sums(keep_j, came_j, half, (j1x, 0), (j2y, 0), (j1y, 1), (j2x, 0))
+        joined_sum = joined_mix[:, :joined_width].reshape(proj_weight.shape)
+        eu, ed, joined_sum, mix_sum = cut(eu, ed, joined_sum, joined_mix[:, joined_width:].T)
         input_grad = input_grad_rows(*backs, eu, ed, local_tokens, local_grads)
         return output, input_grad, joined_sum, mix_sum, up_sum, down_sum, small
 

time: 494 us -> 484 us (0.980)
  Pallas kernels: 162 us -> 182 us
  other arithmetic: 67.2 us -> 48 us
  waiting for transfers between devices: 87.9 us -> 74.2 us
    ppermute x6, waiting for transfers between devices: 22.1 us -> 1.23 us  [scatter_step(): up = lax.ppermute(to_up, 'tensor', [(i, i + 1) for i in range(s)])]
    pallas_call x1 -> x6, Pallas kernels: 14.2 us -> 35 us  [the longest x1 14.6 us: hidden_back(): pl.pallas_call(functools.partial(slope_kernel, step=256), out_shape=(jax....]
    add x3 -> x0, other arithmetic: 9.6 us -> none  [plus(): return functools.reduce(lambda a, b: a + b, [t.astype(F32) for t in terms])]
    convert_element_type x2 -> x0, other arithmetic: 7.39 us -> none  [the longest x1 3.81 us: staged(): at(keep_d, came_d, 5, 7).astype(BF16)]
    ppermute x35, waiting for transfers between devices: 48.7 us -> 55.7 us  [xor_shift(): return lax.ppermute(values, axis, [(i, i ^ bit) for i in range(size)])]
    ppermute x6, starting transfers between devices: 21.6 us -> 14.9 us  [scatter_step(): up = lax.ppermute(to_up, 'tensor', [(i, i + 1) for i in range(s)])]
    unnamed x114 -> x89, local copies, waits for them, and re-layouts: 14.4 us -> 13.9 us
  transfers between devices with their start and end apart: 59 -> 59, of which waited for: 20 -> 15; matrix products, arithmetic and copies ran while one was open for 16% -> 15% of each run, Pallas kernels for 28% -> 32%
where the time goes in v6:
time: 484 us; the launch traced here: 477 us
  Pallas kernels  182 us (38%)
  starting transfers between devices  85.3 us (18%)
  waiting for transfers between devices  74.2 us (15%)
  other arithmetic  48 us (10%)
  matrix products  47.7 us (10%)
  local copies, waits for them, and re-layouts  37.2 us (8%)
    ppermute x35, waiting for transfers between devices, xor_shift(): return lax.ppermute(values, axis, [(i, i ^ bit) for i in range(size)])  55.7 us
    dot_general x8, matrix products, grad_half(): jnp.einsum('nd,nf->df', chosen, columns, preferred_element_type=F32)  47.7 us
    ppermute x35, starting transfers between devices, xor_shift(): return lax.ppermute(values, axis, [(i, i ^ bit) for i in range(size)])  38.5 us
    pallas_call x2, Pallas kernels, back_half(): pl.pallas_call(functools.partial(back_kernel, step=256), out_shape=(jax.S...  27.9 us
    pallas_call x2, Pallas kernels, branch_half(): pl.pallas_call(functools.partial(branch_kernel, step=256), out_shape=jax....  20.1 us
    pallas_call x6, Pallas kernels, step_terms(): pl.pallas_call(terms_kernel, out_shape=(jax.ShapeDtypeStruct((rows, 2 * w...  19.1 us
    pallas_call x1, Pallas kernels, joined_forward(): pl.pallas_call(functools.partial(joined_forward_kernel, size=size, block=...  17.7 us
    pallas_call x1, Pallas kernels, hidden_half(): pl.pallas_call(functools.partial(hidden_kernel, step=256), out_shape=(jax...  17.5 us
  transfers between devices with their start and end apart: 59, of which 15 were waited for; matrix products, arithmetic and copies ran while one was open for 15% of the time, Pallas kernels for 32%

profile of v6, /device:TPU:0, one launch (start us, length us, event | category | flops | bytes accessed | tf_op | source)
XLA Modules:
  0.0 476.6 jit_solution(8684475970323866327)
XLA Ops:
  52.6 19.1 %collective-permute-done.12 = bf16[32,832]{1,0:T(8,128)(2,1)S(1)} collective-permute-done((bf16[32,832]{1,0:T(8,128)(2,1)S(1)}, bf16[32,832]{1,0:T(8,128)(2,1)S(1)}, u32[]{:S(2)}, u32[]{:S(2)}) %collective-permute-start.12) | collective-permute-done | bytes 53280 | tf_op jit(solution)/shard_map/ppermute | solution.py:36
  78.3 6.5 %lay.2 = bf16[2048,2048]{1,0:T(8,128)(2,1)} custom-call(bf16[256,2048]{1,0:T(8,128)(2,1)} %refs_0_.1, bf16[256,2048]{1,0:T(8,128)(2,1)} %copy-done.20, bf16[256,2048]{1,0:T(8,128)(2,1)} %collective-permute-done.4.refs_2_, bf16[256,2048]{1,0:T(8,128)(2,1)} %copy-done.12, bf16[256,2048]{1,0:T(8,128)(2,1)} %collective-permute-done.10.refs_4_, ...), custom_call_target="tpu_custom_call" | custom-call | flops 1000 | bytes 1000 | tf_op jit(solution)/shard_map/lay/pallas_call | solution.py:505
  84.8 9.1 %collective-permute-done.15 = bf16[256,2048]{1,0:T(8,128)(2,1)} collective-permute-done((bf16[256,2048]{1,0:T(8,128)(2,1)}, bf16[256,2048]{1,0:T(8,128)(2,1)}, u32[]{:S(2)}, u32[]{:S(2)}) %collective-permute-start.15) | collective-permute-done | bytes 1048608 | tf_op jit(solution)/shard_map/ppermute | solution.py:36
  94.0 6.1 %collective-permute-done.14 = bf16[256,2048]{1,0:T(8,128)(2,1)} collective-permute-done((bf16[256,2048]{1,0:T(8,128)(2,1)}, bf16[256,2048]{1,0:T(8,128)(2,1)}, u32[]{:S(2)}, u32[]{:S(2)}) %collective-permute-start.14) | collective-permute-done | bytes 1048608 | tf_op jit(solution)/shard_map/ppermute | solution.py:958
  107.0 4.6 collective-permute-start.18
  123.5 5.0 %fusion.7 = (bf16[1024,2048]{1,0:T(8,128)(2,1)}, bf16[1024,2048]{1,0:T(8,128)(2,1)}) fusion(bf16[1024,2048]{1,0:T(8,128)(2,1)S(1)} %get-tuple-element.373.tok_ref, f32[2048]{0:T(1024)S(1)} %bitcast.65, f32[2048]{0:T(1024)S(1)} %bitcast.66, f32[1024]{0:T(1024)S(1)} %add_rsqrt_fusion, f32[1024]{0:T(1024)S(1)} %broadcast_multiply_fusion, f32[2048]{0:T(1024)S(1)} %bitcast.67, ...), kind=kLoop, calls=%fused_computation.9 | loop fusion | flops 18874368 | bytes 12623872 | tf_op jit(solution)/shard_map/convert_element_type | solution.py:755
  128.5 17.5 %hidden.1 = (bf16[1024,2048]{1,0:T(8,128)(2,1)}, bf16[1024,2048]{1,0:T(8,128)(2,1)}) custom-call(bf16[1024,2048]{1,0:T(8,128)(2,1)} %get-tuple-element.255.rows_ref, bf16[2048,2048]{1,0:T(8,128)(2,1)} %constant_dynamic-update-slice_fusion.3.a_ref.qa_ref.ka_ref.va_ref.mix_ref.up_ref.join_ref, ...), custom_call_target="tpu_custom_call" | custom-call | flops 1000 | bytes 1000 | tf_op jit(solution)/shard_map/hidden/pallas_call | solution.py:371
  155.4 17.7 %joined_forward.1 = (bf16[1024,512]{1,0:T(8,128)(2,1)}, bf16[1024,512]{1,0:T(8,128)(2,1)}, bf16[1024,512]{1,0:T(8,128)(2,1)}, bf16[1024,512]{1,0:T(8,128)(2,1)}, f32[2,1024,128]{2,1,0:T(8,128)}) custom-call(s32[1]{0:T(128)} %bitcast.11.me_ref, bf16[1024,2048]{1,0:T(8,128)(2,1)} %get-tuple-element.298.rows_ref, ...), custom_call_target="tpu_custom_call" | custom-call | flops 1000 | bytes 1000 | tf_op jit(solution)/shard_map/joined_forward/pallas_call | solution.py:633
  181.0 10.1 %branches.2.refs_0_.refs_2_ = bf16[1024,1024]{1,0:T(8,128)(2,1)} custom-call(bf16[1024,512]{1,0:T(8,128)(2,1)} %get-tuple-element.301.att_ref, bf16[2048,2048]{1,0:T(8,128)(2,1)} %constant_dynamic-update-slice_fusion.3.a_ref.qa_ref.ka_ref.va_ref.mix_ref.up_ref.join_ref, bf16[1024,2048]{1,0:T(8,128)(2,1)} %get-tuple-element.238.act_ref, ...), custom_call_target="tpu_custom_call" | custom-call | flops 1000 | bytes 1000 | tf_op jit(solution)/shard_map/branches/pallas_call | solution.py:428
  192.4 10.1 %branches.3.refs_1_.refs_3_ = bf16[1024,1024]{1,0:T(8,128)(2,1)} custom-call(bf16[1024,512]{1,0:T(8,128)(2,1)} %get-tuple-element.301.att_ref, bf16[2048,2048]{1,0:T(8,128)(2,1)} %collective-permute-done.22.b_ref.qb_ref.kb_ref.vb_ref.mix_ref.up_ref.join_ref, bf16[1024,2048]{1,0:T(8,128)(2,1)} %get-tuple-element.238.act_ref, ...), custom_call_target="tpu_custom_call" | custom-call | flops 1000 | bytes 1000 | tf_op jit(solution)/shard_map/branches/pallas_call | solution.py:428
  202.5 5.0 %collective-permute-done.27 = bf16[256,2048]{1,0:T(8,128)(2,1)} collective-permute-done((bf16[256,2048]{1,0:T(8,128)(2,1)}, bf16[256,2048]{1,0:T(8,128)(2,1)}, u32[]{:S(2)}, u32[]{:S(2)}) %collective-permute-start.27) | collective-permute-done | bytes 1048608 | tf_op jit(solution)/shard_map/ppermute | solution.py:958
  215.0 6.3 %convolution_convert_fusion.5 = bf16[1024,2048]{1,0:T(8,128)(2,1)} fusion(bf16[1024,2048]{1,0:T(8,128)(2,1)S(1)} %copy-done.5, bf16[1024,2048]{1,0:T(8,128)(2,1)S(1)} %pad_maximum_fusion.1.rows_ref.g_ref), kind=kOutput, calls=%fused_computation.21 | convolution fusion | flops 4297064448 | bytes 10485760 | tf_op jit(solution)/shard_map/nd,nf->df/dot_general | solution.py:790
  223.7 14.6 %hidden_back.1 = (bf16[1024,2048]{1,0:T(8,128)(2,1)}, f32[1,2048]{1,0:T(1,128)}) custom-call(bf16[1024,2048]{1,0:T(8,128)(2,1)} %copy-done.3, bf16[1024,2048]{1,0:T(8,128)(2,1)} %constant_dynamic-update-slice_fusion.2.down_ref.a_ref, bf16[1024,2048]{1,0:T(8,128)(2,1)} %collective-permute-done.28.down_ref.b_ref, bf16[1024,2048]{1,0:T(8,128)(2,1)} %get-tuple-element.239.slope_ref), custom_call_target="tpu_custom_call" | custom-call | flops 1000 | bytes 1000 | tf_op jit(solution)/shard_map/hidden_back/pallas_call | solution.py:403
  238.2 9.5 %convolution_convert_fusion.4.kept_x.kept_y.kept = bf16[1024,2048]{1,0:T(8,128)(2,1)} fusion(bf16[1024,2048]{1,0:T(8,128)(2,1)} %get-tuple-element.238.act_ref, bf16[1024,2048]{1,0:T(8,128)(2,1)} %copy-done.3), kind=kOutput, calls=%fused_computation.20 | convolution fusion | flops 4297064448 | bytes 10485760 | tf_op jit(solution)/shard_map/nd,nf->df/dot_general | solution.py:790
  255.4 9.5 %convolution_convert_fusion.3 = bf16[1024,2048]{1,0:T(8,128)(2,1)} fusion(bf16[1024,2048]{1,0:T(8,128)(2,1)} %get-tuple-element.277.hid_ref, bf16[1024,2048]{1,0:T(8,128)(2,1)} %get-tuple-element.255.rows_ref), kind=kOutput, calls=%fused_computation.19 | convolution fusion | flops 4297064448 | bytes 10485760 | tf_op jit(solution)/shard_map/nd,nf->df/dot_general | solution.py:790
  274.0 15.2 %mixed_backward.1.proj_ref = bf16[1024,1536]{1,0:T(8,128)(2,1)} custom-call(s32[1]{0:T(128)} %bitcast.11.me_ref, bf16[1024,512]{1,0:T(8,128)(2,1)} %get-tuple-element.257.q_ref, bf16[1024,512]{1,0:T(8,128)(2,1)} %get-tuple-element.258.k_ref, bf16[1024,512]{1,0:T(8,128)(2,1)} %get-tuple-element.259.v_ref, bf16[1024,2048]{1,0:T(8,128)(2,1)} %copy-done.3, ...), custom_call_target="tpu_custom_call" | custom-call | flops 1000 | bytes 1000 | tf_op jit(solution)/shard_map/mixed_backward/pallas_call | solution.py:656
  289.1 7.4 %convolution_convert_fusion.2.kept = bf16[1024,2048]{1,0:T(8,128)(2,1)S(1)} fusion(bf16[1024,2048]{1,0:T(8,128)(2,1)} %get-tuple-element.277.hid_ref, bf16[1024,2048]{1,0:T(8,128)(2,1)} %get-tuple-element.255.rows_ref), kind=kOutput, calls=%fused_computation.18 | convolution fusion | flops 4297064448 | bytes 10485760 | tf_op jit(solution)/shard_map/nd,nf->df/dot_general | solution.py:790
  307.9 5.8 %convolution_convert_fusion.1 = bf16[1024,1536]{1,0:T(8,128)(2,1)S(1)} fusion(bf16[1024,1536]{1,0:T(8,128)(2,1)S(1)} %copy-done.1, bf16[1024,2048]{1,0:T(8,128)(2,1)} %get-tuple-element.298.rows_ref), kind=kOutput, calls=%fused_computation.17 | convolution fusion | flops 3222798336 | bytes 8388608 | tf_op jit(solution)/shard_map/nd,nf->df/dot_general | solution.py:790
  324.3 14.0 %back.3 = (bf16[1024,1024]{1,0:T(8,128)(2,1)}, f32[8,1024]{1,0:T(8,128)}) custom-call(bf16[1024,2048]{1,0:T(8,128)(2,1)} %get-tuple-element.277.hid_ref, bf16[1024,1536]{1,0:T(8,128)(2,1)} %mixed_backward.1.proj_ref, bf16[2048,2048]{1,0:T(8,128)(2,1)} %collective-permute-done.22.b_ref.qb_ref.kb_ref.vb_ref.mix_ref.up_ref.join_ref, ...), custom_call_target="tpu_custom_call" | custom-call | flops 1000 | bytes 1000 | tf_op jit(solution)/shard_map/back/pallas_call | solution.py:467
  338.3 13.9 %back.2 = (bf16[1024,1024]{1,0:T(8,128)(2,1)}, f32[8,1024]{1,0:T(8,128)}) custom-call(bf16[1024,2048]{1,0:T(8,128)(2,1)} %get-tuple-element.277.hid_ref, bf16[1024,1536]{1,0:T(8,128)(2,1)} %mixed_backward.1.proj_ref, bf16[2048,2048]{1,0:T(8,128)(2,1)} %constant_dynamic-update-slice_fusion.3.a_ref.qa_ref.ka_ref.va_ref.mix_ref.up_ref.join_ref, ...), custom_call_target="tpu_custom_call" | custom-call | flops 1000 | bytes 1000 | tf_op jit(solution)/shard_map/back/pallas_call | solution.py:467
  352.4 5.7 %add_convert_fusion.1 = (bf16[256,2048]{1,0:T(8,128)(2,1)}, bf16[256,2048]{1,0:T(8,128)(2,1)}) fusion(bf16[128,2048]{1,0:T(8,128)(2,1)S(1)} %slice.198, bf16[1024,2048]{1,0:T(8,128)(2,1)} %collective-permute-done.36.came, bf16[1024,2048]{1,0:T(8,128)(2,1)} %copy-done.11, bf16[128,2048]{1,0:T(8,128)(2,1)S(1)} %slice.195), kind=kLoop, calls=%fused_computation.29 | loop fusion | flops 6291456 | bytes 7340032 | tf_op jit(solution)/shard_map/convert_element_type | solution.py:1083
  388.8 4.9 %collective-permute-done.44.a.c = bf16[256,2048]{1,0:T(8,128)(2,1)} collective-permute-done((bf16[256,2048]{1,0:T(8,128)(2,1)}, bf16[256,2048]{1,0:T(8,128)(2,1)}, u32[]{:S(2)}, u32[]{:S(2)}) %collective-permute-start.44) | collective-permute-done | bytes 1048608 | tf_op jit(solution)/shard_map/ppermute | solution.py:36
  415.6 12.0 %collective-permute-done.51 = f32[1,10240]{1,0:T(1,128)S(1)} collective-permute-done((f32[1,10240]{1,0:T(1,128)S(1)}, f32[1,10240]{1,0:T(1,128)S(1)}, u32[]{:S(2)}, u32[]{:S(2)}) %collective-permute-start.51) | collective-permute-done | bytes 40992 | tf_op jit(solution)/shard_map/ppermute | solution.py:36
  470.4 6.1 %input_grad.1 = f32[256,2048]{1,0:T(8,128)} custom-call(s32[16]{0:T(128)} %fusion.27.index_ref, bf16[1024,1024]{1,0:T(8,128)(2,1)} %get-tuple-element.284.refs_0_.refs_2_.one_ref, bf16[1024,1024]{1,0:T(8,128)(2,1)} %get-tuple-element.285.refs_1_.refs_3_.two_ref, bf16[256,2048]{1,0:T(8,128)(2,1)} %collective-permute-done.52.up_ref, ...), custom_call_target="tpu_custom_call" | custom-call | flops 1000 | bytes 1000 | tf_op jit(solution)/shard_map/input_grad/pallas_call | solution.py:608
  (321 shorter events, 239.4 us)
Async XLA Ops:
  41.7 31.6 %collective-permute-start.10 = (bf16[256,2048]{1,0:T(8,128)(2,1)S(1)}, bf16[256,2048]{1,0:T(8,128)(2,1)}, u32[]{:S(2)}, u32[]{:S(2)}) collective-permute-start(bf16[256,2048]{1,0:T(8,128)(2,1)S(1)} %pad_maximum_fusion.4.refs_3_), channel_id=1, source_target_pairs={{0,8},{4,12},{8,0},{12,4},{16,24},{20,28},{24,16},{28,20},{1,9},{5... | collective-permute-start | bytes 3145736 | tf_op jit(solution)/shard_map/ppermute | solution.py:36
  42.2 31.0 %collective-permute-start.11 = (bf16[256,2048]{1,0:T(8,128)(2,1)S(1)}, bf16[256,2048]{1,0:T(8,128)(2,1)S(1)}, u32[]{:S(2)}, u32[]{:S(2)}) collective-permute-start(bf16[256,2048]{1,0:T(8,128)(2,1)S(1)} %pad_maximum_fusion.4.refs_3_), channel_id=1, source_target_pairs={{0,16},{4,20},{8,24},{12,28},{16,0},{20,4},{24,8},{28,12},{1,17},{... | collective-permute-start | bytes 3145736 | tf_op jit(solution)/shard_map/ppermute | solution.py:36
  42.7 30.6 %collective-permute-start.8 = (bf16[256,2048]{1,0:T(8,128)(2,1)}, bf16[256,2048]{1,0:T(8,128)(2,1)}, u32[]{:S(2)}, u32[]{:S(2)}) collective-permute-start(bf16[256,2048]{1,0:T(8,128)(2,1)} %collective-permute-done), channel_id=1, source_target_pairs={{1,2},{2,3},{5,6},{6,7},{9,10},{10,11},{13,14},{14,15},{17,18},{18... | collective-permute-start | bytes 3145736 | tf_op jit(solution)/shard_map/ppermute | solution.py:957
  44.4 28.9 %collective-permute-start.9 = (bf16[256,2048]{1,0:T(8,128)(2,1)}, bf16[256,2048]{1,0:T(8,128)(2,1)}, u32[]{:S(2)}, u32[]{:S(2)}) collective-permute-start(bf16[256,2048]{1,0:T(8,128)(2,1)} %collective-permute-done.1), channel_id=1, source_target_pairs={{1,0},{2,1},{5,4},{6,5},{9,8},{10,9},{13,12},{14,13},{17,16},{18,1... | collective-permute-start | bytes 3145736 | tf_op jit(solution)/shard_map/ppermute | solution.py:958
  107.0 39.0 %collective-permute-start.18 = (bf16[256,2048]{1,0:T(8,128)(2,1)S(1)}, bf16[256,2048]{1,0:T(8,128)(2,1)}, u32[]{:S(2)}, u32[]{:S(2)}) collective-permute-start(bf16[256,2048]{1,0:T(8,128)(2,1)S(1)} %copy-done.8), channel_id=1, source_target_pairs={{0,1},{1,2},{2,3},{4,5},{5,6},{6,7},{8,9},{9,10},{10,11},{12,13},{... | collective-permute-start | bytes 3145736 | tf_op jit(solution)/shard_map/ppermute | solution.py:957
  111.6 34.4 %collective-permute-start.19 = (bf16[256,2048]{1,0:T(8,128)(2,1)S(1)}, bf16[256,2048]{1,0:T(8,128)(2,1)}, u32[]{:S(2)}, u32[]{:S(2)}) collective-permute-start(bf16[256,2048]{1,0:T(8,128)(2,1)S(1)} %copy-done.8), channel_id=1, source_target_pairs={{1,0},{2,1},{3,2},{5,4},{6,5},{7,6},{9,8},{10,9},{11,10},{13,12},{... | collective-permute-start | bytes 3145736 | tf_op jit(solution)/shard_map/ppermute | solution.py:958
  114.0 32.0 %collective-permute-start.20 = (bf16[256,2048]{1,0:T(8,128)(2,1)S(1)}, bf16[256,2048]{1,0:T(8,128)(2,1)}, u32[]{:S(2)}, u32[]{:S(2)}) collective-permute-start(bf16[256,2048]{1,0:T(8,128)(2,1)S(1)} %bitcast.49), channel_id=1, source_target_pairs={{0,8},{4,12},{8,0},{12,4},{16,24},{20,28},{24,16},{28,20},{1,9},{5... | collective-permute-start | bytes 3145736 | tf_op jit(solution)/shard_map/ppermute | solution.py:36
  114.5 31.5 %collective-permute-start.21 = (bf16[256,2048]{1,0:T(8,128)(2,1)S(1)}, bf16[256,2048]{1,0:T(8,128)(2,1)}, u32[]{:S(2)}, u32[]{:S(2)}) collective-permute-start(bf16[256,2048]{1,0:T(8,128)(2,1)S(1)} %bitcast.50), channel_id=1, source_target_pairs={{0,16},{4,20},{8,24},{12,28},{16,0},{20,4},{24,8},{28,12},{1,17},{... | collective-permute-start | bytes 3145736 | tf_op jit(solution)/shard_map/ppermute | solution.py:36
  146.1 27.1 %collective-permute-start.23 = (bf16[256,2048]{1,0:T(8,128)(2,1)}, bf16[256,2048]{1,0:T(8,128)(2,1)S(1)}, u32[]{:S(2)}, u32[]{:S(2)}) collective-permute-start(bf16[256,2048]{1,0:T(8,128)(2,1)} %collective-permute-done.18), channel_id=1, source_target_pairs={{1,2},{2,3},{5,6},{6,7},{9,10},{10,11},{13,14},{14,15},{17,18},{18... | collective-permute-start | bytes 3145736 | tf_op jit(solution)/shard_map/ppermute | solution.py:957
  146.8 28.2 %collective-permute-start.24 = (bf16[256,2048]{1,0:T(8,128)(2,1)}, bf16[256,2048]{1,0:T(8,128)(2,1)}, u32[]{:S(2)}, u32[]{:S(2)}) collective-permute-start(bf16[256,2048]{1,0:T(8,128)(2,1)} %collective-permute-done.19), channel_id=1, source_target_pairs={{1,0},{2,1},{5,4},{6,5},{9,8},{10,9},{13,12},{14,13},{17,16},{18,1... | collective-permute-start | bytes 3145736 | tf_op jit(solution)/shard_map/ppermute | solution.py:958
  179.7 27.8 %collective-permute-start.27 = (bf16[256,2048]{1,0:T(8,128)(2,1)}, bf16[256,2048]{1,0:T(8,128)(2,1)}, u32[]{:S(2)}, u32[]{:S(2)}) collective-permute-start(bf16[256,2048]{1,0:T(8,128)(2,1)} %collective-permute-done.24), channel_id=1, source_target_pairs={{1,0},{5,4},{9,8},{13,12},{17,16},{21,20},{25,24},{29,28}} | collective-permute-start | bytes 3145736 | tf_op jit(solution)/shard_map/ppermute | solution.py:958
  264.9 31.7 %collective-permute-start.36 = (bf16[1024,2048]{1,0:T(8,128)(2,1)}, bf16[1024,2048]{1,0:T(8,128)(2,1)}, u32[]{:S(2)}, u32[]{:S(2)}) collective-permute-start(bf16[1024,2048]{1,0:T(8,128)(2,1)} %convolution_convert_fusion.3), channel_id=1, source_target_pairs={{0,4},{4,0},{8,12},{12,8},{16,20},{20,16},{24,28},{28,24},{1,5},{5... | collective-permute-start | bytes 12582920 | tf_op jit(solution)/shard_map/ppermute | solution.py:36
  265.3 31.3 %collective-permute-start.32 = (bf16[256,2048]{1,0:T(8,128)(2,1)}, bf16[256,2048]{1,0:T(8,128)(2,1)S(1)}, u32[]{:S(2)}, u32[]{:S(2)}) collective-permute-start(bf16[256,2048]{1,0:T(8,128)(2,1)} %get-tuple-element.251), channel_id=1, source_target_pairs={{0,1},{1,2},{4,5},{5,6},{8,9},{9,10},{12,13},{13,14},{16,17},{17,1... | collective-permute-start | bytes 3145736 | tf_op jit(solution)/shard_map/ppermute | solution.py:966
  267.8 28.8 %collective-permute-start.33 = (bf16[256,2048]{1,0:T(8,128)(2,1)}, bf16[256,2048]{1,0:T(8,128)(2,1)}, u32[]{:S(2)}, u32[]{:S(2)}) collective-permute-start(bf16[256,2048]{1,0:T(8,128)(2,1)} %get-tuple-element.252), channel_id=1, source_target_pairs={{2,1},{3,2},{6,5},{7,6},{10,9},{11,10},{14,13},{15,14},{18,17},{19... | collective-permute-start | bytes 3145736 | tf_op jit(solution)/shard_map/ppermute | solution.py:967
  269.6 26.9 %collective-permute-start.34 = (bf16[256,2048]{1,0:T(8,128)(2,1)}, bf16[256,2048]{1,0:T(8,128)(2,1)S(1)}, u32[]{:S(2)}, u32[]{:S(2)}) collective-permute-start(bf16[256,2048]{1,0:T(8,128)(2,1)} %get-tuple-element.253), channel_id=1, source_target_pairs={{0,8},{4,12},{8,0},{12,4},{16,24},{20,28},{24,16},{28,20},{1,9},{5... | collective-permute-start | bytes 3145736 | tf_op jit(solution)/shard_map/ppermute | solution.py:36
  316.3 36.0 %collective-permute-start.41 = (bf16[1024,2048]{1,0:T(8,128)(2,1)}, bf16[1024,2048]{1,0:T(8,128)(2,1)}, u32[]{:S(2)}, u32[]{:S(2)}) collective-permute-start(bf16[1024,2048]{1,0:T(8,128)(2,1)} %pad_maximum_fusion.2), channel_id=1, source_target_pairs={{0,4},{4,0},{8,12},{12,8},{16,20},{20,16},{24,28},{28,24},{1,5},{5... | collective-permute-start | bytes 12582920 | tf_op jit(solution)/shard_map/ppermute | solution.py:36
  316.3 35.9 %collective-permute-start.37 = (bf16[256,2048]{1,0:T(8,128)(2,1)}, bf16[256,2048]{1,0:T(8,128)(2,1)S(1)}, u32[]{:S(2)}, u32[]{:S(2)}) collective-permute-start(bf16[256,2048]{1,0:T(8,128)(2,1)} %get-tuple-element.272), channel_id=1, source_target_pairs={{0,1},{1,2},{2,3},{4,5},{5,6},{6,7},{8,9},{9,10},{10,11},{12,13},{... | collective-permute-start | bytes 3145736 | tf_op jit(solution)/shard_map/ppermute | solution.py:966
  318.8 33.4 %collective-permute-start.38 = (bf16[256,2048]{1,0:T(8,128)(2,1)}, bf16[256,2048]{1,0:T(8,128)(2,1)}, u32[]{:S(2)}, u32[]{:S(2)}) collective-permute-start(bf16[256,2048]{1,0:T(8,128)(2,1)} %get-tuple-element.273), channel_id=1, source_target_pairs={{1,0},{2,1},{3,2},{5,4},{6,5},{7,6},{9,8},{10,9},{11,10},{13,12},{... | collective-permute-start | bytes 3145736 | tf_op jit(solution)/shard_map/ppermute | solution.py:967
  320.1 32.1 %collective-permute-start.39 = (bf16[256,2048]{1,0:T(8,128)(2,1)}, bf16[256,2048]{1,0:T(8,128)(2,1)S(1)}, u32[]{:S(2)}, u32[]{:S(2)}) collective-permute-start(bf16[256,2048]{1,0:T(8,128)(2,1)} %pad_maximum_fusion.5), channel_id=1, source_target_pairs={{0,8},{4,12},{8,0},{12,4},{16,24},{20,28},{24,16},{28,20},{1,9},{5... | collective-permute-start | bytes 3145736 | tf_op jit(solution)/shard_map/ppermute | solution.py:36
  320.7 31.5 %collective-permute-start.40 = (bf16[256,2048]{1,0:T(8,128)(2,1)}, bf16[256,2048]{1,0:T(8,128)(2,1)S(1)}, u32[]{:S(2)}, u32[]{:S(2)}) collective-permute-start(bf16[256,2048]{1,0:T(8,128)(2,1)} %pad_maximum_fusion.6), channel_id=1, source_target_pairs={{0,16},{4,20},{8,24},{12,28},{16,0},{20,4},{24,8},{28,12},{1,17},{... | collective-permute-start | bytes 3145736 | tf_op jit(solution)/shard_map/ppermute | solution.py:36
  398.3 29.3 %collective-permute-start.47 = (bf16[256,2048]{1,0:T(8,128)(2,1)}, bf16[256,2048]{1,0:T(8,128)(2,1)}, u32[]{:S(2)}, u32[]{:S(2)}) collective-permute-start(bf16[256,2048]{1,0:T(8,128)(2,1)} %get-tuple-element.318), channel_id=1, source_target_pairs={{0,1},{1,2},{4,5},{5,6},{8,9},{9,10},{12,13},{13,14},{16,17},{17,1... | collective-permute-start | bytes 3145736 | tf_op jit(solution)/shard_map/ppermute | solution.py:966
  400.6 27.0 %collective-permute-start.48 = (bf16[256,2048]{1,0:T(8,128)(2,1)}, bf16[256,2048]{1,0:T(8,128)(2,1)}, u32[]{:S(2)}, u32[]{:S(2)}) collective-permute-start(bf16[256,2048]{1,0:T(8,128)(2,1)} %get-tuple-element.319), channel_id=1, source_target_pairs={{2,1},{3,2},{6,5},{7,6},{10,9},{11,10},{14,13},{15,14},{18,17},{19... | collective-permute-start | bytes 3145736 | tf_op jit(solution)/shard_map/ppermute | solution.py:967
  437.7 30.1 %collective-permute-start.52 = (bf16[256,2048]{1,0:T(8,128)(2,1)}, bf16[256,2048]{1,0:T(8,128)(2,1)}, u32[]{:S(2)}, u32[]{:S(2)}) collective-permute-start(bf16[256,2048]{1,0:T(8,128)(2,1)} %get-tuple-element.340), channel_id=1, source_target_pairs={{0,1},{1,2},{2,3},{4,5},{5,6},{6,7},{8,9},{9,10},{10,11},{12,13},{... | collective-permute-start | bytes 3145736 | tf_op jit(solution)/shard_map/ppermute | solution.py:966
  440.7 27.1 %collective-permute-start.53 = (bf16[256,2048]{1,0:T(8,128)(2,1)}, bf16[256,2048]{1,0:T(8,128)(2,1)}, u32[]{:S(2)}, u32[]{:S(2)}) collective-permute-start(bf16[256,2048]{1,0:T(8,128)(2,1)} %get-tuple-element.341), channel_id=1, source_target_pairs={{1,0},{2,1},{3,2},{5,4},{6,5},{7,6},{9,8},{10,9},{11,10},{13,12},{... | collective-permute-start | bytes 3145736 | tf_op jit(solution)/shard_map/ppermute | solution.py:967
  (77 other events, 1160.7 us)

commit v7 on v6

--- a/solution.py
+++ b/solution.py
@@ -442,46 +442,60 @@
 
 
 def back_kernel(
-    hid_ref, proj_ref, up_ref, join_ref, tok_ref, mean_ref, scale_ref, gain_ref, back_ref, sum_ref, *, step
+    hid_ref, proj_ref, up_1, up_2, join_1, join_2, tok_ref, mean_ref, scale_ref, gain_ref, back_ref, sum_ref,
+    *, step, tiles,
 ):
-    sums = [0.0] * 4
-    for i in range(hid_ref.shape[0] // step):
-        here = slice(i * step, (i + 1) * step)
-        two = contract(hid_ref[here, :], up_ref[:, :], ((1,), (1,)))
-        one = contract(proj_ref[here, :], join_ref[:, :], ((1,), (1,)))
-        back_ref[here, :] = (one * gain_ref[:1, :] + two * gain_ref[1:2, :]).astype(BF16)
-        xhat = (tok_ref[here, :].astype(F32) - mean_ref[here, :1]) * scale_ref[here, :1]
-        for k, term in enumerate((one * xhat, two * xhat, one, two)):
-            sums[k] = sums[k] + jnp.sum(term, axis=0, keepdims=True)
-    for k in range(4):
-        sum_ref[k : k + 1, :] = sums[k]
-
-
-def back_half(grad_hidden, grad_projected, both, token_rows, mean, scale, gains, part):
+    def work(up_ref, join_ref):
+        sums = [0.0] * 4
+        for i in range(hid_ref.shape[0] // step):
+            here = slice(i * step, (i + 1) * step)
+            two = contract(hid_ref[here, :], up_ref[:, :], ((1,), (1,)))
+            one = contract(proj_ref[here, :], join_ref[:, :], ((1,), (1,)))
+            back_ref[here, :] = (one * gain_ref[:1, :] + two * gain_ref[1:2, :]).astype(BF16)
+            xhat = (tok_ref[here, :].astype(F32) - mean_ref[here, :1]) * scale_ref[here, :1]
+            for k, term in enumerate((one * xhat, two * xhat, one, two)):
+                sums[k] = sums[k] + jnp.sum(term, axis=0, keepdims=True)
+        for k in range(4):
+            sum_ref[k : k + 1, :] = sums[k]
+
+    @pl.when(pl.program_id(0) < tiles)
+    def _():
+        work(up_1, join_1)
+
+    @pl.when(pl.program_id(0) >= tiles)
+    def _():
+        work(up_2, join_2)
+
+
+def back_whole(grad_hidden, grad_projected, both_1, both_2, token_rows, mean, scale, gains):
     count, units = grad_hidden.shape
     joined = grad_projected.shape[1]
-    width = both.shape[0] // 2
+    width = both_1.shape[0] // 2
     tile = 256
     tiles = width // tile
     whole = lambda j: (0, 0)
-    return pl.pallas_call(
-        functools.partial(back_kernel, step=256),
-        out_shape=(jax.ShapeDtypeStruct((count, width), BF16), jax.ShapeDtypeStruct((8, width), F32)),
-        grid=(tiles,),
-        in_specs=[
-            pl.BlockSpec((count, units), whole),
-            pl.BlockSpec((count, joined), whole),
-            pl.BlockSpec((tile, units), lambda j: (j, 0)),
-            pl.BlockSpec((tile, joined), lambda j: (j + tiles, 0)),
-            pl.BlockSpec((count, tile), lambda j: (0, j + part * tiles)),
+
+    def of(columns, block):
+        low = pl.BlockSpec((tile, columns), lambda j: (block + jnp.minimum(j, tiles - 1), 0))
+        high = pl.BlockSpec((tile, columns), lambda j: (block + jnp.maximum(j - tiles, 0), 0))
+        return [low, high]
+
+    return pl.pallas_call(
+        functools.partial(back_kernel, step=256, tiles=tiles),
+        out_shape=(jax.ShapeDtypeStruct((count, 2 * width), BF16), jax.ShapeDtypeStruct((8, 2 * width), F32)),
+        grid=(2 * tiles,),
+        in_specs=[pl.BlockSpec((count, units), whole), pl.BlockSpec((count, joined), whole)]
+        + of(units, 0) + of(joined, tiles)
+        + [
+            pl.BlockSpec((count, tile), lambda j: (0, j)),
             pl.BlockSpec((count, 128), whole),
             pl.BlockSpec((count, 128), whole),
-            pl.BlockSpec((2, tile), lambda j: (0, j + part * tiles)),
+            pl.BlockSpec((2, tile), lambda j: (0, j)),
         ],
         out_specs=(pl.BlockSpec((count, tile), lambda j: (0, j)), pl.BlockSpec((8, tile), lambda j: (0, j))),
         cost_estimate=SMALL,
         name="back",
-    )(grad_hidden, grad_projected, both, both, token_rows, mean, scale, gains)
+    )(grad_hidden, grad_projected, both_1, both_2, both_1, both_2, token_rows, mean, scale, gains)
 
 
 def lay_kernel(*refs):
@@ -568,15 +582,15 @@
     to_down[:, :] = down
 
 
-def step_terms(halves, up_block, down_block, rows, *came):
-    width = halves[0].shape[1]
+def step_terms(halves, up_block, down_block, rows, width, *came):
     tiles = 2
     tile = rows // tiles
 
     def of(block):
-        return [pl.BlockSpec((tile, width), lambda i: (block * tiles + i, 0))] * 2
+        return [pl.BlockSpec((tile, width), lambda i, k=k: (block * tiles + i, k)) for _, k in halves]
 
     full = pl.BlockSpec((tile, 2 * width), lambda i: (i, 0))
+    arrays = [v for v, _ in halves]
     return pl.pallas_call(
         terms_kernel,
         out_shape=(jax.ShapeDtypeStruct((rows, 2 * width), BF16),) * 2,
@@ -585,12 +599,11 @@
         out_specs=(full, full),
         cost_estimate=SMALL,
         name="terms",
-    )(*halves, *halves, *came)
-
-
-def input_grad_kernel(index_ref, one_ref, two_ref, up_ref, down_ref, tok_ref, grad_ref, out_ref):
-    back = jnp.concatenate([one_ref[:, :], two_ref[:, :]], axis=1).astype(F32)
-    back = back + up_ref[:, :].astype(F32) + down_ref[:, :].astype(F32)
+    )(*arrays, *arrays, *came)
+
+
+def input_grad_kernel(index_ref, own_ref, up_ref, down_ref, tok_ref, grad_ref, out_ref):
+    back = own_ref[:, :].astype(F32) + up_ref[:, :].astype(F32) + down_ref[:, :].astype(F32)
     xhat, scale = standardize(tok_ref[:, :])
     back = back - jnp.mean(back, axis=-1, keepdims=True) - xhat * jnp.mean(back * xhat, axis=-1, keepdims=True)
     total = grad_ref[:, :].astype(F32) + back * scale
@@ -600,10 +613,9 @@
         out_ref[:, pl.ds(pl.multiple_of(index_ref[j] * step, step), step)] = total[:, j * step : (j + 1) * step]
 
 
-def input_grad_rows(one, two, up, down, tokens, grads):
+def input_grad_rows(own, up, down, tokens, grads):
     rows, width = tokens.shape
     tile = rows // 4
-    half = pl.BlockSpec((tile, width // 2), lambda i, s: (i, 0))
     full = pl.BlockSpec((tile, width), lambda i, s: (i, 0))
     return pl.pallas_call(
         input_grad_kernel,
@@ -611,12 +623,12 @@
         grid_spec=pltpu.PrefetchScalarGridSpec(
             num_scalar_prefetch=1,
             grid=(rows // tile,),
-            in_specs=[half, half, full, full, full, full],
+            in_specs=[full] * 5,
             out_specs=full,
         ),
         cost_estimate=SMALL,
         name="input_grad",
-    )(frame_index(), one, two, up, down, tokens, grads)
+    )(frame_index(), own, up, down, tokens, grads)
 
 
 def joined_forward(rows, top, low, bias, tables, me, heads, head, size):
@@ -960,7 +972,7 @@
 
         def scatter_terms(halves, up, down, s):
             came = () if s == 1 else (up, down)
-            return step_terms(halves, 4 - s, s, local_rows, *came)
+            return step_terms(halves, 4 - s, s, local_rows, width // 2, *came)
 
         def scatter_step(to_up, to_down, s):
             up = lax.ppermute(to_up, "tensor", [(i, i + 1) for i in range(s)])
@@ -1034,7 +1046,7 @@
         branch_1 = branch_half(attended, both_1, activated, down_1)
         branch_2 = branch_half(attended, both_2, activated, down_2)
         cu3, cd3, branch_1, branch_2, activated = cut(cu3, cd3, branch_1, branch_2, activated)
-        branches = (branch_1, branch_2)
+        branches = ((branch_1, 0), (branch_2, 0))
         zu, zd, activated, cu3, cd3 = cut(*scatter_terms(branches, None, None, 1), activated, cu3, cd3)
         bu, bd = scatter_step(zu, zd, 1)
         grad_rows = in_turn(local_grads1, (cu1, cu2, cu3), (cd1, cd2, cd3))
@@ -1070,25 +1082,26 @@
         bu, bd = scatter_step(zu, zd, 3)
         s9x, s9y = x(sx), y(sy)
         came_j = core(joined_half(first_rows, grad_projected, grad_rows, attended, 1))
-        back_1, sums_1 = back_half(grad_hidden, grad_projected, both_1, token_rows, mean, scale, gain_rows, 0)
-        back_2, sums_2 = back_half(grad_hidden, grad_projected, both_2, token_rows, mean, scale, gain_rows, 1)
-        bu, bd, s9x, s9y, came_j, back_1, back_2, sums_1, sums_2, grad_projected, attended = cut(
-            bu, bd, s9x, s9y, came_j, back_1, back_2, sums_1, sums_2, grad_projected, attended
-        )
-        backs = (back_1, back_2)
+        back, sums = back_whole(
+            grad_hidden, grad_projected, both_1, both_2, token_rows, mean, scale, gain_rows
+        )
+        bu, bd, s9x, s9y, came_j, back, sums, grad_projected, attended = cut(
+            bu, bd, s9x, s9y, came_j, back, sums, grad_projected, attended
+        )
+        backs = ((back, 0), (back, 1))
         none = jnp.zeros((half, s9x.shape[1]), BF16)
-        zu, zd, sx, sy, first_rows, grad_rows, bu, bd, sums_1, sums_2 = cut(
+        zu, zd, sx, sy, first_rows, grad_rows, bu, bd, sums = cut(
             *scatter_terms(backs, None, None, 1),
             plus(at(keep_u, came_u, 2, 4), pair(s9y[second], none)).astype(BF16),
             plus(at(keep_u, came_u, 6, 8), pair(none, s9x[second])).astype(BF16),
-            first_rows, grad_rows, bu, bd, sums_1, sums_2,
+            first_rows, grad_rows, bu, bd, sums,
         )
         eu, ed = scatter_step(zu, zd, 1)
         s10x, s10y = x(sx), y(sy)
         keep_j = joined_half(first_rows, grad_projected, grad_rows, attended, 0)
         five = jnp.concatenate(
             [
-                jnp.concatenate([sums_1[:4], sums_2[:4]], axis=1),
+                sums[:4],
                 jnp.sum(local_grads.astype(F32), axis=0, keepdims=True),
             ],
             axis=0,
@@ -1126,9 +1139,13 @@
         )
         eu, ed = scatter_step(zu, zd, 3)
         j2x, j2y = x(sx), y(sy)
-        own = jnp.concatenate([h[:local_rows] for h in branches], axis=1)
+        own = jnp.concatenate([branch_1[:local_rows], branch_2[:local_rows]], axis=1)
         output = finish_output(plus(own, bu, bd), shift_rows)
-        terms = butterfly(jnp.concatenate([five, terms], axis=1), "dp")
+        terms = jnp.concatenate([five, terms], axis=1)
+        terms = terms + core(terms)
+        terms = terms + x(terms)
+        terms, j2x, j2y = cut(terms, j2x, j2y)
+        terms = terms + y(terms)
         small = small_shares(
             terms[:, : 5 * width], terms[0, 5 * width : 5 * width + joined_width],
             terms[:, 5 * width + joined_width :],
@@ -1136,7 +1153,7 @@
         joined_mix = own_sums(keep_j, came_j, half, (j1x, 0), (j2y, 0), (j1y, 1), (j2x, 0))
         joined_sum = joined_mix[:, :joined_width].reshape(proj_weight.shape)
         eu, ed, joined_sum, mix_sum = cut(eu, ed, joined_sum, joined_mix[:, joined_width:].T)
-        input_grad = input_grad_rows(*backs, eu, ed, local_tokens, local_grads)
+        input_grad = input_grad_rows(back, eu, ed, local_tokens, local_grads)
         return output, input_grad, joined_sum, mix_sum, up_sum, down_sum, small
 
     parts = staged() if fast_dp() and n_tensor == 4 else plain()

time: 484 us -> 483 us (level)
  starting transfers between devices: 85.3 us -> 98.9 us
  waiting for transfers between devices: 74.2 us -> 65.9 us
  Pallas kernels: 182 us -> 177 us
    ppermute x35, starting transfers between devices: 38.5 us -> 48.4 us  [xor_shift(): return lax.ppermute(values, axis, [(i, i ^ bit) for i in range(size)])]
    ppermute x35, waiting for transfers between devices: 55.7 us -> 46.3 us  [xor_shift(): return lax.ppermute(values, axis, [(i, i ^ bit) for i in range(size)])]
    ppermute x6, waiting for transfers between devices: 17.2 us -> 11.4 us  [gather_step(): down = lax.ppermute(down, 'tensor', [(i + 1, i) for i in range(3 - s)])]
    ppermute x6, waiting for transfers between devices: 0.02 us -> 5.12 us  [scatter_step(): lax.ppermute(to_down, 'tensor', [(i, i - 1) for i in range(4 - s, 4)])]
    pallas_call x2 -> x1, Pallas kernels: 27.9 us -> 23.5 us  [back_whole(): pl.pallas_call(functools.partial(back_kernel, step=256, tiles=tiles), out...]
    unnamed x89 -> x87, local copies, waits for them, and re-layouts: 13.9 us -> 17.8 us
  transfers between devices with their start and end apart: 59 -> 59, of which waited for: 15 -> 13; matrix products, arithmetic and copies ran while one was open for 15% -> 15% of each run, Pallas kernels for 32% -> 31%
where the time goes in v7:
time: 483 us; the launch traced here: 476 us
  Pallas kernels  177 us (37%)
  starting transfers between devices  98.9 us (20%)
  waiting for transfers between devices  65.9 us (14%)
  other arithmetic  46 us (10%)
  matrix products  45.5 us (9%)
  local copies, waits for them, and re-layouts  40.7 us (8%)
    ppermute x35, starting transfers between devices, xor_shift(): return lax.ppermute(values, axis, [(i, i ^ bit) for i in range(size)])  48.4 us
    ppermute x35, waiting for transfers between devices, xor_shift(): return lax.ppermute(values, axis, [(i, i ^ bit) for i in range(size)])  46.3 us
    dot_general x8, matrix products, grad_half(): jnp.einsum('nd,nf->df', chosen, columns, preferred_element_type=F32)  45.5 us
    pallas_call x1, Pallas kernels, back_whole(): pl.pallas_call(functools.partial(back_kernel, step=256, tiles=tiles), out...  23.5 us
    pallas_call x2, Pallas kernels, branch_half(): pl.pallas_call(functools.partial(branch_kernel, step=256), out_shape=jax....  20.1 us
    pallas_call x6, Pallas kernels, step_terms(): pl.pallas_call(terms_kernel, out_shape=(jax.ShapeDtypeStruct((rows, 2 * w...  18.7 us
    ppermute x6, starting transfers between devices, gather_step(): up = lax.ppermute(up, 'tensor', [(i, i + 1) for i in range(s, 3)])  18.1 us
    unnamed x87, local copies, waits for them, and re-layouts  17.8 us
  transfers between devices with their start and end apart: 59, of which 13 were waited for; matrix products, arithmetic and copies ran while one was open for 15% of the time, Pallas kernels for 31%

profile of v7, /device:TPU:0, one launch (start us, length us, event | category | flops | bytes accessed | tf_op | source)
XLA Modules:
  0.0 475.9 jit_solution(4147311017811509994)
XLA Ops:
  6.0 6.6 %collective-permute-start = (bf16[256,2048]{1,0:T(8,128)(2,1)}, bf16[256,2048]{1,0:T(8,128)(2,1)}, u32[]{:S(2)}, u32[]{:S(2)}) collective-permute-start(bf16[256,2048]{1,0:T(8,128)(2,1)} %columns.5.tok_ref), channel_id=1, source_target_pairs={{0,1},{1,2},{2,3},{4,5},{5,6},{6,7},{8,9},{9,10},{10,11},{12,13},{... | collective-permute-start | bytes 3145736 | tf_op jit(solution)/shard_map/ppermute | solution.py:969
  27.2 10.2 %collective-permute-done.3.refs_1_ = bf16[256,2048]{1,0:T(8,128)(2,1)S(1)} collective-permute-done((bf16[256,2048]{1,0:T(8,128)(2,1)}, bf16[256,2048]{1,0:T(8,128)(2,1)S(1)}, u32[]{:S(2)}, u32[]{:S(2)}) %collective-permute-start.3) | collective-permute-done | bytes 1048608 | tf_op jit(solution)/shard_map/ppermute | solution.py:36
  52.8 5.1 %collective-permute-start.12 = (bf16[32,832]{1,0:T(8,128)(2,1)S(1)}, bf16[32,832]{1,0:T(8,128)(2,1)S(1)}, u32[]{:S(2)}, u32[]{:S(2)}) collective-permute-start(bf16[32,832]{1,0:T(8,128)(2,1)S(1)} %add_add_fusion), channel_id=1, source_target_pairs={{0,1},{1,0},{2,3},{3,2},{4,5},{5,4},{6,7},{7,6},{8,9},{9,8},{10,11... | collective-permute-start | bytes 159752 | tf_op jit(solution)/shard_map/ppermute | solution.py:36
  60.8 15.8 %collective-permute-done.12 = bf16[32,832]{1,0:T(8,128)(2,1)S(1)} collective-permute-done((bf16[32,832]{1,0:T(8,128)(2,1)S(1)}, bf16[32,832]{1,0:T(8,128)(2,1)S(1)}, u32[]{:S(2)}, u32[]{:S(2)}) %collective-permute-start.12) | collective-permute-done | bytes 53280 | tf_op jit(solution)/shard_map/ppermute | solution.py:36
  82.0 7.4 %collective-permute-start.17 = (bf16[32,832]{1,0:T(8,128)(2,1)S(1)}, bf16[32,832]{1,0:T(8,128)(2,1)S(1)}, u32[]{:S(2)}, u32[]{:S(2)}) collective-permute-start(bf16[32,832]{1,0:T(8,128)(2,1)S(1)} %add.196), channel_id=1, source_target_pairs={{0,2},{1,3},{2,0},{3,1},{4,6},{5,7},{6,4},{7,5},{8,10},{9,11},{10,... | collective-permute-start | bytes 159752 | tf_op jit(solution)/shard_map/ppermute | solution.py:36
  89.5 6.5 %lay.2 = bf16[2048,2048]{1,0:T(8,128)(2,1)} custom-call(bf16[256,2048]{1,0:T(8,128)(2,1)} %refs_0_.1, bf16[256,2048]{1,0:T(8,128)(2,1)} %copy-done.22, bf16[256,2048]{1,0:T(8,128)(2,1)} %collective-permute-done.4.refs_2_, bf16[256,2048]{1,0:T(8,128)(2,1)} %copy-done.13, bf16[256,2048]{1,0:T(8,128)(2,1)} %collective-permute-done.10.refs_4_, ...), custom_call_target="tpu_custom_call" | custom-call | flops 1000 | bytes 1000 | tf_op jit(solution)/shard_map/lay/pallas_call | solution.py:519
  98.3 4.8 %collective-permute-done.14 = bf16[256,2048]{1,0:T(8,128)(2,1)} collective-permute-done((bf16[256,2048]{1,0:T(8,128)(2,1)}, bf16[256,2048]{1,0:T(8,128)(2,1)}, u32[]{:S(2)}, u32[]{:S(2)}) %collective-permute-start.14) | collective-permute-done | bytes 1048608 | tf_op jit(solution)/shard_map/ppermute | solution.py:970
  111.6 5.8 %collective-permute-start.18 = (bf16[256,2048]{1,0:T(8,128)(2,1)S(1)}, bf16[256,2048]{1,0:T(8,128)(2,1)}, u32[]{:S(2)}, u32[]{:S(2)}) collective-permute-start(bf16[256,2048]{1,0:T(8,128)(2,1)S(1)} %copy-done.9), channel_id=1, source_target_pairs={{0,1},{1,2},{2,3},{4,5},{5,6},{6,7},{8,9},{9,10},{10,11},{12,13},{... | collective-permute-start | bytes 3145736 | tf_op jit(solution)/shard_map/ppermute | solution.py:969
  129.0 4.9 %fusion.7 = (bf16[1024,2048]{1,0:T(8,128)(2,1)}, bf16[1024,2048]{1,0:T(8,128)(2,1)}) fusion(bf16[1024,2048]{1,0:T(8,128)(2,1)S(1)} %get-tuple-element.369.tok_ref, f32[2048]{0:T(1024)S(1)} %bitcast.65, f32[2048]{0:T(1024)S(1)} %bitcast.66, f32[1024]{0:T(1024)S(1)} %add_rsqrt_fusion, f32[1024]{0:T(1024)S(1)} %broadcast_multiply_fusion, f32[2048]{0:T(1024)S(1)} %bitcast.67, ...), kind=kLoop, calls=%fused_computation.9 | loop fusion | flops 18874368 | bytes 12623872 | tf_op jit(solution)/shard_map/convert_element_type | solution.py:767
  133.9 17.5 %hidden.1 = (bf16[1024,2048]{1,0:T(8,128)(2,1)}, bf16[1024,2048]{1,0:T(8,128)(2,1)}) custom-call(bf16[1024,2048]{1,0:T(8,128)(2,1)} %get-tuple-element.253.rows_ref, bf16[2048,2048]{1,0:T(8,128)(2,1)} %constant_dynamic-update-slice_fusion.3.a_ref.qa_ref.ka_ref.va_ref.mix_ref.up_1.join_1, ...), custom_call_target="tpu_custom_call" | custom-call | flops 1000 | bytes 1000 | tf_op jit(solution)/shard_map/hidden/pallas_call | solution.py:371
  159.7 17.7 %joined_forward.1 = (bf16[1024,512]{1,0:T(8,128)(2,1)}, bf16[1024,512]{1,0:T(8,128)(2,1)}, bf16[1024,512]{1,0:T(8,128)(2,1)}, bf16[1024,512]{1,0:T(8,128)(2,1)}, f32[2,1024,128]{2,1,0:T(8,128)}) custom-call(s32[1]{0:T(128)} %bitcast.11.me_ref, bf16[1024,2048]{1,0:T(8,128)(2,1)} %get-tuple-element.292.rows_ref, ...), custom_call_target="tpu_custom_call" | custom-call | flops 1000 | bytes 1000 | tf_op jit(solution)/shard_map/joined_forward/pallas_call | solution.py:645
  185.0 10.1 %branches.2.refs_0_.refs_2_ = bf16[1024,1024]{1,0:T(8,128)(2,1)} custom-call(bf16[1024,512]{1,0:T(8,128)(2,1)} %get-tuple-element.295.att_ref, bf16[2048,2048]{1,0:T(8,128)(2,1)} %constant_dynamic-update-slice_fusion.3.a_ref.qa_ref.ka_ref.va_ref.mix_ref.up_1.join_1, bf16[1024,2048]{1,0:T(8,128)(2,1)} %get-tuple-element.236.act_ref, ...), custom_call_target="tpu_custom_call" | custom-call | flops 1000 | bytes 1000 | tf_op jit(solution)/shard_map/branches/pallas_call | solution.py:428
  196.4 10.1 %branches.3.refs_1_.refs_3_ = bf16[1024,1024]{1,0:T(8,128)(2,1)} custom-call(bf16[1024,512]{1,0:T(8,128)(2,1)} %get-tuple-element.295.att_ref, bf16[2048,2048]{1,0:T(8,128)(2,1)} %collective-permute-done.22.b_ref.qb_ref.kb_ref.vb_ref.mix_ref.up_2.join_2, bf16[1024,2048]{1,0:T(8,128)(2,1)} %get-tuple-element.236.act_ref, ...), custom_call_target="tpu_custom_call" | custom-call | flops 1000 | bytes 1000 | tf_op jit(solution)/shard_map/branches/pallas_call | solution.py:428
  206.4 5.0 %collective-permute-done.27 = bf16[256,2048]{1,0:T(8,128)(2,1)} collective-permute-done((bf16[256,2048]{1,0:T(8,128)(2,1)}, bf16[256,2048]{1,0:T(8,128)(2,1)}, u32[]{:S(2)}, u32[]{:S(2)}) %collective-permute-start.27) | collective-permute-done | bytes 1048608 | tf_op jit(solution)/shard_map/ppermute | solution.py:970
  218.9 6.3 %convolution_convert_fusion.5 = bf16[1024,2048]{1,0:T(8,128)(2,1)} fusion(bf16[1024,2048]{1,0:T(8,128)(2,1)S(1)} %copy-done.6, bf16[1024,2048]{1,0:T(8,128)(2,1)S(1)} %pad_maximum_fusion.1.rows_ref.g_ref), kind=kOutput, calls=%fused_computation.21 | convolution fusion | flops 4297064448 | bytes 10485760 | tf_op jit(solution)/shard_map/nd,nf->df/dot_general | solution.py:802
  227.7 14.6 %hidden_back.1 = (bf16[1024,2048]{1,0:T(8,128)(2,1)}, f32[1,2048]{1,0:T(1,128)}) custom-call(bf16[1024,2048]{1,0:T(8,128)(2,1)} %copy-done.1, bf16[1024,2048]{1,0:T(8,128)(2,1)} %constant_dynamic-update-slice_fusion.2.down_ref.a_ref, bf16[1024,2048]{1,0:T(8,128)(2,1)} %collective-permute-done.28.down_ref.b_ref, bf16[1024,2048]{1,0:T(8,128)(2,1)} %get-tuple-element.237.slope_ref), custom_call_target="tpu_custom_call" | custom-call | flops 1000 | bytes 1000 | tf_op jit(solution)/shard_map/hidden_back/pallas_call | solution.py:403
  242.3 9.3 %convolution_convert_fusion.4.kept_x.kept_y.kept = bf16[1024,2048]{1,0:T(8,128)(2,1)} fusion(bf16[1024,2048]{1,0:T(8,128)(2,1)} %get-tuple-element.236.act_ref, bf16[1024,2048]{1,0:T(8,128)(2,1)} %copy-done.1), kind=kOutput, calls=%fused_computation.20 | convolution fusion | flops 4297064448 | bytes 10485760 | tf_op jit(solution)/shard_map/nd,nf->df/dot_general | solution.py:802
  259.8 9.6 %convolution_convert_fusion.3 = bf16[1024,2048]{1,0:T(8,128)(2,1)} fusion(bf16[1024,2048]{1,0:T(8,128)(2,1)} %get-tuple-element.275.hid_ref, bf16[1024,2048]{1,0:T(8,128)(2,1)} %get-tuple-element.253.rows_ref), kind=kOutput, calls=%fused_computation.19 | convolution fusion | flops 4297064448 | bytes 10485760 | tf_op jit(solution)/shard_map/nd,nf->df/dot_general | solution.py:802
  278.8 15.4 %mixed_backward.1.proj_ref = bf16[1024,1536]{1,0:T(8,128)(2,1)} custom-call(s32[1]{0:T(128)} %bitcast.11.me_ref, bf16[1024,512]{1,0:T(8,128)(2,1)} %get-tuple-element.255.q_ref, bf16[1024,512]{1,0:T(8,128)(2,1)} %get-tuple-element.256.k_ref, bf16[1024,512]{1,0:T(8,128)(2,1)} %get-tuple-element.257.v_ref, bf16[1024,2048]{1,0:T(8,128)(2,1)} %copy-done.1, ...), custom_call_target="tpu_custom_call" | custom-call | flops 1000 | bytes 1000 | tf_op jit(solution)/shard_map/mixed_backward/pallas_call | solution.py:668
  294.2 9.4 %convolution_convert_fusion.2.kept = bf16[1024,2048]{1,0:T(8,128)(2,1)} fusion(bf16[1024,2048]{1,0:T(8,128)(2,1)} %get-tuple-element.275.hid_ref, bf16[1024,2048]{1,0:T(8,128)(2,1)} %get-tuple-element.253.rows_ref), kind=kOutput, calls=%fused_computation.18 | convolution fusion | flops 4297064448 | bytes 10485760 | tf_op jit(solution)/shard_map/nd,nf->df/dot_general | solution.py:802
  328.5 23.5 %back.1 = (bf16[1024,2048]{1,0:T(8,128)(2,1)}, f32[8,2048]{1,0:T(8,128)}) custom-call(bf16[1024,2048]{1,0:T(8,128)(2,1)} %get-tuple-element.275.hid_ref, bf16[1024,1536]{1,0:T(8,128)(2,1)} %mixed_backward.1.proj_ref, bf16[2048,2048]{1,0:T(8,128)(2,1)} %constant_dynamic-update-slice_fusion.3.a_ref.qa_ref.ka_ref.va_ref.mix_ref.up_1.join_1, ...), custom_call_target="tpu_custom_call" | custom-call | flops 1000 | bytes 1000 | tf_op jit(solution)/shard_map/back/pallas_call | solution.py:483
  415.8 10.8 %collective-permute-done.51 = f32[1,10240]{1,0:T(1,128)S(1)} collective-permute-done((f32[1,10240]{1,0:T(1,128)S(1)}, f32[1,10240]{1,0:T(1,128)S(1)}, u32[]{:S(2)}, u32[]{:S(2)}) %collective-permute-start.51) | collective-permute-done | bytes 40992 | tf_op jit(solution)/shard_map/ppermute | solution.py:36
  461.1 5.1 %collective-permute-done.53.down_ref = bf16[256,2048]{1,0:T(8,128)(2,1)} collective-permute-done((bf16[256,2048]{1,0:T(8,128)(2,1)}, bf16[256,2048]{1,0:T(8,128)(2,1)}, u32[]{:S(2)}, u32[]{:S(2)}) %collective-permute-start.53) | collective-permute-done | bytes 1048608 | tf_op jit(solution)/shard_map/ppermute | solution.py:979
  469.8 5.9 %input_grad.1 = f32[256,2048]{1,0:T(8,128)} custom-call(s32[16]{0:T(128)} %fusion.27.index_ref, bf16[1024,2048]{1,0:T(8,128)(2,1)} %get-tuple-element.280.refs_0_.refs_1_.refs_2_.refs_3_.own_ref, bf16[256,2048]{1,0:T(8,128)(2,1)} %collective-permute-done.52.up_ref, bf16[256,2048]{1,0:T(8,128)(2,1)} %collective-permute-done.53.down_ref, ...), custom_call_target="tpu_custom_call" | custom-call | flops 1000 | bytes 1000 | tf_op jit(solution)/shard_map/input_grad/pallas_call | solution.py:620
  (317 shorter events, 236.5 us)
Async XLA Ops:
  4.7 40.2 %collective-permute-start.1 = (bf16[256,2048]{1,0:T(8,128)(2,1)}, bf16[256,2048]{1,0:T(8,128)(2,1)}, u32[]{:S(2)}, u32[]{:S(2)}) collective-permute-start(bf16[256,2048]{1,0:T(8,128)(2,1)} %columns.5.tok_ref), channel_id=1, source_target_pairs={{1,0},{2,1},{3,2},{5,4},{6,5},{7,6},{9,8},{10,9},{11,10},{13,12},{... | collective-permute-start | bytes 3145736 | tf_op jit(solution)/shard_map/ppermute | solution.py:970
  6.0 39.0 %collective-permute-start = (bf16[256,2048]{1,0:T(8,128)(2,1)}, bf16[256,2048]{1,0:T(8,128)(2,1)}, u32[]{:S(2)}, u32[]{:S(2)}) collective-permute-start(bf16[256,2048]{1,0:T(8,128)(2,1)} %columns.5.tok_ref), channel_id=1, source_target_pairs={{0,1},{1,2},{2,3},{4,5},{5,6},{6,7},{8,9},{9,10},{10,11},{12,13},{... | collective-permute-start | bytes 3145736 | tf_op jit(solution)/shard_map/ppermute | solution.py:969
  46.8 30.5 %collective-permute-start.8 = (bf16[256,2048]{1,0:T(8,128)(2,1)}, bf16[256,2048]{1,0:T(8,128)(2,1)}, u32[]{:S(2)}, u32[]{:S(2)}) collective-permute-start(bf16[256,2048]{1,0:T(8,128)(2,1)} %collective-permute-done), channel_id=1, source_target_pairs={{1,2},{2,3},{5,6},{6,7},{9,10},{10,11},{13,14},{14,15},{17,18},{18... | collective-permute-start | bytes 3145736 | tf_op jit(solution)/shard_map/ppermute | solution.py:969
  48.4 28.8 %collective-permute-start.9 = (bf16[256,2048]{1,0:T(8,128)(2,1)}, bf16[256,2048]{1,0:T(8,128)(2,1)}, u32[]{:S(2)}, u32[]{:S(2)}) collective-permute-start(bf16[256,2048]{1,0:T(8,128)(2,1)} %collective-permute-done.1), channel_id=1, source_target_pairs={{1,0},{2,1},{5,4},{6,5},{9,8},{10,9},{13,12},{14,13},{17,16},{18,1... | collective-permute-start | bytes 3145736 | tf_op jit(solution)/shard_map/ppermute | solution.py:970
  49.7 27.6 %collective-permute-start.11 = (bf16[256,2048]{1,0:T(8,128)(2,1)S(1)}, bf16[256,2048]{1,0:T(8,128)(2,1)S(1)}, u32[]{:S(2)}, u32[]{:S(2)}) collective-permute-start(bf16[256,2048]{1,0:T(8,128)(2,1)S(1)} %pad_maximum_fusion.4.refs_3_), channel_id=1, source_target_pairs={{0,16},{4,20},{8,24},{12,28},{16,0},{20,4},{24,8},{28,12},{1,17},{... | collective-permute-start | bytes 3145736 | tf_op jit(solution)/shard_map/ppermute | solution.py:36
  110.2 41.3 %collective-permute-start.19 = (bf16[256,2048]{1,0:T(8,128)(2,1)S(1)}, bf16[256,2048]{1,0:T(8,128)(2,1)}, u32[]{:S(2)}, u32[]{:S(2)}) collective-permute-start(bf16[256,2048]{1,0:T(8,128)(2,1)S(1)} %copy-done.9), channel_id=1, source_target_pairs={{1,0},{2,1},{3,2},{5,4},{6,5},{7,6},{9,8},{10,9},{11,10},{13,12},{... | collective-permute-start | bytes 3145736 | tf_op jit(solution)/shard_map/ppermute | solution.py:970
  111.6 39.9 %collective-permute-start.18 = (bf16[256,2048]{1,0:T(8,128)(2,1)S(1)}, bf16[256,2048]{1,0:T(8,128)(2,1)}, u32[]{:S(2)}, u32[]{:S(2)}) collective-permute-start(bf16[256,2048]{1,0:T(8,128)(2,1)S(1)} %copy-done.9), channel_id=1, source_target_pairs={{0,1},{1,2},{2,3},{4,5},{5,6},{6,7},{8,9},{9,10},{10,11},{12,13},{... | collective-permute-start | bytes 3145736 | tf_op jit(solution)/shard_map/ppermute | solution.py:969
  118.3 33.2 %collective-permute-start.21 = (bf16[256,2048]{1,0:T(8,128)(2,1)S(1)}, bf16[256,2048]{1,0:T(8,128)(2,1)}, u32[]{:S(2)}, u32[]{:S(2)}) collective-permute-start(bf16[256,2048]{1,0:T(8,128)(2,1)S(1)} %bitcast.49), channel_id=1, source_target_pairs={{0,16},{4,20},{8,24},{12,28},{16,0},{20,4},{24,8},{28,12},{1,17},{... | collective-permute-start | bytes 3145736 | tf_op jit(solution)/shard_map/ppermute | solution.py:36
  119.9 31.6 %collective-permute-start.20 = (bf16[256,2048]{1,0:T(8,128)(2,1)S(1)}, bf16[256,2048]{1,0:T(8,128)(2,1)}, u32[]{:S(2)}, u32[]{:S(2)}) collective-permute-start(bf16[256,2048]{1,0:T(8,128)(2,1)S(1)} %bitcast.50), channel_id=1, source_target_pairs={{0,8},{4,12},{8,0},{12,4},{16,24},{20,28},{24,16},{28,20},{1,9},{5... | collective-permute-start | bytes 3145736 | tf_op jit(solution)/shard_map/ppermute | solution.py:36
  152.2 26.7 %collective-permute-start.24 = (bf16[256,2048]{1,0:T(8,128)(2,1)}, bf16[256,2048]{1,0:T(8,128)(2,1)}, u32[]{:S(2)}, u32[]{:S(2)}) collective-permute-start(bf16[256,2048]{1,0:T(8,128)(2,1)} %collective-permute-done.19), channel_id=1, source_target_pairs={{1,0},{2,1},{5,4},{6,5},{9,8},{10,9},{13,12},{14,13},{17,16},{18,1... | collective-permute-start | bytes 3145736 | tf_op jit(solution)/shard_map/ppermute | solution.py:970
  183.7 27.8 %collective-permute-start.27 = (bf16[256,2048]{1,0:T(8,128)(2,1)}, bf16[256,2048]{1,0:T(8,128)(2,1)}, u32[]{:S(2)}, u32[]{:S(2)}) collective-permute-start(bf16[256,2048]{1,0:T(8,128)(2,1)} %collective-permute-done.24), channel_id=1, source_target_pairs={{1,0},{5,4},{9,8},{13,12},{17,16},{21,20},{25,24},{29,28}} | collective-permute-start | bytes 3145736 | tf_op jit(solution)/shard_map/ppermute | solution.py:970
  225.2 26.4 %collective-permute-start.31 = (bf16[1024,2048]{1,0:T(8,128)(2,1)}, bf16[1024,2048]{1,0:T(8,128)(2,1)}, u32[]{:S(2)}, u32[]{:S(2)}) collective-permute-start(bf16[1024,2048]{1,0:T(8,128)(2,1)} %convolution_convert_fusion.5), channel_id=1, source_target_pairs={{0,4},{4,0},{8,12},{12,8},{16,20},{20,16},{24,28},{28,24},{1,5},{5... | collective-permute-start | bytes 12582920 | tf_op jit(solution)/shard_map/ppermute | solution.py:36
  269.4 34.1 %collective-permute-start.36 = (bf16[1024,2048]{1,0:T(8,128)(2,1)}, bf16[1024,2048]{1,0:T(8,128)(2,1)}, u32[]{:S(2)}, u32[]{:S(2)}) collective-permute-start(bf16[1024,2048]{1,0:T(8,128)(2,1)} %convolution_convert_fusion.3), channel_id=1, source_target_pairs={{0,4},{4,0},{8,12},{12,8},{16,20},{20,16},{24,28},{28,24},{1,5},{5... | collective-permute-start | bytes 12582920 | tf_op jit(solution)/shard_map/ppermute | solution.py:36
  269.8 33.7 %collective-permute-start.32 = (bf16[256,2048]{1,0:T(8,128)(2,1)}, bf16[256,2048]{1,0:T(8,128)(2,1)S(1)}, u32[]{:S(2)}, u32[]{:S(2)}) collective-permute-start(bf16[256,2048]{1,0:T(8,128)(2,1)} %get-tuple-element.249), channel_id=1, source_target_pairs={{0,1},{1,2},{4,5},{5,6},{8,9},{9,10},{12,13},{13,14},{16,17},{17,1... | collective-permute-start | bytes 3145736 | tf_op jit(solution)/shard_map/ppermute | solution.py:978
  272.4 31.2 %collective-permute-start.33 = (bf16[256,2048]{1,0:T(8,128)(2,1)}, bf16[256,2048]{1,0:T(8,128)(2,1)}, u32[]{:S(2)}, u32[]{:S(2)}) collective-permute-start(bf16[256,2048]{1,0:T(8,128)(2,1)} %get-tuple-element.250), channel_id=1, source_target_pairs={{2,1},{3,2},{6,5},{7,6},{10,9},{11,10},{14,13},{15,14},{18,17},{19... | collective-permute-start | bytes 3145736 | tf_op jit(solution)/shard_map/ppermute | solution.py:979
  274.1 29.5 %collective-permute-start.34 = (bf16[256,2048]{1,0:T(8,128)(2,1)}, bf16[256,2048]{1,0:T(8,128)(2,1)S(1)}, u32[]{:S(2)}, u32[]{:S(2)}) collective-permute-start(bf16[256,2048]{1,0:T(8,128)(2,1)} %get-tuple-element.251), channel_id=1, source_target_pairs={{0,8},{4,12},{8,0},{12,4},{16,24},{20,28},{24,16},{28,20},{1,9},{5... | collective-permute-start | bytes 3145736 | tf_op jit(solution)/shard_map/ppermute | solution.py:36
  275.1 28.5 %collective-permute-start.35 = (bf16[256,2048]{1,0:T(8,128)(2,1)}, bf16[256,2048]{1,0:T(8,128)(2,1)S(1)}, u32[]{:S(2)}, u32[]{:S(2)}) collective-permute-start(bf16[256,2048]{1,0:T(8,128)(2,1)} %get-tuple-element.252), channel_id=1, source_target_pairs={{0,16},{4,20},{8,24},{12,28},{16,0},{20,4},{24,8},{28,12},{1,17},{... | collective-permute-start | bytes 3145736 | tf_op jit(solution)/shard_map/ppermute | solution.py:36
  320.6 31.4 %collective-permute-start.41 = (bf16[1024,2048]{1,0:T(8,128)(2,1)}, bf16[1024,2048]{1,0:T(8,128)(2,1)}, u32[]{:S(2)}, u32[]{:S(2)}) collective-permute-start(bf16[1024,2048]{1,0:T(8,128)(2,1)} %pad_maximum_fusion.2), channel_id=1, source_target_pairs={{0,4},{4,0},{8,12},{12,8},{16,20},{20,16},{24,28},{28,24},{1,5},{5... | collective-permute-start | bytes 12582920 | tf_op jit(solution)/shard_map/ppermute | solution.py:36
  320.6 31.4 %collective-permute-start.37 = (bf16[256,2048]{1,0:T(8,128)(2,1)}, bf16[256,2048]{1,0:T(8,128)(2,1)S(1)}, u32[]{:S(2)}, u32[]{:S(2)}) collective-permute-start(bf16[256,2048]{1,0:T(8,128)(2,1)} %get-tuple-element.270), channel_id=1, source_target_pairs={{0,1},{1,2},{2,3},{4,5},{5,6},{6,7},{8,9},{9,10},{10,11},{12,13},{... | collective-permute-start | bytes 3145736 | tf_op jit(solution)/shard_map/ppermute | solution.py:978
  323.6 28.5 %collective-permute-start.38 = (bf16[256,2048]{1,0:T(8,128)(2,1)}, bf16[256,2048]{1,0:T(8,128)(2,1)}, u32[]{:S(2)}, u32[]{:S(2)}) collective-permute-start(bf16[256,2048]{1,0:T(8,128)(2,1)} %get-tuple-element.271), channel_id=1, source_target_pairs={{1,0},{2,1},{3,2},{5,4},{6,5},{7,6},{9,8},{10,9},{11,10},{13,12},{... | collective-permute-start | bytes 3145736 | tf_op jit(solution)/shard_map/ppermute | solution.py:979
  324.9 27.2 %collective-permute-start.39 = (bf16[256,2048]{1,0:T(8,128)(2,1)}, bf16[256,2048]{1,0:T(8,128)(2,1)S(1)}, u32[]{:S(2)}, u32[]{:S(2)}) collective-permute-start(bf16[256,2048]{1,0:T(8,128)(2,1)} %pad_maximum_fusion.5), channel_id=1, source_target_pairs={{0,8},{4,12},{8,0},{12,4},{16,24},{20,28},{24,16},{28,20},{1,9},{5... | collective-permute-start | bytes 3145736 | tf_op jit(solution)/shard_map/ppermute | solution.py:36
  397.4 29.4 %collective-permute-start.47 = (bf16[256,2048]{1,0:T(8,128)(2,1)}, bf16[256,2048]{1,0:T(8,128)(2,1)}, u32[]{:S(2)}, u32[]{:S(2)}) collective-permute-start(bf16[256,2048]{1,0:T(8,128)(2,1)} %get-tuple-element.311), channel_id=1, source_target_pairs={{0,1},{1,2},{4,5},{5,6},{8,9},{9,10},{12,13},{13,14},{16,17},{17,1... | collective-permute-start | bytes 3145736 | tf_op jit(solution)/shard_map/ppermute | solution.py:978
  399.6 27.2 %collective-permute-start.48 = (bf16[256,2048]{1,0:T(8,128)(2,1)}, bf16[256,2048]{1,0:T(8,128)(2,1)}, u32[]{:S(2)}, u32[]{:S(2)}) collective-permute-start(bf16[256,2048]{1,0:T(8,128)(2,1)} %get-tuple-element.312), channel_id=1, source_target_pairs={{2,1},{3,2},{6,5},{7,6},{10,9},{11,10},{14,13},{15,14},{18,17},{19... | collective-permute-start | bytes 3145736 | tf_op jit(solution)/shard_map/ppermute | solution.py:979
  439.3 26.9 %collective-permute-start.53 = (bf16[256,2048]{1,0:T(8,128)(2,1)}, bf16[256,2048]{1,0:T(8,128)(2,1)}, u32[]{:S(2)}, u32[]{:S(2)}) collective-permute-start(bf16[256,2048]{1,0:T(8,128)(2,1)} %get-tuple-element.334), channel_id=1, source_target_pairs={{1,0},{2,1},{3,2},{5,4},{6,5},{7,6},{9,8},{10,9},{11,10},{13,12},{... | collective-permute-start | bytes 3145736 | tf_op jit(solution)/shard_map/ppermute | solution.py:979
  (76 other events, 1145.9 us)

commit v8 on v7

--- a/solution.py
+++ b/solution.py
@@ -369,7 +369,7 @@
     half = pl.BlockSpec((width // 2, tile), lambda j: (0, j))
     made = pl.BlockSpec((count, tile), lambda j: (0, j))
     return pl.pallas_call(
-        functools.partial(hidden_kernel, step=256),
+        functools.partial(hidden_kernel, step=512),
         out_shape=(jax.ShapeDtypeStruct((count, out), BF16),) * 2,
         grid=(out // tile,),
         in_specs=[
@@ -401,7 +401,7 @@
     half = pl.BlockSpec((top.shape[0], tile), lambda j: (0, j))
     made = pl.BlockSpec((count, tile), lambda j: (0, j))
     return pl.pallas_call(
-        functools.partial(slope_kernel, step=256),
+        functools.partial(slope_kernel, step=512),
         out_shape=(jax.ShapeDtypeStruct((count, out), BF16), jax.ShapeDtypeStruct((1, out), F32)),
         grid=(out // tile,),
         in_specs=[pl.BlockSpec((count, width), lambda j: (0, 0)), half, half, made],
@@ -426,7 +426,7 @@
     tile = 256
     spot = mixed.shape[1] // inner - 1
     return pl.pallas_call(
-        functools.partial(branch_kernel, step=256),
+        functools.partial(branch_kernel, step=512),
         out_shape=jax.ShapeDtypeStruct((count, width), BF16),
         grid=(width // tile,),
         in_specs=[
@@ -481,7 +481,7 @@
         return [low, high]
 
     return pl.pallas_call(
-        functools.partial(back_kernel, step=256, tiles=tiles),
+        functools.partial(back_kernel, step=512, tiles=tiles),
         out_shape=(jax.ShapeDtypeStruct((count, 2 * width), BF16), jax.ShapeDtypeStruct((8, 2 * width), F32)),
         grid=(2 * tiles,),
         in_specs=[pl.BlockSpec((count, units), whole), pl.BlockSpec((count, joined), whole)]

time: 483 us -> 483 us (level)
  no operation moved by 1% of the time
where the time goes in v8:
time: 483 us; the launch traced here: 475 us
  Pallas kernels  177 us (37%)
  starting transfers between devices  97.8 us (20%)
  waiting for transfers between devices  66.4 us (14%)
  other arithmetic  46 us (10%)
  matrix products  45.5 us (9%)
  local copies, waits for them, and re-layouts  40.7 us (8%)
    ppermute x35, starting transfers between devices, xor_shift(): return lax.ppermute(values, axis, [(i, i ^ bit) for i in range(size)])  48.4 us
    ppermute x35, waiting for transfers between devices, xor_shift(): return lax.ppermute(values, axis, [(i, i ^ bit) for i in range(size)])  46.3 us
    dot_general x8, matrix products, grad_half(): jnp.einsum('nd,nf->df', chosen, columns, preferred_element_type=F32)  45.5 us
    pallas_call x1, Pallas kernels, back_whole(): pl.pallas_call(functools.partial(back_kernel, step=512, tiles=tiles), out...  23.5 us
    pallas_call x2, Pallas kernels, branch_half(): pl.pallas_call(functools.partial(branch_kernel, step=512), out_shape=jax....  20.1 us
    pallas_call x6, Pallas kernels, step_terms(): pl.pallas_call(terms_kernel, out_shape=(jax.ShapeDtypeStruct((rows, 2 * w...  18.7 us
    ppermute x6, starting transfers between devices, gather_step(): up = lax.ppermute(up, 'tensor', [(i, i + 1) for i in range(s, 3)])  18.3 us
    unnamed x87, local copies, waits for them, and re-layouts  17.8 us
  transfers between devices with their start and end apart: 59, of which 13 were waited for; matrix products, arithmetic and copies ran while one was open for 15% of the time, Pallas kernels for 31%

profile of v8, /device:TPU:0, one launch (start us, length us, event | category | flops | bytes accessed | tf_op | source)
XLA Modules:
  0.0 475.5 jit_solution(4630872905388594327)
XLA Ops:
  6.0 6.6 %collective-permute-start = (bf16[256,2048]{1,0:T(8,128)(2,1)}, bf16[256,2048]{1,0:T(8,128)(2,1)}, u32[]{:S(2)}, u32[]{:S(2)}) collective-permute-start(bf16[256,2048]{1,0:T(8,128)(2,1)} %columns.5.tok_ref), channel_id=1, source_target_pairs={{0,1},{1,2},{2,3},{4,5},{5,6},{6,7},{8,9},{9,10},{10,11},{12,13},{... | collective-permute-start | bytes 3145736 | tf_op jit(solution)/shard_map/ppermute | solution.py:969
  27.2 10.2 %collective-permute-done.3.refs_1_ = bf16[256,2048]{1,0:T(8,128)(2,1)S(1)} collective-permute-done((bf16[256,2048]{1,0:T(8,128)(2,1)}, bf16[256,2048]{1,0:T(8,128)(2,1)S(1)}, u32[]{:S(2)}, u32[]{:S(2)}) %collective-permute-start.3) | collective-permute-done | bytes 1048608 | tf_op jit(solution)/shard_map/ppermute | solution.py:36
  52.8 5.1 %collective-permute-start.12 = (bf16[32,832]{1,0:T(8,128)(2,1)S(1)}, bf16[32,832]{1,0:T(8,128)(2,1)S(1)}, u32[]{:S(2)}, u32[]{:S(2)}) collective-permute-start(bf16[32,832]{1,0:T(8,128)(2,1)S(1)} %add_add_fusion), channel_id=1, source_target_pairs={{0,1},{1,0},{2,3},{3,2},{4,5},{5,4},{6,7},{7,6},{8,9},{9,8},{10,11... | collective-permute-start | bytes 159752 | tf_op jit(solution)/shard_map/ppermute | solution.py:36
  60.8 15.8 %collective-permute-done.12 = bf16[32,832]{1,0:T(8,128)(2,1)S(1)} collective-permute-done((bf16[32,832]{1,0:T(8,128)(2,1)S(1)}, bf16[32,832]{1,0:T(8,128)(2,1)S(1)}, u32[]{:S(2)}, u32[]{:S(2)}) %collective-permute-start.12) | collective-permute-done | bytes 53280 | tf_op jit(solution)/shard_map/ppermute | solution.py:36
  82.0 7.4 %collective-permute-start.17 = (bf16[32,832]{1,0:T(8,128)(2,1)S(1)}, bf16[32,832]{1,0:T(8,128)(2,1)S(1)}, u32[]{:S(2)}, u32[]{:S(2)}) collective-permute-start(bf16[32,832]{1,0:T(8,128)(2,1)S(1)} %add.196), channel_id=1, source_target_pairs={{0,2},{1,3},{2,0},{3,1},{4,6},{5,7},{6,4},{7,5},{8,10},{9,11},{10,... | collective-permute-start | bytes 159752 | tf_op jit(solution)/shard_map/ppermute | solution.py:36
  89.5 6.5 %lay.2 = bf16[2048,2048]{1,0:T(8,128)(2,1)} custom-call(bf16[256,2048]{1,0:T(8,128)(2,1)} %refs_0_.1, bf16[256,2048]{1,0:T(8,128)(2,1)} %copy-done.22, bf16[256,2048]{1,0:T(8,128)(2,1)} %collective-permute-done.4.refs_2_, bf16[256,2048]{1,0:T(8,128)(2,1)} %copy-done.13, bf16[256,2048]{1,0:T(8,128)(2,1)} %collective-permute-done.10.refs_4_, ...), custom_call_target="tpu_custom_call" | custom-call | flops 1000 | bytes 1000 | tf_op jit(solution)/shard_map/lay/pallas_call | solution.py:519
  98.3 4.8 %collective-permute-done.14 = bf16[256,2048]{1,0:T(8,128)(2,1)} collective-permute-done((bf16[256,2048]{1,0:T(8,128)(2,1)}, bf16[256,2048]{1,0:T(8,128)(2,1)}, u32[]{:S(2)}, u32[]{:S(2)}) %collective-permute-start.14) | collective-permute-done | bytes 1048608 | tf_op jit(solution)/shard_map/ppermute | solution.py:970
  111.6 6.1 %collective-permute-start.18 = (bf16[256,2048]{1,0:T(8,128)(2,1)S(1)}, bf16[256,2048]{1,0:T(8,128)(2,1)}, u32[]{:S(2)}, u32[]{:S(2)}) collective-permute-start(bf16[256,2048]{1,0:T(8,128)(2,1)S(1)} %copy-done.9), channel_id=1, source_target_pairs={{0,1},{1,2},{2,3},{4,5},{5,6},{6,7},{8,9},{9,10},{10,11},{12,13},{... | collective-permute-start | bytes 3145736 | tf_op jit(solution)/shard_map/ppermute | solution.py:969
  129.2 4.9 %fusion.7 = (bf16[1024,2048]{1,0:T(8,128)(2,1)}, bf16[1024,2048]{1,0:T(8,128)(2,1)}) fusion(bf16[1024,2048]{1,0:T(8,128)(2,1)S(1)} %get-tuple-element.369.tok_ref, f32[2048]{0:T(1024)S(1)} %bitcast.65, f32[2048]{0:T(1024)S(1)} %bitcast.66, f32[1024]{0:T(1024)S(1)} %add_rsqrt_fusion, f32[1024]{0:T(1024)S(1)} %broadcast_multiply_fusion, f32[2048]{0:T(1024)S(1)} %bitcast.67, ...), kind=kLoop, calls=%fused_computation.9 | loop fusion | flops 18874368 | bytes 12623872 | tf_op jit(solution)/shard_map/convert_element_type | solution.py:767
  134.2 17.5 %hidden.1 = (bf16[1024,2048]{1,0:T(8,128)(2,1)}, bf16[1024,2048]{1,0:T(8,128)(2,1)}) custom-call(bf16[1024,2048]{1,0:T(8,128)(2,1)} %get-tuple-element.253.rows_ref, bf16[2048,2048]{1,0:T(8,128)(2,1)} %constant_dynamic-update-slice_fusion.3.a_ref.qa_ref.ka_ref.va_ref.mix_ref.up_1.join_1, ...), custom_call_target="tpu_custom_call" | custom-call | flops 1000 | bytes 1000 | tf_op jit(solution)/shard_map/hidden/pallas_call | solution.py:371
  159.4 17.7 %joined_forward.1 = (bf16[1024,512]{1,0:T(8,128)(2,1)}, bf16[1024,512]{1,0:T(8,128)(2,1)}, bf16[1024,512]{1,0:T(8,128)(2,1)}, bf16[1024,512]{1,0:T(8,128)(2,1)}, f32[2,1024,128]{2,1,0:T(8,128)}) custom-call(s32[1]{0:T(128)} %bitcast.11.me_ref, bf16[1024,2048]{1,0:T(8,128)(2,1)} %get-tuple-element.292.rows_ref, ...), custom_call_target="tpu_custom_call" | custom-call | flops 1000 | bytes 1000 | tf_op jit(solution)/shard_map/joined_forward/pallas_call | solution.py:645
  185.3 10.0 %branches.2.refs_0_.refs_2_ = bf16[1024,1024]{1,0:T(8,128)(2,1)} custom-call(bf16[1024,512]{1,0:T(8,128)(2,1)} %get-tuple-element.295.att_ref, bf16[2048,2048]{1,0:T(8,128)(2,1)} %constant_dynamic-update-slice_fusion.3.a_ref.qa_ref.ka_ref.va_ref.mix_ref.up_1.join_1, bf16[1024,2048]{1,0:T(8,128)(2,1)} %get-tuple-element.236.act_ref, ...), custom_call_target="tpu_custom_call" | custom-call | flops 1000 | bytes 1000 | tf_op jit(solution)/shard_map/branches/pallas_call | solution.py:428
  196.7 10.0 %branches.3.refs_1_.refs_3_ = bf16[1024,1024]{1,0:T(8,128)(2,1)} custom-call(bf16[1024,512]{1,0:T(8,128)(2,1)} %get-tuple-element.295.att_ref, bf16[2048,2048]{1,0:T(8,128)(2,1)} %collective-permute-done.22.b_ref.qb_ref.kb_ref.vb_ref.mix_ref.up_2.join_2, bf16[1024,2048]{1,0:T(8,128)(2,1)} %get-tuple-element.236.act_ref, ...), custom_call_target="tpu_custom_call" | custom-call | flops 1000 | bytes 1000 | tf_op jit(solution)/shard_map/branches/pallas_call | solution.py:428
  206.7 5.0 %collective-permute-done.27 = bf16[256,2048]{1,0:T(8,128)(2,1)} collective-permute-done((bf16[256,2048]{1,0:T(8,128)(2,1)}, bf16[256,2048]{1,0:T(8,128)(2,1)}, u32[]{:S(2)}, u32[]{:S(2)}) %collective-permute-start.27) | collective-permute-done | bytes 1048608 | tf_op jit(solution)/shard_map/ppermute | solution.py:970
  219.3 6.3 %convolution_convert_fusion.5 = bf16[1024,2048]{1,0:T(8,128)(2,1)} fusion(bf16[1024,2048]{1,0:T(8,128)(2,1)S(1)} %copy-done.6, bf16[1024,2048]{1,0:T(8,128)(2,1)S(1)} %pad_maximum_fusion.1.rows_ref.g_ref), kind=kOutput, calls=%fused_computation.21 | convolution fusion | flops 4297064448 | bytes 10485760 | tf_op jit(solution)/shard_map/nd,nf->df/dot_general | solution.py:802
  227.8 14.6 %hidden_back.1 = (bf16[1024,2048]{1,0:T(8,128)(2,1)}, f32[1,2048]{1,0:T(1,128)}) custom-call(bf16[1024,2048]{1,0:T(8,128)(2,1)} %copy-done.1, bf16[1024,2048]{1,0:T(8,128)(2,1)} %constant_dynamic-update-slice_fusion.2.down_ref.a_ref, bf16[1024,2048]{1,0:T(8,128)(2,1)} %collective-permute-done.28.down_ref.b_ref, bf16[1024,2048]{1,0:T(8,128)(2,1)} %get-tuple-element.237.slope_ref), custom_call_target="tpu_custom_call" | custom-call | flops 1000 | bytes 1000 | tf_op jit(solution)/shard_map/hidden_back/pallas_call | solution.py:403
  242.5 9.3 %convolution_convert_fusion.4.kept_x.kept_y.kept = bf16[1024,2048]{1,0:T(8,128)(2,1)} fusion(bf16[1024,2048]{1,0:T(8,128)(2,1)} %get-tuple-element.236.act_ref, bf16[1024,2048]{1,0:T(8,128)(2,1)} %copy-done.1), kind=kOutput, calls=%fused_computation.20 | convolution fusion | flops 4297064448 | bytes 10485760 | tf_op jit(solution)/shard_map/nd,nf->df/dot_general | solution.py:802
  260.0 9.6 %convolution_convert_fusion.3 = bf16[1024,2048]{1,0:T(8,128)(2,1)} fusion(bf16[1024,2048]{1,0:T(8,128)(2,1)} %get-tuple-element.275.hid_ref, bf16[1024,2048]{1,0:T(8,128)(2,1)} %get-tuple-element.253.rows_ref), kind=kOutput, calls=%fused_computation.19 | convolution fusion | flops 4297064448 | bytes 10485760 | tf_op jit(solution)/shard_map/nd,nf->df/dot_general | solution.py:802
  279.2 15.6 %mixed_backward.1.proj_ref = bf16[1024,1536]{1,0:T(8,128)(2,1)} custom-call(s32[1]{0:T(128)} %bitcast.11.me_ref, bf16[1024,512]{1,0:T(8,128)(2,1)} %get-tuple-element.255.q_ref, bf16[1024,512]{1,0:T(8,128)(2,1)} %get-tuple-element.256.k_ref, bf16[1024,512]{1,0:T(8,128)(2,1)} %get-tuple-element.257.v_ref, bf16[1024,2048]{1,0:T(8,128)(2,1)} %copy-done.1, ...), custom_call_target="tpu_custom_call" | custom-call | flops 1000 | bytes 1000 | tf_op jit(solution)/shard_map/mixed_backward/pallas_call | solution.py:668
  294.7 9.4 %convolution_convert_fusion.2.kept = bf16[1024,2048]{1,0:T(8,128)(2,1)} fusion(bf16[1024,2048]{1,0:T(8,128)(2,1)} %get-tuple-element.275.hid_ref, bf16[1024,2048]{1,0:T(8,128)(2,1)} %get-tuple-element.253.rows_ref), kind=kOutput, calls=%fused_computation.18 | convolution fusion | flops 4297064448 | bytes 10485760 | tf_op jit(solution)/shard_map/nd,nf->df/dot_general | solution.py:802
  328.0 23.5 %back.1 = (bf16[1024,2048]{1,0:T(8,128)(2,1)}, f32[8,2048]{1,0:T(8,128)}) custom-call(bf16[1024,2048]{1,0:T(8,128)(2,1)} %get-tuple-element.275.hid_ref, bf16[1024,1536]{1,0:T(8,128)(2,1)} %mixed_backward.1.proj_ref, bf16[2048,2048]{1,0:T(8,128)(2,1)} %constant_dynamic-update-slice_fusion.3.a_ref.qa_ref.ka_ref.va_ref.mix_ref.up_1.join_1, ...), custom_call_target="tpu_custom_call" | custom-call | flops 1000 | bytes 1000 | tf_op jit(solution)/shard_map/back/pallas_call | solution.py:483
  415.4 10.8 %collective-permute-done.51 = f32[1,10240]{1,0:T(1,128)S(1)} collective-permute-done((f32[1,10240]{1,0:T(1,128)S(1)}, f32[1,10240]{1,0:T(1,128)S(1)}, u32[]{:S(2)}, u32[]{:S(2)}) %collective-permute-start.51) | collective-permute-done | bytes 40992 | tf_op jit(solution)/shard_map/ppermute | solution.py:36
  460.6 5.1 %collective-permute-done.53.down_ref = bf16[256,2048]{1,0:T(8,128)(2,1)} collective-permute-done((bf16[256,2048]{1,0:T(8,128)(2,1)}, bf16[256,2048]{1,0:T(8,128)(2,1)}, u32[]{:S(2)}, u32[]{:S(2)}) %collective-permute-start.53) | collective-permute-done | bytes 1048608 | tf_op jit(solution)/shard_map/ppermute | solution.py:979
  469.3 5.9 %input_grad.1 = f32[256,2048]{1,0:T(8,128)} custom-call(s32[16]{0:T(128)} %fusion.27.index_ref, bf16[1024,2048]{1,0:T(8,128)(2,1)} %get-tuple-element.280.refs_0_.refs_1_.refs_2_.refs_3_.own_ref, bf16[256,2048]{1,0:T(8,128)(2,1)} %collective-permute-done.52.up_ref, bf16[256,2048]{1,0:T(8,128)(2,1)} %collective-permute-done.53.down_ref, ...), custom_call_target="tpu_custom_call" | custom-call | flops 1000 | bytes 1000 | tf_op jit(solution)/shard_map/input_grad/pallas_call | solution.py:620
  (317 shorter events, 235.8 us)
Async XLA Ops:
  4.7 40.2 %collective-permute-start.1 = (bf16[256,2048]{1,0:T(8,128)(2,1)}, bf16[256,2048]{1,0:T(8,128)(2,1)}, u32[]{:S(2)}, u32[]{:S(2)}) collective-permute-start(bf16[256,2048]{1,0:T(8,128)(2,1)} %columns.5.tok_ref), channel_id=1, source_target_pairs={{1,0},{2,1},{3,2},{5,4},{6,5},{7,6},{9,8},{10,9},{11,10},{13,12},{... | collective-permute-start | bytes 3145736 | tf_op jit(solution)/shard_map/ppermute | solution.py:970
  6.0 39.0 %collective-permute-start = (bf16[256,2048]{1,0:T(8,128)(2,1)}, bf16[256,2048]{1,0:T(8,128)(2,1)}, u32[]{:S(2)}, u32[]{:S(2)}) collective-permute-start(bf16[256,2048]{1,0:T(8,128)(2,1)} %columns.5.tok_ref), channel_id=1, source_target_pairs={{0,1},{1,2},{2,3},{4,5},{5,6},{6,7},{8,9},{9,10},{10,11},{12,13},{... | collective-permute-start | bytes 3145736 | tf_op jit(solution)/shard_map/ppermute | solution.py:969
  46.8 30.5 %collective-permute-start.8 = (bf16[256,2048]{1,0:T(8,128)(2,1)}, bf16[256,2048]{1,0:T(8,128)(2,1)}, u32[]{:S(2)}, u32[]{:S(2)}) collective-permute-start(bf16[256,2048]{1,0:T(8,128)(2,1)} %collective-permute-done), channel_id=1, source_target_pairs={{1,2},{2,3},{5,6},{6,7},{9,10},{10,11},{13,14},{14,15},{17,18},{18... | collective-permute-start | bytes 3145736 | tf_op jit(solution)/shard_map/ppermute | solution.py:969
  48.4 28.8 %collective-permute-start.9 = (bf16[256,2048]{1,0:T(8,128)(2,1)}, bf16[256,2048]{1,0:T(8,128)(2,1)}, u32[]{:S(2)}, u32[]{:S(2)}) collective-permute-start(bf16[256,2048]{1,0:T(8,128)(2,1)} %collective-permute-done.1), channel_id=1, source_target_pairs={{1,0},{2,1},{5,4},{6,5},{9,8},{10,9},{13,12},{14,13},{17,16},{18,1... | collective-permute-start | bytes 3145736 | tf_op jit(solution)/shard_map/ppermute | solution.py:970
  49.7 27.6 %collective-permute-start.11 = (bf16[256,2048]{1,0:T(8,128)(2,1)S(1)}, bf16[256,2048]{1,0:T(8,128)(2,1)S(1)}, u32[]{:S(2)}, u32[]{:S(2)}) collective-permute-start(bf16[256,2048]{1,0:T(8,128)(2,1)S(1)} %pad_maximum_fusion.4.refs_3_), channel_id=1, source_target_pairs={{0,16},{4,20},{8,24},{12,28},{16,0},{20,4},{24,8},{28,12},{1,17},{... | collective-permute-start | bytes 3145736 | tf_op jit(solution)/shard_map/ppermute | solution.py:36
  107.8 26.3 %collective-permute-start.22 = (bf16[2048,2048]{1,0:T(8,128)(2,1)}, bf16[2048,2048]{1,0:T(8,128)(2,1)}, u32[]{:S(2)}, u32[]{:S(2)}) collective-permute-start(bf16[2048,2048]{1,0:T(8,128)(2,1)} %constant_dynamic-update-slice_fusion.3.a_ref.qa_ref.ka_ref.va_ref.mix_ref.up_1.join_1), channel_id=1, source_target_pairs={{0,4},{4,0},{8,12},{12,8},{16,20},{20,16},{24,28},{28,24},{1,5},{5... | collective-permute-start | bytes 25165832 | tf_op jit(solution)/shard_map/ppermute | solution.py:36
  110.2 41.5 %collective-permute-start.19 = (bf16[256,2048]{1,0:T(8,128)(2,1)S(1)}, bf16[256,2048]{1,0:T(8,128)(2,1)}, u32[]{:S(2)}, u32[]{:S(2)}) collective-permute-start(bf16[256,2048]{1,0:T(8,128)(2,1)S(1)} %copy-done.9), channel_id=1, source_target_pairs={{1,0},{2,1},{3,2},{5,4},{6,5},{7,6},{9,8},{10,9},{11,10},{13,12},{... | collective-permute-start | bytes 3145736 | tf_op jit(solution)/shard_map/ppermute | solution.py:970
  111.6 40.0 %collective-permute-start.18 = (bf16[256,2048]{1,0:T(8,128)(2,1)S(1)}, bf16[256,2048]{1,0:T(8,128)(2,1)}, u32[]{:S(2)}, u32[]{:S(2)}) collective-permute-start(bf16[256,2048]{1,0:T(8,128)(2,1)S(1)} %copy-done.9), channel_id=1, source_target_pairs={{0,1},{1,2},{2,3},{4,5},{5,6},{6,7},{8,9},{9,10},{10,11},{12,13},{... | collective-permute-start | bytes 3145736 | tf_op jit(solution)/shard_map/ppermute | solution.py:969
  118.5 33.1 %collective-permute-start.21 = (bf16[256,2048]{1,0:T(8,128)(2,1)S(1)}, bf16[256,2048]{1,0:T(8,128)(2,1)}, u32[]{:S(2)}, u32[]{:S(2)}) collective-permute-start(bf16[256,2048]{1,0:T(8,128)(2,1)S(1)} %bitcast.49), channel_id=1, source_target_pairs={{0,16},{4,20},{8,24},{12,28},{16,0},{20,4},{24,8},{28,12},{1,17},{... | collective-permute-start | bytes 3145736 | tf_op jit(solution)/shard_map/ppermute | solution.py:36
  120.1 31.5 %collective-permute-start.20 = (bf16[256,2048]{1,0:T(8,128)(2,1)S(1)}, bf16[256,2048]{1,0:T(8,128)(2,1)}, u32[]{:S(2)}, u32[]{:S(2)}) collective-permute-start(bf16[256,2048]{1,0:T(8,128)(2,1)S(1)} %bitcast.50), channel_id=1, source_target_pairs={{0,8},{4,12},{8,0},{12,4},{16,24},{20,28},{24,16},{28,20},{1,9},{5... | collective-permute-start | bytes 3145736 | tf_op jit(solution)/shard_map/ppermute | solution.py:36
  152.4 26.7 %collective-permute-start.24 = (bf16[256,2048]{1,0:T(8,128)(2,1)}, bf16[256,2048]{1,0:T(8,128)(2,1)}, u32[]{:S(2)}, u32[]{:S(2)}) collective-permute-start(bf16[256,2048]{1,0:T(8,128)(2,1)} %collective-permute-done.19), channel_id=1, source_target_pairs={{1,0},{2,1},{5,4},{6,5},{9,8},{10,9},{13,12},{14,13},{17,16},{18,1... | collective-permute-start | bytes 3145736 | tf_op jit(solution)/shard_map/ppermute | solution.py:970
  183.8 27.9 %collective-permute-start.27 = (bf16[256,2048]{1,0:T(8,128)(2,1)}, bf16[256,2048]{1,0:T(8,128)(2,1)}, u32[]{:S(2)}, u32[]{:S(2)}) collective-permute-start(bf16[256,2048]{1,0:T(8,128)(2,1)} %collective-permute-done.24), channel_id=1, source_target_pairs={{1,0},{5,4},{9,8},{13,12},{17,16},{21,20},{25,24},{29,28}} | collective-permute-start | bytes 3145736 | tf_op jit(solution)/shard_map/ppermute | solution.py:970
  269.6 34.5 %collective-permute-start.36 = (bf16[1024,2048]{1,0:T(8,128)(2,1)}, bf16[1024,2048]{1,0:T(8,128)(2,1)}, u32[]{:S(2)}, u32[]{:S(2)}) collective-permute-start(bf16[1024,2048]{1,0:T(8,128)(2,1)} %convolution_convert_fusion.3), channel_id=1, source_target_pairs={{0,4},{4,0},{8,12},{12,8},{16,20},{20,16},{24,28},{28,24},{1,5},{5... | collective-permute-start | bytes 12582920 | tf_op jit(solution)/shard_map/ppermute | solution.py:36
  270.0 34.1 %collective-permute-start.32 = (bf16[256,2048]{1,0:T(8,128)(2,1)}, bf16[256,2048]{1,0:T(8,128)(2,1)S(1)}, u32[]{:S(2)}, u32[]{:S(2)}) collective-permute-start(bf16[256,2048]{1,0:T(8,128)(2,1)} %get-tuple-element.249), channel_id=1, source_target_pairs={{0,1},{1,2},{4,5},{5,6},{8,9},{9,10},{12,13},{13,14},{16,17},{17,1... | collective-permute-start | bytes 3145736 | tf_op jit(solution)/shard_map/ppermute | solution.py:978
  272.7 31.3 %collective-permute-start.33 = (bf16[256,2048]{1,0:T(8,128)(2,1)}, bf16[256,2048]{1,0:T(8,128)(2,1)}, u32[]{:S(2)}, u32[]{:S(2)}) collective-permute-start(bf16[256,2048]{1,0:T(8,128)(2,1)} %get-tuple-element.250), channel_id=1, source_target_pairs={{2,1},{3,2},{6,5},{7,6},{10,9},{11,10},{14,13},{15,14},{18,17},{19... | collective-permute-start | bytes 3145736 | tf_op jit(solution)/shard_map/ppermute | solution.py:979
  274.4 29.7 %collective-permute-start.34 = (bf16[256,2048]{1,0:T(8,128)(2,1)}, bf16[256,2048]{1,0:T(8,128)(2,1)S(1)}, u32[]{:S(2)}, u32[]{:S(2)}) collective-permute-start(bf16[256,2048]{1,0:T(8,128)(2,1)} %get-tuple-element.251), channel_id=1, source_target_pairs={{0,8},{4,12},{8,0},{12,4},{16,24},{20,28},{24,16},{28,20},{1,9},{5... | collective-permute-start | bytes 3145736 | tf_op jit(solution)/shard_map/ppermute | solution.py:36
  275.4 28.7 %collective-permute-start.35 = (bf16[256,2048]{1,0:T(8,128)(2,1)}, bf16[256,2048]{1,0:T(8,128)(2,1)S(1)}, u32[]{:S(2)}, u32[]{:S(2)}) collective-permute-start(bf16[256,2048]{1,0:T(8,128)(2,1)} %get-tuple-element.252), channel_id=1, source_target_pairs={{0,16},{4,20},{8,24},{12,28},{16,0},{20,4},{24,8},{28,12},{1,17},{... | collective-permute-start | bytes 3145736 | tf_op jit(solution)/shard_map/ppermute | solution.py:36
  321.1 30.5 %collective-permute-start.41 = (bf16[1024,2048]{1,0:T(8,128)(2,1)}, bf16[1024,2048]{1,0:T(8,128)(2,1)}, u32[]{:S(2)}, u32[]{:S(2)}) collective-permute-start(bf16[1024,2048]{1,0:T(8,128)(2,1)} %pad_maximum_fusion.2), channel_id=1, source_target_pairs={{0,4},{4,0},{8,12},{12,8},{16,20},{20,16},{24,28},{28,24},{1,5},{5... | collective-permute-start | bytes 12582920 | tf_op jit(solution)/shard_map/ppermute | solution.py:36
  321.1 30.4 %collective-permute-start.37 = (bf16[256,2048]{1,0:T(8,128)(2,1)}, bf16[256,2048]{1,0:T(8,128)(2,1)S(1)}, u32[]{:S(2)}, u32[]{:S(2)}) collective-permute-start(bf16[256,2048]{1,0:T(8,128)(2,1)} %get-tuple-element.270), channel_id=1, source_target_pairs={{0,1},{1,2},{2,3},{4,5},{5,6},{6,7},{8,9},{9,10},{10,11},{12,13},{... | collective-permute-start | bytes 3145736 | tf_op jit(solution)/shard_map/ppermute | solution.py:978
  323.1 28.4 %collective-permute-start.38 = (bf16[256,2048]{1,0:T(8,128)(2,1)}, bf16[256,2048]{1,0:T(8,128)(2,1)}, u32[]{:S(2)}, u32[]{:S(2)}) collective-permute-start(bf16[256,2048]{1,0:T(8,128)(2,1)} %get-tuple-element.271), channel_id=1, source_target_pairs={{1,0},{2,1},{3,2},{5,4},{6,5},{7,6},{9,8},{10,9},{11,10},{13,12},{... | collective-permute-start | bytes 3145736 | tf_op jit(solution)/shard_map/ppermute | solution.py:979
  324.4 27.2 %collective-permute-start.39 = (bf16[256,2048]{1,0:T(8,128)(2,1)}, bf16[256,2048]{1,0:T(8,128)(2,1)S(1)}, u32[]{:S(2)}, u32[]{:S(2)}) collective-permute-start(bf16[256,2048]{1,0:T(8,128)(2,1)} %pad_maximum_fusion.5), channel_id=1, source_target_pairs={{0,8},{4,12},{8,0},{12,4},{16,24},{20,28},{24,16},{28,20},{1,9},{5... | collective-permute-start | bytes 3145736 | tf_op jit(solution)/shard_map/ppermute | solution.py:36
  396.9 29.4 %collective-permute-start.47 = (bf16[256,2048]{1,0:T(8,128)(2,1)}, bf16[256,2048]{1,0:T(8,128)(2,1)}, u32[]{:S(2)}, u32[]{:S(2)}) collective-permute-start(bf16[256,2048]{1,0:T(8,128)(2,1)} %get-tuple-element.311), channel_id=1, source_target_pairs={{0,1},{1,2},{4,5},{5,6},{8,9},{9,10},{12,13},{13,14},{16,17},{17,1... | collective-permute-start | bytes 3145736 | tf_op jit(solution)/shard_map/ppermute | solution.py:978
  399.1 27.2 %collective-permute-start.48 = (bf16[256,2048]{1,0:T(8,128)(2,1)}, bf16[256,2048]{1,0:T(8,128)(2,1)}, u32[]{:S(2)}, u32[]{:S(2)}) collective-permute-start(bf16[256,2048]{1,0:T(8,128)(2,1)} %get-tuple-element.312), channel_id=1, source_target_pairs={{2,1},{3,2},{6,5},{7,6},{10,9},{11,10},{14,13},{15,14},{18,17},{19... | collective-permute-start | bytes 3145736 | tf_op jit(solution)/shard_map/ppermute | solution.py:979
  438.8 26.9 %collective-permute-start.53 = (bf16[256,2048]{1,0:T(8,128)(2,1)}, bf16[256,2048]{1,0:T(8,128)(2,1)}, u32[]{:S(2)}, u32[]{:S(2)}) collective-permute-start(bf16[256,2048]{1,0:T(8,128)(2,1)} %get-tuple-element.334), channel_id=1, source_target_pairs={{1,0},{2,1},{3,2},{5,4},{6,5},{7,6},{9,8},{10,9},{11,10},{13,12},{... | collective-permute-start | bytes 3145736 | tf_op jit(solution)/shard_map/ppermute | solution.py:979
  (76 other events, 1145.7 us)
